TPU v7x, 32 devices: a whole 2x2x4 slice. The times are simulated.
32 devices in a mesh: fsdp: 2 (over x), ctx: 4 (over y, core), tp: 4 (over z).
Axes of the slice: x: 2, y: 2, z: 4, core: 2. Of those that a mesh axis runs over, the one named last changes fastest.
Arguments:
- hidden_in: bfloat16 [2048, 2048], P(('fsdp', 'ctx'), 'tp'), may hold values from -6 to 6
- out_grad: bfloat16 [2048, 2048], P(('fsdp', 'ctx'), 'tp'), may hold values from -6 to 6
- attn_gain: bfloat16 [2048], P('fsdp'), may hold values from 0.5 to 1.5
- w_query: bfloat16 [2048, 2048], P('fsdp', 'tp'), may hold values from -0.1875 to 0.1875
- w_key: bfloat16 [2048, 2048], P('fsdp', 'tp'), may hold values from -0.1875 to 0.1875
- w_value: bfloat16 [2048, 2048], P('fsdp', 'tp'), may hold values from -0.125 to 0.125
- w_output: bfloat16 [2048, 2048], P('fsdp', 'tp'), may hold values from -0.75 to 0.75
- ffn_gain: bfloat16 [2048], P('fsdp'), may hold values from 0.5 to 1.5
- w_router: bfloat16 [2048, 4], P('fsdp'), may hold values from -0.09375 to 0.09375
- w_gate: bfloat16 [4, 2048, 5632], P(None, 'fsdp', 'tp'), may hold values from -0.125 to 0.125
- w_up: bfloat16 [4, 2048, 5632], P(None, 'fsdp', 'tp'), may hold values from -0.125 to 0.125
- w_down: bfloat16 [4, 2048, 5632], P(None, 'fsdp', 'tp'), may hold values from -0.15625 to 0.15625
- routes: int32 [2048, 2], P(('fsdp', 'ctx')), may hold values from 0 to 3, all different within a row; in each aligned block of 256 rows (0 to 255, 256 to 511, ...) at most 160 rows name the same one
Outputs:
- block_out: bfloat16 [2048, 2048], P(('fsdp', 'ctx'), 'tp')
- in_grad: float32 [2048, 2048], P(('fsdp', 'ctx'), 'tp')
- grad_attn_gain: float32 [2048], P(('fsdp', 'ctx'))
- grad_query: float32 [2048, 2048], P(('fsdp', 'ctx'), 'tp')
- grad_key: float32 [2048, 2048], P(('fsdp', 'ctx'), 'tp')
- grad_value: float32 [2048, 2048], P(('fsdp', 'ctx'), 'tp')
- grad_output: float32 [2048, 2048], P(('fsdp', 'ctx'), 'tp')
- grad_ffn_gain: float32 [2048], P(('fsdp', 'ctx'))
- grad_router: float32 [2048, 4], P(('fsdp', 'ctx'))
- grad_gate: float32 [4, 2048, 5632], P(None, ('fsdp', 'ctx'), 'tp')
- grad_up: float32 [4, 2048, 5632], P(None, ('fsdp', 'ctx'), 'tp')
- grad_down: float32 [4, 2048, 5632], P(None, ('fsdp', 'ctx'), 'tp')
Inputs may be any that keep to these rules, and one draw needn't show every extreme that they name: `routes`: each row names 2 different experts. Among the 256 rows of one device no expert is named by more than 160 rows, and in every draw some device has an expert named by exactly 160 rows.
All inputs are finite; a program needn't handle non-finite values.
Results may differ from a plain program's by a relative error of at most 0.02.
Values may be sent and summed in bfloat16 or wider, within the bound.
A program may use at most 320 MiB of HBM per device.

v0:
```python
from functools import partial
import math

import jax
import jax.numpy as jnp
from jax import lax
from jax.sharding import PartitionSpec as P

HD = 128
CAP = 160


EPS = 1e-05
THETA = 10000.0
NEG = -1e30


def rotary_tables(positions):
    half_size = HD // 2
    frequency = THETA ** (-(jnp.arange(half_size, dtype=jnp.float32) * 2.0 / HD))
    angles = positions.astype(jnp.float32)[:, None] * frequency[None, :]
    return (jnp.cos(angles)[:, None, :], jnp.sin(angles)[:, None, :])


def rotate(values, cosine, sine_table):
    half_size = values.shape[-1] // 2
    first_half = values[..., :half_size]
    second_half = values[..., half_size:]
    return jnp.concatenate(
        [
            first_half * cosine - second_half * sine_table,
            second_half * cosine + first_half * sine_table,
        ],
        axis=-1,
    )


def rotate_back(values, cosine, sine_table):
    half_size = values.shape[-1] // 2
    first_half = values[..., :half_size]
    second_half = values[..., half_size:]
    return jnp.concatenate(
        [
            first_half * cosine + second_half * sine_table,
            second_half * cosine - first_half * sine_table,
        ],
        axis=-1,
    )


def route_table(routes, expert_count):
    return (routes[:, :, None] == jnp.arange(expert_count, dtype=jnp.int32)[None, None, :]).astype(
        jnp.float32
    )


def gate_values(logits, route_onehot):
    picked = jnp.sum(route_onehot * logits[:, None, :], axis=-1)
    weights = jax.nn.softmax(picked, axis=-1)
    return (jnp.sum(weights[:, :, None] * route_onehot, axis=1), weights)


def dispatch(routes, expert, capacity):
    count_rows = routes.shape[0]
    chosen = jnp.sum((routes == expert).astype(jnp.int32), axis=1)
    slot_of = jnp.cumsum(chosen) - 1
    target = jnp.where(chosen > 0, slot_of, capacity)
    row_index = (
        jnp.zeros((capacity,), jnp.int32)
        .at[target]
        .set(jnp.arange(count_rows, dtype=jnp.int32), mode="drop")
    )
    slot_live = (jnp.arange(capacity, dtype=jnp.int32) < jnp.sum(chosen)).astype(jnp.float32)
    return (row_index, slot_live, jnp.maximum(slot_of, 0), chosen.astype(jnp.float32))


def piece_scores(query_rot, key_piece, query_pos, key_pos):
    raw_scores = jnp.einsum(
        "qhd,khd->hqk", query_rot, key_piece, preferred_element_type=jnp.float32
    ) * (1.0 / math.sqrt(HD))
    return jnp.where(key_pos[None, None, :] <= query_pos[None, :, None], raw_scores, NEG)


def keep_state(state_in):
    return state_in


def max_step(query_rot, key_piece, query_pos, key_pos, state_in):
    old_max, old_sum = state_in
    scores = piece_scores(query_rot, key_piece, query_pos, key_pos)
    new_max = jnp.maximum(old_max, jnp.max(scores, axis=-1))
    new_sum = old_sum * jnp.exp(old_max - new_max) + jnp.sum(
        jnp.exp(scores - new_max[:, :, None]), axis=-1
    )
    return (new_max, new_sum)


def value_step(query_rot, key_piece, value_piece, query_pos, key_pos, log_total, attended):
    scores = piece_scores(query_rot, key_piece, query_pos, key_pos)
    prob_rows = jnp.exp(scores - log_total[:, :, None]).astype(jnp.bfloat16)
    return attended + jnp.einsum(
        "hqk,khd->qhd", prob_rows, value_piece, preferred_element_type=jnp.float32
    )


def delta_step(
    query_rot, key_piece, value_piece, query_pos, key_pos, log_total, d_attended, delta_sum
):
    scores = piece_scores(query_rot, key_piece, query_pos, key_pos)
    prob_rows = jnp.exp(scores - log_total[:, :, None])
    d_prob_rows = jnp.einsum(
        "qhd,khd->hqk", d_attended, value_piece, preferred_element_type=jnp.float32
    )
    return delta_sum + jnp.sum(prob_rows * d_prob_rows, axis=-1)


def grad_step(
    query_rot, key_piece, value_piece, query_pos, key_pos, log_total, d_attended, delta_sum, d_query
):
    scores = piece_scores(query_rot, key_piece, query_pos, key_pos)
    prob_rows = jnp.exp(scores - log_total[:, :, None])
    d_prob_rows = jnp.einsum(
        "qhd,khd->hqk", d_attended, value_piece, preferred_element_type=jnp.float32
    )
    d_scores = (prob_rows * (d_prob_rows - delta_sum[:, :, None])).astype(jnp.bfloat16)
    d_query = d_query + jnp.einsum(
        "hqk,khd->qhd", d_scores, key_piece, preferred_element_type=jnp.float32
    )
    key_grad = jnp.einsum("hqk,qhd->khd", d_scores, query_rot, preferred_element_type=jnp.float32)
    value_grad = jnp.einsum(
        "hqk,qhd->khd",
        prob_rows.astype(jnp.bfloat16),
        d_attended,
        preferred_element_type=jnp.float32,
    )
    return (d_query, key_grad, value_grad)


def skip_grad(piece_shape, d_query):
    return (d_query, jnp.zeros(piece_shape, jnp.float32), jnp.zeros(piece_shape, jnp.float32))


def shards(
    hidden_in,
    out_grad,
    attn_gain,
    w_query,
    w_key,
    w_value,
    w_output,
    ffn_gain,
    w_router,
    w_gate,
    w_up,
    w_down,
    routes,
):
    rows_here = hidden_in.shape[0]
    width_tp = hidden_in.shape[1]
    here_tp = lax.axis_index("tp")
    here_ctx = lax.axis_index("ctx")
    ctx_count = lax.axis_size("ctx")
    experts_here = w_gate.shape[0]
    score_scale = 1.0 / math.sqrt(HD)
    inputs_full, grad_full = (
        lax.all_gather(hidden_in, "tp", axis=1, tiled=True),
        lax.all_gather(out_grad, "tp", axis=1, tiled=True),
    )
    gain_one, gain_two, router_w, query_w, key_w, value_w, output_w = (
        lax.all_gather(attn_gain, "fsdp", axis=0, tiled=True),
        lax.all_gather(ffn_gain, "fsdp", axis=0, tiled=True),
        lax.all_gather(w_router, "fsdp", axis=0, tiled=True),
        lax.all_gather(w_query, "fsdp", axis=0, tiled=True),
        lax.all_gather(w_key, "fsdp", axis=0, tiled=True),
        lax.all_gather(w_value, "fsdp", axis=0, tiled=True),
        lax.all_gather(w_output, "fsdp", axis=0, tiled=True),
    )
    gain_one = gain_one.astype(jnp.float32)
    gain_two = gain_two.astype(jnp.float32)
    inputs_wide = inputs_full.astype(jnp.float32)
    grad_wide = grad_full.astype(jnp.float32)
    scale_one = lax.rsqrt(jnp.mean(inputs_wide * inputs_wide, axis=-1, keepdims=True) + EPS)
    unit_one = inputs_wide * scale_one
    normed_one = (unit_one * gain_one).astype(jnp.bfloat16)
    heads_here = query_w.shape[1] // HD
    head_shape = (rows_here, heads_here, HD)
    local_rows = jnp.arange(rows_here, dtype=jnp.int32)
    positions = here_ctx * rows_here + local_rows
    cosine, sine_table = rotary_tables(positions)
    query_pre = jnp.dot(normed_one, query_w, preferred_element_type=jnp.float32).reshape(head_shape)
    key_pre = jnp.dot(normed_one, key_w, preferred_element_type=jnp.float32).reshape(head_shape)
    value_pre = jnp.dot(normed_one, value_w, preferred_element_type=jnp.float32).reshape(head_shape)
    query_rot = rotate(query_pre, cosine, sine_table).astype(jnp.bfloat16)
    key_rot = rotate(key_pre, cosine, sine_table).astype(jnp.bfloat16)
    value_low = value_pre.astype(jnp.bfloat16)
    key_full, value_full = (
        lax.all_gather(key_rot, "ctx", axis=0, tiled=True),
        lax.all_gather(value_low, "ctx", axis=0, tiled=True),
    )
    key_pieces = [
        key_full[block_index * rows_here : (block_index + 1) * rows_here]
        for block_index in range(ctx_count)
    ]
    value_pieces = [
        value_full[block_index * rows_here : (block_index + 1) * rows_here]
        for block_index in range(ctx_count)
    ]
    key_places = [block_index * rows_here + local_rows for block_index in range(ctx_count)]
    stats = (
        jnp.full((heads_here, rows_here), NEG, jnp.float32),
        jnp.zeros((heads_here, rows_here), jnp.float32),
    )
    for block_index in range(ctx_count):
        stats = lax.cond(
            block_index <= here_ctx,
            partial(
                max_step, query_rot, key_pieces[block_index], positions, key_places[block_index]
            ),
            keep_state,
            stats,
        )
    log_total = stats[0] + jnp.log(stats[1])
    attended = jnp.zeros(head_shape, jnp.float32)
    for block_index in range(ctx_count):
        attended = lax.cond(
            block_index <= here_ctx,
            partial(
                value_step,
                query_rot,
                key_pieces[block_index],
                value_pieces[block_index],
                positions,
                key_places[block_index],
                log_total,
            ),
            keep_state,
            attended,
        )
    attended_low = attended.astype(jnp.bfloat16).reshape(rows_here, heads_here * HD)
    attn_part = jnp.dot(attended_low, output_w.T, preferred_element_type=jnp.float32)
    attn_full = lax.psum(attn_part, "tp")
    resid = inputs_wide + attn_full
    scale_two = lax.rsqrt(jnp.mean(resid * resid, axis=-1, keepdims=True) + EPS)
    unit_two = resid * scale_two
    normed_two = (unit_two * gain_two).astype(jnp.bfloat16)
    logits = jnp.dot(normed_two, router_w, preferred_element_type=jnp.float32)
    route_onehot = route_table(routes, experts_here)
    mix_gates, gate_pair = gate_values(logits, route_onehot)
    moe_part = jnp.zeros(inputs_wide.shape, jnp.float32)
    gate_terms = []
    saved = []
    for expert in range(experts_here):
        gate_w, up_w, down_w = (
            lax.all_gather(w_gate[expert], "fsdp", axis=0, tiled=True),
            lax.all_gather(w_up[expert], "fsdp", axis=0, tiled=True),
            lax.all_gather(w_down[expert], "fsdp", axis=0, tiled=True),
        )
        row_index, slot_live, slot_of, chosen = dispatch(routes, expert, CAP)
        picked = normed_two[row_index]
        gate_act = jnp.dot(picked, gate_w, preferred_element_type=jnp.float32)
        up_act = jnp.dot(picked, up_w, preferred_element_type=jnp.float32)
        sigma_act = jax.nn.sigmoid(gate_act)
        hidden_act = (gate_act * sigma_act * up_act).astype(jnp.bfloat16)
        result = jnp.dot(hidden_act, down_w.T, preferred_element_type=jnp.float32)
        spread = result[slot_of]
        token_weight = mix_gates[:, expert] * chosen
        moe_part = moe_part + token_weight[:, None] * spread
        gate_terms.append(jnp.sum(spread * grad_wide, axis=-1) * chosen)
        kept_w = None
        saved.append(
            (
                kept_w,
                row_index,
                slot_live,
                token_weight,
                picked,
                gate_act,
                up_act,
                sigma_act,
                hidden_act,
            )
        )
    moe_share = lax.psum_scatter(
        moe_part.astype(jnp.bfloat16), "tp", scatter_dimension=1, tiled=True
    ).astype(jnp.float32)
    resid_share = lax.dynamic_slice_in_dim(resid, here_tp * width_tp, width_tp, 1)
    block_out = (resid_share + moe_share).astype(jnp.bfloat16)
    d_normed_part = jnp.zeros(inputs_wide.shape, jnp.float32)
    gate_list = []
    up_list = []
    down_list = []
    for expert in range(experts_here):
        (
            kept_w,
            row_index,
            slot_live,
            token_weight,
            picked,
            gate_act,
            up_act,
            sigma_act,
            hidden_act,
        ) = saved[expert]
        gate_w, up_w, down_w = (
            lax.all_gather(w_gate[expert], "fsdp", axis=0, tiled=True),
            lax.all_gather(w_up[expert], "fsdp", axis=0, tiled=True),
            lax.all_gather(w_down[expert], "fsdp", axis=0, tiled=True),
        )
        slot_weight = token_weight[row_index] * slot_live
        d_result = (slot_weight[:, None] * grad_wide[row_index]).astype(jnp.bfloat16)
        d_hidden = jnp.dot(d_result, down_w, preferred_element_type=jnp.float32)
        d_gate_act = (d_hidden * up_act * sigma_act * (1.0 + gate_act * (1.0 - sigma_act))).astype(
            jnp.bfloat16
        )
        d_up_act = (d_hidden * gate_act * sigma_act).astype(jnp.bfloat16)
        d_picked = jnp.dot(d_gate_act, gate_w.T, preferred_element_type=jnp.float32) + jnp.dot(
            d_up_act, up_w.T, preferred_element_type=jnp.float32
        )
        d_normed_part = d_normed_part.at[row_index].add(d_picked)
        gate_share, up_share, down_share = (
            lax.psum_scatter(
                jnp.dot(picked.T, d_gate_act, preferred_element_type=jnp.float32).astype(
                    jnp.bfloat16
                ),
                "fsdp",
                scatter_dimension=0,
                tiled=True,
            ).astype(jnp.float32),
            lax.psum_scatter(
                jnp.dot(picked.T, d_up_act, preferred_element_type=jnp.float32).astype(
                    jnp.bfloat16
                ),
                "fsdp",
                scatter_dimension=0,
                tiled=True,
            ).astype(jnp.float32),
            lax.psum_scatter(
                jnp.dot(d_result.T, hidden_act, preferred_element_type=jnp.float32).astype(
                    jnp.bfloat16
                ),
                "fsdp",
                scatter_dimension=0,
                tiled=True,
            ).astype(jnp.float32),
        )
        gate_list.append(gate_share)
        up_list.append(up_share)
        down_list.append(down_share)
    grad_gate, grad_up, grad_down = (
        lax.psum_scatter(
            jnp.stack(gate_list).astype(jnp.bfloat16), "ctx", scatter_dimension=1, tiled=True
        ).astype(jnp.float32),
        lax.psum_scatter(
            jnp.stack(up_list).astype(jnp.bfloat16), "ctx", scatter_dimension=1, tiled=True
        ).astype(jnp.float32),
        lax.psum_scatter(
            jnp.stack(down_list).astype(jnp.bfloat16), "ctx", scatter_dimension=1, tiled=True
        ).astype(jnp.float32),
    )
    d_normed, gate_grad = lax.psum((d_normed_part, jnp.stack(gate_terms, axis=1)), "tp")
    pair_grad = jnp.sum(route_onehot * gate_grad[:, None, :], axis=-1)
    pick_grad = gate_pair * (pair_grad - jnp.sum(gate_pair * pair_grad, axis=-1, keepdims=True))
    logit_grad = jnp.sum(pick_grad[:, :, None] * route_onehot, axis=1).astype(jnp.bfloat16)
    d_normed = d_normed + jnp.dot(logit_grad, router_w.T, preferred_element_type=jnp.float32)
    grad_router_part = jnp.dot(normed_two.T, logit_grad, preferred_element_type=jnp.float32)
    grad_gain_two_part = jnp.sum(d_normed * unit_two, axis=0)
    gained_two = gain_two * d_normed
    d_resid = grad_wide + scale_two * (
        gained_two - unit_two * jnp.mean(unit_two * gained_two, axis=-1, keepdims=True)
    )
    back_query, back_key, back_value, back_output = (
        lax.all_gather(w_query, "fsdp", axis=0, tiled=True),
        lax.all_gather(w_key, "fsdp", axis=0, tiled=True),
        lax.all_gather(w_value, "fsdp", axis=0, tiled=True),
        lax.all_gather(w_output, "fsdp", axis=0, tiled=True),
    )
    d_attn = d_resid.astype(jnp.bfloat16)
    grad_output_part = jnp.dot(d_attn.T, attended_low, preferred_element_type=jnp.float32)
    d_attended = (
        jnp.dot(d_attn, back_output, preferred_element_type=jnp.float32)
        .astype(jnp.bfloat16)
        .reshape(head_shape)
    )
    delta_sum = jnp.zeros((heads_here, rows_here), jnp.float32)
    for block_index in range(ctx_count):
        delta_sum = lax.cond(
            block_index <= here_ctx,
            partial(
                delta_step,
                query_rot,
                key_pieces[block_index],
                value_pieces[block_index],
                positions,
                key_places[block_index],
                log_total,
                d_attended,
            ),
            keep_state,
            delta_sum,
        )
    d_query = jnp.zeros(head_shape, jnp.float32)
    key_parts = []
    value_parts = []
    for block_index in range(ctx_count):
        d_query, key_piece_grad, value_piece_grad = lax.cond(
            block_index <= here_ctx,
            partial(
                grad_step,
                query_rot,
                key_pieces[block_index],
                value_pieces[block_index],
                positions,
                key_places[block_index],
                log_total,
                d_attended,
                delta_sum,
            ),
            partial(skip_grad, head_shape),
            d_query,
        )
        key_parts.append(key_piece_grad)
        value_parts.append(value_piece_grad)
    key_grad, value_grad = (
        lax.psum_scatter(
            (jnp.concatenate(key_parts, axis=0) * score_scale).astype(jnp.bfloat16),
            "ctx",
            scatter_dimension=0,
            tiled=True,
        ).astype(jnp.float32),
        lax.psum_scatter(
            jnp.concatenate(value_parts, axis=0).astype(jnp.bfloat16),
            "ctx",
            scatter_dimension=0,
            tiled=True,
        ).astype(jnp.float32),
    )
    flat_shape = (rows_here, heads_here * HD)
    d_query_pre = (
        rotate_back(d_query * score_scale, cosine, sine_table)
        .astype(jnp.bfloat16)
        .reshape(flat_shape)
    )
    d_key_pre = rotate_back(key_grad, cosine, sine_table).astype(jnp.bfloat16).reshape(flat_shape)
    d_value_pre = value_grad.astype(jnp.bfloat16).reshape(flat_shape)
    grad_query_part = jnp.dot(normed_one.T, d_query_pre, preferred_element_type=jnp.float32)
    grad_key_part = jnp.dot(normed_one.T, d_key_pre, preferred_element_type=jnp.float32)
    grad_value_part = jnp.dot(normed_one.T, d_value_pre, preferred_element_type=jnp.float32)
    d_normed_one_part = (
        jnp.dot(d_query_pre, back_query.T, preferred_element_type=jnp.float32)
        + jnp.dot(d_key_pre, back_key.T, preferred_element_type=jnp.float32)
        + jnp.dot(d_value_pre, back_value.T, preferred_element_type=jnp.float32)
    )
    d_normed_one = lax.psum(d_normed_one_part.astype(jnp.bfloat16), "tp").astype(jnp.float32)
    grad_gain_one_part = jnp.sum(d_normed_one * unit_one, axis=0)
    gained_one = gain_one * d_normed_one
    d_inputs = d_resid + scale_one * (
        gained_one - unit_one * jnp.mean(unit_one * gained_one, axis=-1, keepdims=True)
    )
    in_grad = lax.dynamic_slice_in_dim(d_inputs, here_tp * width_tp, width_tp, 1)
    grad_query, grad_key, grad_value, grad_output, grad_attn_gain, grad_ffn_gain, grad_router = (
        lax.psum_scatter(grad_query_part, ("fsdp", "ctx"), scatter_dimension=0, tiled=True),
        lax.psum_scatter(grad_key_part, ("fsdp", "ctx"), scatter_dimension=0, tiled=True),
        lax.psum_scatter(grad_value_part, ("fsdp", "ctx"), scatter_dimension=0, tiled=True),
        lax.psum_scatter(grad_output_part, ("fsdp", "ctx"), scatter_dimension=0, tiled=True),
        lax.psum_scatter(grad_gain_one_part, ("fsdp", "ctx"), scatter_dimension=0, tiled=True),
        lax.psum_scatter(grad_gain_two_part, ("fsdp", "ctx"), scatter_dimension=0, tiled=True),
        lax.psum_scatter(grad_router_part, ("fsdp", "ctx"), scatter_dimension=0, tiled=True),
    )
    return (
        block_out,
        in_grad,
        grad_attn_gain,
        grad_query,
        grad_key,
        grad_value,
        grad_output,
        grad_ffn_gain,
        grad_router,
        grad_gate,
        grad_up,
        grad_down,
    )


def solution(mesh):
    placed = (
        P(("fsdp", "ctx"), "tp"),
        P(("fsdp", "ctx"), "tp"),
        P("fsdp"),
        P("fsdp", "tp"),
        P("fsdp", "tp"),
        P("fsdp", "tp"),
        P("fsdp", "tp"),
        P("fsdp"),
        P("fsdp", None),
        P(None, "fsdp", "tp"),
        P(None, "fsdp", "tp"),
        P(None, "fsdp", "tp"),
        P(("fsdp", "ctx"), None),
    )
    return jax.shard_map(
        shards,
        mesh=mesh,
        in_specs=placed,
        out_specs=(
            P(("fsdp", "ctx"), "tp"),
            P(("fsdp", "ctx"), "tp"),
            P(("fsdp", "ctx")),
            P(("fsdp", "ctx"), "tp"),
            P(("fsdp", "ctx"), "tp"),
            P(("fsdp", "ctx"), "tp"),
            P(("fsdp", "ctx"), "tp"),
            P(("fsdp", "ctx")),
            P(("fsdp", "ctx"), None),
            P(None, ("fsdp", "ctx"), "tp"),
            P(None, ("fsdp", "ctx"), "tp"),
            P(None, ("fsdp", "ctx"), "tp"),
        ),
        check_vma=False,
    )
```

profile of v0, /device:TPU:0, one launch (start us, length us, event | category | flops | bytes accessed | tf_op | source)
XLA Modules:
  0.0 3086.8 jit_solution(923202515241651988)
XLA Ops:
  279.2 54.7 %all-reduce.7.cloned.1.call-done = f32[256,2048]{1,0:T(8,128)} async-done(((f32[256,2048]{1,0:T(8,128)}), f32[256,2048]{1,0:T(8,128)}) %all-reduce.7.cloned.1.call-update) | async-done | bytes 2097168 | tf_op jit(solution)/shard_map/psum | solution.py:241
  343.4 66.1 %all-gather.67.cloned.1.call-done = bf16[1,2048,1408]{2,1,0:T(8,128)(2,1)} async-done(((bf16[1,1024,1408]{2,1,0:T(8,128)(2,1)}), bf16[1,2048,1408]{2,1,0:T(8,128)(2,1)}) %all-gather.67.cloned.1.call-update) | async-done | bytes 5767184 | tf_op jit(solution)/shard_map/all_gather | solution.py:254
  414.2 71.4 %all-gather.69.cloned.1.call-done = bf16[1,2048,1408]{2,1,0:T(8,128)(2,1)} async-done(((bf16[1,1024,1408]{2,1,0:T(8,128)(2,1)}), bf16[1,2048,1408]{2,1,0:T(8,128)(2,1)}) %all-gather.69.cloned.1.call-update) | async-done | bytes 5767184 | tf_op jit(solution)/shard_map/all_gather | solution.py:255
  490.7 70.8 %all-gather.71.cloned.1.call-done = bf16[1,2048,1408]{2,1,0:T(8,128)(2,1)} async-done(((bf16[1,1024,1408]{2,1,0:T(8,128)(2,1)}), bf16[1,2048,1408]{2,1,0:T(8,128)(2,1)}) %all-gather.71.cloned.1.call-update) | async-done | bytes 5767184 | tf_op jit(solution)/shard_map/all_gather | solution.py:256
  569.0 68.6 %all-gather.61.cloned.1.call-done = bf16[1,2048,1408]{2,1,0:T(8,128)(2,1)} async-done(((bf16[1,1024,1408]{2,1,0:T(8,128)(2,1)}), bf16[1,2048,1408]{2,1,0:T(8,128)(2,1)}) %all-gather.61.cloned.1.call-update) | async-done | bytes 5767184 | tf_op jit(solution)/shard_map/all_gather | solution.py:254
  642.6 71.0 %all-gather.63.cloned.1.call-done = bf16[1,2048,1408]{2,1,0:T(8,128)(2,1)} async-done(((bf16[1,1024,1408]{2,1,0:T(8,128)(2,1)}), bf16[1,2048,1408]{2,1,0:T(8,128)(2,1)}) %all-gather.63.cloned.1.call-update) | async-done | bytes 5767184 | tf_op jit(solution)/shard_map/all_gather | solution.py:255
  718.7 70.8 %all-gather.65.cloned.1.call-done = bf16[1,2048,1408]{2,1,0:T(8,128)(2,1)} async-done(((bf16[1,1024,1408]{2,1,0:T(8,128)(2,1)}), bf16[1,2048,1408]{2,1,0:T(8,128)(2,1)}) %all-gather.65.cloned.1.call-update) | async-done | bytes 5767184 | tf_op jit(solution)/shard_map/all_gather | solution.py:256
  797.2 68.9 %all-gather.55.cloned.1.call-done = bf16[1,2048,1408]{2,1,0:T(8,128)(2,1)} async-done(((bf16[1,1024,1408]{2,1,0:T(8,128)(2,1)}), bf16[1,2048,1408]{2,1,0:T(8,128)(2,1)}) %all-gather.55.cloned.1.call-update) | async-done | bytes 5767184 | tf_op jit(solution)/shard_map/all_gather | solution.py:254
  871.1 71.0 %all-gather.57.cloned.1.call-done = bf16[1,2048,1408]{2,1,0:T(8,128)(2,1)} async-done(((bf16[1,1024,1408]{2,1,0:T(8,128)(2,1)}), bf16[1,2048,1408]{2,1,0:T(8,128)(2,1)}) %all-gather.57.cloned.1.call-update) | async-done | bytes 5767184 | tf_op jit(solution)/shard_map/all_gather | solution.py:255
  947.3 70.8 %all-gather.59.cloned.1.call-done = bf16[1,2048,1408]{2,1,0:T(8,128)(2,1)} async-done(((bf16[1,1024,1408]{2,1,0:T(8,128)(2,1)}), bf16[1,2048,1408]{2,1,0:T(8,128)(2,1)}) %all-gather.59.cloned.1.call-update) | async-done | bytes 5767184 | tf_op jit(solution)/shard_map/all_gather | solution.py:256
  1025.5 69.2 %all-gather.49.cloned.1.call-done = bf16[1,2048,1408]{2,1,0:T(8,128)(2,1)} async-done(((bf16[1,1024,1408]{2,1,0:T(8,128)(2,1)}), bf16[1,2048,1408]{2,1,0:T(8,128)(2,1)}) %all-gather.49.cloned.1.call-update) | async-done | bytes 5767184 | tf_op jit(solution)/shard_map/all_gather | solution.py:254
  1098.6 72.1 %all-gather.51.cloned.1.call-done = bf16[1,2048,1408]{2,1,0:T(8,128)(2,1)} async-done(((bf16[1,1024,1408]{2,1,0:T(8,128)(2,1)}), bf16[1,2048,1408]{2,1,0:T(8,128)(2,1)}) %all-gather.51.cloned.1.call-update) | async-done | bytes 5767184 | tf_op jit(solution)/shard_map/all_gather | solution.py:255
  1175.6 71.2 %all-gather.53.cloned.1.call-done = bf16[1,2048,1408]{2,1,0:T(8,128)(2,1)} async-done(((bf16[1,1024,1408]{2,1,0:T(8,128)(2,1)}), bf16[1,2048,1408]{2,1,0:T(8,128)(2,1)}) %all-gather.53.cloned.1.call-update) | async-done | bytes 5767184 | tf_op jit(solution)/shard_map/all_gather | solution.py:256
  1358.4 83.7 %all-reduce.9.cloned.1.call-done = f32[256,2048]{1,0:T(8,128)} async-done(((f32[256,2048]{1,0:T(8,128)}), f32[256,2048]{1,0:T(8,128)}) %all-reduce.9.cloned.1.call-update) | async-done | bytes 2097168 | tf_op jit(solution)/shard_map/psum | solution.py:360
  1571.4 70.1 %reduce-scatter.46.cloned.1.call-done = bf16[1024,1408]{1,0:T(8,128)(2,1)} async-done(((bf16[2048,1408]{1,0:T(8,128)(2,1)}), bf16[1024,1408]{1,0:T(8,128)(2,1)}) %reduce-scatter.46.cloned.1.call-update) | async-done | bytes 2883600 | tf_op jit(solution)/shard_map/reduce_scatter | solution.py:321
  1641.5 74.2 %reduce-scatter.44.cloned.1.call-done = bf16[1024,1408]{1,0:T(8,128)(2,1)} async-done(((bf16[2048,1408]{1,0:T(8,128)(2,1)}), bf16[1024,1408]{1,0:T(8,128)(2,1)}) %reduce-scatter.44.cloned.1.call-update) | async-done | bytes 2883600 | tf_op jit(solution)/shard_map/reduce_scatter | solution.py:321
  1715.8 74.1 %reduce-scatter.42.cloned.1.call-done = bf16[1024,1408]{1,0:T(8,128)(2,1)} async-done(((bf16[2048,1408]{1,0:T(8,128)(2,1)}), bf16[1024,1408]{1,0:T(8,128)(2,1)}) %reduce-scatter.42.cloned.1.call-update) | async-done | bytes 2883600 | tf_op jit(solution)/shard_map/reduce_scatter | solution.py:321
  1789.9 73.8 %reduce-scatter.40.cloned.1.call-done = bf16[1024,1408]{1,0:T(8,128)(2,1)} async-done(((bf16[2048,1408]{1,0:T(8,128)(2,1)}), bf16[1024,1408]{1,0:T(8,128)(2,1)}) %reduce-scatter.40.cloned.1.call-update) | async-done | bytes 2883600 | tf_op jit(solution)/shard_map/reduce_scatter | solution.py:321
  1874.6 62.8 %reduce-scatter.56.cloned.1.call-done = bf16[1024,1408]{1,0:T(8,128)(2,1)} async-done(((bf16[2048,1408]{1,0:T(8,128)(2,1)}), bf16[1024,1408]{1,0:T(8,128)(2,1)}) %reduce-scatter.56.cloned.1.call-update) | async-done | bytes 2883600 | tf_op jit(solution)/shard_map/reduce_scatter | solution.py:329
  1937.4 73.7 %reduce-scatter.54.cloned.1.call-done = bf16[1024,1408]{1,0:T(8,128)(2,1)} async-done(((bf16[2048,1408]{1,0:T(8,128)(2,1)}), bf16[1024,1408]{1,0:T(8,128)(2,1)}) %reduce-scatter.54.cloned.1.call-update) | async-done | bytes 2883600 | tf_op jit(solution)/shard_map/reduce_scatter | solution.py:329
  2011.1 73.7 %reduce-scatter.52.cloned.1.call-done = bf16[1024,1408]{1,0:T(8,128)(2,1)} async-done(((bf16[2048,1408]{1,0:T(8,128)(2,1)}), bf16[1024,1408]{1,0:T(8,128)(2,1)}) %reduce-scatter.52.cloned.1.call-update) | async-done | bytes 2883600 | tf_op jit(solution)/shard_map/reduce_scatter | solution.py:329
  2084.8 73.8 %reduce-scatter.50.cloned.1.call-done = bf16[1024,1408]{1,0:T(8,128)(2,1)} async-done(((bf16[2048,1408]{1,0:T(8,128)(2,1)}), bf16[1024,1408]{1,0:T(8,128)(2,1)}) %reduce-scatter.50.cloned.1.call-update) | async-done | bytes 2883600 | tf_op jit(solution)/shard_map/reduce_scatter | solution.py:329
  2169.6 62.6 %reduce-scatter.66.cloned.1.call-done = bf16[1024,1408]{1,0:T(8,128)(2,1)} async-done(((bf16[2048,1408]{1,0:T(8,128)(2,1)}), bf16[1024,1408]{1,0:T(8,128)(2,1)}) %reduce-scatter.66.cloned.1.call-update) | async-done | bytes 2883600 | tf_op jit(solution)/shard_map/reduce_scatter | solution.py:337
  2232.2 73.8 %reduce-scatter.64.cloned.1.call-done = bf16[1024,1408]{1,0:T(8,128)(2,1)} async-done(((bf16[2048,1408]{1,0:T(8,128)(2,1)}), bf16[1024,1408]{1,0:T(8,128)(2,1)}) %reduce-scatter.64.cloned.1.call-update) | async-done | bytes 2883600 | tf_op jit(solution)/shard_map/reduce_scatter | solution.py:337
  2306.0 73.7 %reduce-scatter.62.cloned.1.call-done = bf16[1024,1408]{1,0:T(8,128)(2,1)} async-done(((bf16[2048,1408]{1,0:T(8,128)(2,1)}), bf16[1024,1408]{1,0:T(8,128)(2,1)}) %reduce-scatter.62.cloned.1.call-update) | async-done | bytes 2883600 | tf_op jit(solution)/shard_map/reduce_scatter | solution.py:337
  2379.7 73.7 %reduce-scatter.60.cloned.1.call-done = bf16[1024,1408]{1,0:T(8,128)(2,1)} async-done(((bf16[2048,1408]{1,0:T(8,128)(2,1)}), bf16[1024,1408]{1,0:T(8,128)(2,1)}) %reduce-scatter.60.cloned.1.call-update) | async-done | bytes 2883600 | tf_op jit(solution)/shard_map/reduce_scatter | solution.py:337
  2605.9 63.1 %reduce-scatter.48.cloned.1.call-done = bf16[4,256,1408]{2,1,0:T(8,128)(2,1)} async-done(((bf16[4,1024,1408]{2,1,0:T(8,128)(2,1)}), bf16[4,256,1408]{2,1,0:T(8,128)(2,1)}) %reduce-scatter.48.cloned.1.call-update) | async-done | bytes 2883600 | tf_op jit(solution)/shard_map/reduce_scatter | solution.py:350
  2673.7 90.1 %reduce-scatter.58.cloned.1.call-done = bf16[4,256,1408]{2,1,0:T(8,128)(2,1)} async-done(((bf16[4,1024,1408]{2,1,0:T(8,128)(2,1)}), bf16[4,256,1408]{2,1,0:T(8,128)(2,1)}) %reduce-scatter.58.cloned.1.call-update) | async-done | bytes 2883600 | tf_op jit(solution)/shard_map/reduce_scatter | solution.py:353
  2768.5 90.1 %reduce-scatter.68.cloned.1.call-done = bf16[4,256,1408]{2,1,0:T(8,128)(2,1)} async-done(((bf16[4,1024,1408]{2,1,0:T(8,128)(2,1)}), bf16[4,256,1408]{2,1,0:T(8,128)(2,1)}) %reduce-scatter.68.cloned.1.call-update) | async-done | bytes 2883600 | tf_op jit(solution)/shard_map/reduce_scatter | solution.py:356
  2913.7 55.7 %reduce-scatter.32.cloned.1.call-done = f32[256,512]{1,0:T(8,128)} async-done(((f32[2048,512]{1,0:T(8,128)}), f32[256,512]{1,0:T(8,128)}) %reduce-scatter.32.cloned.1.call-update) | async-done | bytes 524304 | tf_op jit(solution)/shard_map/reduce_scatter | solution.py:461
  2969.4 55.1 %reduce-scatter.34.cloned.1.call-done = f32[256,512]{1,0:T(8,128)} async-done(((f32[2048,512]{1,0:T(8,128)}), f32[256,512]{1,0:T(8,128)}) %reduce-scatter.34.cloned.1.call-update) | async-done | bytes 524304 | tf_op jit(solution)/shard_map/reduce_scatter | solution.py:462
  3024.5 55.5 %reduce-scatter.36.cloned.1.call-done = f32[256,512]{1,0:T(8,128)} async-done(((f32[2048,512]{1,0:T(8,128)}), f32[256,512]{1,0:T(8,128)}) %reduce-scatter.36.cloned.1.call-update) | async-done | bytes 524304 | tf_op jit(solution)/shard_map/reduce_scatter | solution.py:463
  (474 shorter events, 843.1 us)
Async XLA Ops:
  228.2 257.3 %all-gather.69.cloned.1.call-start = ((), (), s32[]{:S(2)}) async-start(), calls=%async_computation.66 | async-start | bytes 8650752 | tf_op jit(solution)/shard_map/all_gather | solution.py:255
  236.8 324.7 %all-gather.71.cloned.1.call-start = ((), (), s32[]{:S(2)}) async-start(), calls=%async_computation.67 | async-start | bytes 8650752 | tf_op jit(solution)/shard_map/all_gather | solution.py:256
  245.7 392.0 %all-gather.61.cloned.1.call-start = ((), (), s32[]{:S(2)}) async-start(), calls=%async_computation.62 | async-start | bytes 8650752 | tf_op jit(solution)/shard_map/all_gather | solution.py:254
  246.4 467.2 %all-gather.63.cloned.1.call-start = ((), (), s32[]{:S(2)}) async-start(), calls=%async_computation.63 | async-start | bytes 8650752 | tf_op jit(solution)/shard_map/all_gather | solution.py:255
  247.0 542.6 %all-gather.65.cloned.1.call-start = ((), (), s32[]{:S(2)}) async-start(), calls=%async_computation.64 | async-start | bytes 8650752 | tf_op jit(solution)/shard_map/all_gather | solution.py:256
  247.6 618.5 %all-gather.55.cloned.1.call-start = ((), (), s32[]{:S(2)}) async-start(), calls=%async_computation.59 | async-start | bytes 8650752 | tf_op jit(solution)/shard_map/all_gather | solution.py:254
  248.2 693.9 %all-gather.57.cloned.1.call-start = ((), (), s32[]{:S(2)}) async-start(), calls=%async_computation.60 | async-start | bytes 8650752 | tf_op jit(solution)/shard_map/all_gather | solution.py:255
  248.8 769.3 %all-gather.59.cloned.1.call-start = ((), (), s32[]{:S(2)}) async-start(), calls=%async_computation.61 | async-start | bytes 8650752 | tf_op jit(solution)/shard_map/all_gather | solution.py:256
  249.3 845.4 %all-gather.49.cloned.1.call-start = ((), (), s32[]{:S(2)}) async-start(), calls=%async_computation.56 | async-start | bytes 8650752 | tf_op jit(solution)/shard_map/all_gather | solution.py:254
  250.1 920.6 %all-gather.51.cloned.1.call-start = ((), (), s32[]{:S(2)}) async-start(), calls=%async_computation.57 | async-start | bytes 8650752 | tf_op jit(solution)/shard_map/all_gather | solution.py:255
  250.7 996.1 %all-gather.53.cloned.1.call-start = ((), (), s32[]{:S(2)}) async-start(), calls=%async_computation.58 | async-start | bytes 8650752 | tf_op jit(solution)/shard_map/all_gather | solution.py:256
  251.4 1190.6 %all-reduce.9.cloned.1.call-start = ((), (), s32[]{:S(2)}) async-start(), calls=%async_computation.33 | async-start | bytes 4194304 | tf_op jit(solution)/shard_map/psum | solution.py:360
  1486.9 303.0 %reduce-scatter.42.cloned.1.call-start = ((), (), s32[]{:S(2)}) async-start(), calls=%async_computation.42 | async-start | bytes 8650752 | tf_op jit(solution)/shard_map/reduce_scatter | solution.py:321
  1492.5 371.2 %reduce-scatter.40.cloned.1.call-start = ((), (), s32[]{:S(2)}) async-start(), calls=%async_computation.41 | async-start | bytes 8650752 | tf_op jit(solution)/shard_map/reduce_scatter | solution.py:321
  1498.2 439.3 %reduce-scatter.56.cloned.1.call-start = ((), (), s32[]{:S(2)}) async-start(), calls=%async_computation.49 | async-start | bytes 8650752 | tf_op jit(solution)/shard_map/reduce_scatter | solution.py:329
  1503.8 507.3 %reduce-scatter.54.cloned.1.call-start = ((), (), s32[]{:S(2)}) async-start(), calls=%async_computation.48 | async-start | bytes 8650752 | tf_op jit(solution)/shard_map/reduce_scatter | solution.py:329
  1509.8 575.0 %reduce-scatter.52.cloned.1.call-start = ((), (), s32[]{:S(2)}) async-start(), calls=%async_computation.47 | async-start | bytes 8650752 | tf_op jit(solution)/shard_map/reduce_scatter | solution.py:329
  1515.4 643.3 %reduce-scatter.50.cloned.1.call-start = ((), (), s32[]{:S(2)}) async-start(), calls=%async_computation.46 | async-start | bytes 8650752 | tf_op jit(solution)/shard_map/reduce_scatter | solution.py:329
  1521.0 711.2 %reduce-scatter.66.cloned.1.call-start = ((), (), s32[]{:S(2)}) async-start(), calls=%async_computation.54 | async-start | bytes 8650752 | tf_op jit(solution)/shard_map/reduce_scatter | solution.py:337
  1527.0 779.0 %reduce-scatter.64.cloned.1.call-start = ((), (), s32[]{:S(2)}) async-start(), calls=%async_computation.53 | async-start | bytes 8650752 | tf_op jit(solution)/shard_map/reduce_scatter | solution.py:337
  1532.8 846.9 %reduce-scatter.62.cloned.1.call-start = ((), (), s32[]{:S(2)}) async-start(), calls=%async_computation.52 | async-start | bytes 8650752 | tf_op jit(solution)/shard_map/reduce_scatter | solution.py:337
  1538.7 914.7 %reduce-scatter.60.cloned.1.call-start = ((), (), s32[]{:S(2)}) async-start(), calls=%async_computation.51 | async-start | bytes 8650752 | tf_op jit(solution)/shard_map/reduce_scatter | solution.py:337
  1544.7 947.8 %reduce-scatter.70.cloned.1.call-start = ((), (), s32[]{:S(2)}) async-start(), calls=%async_computation.68 | async-start | bytes 1179648
  1546.3 975.7 %reduce-scatter.26.cloned.1.call-start = ((), (), s32[]{:S(2)}) async-start(), calls=%async_computation.31 | async-start | bytes 1310720 | tf_op jit(solution)/shard_map/reduce_scatter | solution.py:283
  1551.8 1023.0 %all-reduce.11.cloned.1.call-start = ((), (), s32[]{:S(2)}) async-start(), calls=%async_computation.36 | async-start | bytes 2097152 | tf_op jit(solution)/shard_map/psum | solution.py:453
  1571.3 1097.6 %reduce-scatter.48.cloned.1.call-start = ((), (), s32[]{:S(2)}) async-start(), calls=%async_computation.45 | async-start | bytes 14417920 | tf_op jit(solution)/shard_map/reduce_scatter | solution.py:350
  1874.5 889.2 %reduce-scatter.58.cloned.1.call-start = ((), (), s32[]{:S(2)}) async-start(), calls=%async_computation.50 | async-start | bytes 14417920 | tf_op jit(solution)/shard_map/reduce_scatter | solution.py:353
  2169.5 689.1 %reduce-scatter.68.cloned.1.call-start = ((), (), s32[]{:S(2)}) async-start(), calls=%async_computation.55 | async-start | bytes 14417920 | tf_op jit(solution)/shard_map/reduce_scatter | solution.py:356
  2463.9 449.8 %reduce-scatter.38.cloned.1.call-start = ((), (), s32[]{:S(2)}) async-start(), calls=%async_computation.40 | async-start | bytes 4718592 | tf_op jit(solution)/shard_map/reduce_scatter | solution.py:464
  2469.3 500.1 %reduce-scatter.32.cloned.1.call-start = ((), (), s32[]{:S(2)}) async-start(), calls=%async_computation.37 | async-start | bytes 4718592 | tf_op jit(solution)/shard_map/reduce_scatter | solution.py:461
  2474.3 550.2 %reduce-scatter.34.cloned.1.call-start = ((), (), s32[]{:S(2)}) async-start(), calls=%async_computation.38 | async-start | bytes 4718592 | tf_op jit(solution)/shard_map/reduce_scatter | solution.py:462
  2477.3 602.7 %reduce-scatter.36.cloned.1.call-start = ((), (), s32[]{:S(2)}) async-start(), calls=%async_computation.39 | async-start | bytes 4718592 | tf_op jit(solution)/shard_map/reduce_scatter | solution.py:463
  (76 other events, 4094.4 us)
Sparse Core Ops, SparseCore 0:
  247.9 85.9 all-reduce.6
  336.0 73.4 all-gather.66
  411.0 74.4 all-gather.68
  487.0 74.4 all-gather.70
  563.1 74.4 all-gather.60
  639.1 74.4 all-gather.62
  715.1 74.4 all-gather.64
  791.6 74.4 all-gather.54
  867.6 74.4 all-gather.56
  943.5 74.4 all-gather.58
  1020.2 74.4 all-gather.48
  1096.2 74.4 all-gather.50
  1172.3 74.4 all-gather.52
  1358.3 83.7 all-reduce.8
  1473.2 66.4 reduce-scatter.27
  1570.1 71.3 reduce-scatter.45
  1644.4 71.3 reduce-scatter.43
  1718.5 71.3 reduce-scatter.41
  1792.3 71.3 reduce-scatter.39
  1866.0 71.3 reduce-scatter.55
  1939.7 71.3 reduce-scatter.53
  2013.4 71.3 reduce-scatter.51
  2087.2 71.3 reduce-scatter.49
  2160.8 71.3 reduce-scatter.65
  2234.6 71.3 reduce-scatter.63
  2308.3 71.3 reduce-scatter.61
  2382.0 71.3 reduce-scatter.59
  2577.4 91.5 reduce-scatter.47
  2671.6 92.1 reduce-scatter.57
  2766.4 92.1 reduce-scatter.67
  2918.0 51.3 reduce-scatter.31
  3028.6 51.3 reduce-scatter.35
  (14 shorter events, 464.4 us)
where the time goes:
time: 3100 us; the launch traced here: 3090 us
  waiting for transfers between devices  2590 us (84%)
  matrix products  236 us (8%)
  other arithmetic  101 us (3%)
  local copies, waits for them, and re-layouts  92.1 us (3%)
  blocking collectives  50 us (2%)
    reduce_scatter x4, waiting for transfers between devices, shards(): lax.psum_scatter(jnp.dot(picked.T, d_gate_act, preferred_element_type=jnp...  292 us
    all_gather x4, waiting for transfers between devices, shards(): lax.all_gather(w_up[expert], 'fsdp', axis=0, tiled=True)  285 us
    reduce_scatter x4, waiting for transfers between devices, shards(): lax.psum_scatter(jnp.dot(picked.T, d_up_act, preferred_element_type=jnp.f...  284 us
    reduce_scatter x4, waiting for transfers between devices, shards(): lax.psum_scatter(jnp.dot(d_result.T, hidden_act, preferred_element_type=j...  284 us
    all_gather x4, waiting for transfers between devices, shards(): lax.all_gather(w_down[expert], 'fsdp', axis=0, tiled=True)  284 us
    all_gather x4, waiting for transfers between devices, shards(): lax.all_gather(w_gate[expert], 'fsdp', axis=0, tiled=True)  273 us
    reduce_scatter x1, waiting for transfers between devices, shards(): lax.psum_scatter(jnp.stack(down_list).astype(jnp.bfloat16), 'ctx', scatte...  90.1 us
    reduce_scatter x1, waiting for transfers between devices, shards(): lax.psum_scatter(jnp.stack(up_list).astype(jnp.bfloat16), 'ctx', scatter_...  90.1 us
  transfers between devices with their start and end apart: 46, of which 44 were waited for; matrix products, arithmetic and copies ran while one was open for 10% of the time, Pallas kernels for 0%

commit v1 on v0

v1 whole, which is shorter than its diff:
```python
from functools import partial
import math

import jax
import jax.numpy as jnp
from jax import lax
from jax.experimental import pallas as pl
from jax.experimental.pallas import tpu as pltpu
from jax.sharding import PartitionSpec as P

HD = 128
CAP = 160


EPS = 1e-05
THETA = 10000.0
NEG = -1e30
BF = jnp.bfloat16
F32 = jnp.float32


def mm(left, right):
    return jnp.dot(left, right, preferred_element_type=F32)


def mm_t(left, right):
    return lax.dot_general(left, right, (((1,), (1,)), ((), ())), preferred_element_type=F32)


def t_mm(left, right):
    return lax.dot_general(left, right, (((0,), (0,)), ((), ())), preferred_element_type=F32)


def rotary_tables(positions):
    half_size = HD // 2
    frequency = THETA ** (-(jnp.arange(half_size, dtype=F32) * 2.0 / HD))
    angles = positions.astype(F32)[:, None] * frequency[None, :]
    return (jnp.cos(angles)[:, None, :], jnp.sin(angles)[:, None, :])


def rotate(values, cosine, sine_table):
    half_size = values.shape[-1] // 2
    first_half = values[..., :half_size]
    second_half = values[..., half_size:]
    return jnp.concatenate(
        [
            first_half * cosine - second_half * sine_table,
            second_half * cosine + first_half * sine_table,
        ],
        axis=-1,
    )


def softmax_rows(query, key, first_row):
    scores = mm_t(query, key) * (1.0 / math.sqrt(HD))
    rows = first_row + lax.broadcasted_iota(jnp.int32, scores.shape, 0)
    cols = lax.broadcasted_iota(jnp.int32, scores.shape, 1)
    scores = jnp.where(cols <= rows, scores, NEG)
    top = jnp.max(scores, axis=-1, keepdims=True)
    weights = jnp.exp(scores - top)
    return weights / jnp.sum(weights, axis=-1, keepdims=True)


def attention_forward_kernel(query_ref, key_ref, value_ref, out_ref):
    first_row = lax.axis_index("ctx") * query_ref.shape[0]
    probs = softmax_rows(query_ref[...], key_ref[...], first_row)
    out_ref[...] = mm(probs.astype(BF), value_ref[...]).astype(BF)


def attention_forward(query, kv):
    rows, width = query.shape
    keys = kv.shape[0]
    heads = width // HD
    return pl.pallas_call(
        attention_forward_kernel,
        grid=(heads,),
        out_shape=jax.ShapeDtypeStruct((rows, width), BF),
        in_specs=[
            pl.BlockSpec((rows, HD), lambda h: (0, h)),
            pl.BlockSpec((keys, HD), lambda h: (0, h)),
            pl.BlockSpec((keys, HD), lambda h: (0, h + heads)),
        ],
        out_specs=pl.BlockSpec((rows, HD), lambda h: (0, h)),
        cost_estimate=pl.CostEstimate(
            flops=4 * rows * keys * width,
            bytes_accessed=2 * (2 * rows * width + 2 * keys * width),
            transcendentals=rows * keys * heads,
        ),
        name="attention_forward",
    )(query, kv, kv)


def attention_backward_kernel(query_ref, key_ref, value_ref, dout_ref, dq_ref, dk_ref, dv_ref):
    first_row = lax.axis_index("ctx") * query_ref.shape[0]
    scale = 1.0 / math.sqrt(HD)
    probs = softmax_rows(query_ref[...], key_ref[...], first_row)
    d_probs = mm_t(dout_ref[...], value_ref[...])
    delta = jnp.sum(probs * d_probs, axis=-1, keepdims=True)
    d_scores = (probs * (d_probs - delta)).astype(BF)
    dq_ref[...] = mm(d_scores, key_ref[...]) * scale
    dk_ref[...] = (t_mm(d_scores, query_ref[...]) * scale).astype(BF)
    dv_ref[...] = t_mm(probs.astype(BF), dout_ref[...]).astype(BF)


def attention_backward(query, kv, dout):
    rows, width = query.shape
    keys = kv.shape[0]
    heads = width // HD
    return pl.pallas_call(
        attention_backward_kernel,
        grid=(heads,),
        out_shape=(
            jax.ShapeDtypeStruct((rows, width), F32),
            jax.ShapeDtypeStruct((keys, width), BF),
            jax.ShapeDtypeStruct((keys, width), BF),
        ),
        in_specs=[
            pl.BlockSpec((rows, HD), lambda h: (0, h)),
            pl.BlockSpec((keys, HD), lambda h: (0, h)),
            pl.BlockSpec((keys, HD), lambda h: (0, h + heads)),
            pl.BlockSpec((rows, HD), lambda h: (0, h)),
        ],
        out_specs=(
            pl.BlockSpec((rows, HD), lambda h: (0, h)),
            pl.BlockSpec((keys, HD), lambda h: (0, h)),
            pl.BlockSpec((keys, HD), lambda h: (0, h)),
        ),
        cost_estimate=pl.CostEstimate(
            flops=10 * rows * keys * width,
            bytes_accessed=2 * (4 * rows * width + 4 * keys * width),
            transcendentals=rows * keys * heads,
        ),
        name="attention_backward",
    )(query, kv, kv, dout)


def shards(
    hidden_in,
    out_grad,
    attn_gain,
    w_query,
    w_key,
    w_value,
    w_output,
    ffn_gain,
    w_router,
    w_gate,
    w_up,
    w_down,
    routes,
):
    rows_here, width_tp = hidden_in.shape
    here_tp = lax.axis_index("tp")
    here_ctx = lax.axis_index("ctx")
    here_fsdp = lax.axis_index("fsdp")
    n_fsdp = lax.axis_size("fsdp")
    n_ctx = lax.axis_size("ctx")
    n_tp = lax.axis_size("tp")
    experts = w_gate.shape[0]
    assert experts == n_ctx
    width = width_tp * n_tp
    part = width // n_fsdp
    pair = n_fsdp == 2
    heads_width = w_query.shape[1]

    def shift_ctx(value, k):
        return lax.ppermute(value, "ctx", [(i, (i + k) % n_ctx) for i in range(n_ctx)])

    def swap_fsdp(value):
        return lax.ppermute(value, "fsdp", [(0, 1), (1, 0)])

    def other_parts(weight):
        if pair:
            return [weight, swap_fsdp(weight)]
        return [lax.all_gather(weight, "fsdp", axis=0, tiled=True)]

    def split(values):
        if pair:
            return [
                lax.dynamic_slice_in_dim(values, here_fsdp * part, part, 1),
                lax.dynamic_slice_in_dim(values, (1 - here_fsdp) * part, part, 1),
            ]
        return [values]

    def join(pieces):
        if pair:
            first = here_fsdp == 0
            return jnp.concatenate(
                [jnp.where(first, pieces[0], pieces[1]), jnp.where(first, pieces[1], pieces[0])],
                axis=1,
            )
        return pieces[0]

    def into(values, weights):
        return sum(mm(x, w) for x, w in zip(split(values), weights))

    def back(values, weights):
        return join([mm_t(values, w) for w in weights])

    def my_features(values):
        return lax.dynamic_slice_in_dim(values, here_tp * width_tp, width_tp, values.ndim - 1)

    inputs_full = lax.all_gather(hidden_in, "tp", axis=1, tiled=True)
    attn_w = jnp.concatenate([w_query, w_key, w_value, w_output], axis=1)
    if pair:
        quarter = part // n_ctx
        own_quarter = lax.dynamic_slice_in_dim(attn_w, here_ctx * quarter, quarter, 0)
        other_quarter = swap_fsdp(own_quarter)
        attn_other = lax.all_gather(other_quarter, "ctx", axis=0, tiled=True)
        attn_parts = [attn_w, attn_other]
    else:
        attn_parts = [lax.all_gather(attn_w, "fsdp", axis=0, tiled=True)]
    qkv_parts = [w[:, : 3 * heads_width] for w in attn_parts]
    out_parts = [w[:, 3 * heads_width :] for w in attn_parts]
    small = jnp.concatenate([attn_gain[:, None], ffn_gain[:, None], w_router], axis=1)
    small = lax.all_gather(small, "fsdp", axis=0, tiled=True)
    gain_one = small[:, 0].astype(F32)
    gain_two = small[:, 1].astype(F32)
    router_w = small[:, 2:]

    inputs_wide = inputs_full.astype(F32)
    scale_one = lax.rsqrt(jnp.mean(inputs_wide * inputs_wide, axis=-1, keepdims=True) + EPS)
    normed_one = (inputs_wide * scale_one * gain_one).astype(BF)
    heads_here = heads_width // HD
    head_shape = (rows_here, heads_here, HD)
    flat_shape = (rows_here, heads_width)
    positions = here_ctx * rows_here + jnp.arange(rows_here, dtype=jnp.int32)
    cosine, sine_table = rotary_tables(positions)
    qkv = into(normed_one, qkv_parts)
    query_pre = qkv[:, :heads_width].reshape(head_shape)
    key_pre = qkv[:, heads_width : 2 * heads_width].reshape(head_shape)
    query = rotate(query_pre, cosine, sine_table).astype(BF).reshape(flat_shape)
    key = rotate(key_pre, cosine, sine_table).astype(BF).reshape(flat_shape)
    value = qkv[:, 2 * heads_width :].astype(BF)
    kv = lax.all_gather(jnp.concatenate([key, value], axis=1), "ctx", axis=0, tiled=True)
    attended = attention_forward(query, kv)
    attn_share = lax.psum_scatter(
        back(attended, out_parts).astype(BF), "tp", scatter_dimension=1, tiled=True
    )
    resid = hidden_in.astype(F32) + attn_share.astype(F32)
    square = lax.psum(jnp.sum(resid * resid, axis=-1, keepdims=True), "tp")
    scale_two = lax.rsqrt(square / width + EPS)
    unit_two = resid * scale_two
    gain_two_here = my_features(gain_two)
    normed_two = lax.all_gather(
        (unit_two * gain_two_here).astype(BF), "tp", axis=1, tiled=True
    )

    logits = mm(normed_two, router_w)
    route_onehot = (routes[:, :, None] == jnp.arange(experts, dtype=jnp.int32)).astype(F32)
    picked_logits = jnp.sum(route_onehot * logits[:, None, :], axis=-1)
    gate_pair = jax.nn.softmax(picked_logits, axis=-1)
    relative = (jnp.arange(experts, dtype=jnp.int32) + here_ctx) % experts
    names = (routes[:, :, None] == relative).astype(F32)
    mix_gates = jnp.sum(gate_pair[:, :, None] * names, axis=1)
    chosen = jnp.sum(names, axis=1)
    before = jnp.tril(jnp.ones((rows_here, rows_here), BF), -1)
    slot_of = mm(before, chosen.astype(BF)).astype(jnp.int32)
    slots = jnp.arange(CAP, dtype=jnp.int32)
    pick = (slot_of.T[:, None, :] == slots[None, :, None]) & (chosen.T[:, None, :] > 0)
    pick_low = pick.astype(BF)
    pick_flat = pick_low.reshape(experts * CAP, rows_here)

    def dispatch(slabs):
        return jnp.concatenate(
            [slabs[0]] + [shift_ctx(slabs[k], k) for k in range(1, experts)], axis=0
        )

    def give_back(values):
        slabs = values.reshape(experts, CAP, values.shape[-1])
        return [slabs[0]] + [shift_ctx(slabs[k], -k) for k in range(1, experts)]

    grad_full = lax.all_gather(out_grad, "tp", axis=1, tiled=True)
    grad_rows = dispatch(mm(pick_flat, grad_full).astype(BF).reshape(experts, CAP, width))
    token_rows = dispatch(mm(pick_flat, normed_two).astype(BF).reshape(experts, CAP, width))
    gate_slots = jnp.sum(jnp.where(pick, mix_gates.T[:, None, :], 0.0), axis=-1)
    gate_rows = dispatch(gate_slots[:, :, None])

    gate_w = other_parts(lax.dynamic_index_in_dim(w_gate, here_ctx, 0, False))
    up_w = other_parts(lax.dynamic_index_in_dim(w_up, here_ctx, 0, False))
    down_w = other_parts(lax.dynamic_index_in_dim(w_down, here_ctx, 0, False))
    gate_act = into(token_rows, gate_w)
    up_act = into(token_rows, up_w)
    sigma_act = jax.nn.sigmoid(gate_act)
    hidden_act = (gate_act * sigma_act * up_act).astype(BF)
    result = back(hidden_act, down_w)
    d_result = (gate_rows * grad_rows.astype(F32)).astype(BF)
    gate_dot = jnp.sum(result * grad_rows.astype(F32), axis=-1, keepdims=True)
    returned = give_back(result.astype(BF))
    returned_dot = give_back(gate_dot)
    moe_part = sum(
        mix_gates[:, k][:, None] * t_mm(pick_low[k], returned[k]) for k in range(experts)
    )
    moe_share = lax.psum_scatter(moe_part.astype(BF), "tp", scatter_dimension=1, tiled=True)
    block_out = (resid + moe_share.astype(F32)).astype(BF)

    d_hidden = into(d_result, down_w)
    d_gate_act = (d_hidden * up_act * sigma_act * (1.0 + gate_act * (1.0 - sigma_act))).astype(BF)
    d_up_act = (d_hidden * gate_act * sigma_act).astype(BF)
    d_rows = join(
        [mm_t(d_gate_act, wg) + mm_t(d_up_act, wu) for wg, wu in zip(gate_w, up_w)]
    )
    returned_grad = give_back(d_rows.astype(BF))
    d_normed_part = sum(t_mm(pick_low[k], returned_grad[k]) for k in range(experts))
    d_gate_slots = jnp.stack([jnp.sum(
        jnp.where(pick[k], returned_dot[k], 0.0), axis=0
    ) for k in range(experts)], axis=1)

    def expert_grad(left, right):
        halves = split(left)
        if pair:
            other = swap_fsdp(t_mm(halves[1], right).astype(BF))
            mine = t_mm(halves[0], right) + other.astype(F32)
            mine = mine.astype(BF)
        else:
            mine = lax.psum_scatter(
                t_mm(halves[0], right).astype(BF), "fsdp", scatter_dimension=0, tiled=True
            )
        cut = part // n_ctx
        out = jnp.zeros((experts, cut, right.shape[1]), F32)
        for k in range(experts):
            piece = lax.dynamic_slice_in_dim(mine, ((here_ctx + k) % n_ctx) * cut, cut, 0)
            if k:
                piece = shift_ctx(piece, k)
            out = lax.dynamic_update_index_in_dim(
                out, piece.astype(F32), (here_ctx + n_ctx - k) % n_ctx, 0
            )
        return out

    grad_down = expert_grad(d_result, hidden_act)
    grad_gate = expert_grad(token_rows, d_gate_act)
    grad_up = expert_grad(token_rows, d_up_act)

    d_normed = lax.psum_scatter(d_normed_part.astype(BF), "tp", scatter_dimension=1, tiled=True)
    gate_grad = lax.psum(d_gate_slots, "tp")
    pair_grad = jnp.sum(names * gate_grad[:, None, :], axis=-1)
    pick_grad = gate_pair * (pair_grad - jnp.sum(gate_pair * pair_grad, axis=-1, keepdims=True))
    logit_grad = jnp.sum(pick_grad[:, :, None] * route_onehot, axis=1).astype(BF)
    router_here = lax.dynamic_slice_in_dim(router_w, here_tp * width_tp, width_tp, 0)
    d_normed = d_normed.astype(F32) + mm_t(logit_grad, router_here)
    grad_router_part = t_mm(normed_two, logit_grad)
    grad_gain_two_part = jnp.sum(d_normed * unit_two, axis=0)
    gained_two = gain_two_here * d_normed
    dot_two = lax.psum(jnp.sum(unit_two * gained_two, axis=-1, keepdims=True), "tp") / width
    d_resid = out_grad.astype(F32) + scale_two * (gained_two - unit_two * dot_two)
    d_attn = lax.all_gather(d_resid.astype(BF), "tp", axis=1, tiled=True)

    d_attended = into(d_attn, out_parts).astype(BF)
    d_query, key_grad, value_grad = attention_backward(query, kv, d_attended)
    kv_grad = lax.psum_scatter(
        jnp.concatenate([key_grad, value_grad], axis=1), "ctx", scatter_dimension=0, tiled=True
    ).astype(F32)
    d_query_pre = rotate(d_query.reshape(head_shape), cosine, -sine_table)
    d_key_pre = rotate(kv_grad[:, :heads_width].reshape(head_shape), cosine, -sine_table)
    d_qkv = jnp.concatenate(
        [
            d_query_pre.astype(BF).reshape(flat_shape),
            d_key_pre.astype(BF).reshape(flat_shape),
            kv_grad[:, heads_width:].astype(BF),
        ],
        axis=1,
    )
    d_normed_one = lax.psum_scatter(
        back(d_qkv, qkv_parts).astype(BF), "tp", scatter_dimension=1, tiled=True
    ).astype(F32)
    unit_one = hidden_in.astype(F32) * scale_one
    grad_gain_one_part = jnp.sum(d_normed_one * unit_one, axis=0)
    gained_one = my_features(gain_one) * d_normed_one
    dot_one = lax.psum(jnp.sum(unit_one * gained_one, axis=-1, keepdims=True), "tp") / width
    in_grad = d_resid + scale_one * (gained_one - unit_one * dot_one)

    grad_qkv_part = t_mm(normed_one, d_qkv)
    grad_output_part = t_mm(d_attn, attended)
    grad_attn = lax.psum_scatter(
        jnp.concatenate([grad_qkv_part, grad_output_part], axis=1).astype(BF),
        ("fsdp", "ctx"),
        scatter_dimension=0,
        tiled=True,
    ).astype(F32)
    gains = jnp.stack([grad_gain_one_part, grad_gain_two_part], axis=1)
    gains = lax.dynamic_update_slice_in_dim(
        jnp.zeros((width, 2), F32), gains, here_tp * width_tp, 0
    )
    small_part = jnp.concatenate([gains, grad_router_part / n_tp], axis=1)
    small_grad = lax.psum(
        lax.psum_scatter(small_part, ("fsdp", "ctx"), scatter_dimension=0, tiled=True), "tp"
    )
    return (
        block_out,
        in_grad,
        small_grad[:, 0],
        grad_attn[:, :heads_width],
        grad_attn[:, heads_width : 2 * heads_width],
        grad_attn[:, 2 * heads_width : 3 * heads_width],
        grad_attn[:, 3 * heads_width :],
        small_grad[:, 1],
        small_grad[:, 2:],
        grad_gate,
        grad_up,
        grad_down,
    )


def solution(mesh):
    rows = ("fsdp", "ctx")
    placed = (
        P(rows, "tp"),
        P(rows, "tp"),
        P("fsdp"),
        P("fsdp", "tp"),
        P("fsdp", "tp"),
        P("fsdp", "tp"),
        P("fsdp", "tp"),
        P("fsdp"),
        P("fsdp", None),
        P(None, "fsdp", "tp"),
        P(None, "fsdp", "tp"),
        P(None, "fsdp", "tp"),
        P(rows, None),
    )
    return jax.shard_map(
        shards,
        mesh=mesh,
        in_specs=placed,
        out_specs=(
            P(rows, "tp"),
            P(rows, "tp"),
            P(rows),
            P(rows, "tp"),
            P(rows, "tp"),
            P(rows, "tp"),
            P(rows, "tp"),
            P(rows),
            P(rows, None),
            P(None, rows, "tp"),
            P(None, rows, "tp"),
            P(None, rows, "tp"),
        ),
        check_vma=False,
    )
```

time: 3100 us -> 944 us (0.30)
  waiting for transfers between devices: 2590 us -> 606 us
  matrix products: 236 us -> 119 us
  local copies, waits for them, and re-layouts: 92.1 us -> 39 us
  other arithmetic: 101 us -> 52.6 us
  starting transfers between devices: 2.96 us -> 43.6 us
    reduce_scatter x22 -> x7, waiting for transfers between devices: 1360 us -> 81.7 us  [the longest x1 29.8 us: shards(): lax.psum_scatter(jnp.concatenate([key_grad, value_grad], axis=1), 'ctx',...]
    all_gather x20 -> x6, waiting for transfers between devices: 1020 us -> 108 us  [the longest x1 26.5 us: shards(): d_attn = lax.all_gather(d_resid.astype(BF), 'tp', axis=1, tiled=True)]
    ppermute x0 -> x34, waiting for transfers between devices: none -> 416 us  [the longest x7 320 us: swap_fsdp(): return lax.ppermute(value, 'fsdp', [(0, 1), (1, 0)])]
    psum x3 -> x0, waiting for transfers between devices: 189 us -> none  [the longest x1 83.7 us: shards(): lax.psum((d_normed_part, jnp.stack(gate_terms, axis=1)), 'tp')]
    dot_general x57 -> x42, matrix products: 229 us -> 119 us  [the longest x17 45.5 us: t_mm(): lax.dot_general(left, right, (((0,), (0,)), ((), ())), preferred_element_...]
    ppermute x0 -> x34, starting transfers between devices: none -> 42.7 us  [the longest x27 32.6 us: shift_ctx(): lax.ppermute(value, 'ctx', [(i, (i + k) % n_ctx) for i in range(n_ctx)])]
    another operation x15 -> x3, other arithmetic: 34.4 us -> 2.79 us  [the longest x1 10.8 us: shards(): jnp.stack(up_list).astype(jnp.bfloat16)]
    gather x16 -> x0, local copies, waits for them, and re-layouts: 31.5 us -> none  [the longest x4 10.7 us: shards(): spread = result[slot_of]]
  transfers between devices with their start and end apart: 46 -> 47, of which waited for: 44 -> 28; matrix products, arithmetic and copies ran while one was open for 10% -> 14% of each run, Pallas kernels for 0% -> 0%
where the time goes in v1:
time: 944 us; the launch traced here: 934 us
  waiting for transfers between devices  606 us (64%)
  matrix products  119 us (13%)
  other arithmetic  52.6 us (6%)
  blocking collectives  45.2 us (5%)
  starting transfers between devices  43.6 us (5%)
  local copies, waits for them, and re-layouts  39 us (4%)
  between operations  15.8 us (2%)
  Pallas kernels  12.4 us (1%)
    ppermute x7, waiting for transfers between devices, swap_fsdp(): return lax.ppermute(value, 'fsdp', [(0, 1), (1, 0)])  320 us
    ppermute x27, waiting for transfers between devices, shift_ctx(): lax.ppermute(value, 'ctx', [(i, (i + k) % n_ctx) for i in range(n_ctx)])  95.9 us
    dot_general x17, matrix products, t_mm(): lax.dot_general(left, right, (((0,), (0,)), ((), ())), preferred_element_...  45.5 us
    dot_general x14, matrix products, mm(): return jnp.dot(left, right, preferred_element_type=F32)  41.8 us
    ppermute x27, starting transfers between devices, shift_ctx(): lax.ppermute(value, 'ctx', [(i, (i + k) % n_ctx) for i in range(n_ctx)])  32.6 us
    dot_general x11, matrix products, mm_t(): lax.dot_general(left, right, (((1,), (1,)), ((), ())), preferred_element_...  31.9 us
    reduce_scatter x1, waiting for transfers between devices, shards(): lax.psum_scatter(jnp.concatenate([key_grad, value_grad], axis=1), 'ctx',...  29.8 us
    reduce_scatter x1, waiting for transfers between devices, shards(): lax.psum_scatter(back(attended, out_parts).astype(BF), 'tp', scatter_dime...  27.2 us
  transfers between devices with their start and end apart: 47, of which 28 were waited for; matrix products, arithmetic and copies ran while one was open for 14% of the time, Pallas kernels for 0%

profile of v1, /device:TPU:0, one launch (start us, length us, event | category | flops | bytes accessed | tf_op | source)
XLA Modules:
  0.0 933.8 jit_solution(3549916793143631169)
XLA Ops:
  12.4 23.3 %collective-permute-done = bf16[256,2048]{1,0:T(8,128)(2,1)} collective-permute-done((bf16[256,2048]{1,0:T(8,128)(2,1)S(1)}, bf16[256,2048]{1,0:T(8,128)(2,1)}, u32[]{:S(2)}, u32[]{:S(2)}) %collective-permute-start) | collective-permute-done | bytes 1048608 | tf_op jit(solution)/shard_map/ppermute | solution.py:170
  51.5 24.4 %all-gather.9.cloned.1.call-done = bf16[1024,2048]{1,0:T(8,128)(2,1)} async-done(((bf16[256,2048]{1,0:T(8,128)(2,1)}), bf16[1024,2048]{1,0:T(8,128)(2,1)}) %all-gather.9.cloned.1.call-update) | async-done | bytes 4194320 | tf_op jit(solution)/shard_map/all_gather | solution.py:209
  82.4 21.9 %all-gather.11.cloned.1.call-done.key_ref.value_ref = bf16[1024,1024]{1,0:T(8,128)(2,1)} async-done(((bf16[256,1024]{1,0:T(8,128)(2,1)}), bf16[1024,1024]{1,0:T(8,128)(2,1)}) %all-gather.11.cloned.1.call-update) | async-done | bytes 2097168 | tf_op jit(solution)/shard_map/all_gather | solution.py:235
  104.4 5.3 attention_forward.1
  114.1 27.2 %reduce-scatter.8.cloned.1.call-done = bf16[256,512]{1,0:T(8,128)(2,1)} async-done(((bf16[256,2048]{1,0:T(8,128)(2,1)}), bf16[256,512]{1,0:T(8,128)(2,1)}) %reduce-scatter.8.cloned.1.call-update) | async-done | bytes 262160 | tf_op jit(solution)/shard_map/reduce_scatter | solution.py:237
  142.4 9.4 %psum.35 = f32[256,1]{0,1:T(1,128)S(1)} all-reduce(f32[256,1]{0,1:T(1,128)S(1)} %bitcast.205), channel_id=1, replica_groups=mesh['fsdp'=2,'ctx'=4,'tp'=4] {'tp'}, use_global_device_ids=true, to_apply=%region_3.4 | all-reduce | flops 256 | bytes 2048 | tf_op jit(solution)/shard_map/psum | solution.py:241
  166.8 13.5 %all-gather.13.cloned.1.call-done = bf16[256,2048]{1,0:T(8,128)(2,1)} async-done(((bf16[256,512]{1,0:T(8,128)(2,1)}), bf16[256,2048]{1,0:T(8,128)(2,1)}) %all-gather.13.cloned.1.call-update) | async-done | bytes 1048592 | tf_op jit(solution)/shard_map/all_gather | solution.py:245
  187.8 21.5 %all-gather.15.cloned.1.call-done = bf16[256,2048]{1,0:T(8,128)(2,1)} async-done(((bf16[256,512]{1,0:T(8,128)(2,1)}), bf16[256,2048]{1,0:T(8,128)(2,1)}) %all-gather.15.cloned.1.call-update) | async-done | bytes 1048592 | tf_op jit(solution)/shard_map/all_gather | solution.py:273
  227.0 57.8 %collective-permute-done.4 = bf16[1024,1408]{1,0:T(8,128)(2,1)} collective-permute-done((bf16[1024,1408]{1,0:T(8,128)(2,1)}, bf16[1024,1408]{1,0:T(8,128)(2,1)}, u32[]{:S(2)}, u32[]{:S(2)}) %collective-permute-start.4) | collective-permute-done | bytes 2883616 | tf_op jit(solution)/shard_map/ppermute | solution.py:170
  292.9 7.5 multiply_convert_fusion.2
  302.6 40.8 %collective-permute-done.6 = bf16[1024,1408]{1,0:T(8,128)(2,1)S(1)} collective-permute-done((bf16[1024,1408]{1,0:T(8,128)(2,1)S(1)}, bf16[1024,1408]{1,0:T(8,128)(2,1)S(1)}, u32[]{:S(2)}, u32[]{:S(2)}) %collective-permute-start.6) | collective-permute-done | bytes 2883616 | tf_op jit(solution)/shard_map/ppermute | solution.py:170
  353.3 9.7 %psum.36 = f32[256,4]{0,1:T(4,128)} all-reduce(f32[256,4]{0,1:T(4,128)S(1)} %pad_maximum_fusion.16), channel_id=1, replica_groups=mesh['fsdp'=2,'ctx'=4,'tp'=4] {'tp'}, use_global_device_ids=true, to_apply=%region_17.18 | all-reduce | flops 1024 | bytes 8192 | tf_op jit(solution)/shard_map/psum | solution.py:335
  381.1 5.3 fusion.115
  401.7 13.4 %collective-permute-done.18 = bf16[160,2048]{1,0:T(8,128)(2,1)S(1)} collective-permute-done((bf16[160,2048]{1,0:T(8,128)(2,1)S(1)}, bf16[160,2048]{1,0:T(8,128)(2,1)S(1)}, u32[]{:S(2)}, u32[]{:S(2)}) %collective-permute-start.18) | collective-permute-done | bytes 655392 | tf_op jit(solution)/shard_map/ppermute | solution.py:167
  416.4 13.6 %collective-permute-done.17 = bf16[160,2048]{1,0:T(8,128)(2,1)S(1)} collective-permute-done((bf16[160,2048]{1,0:T(8,128)(2,1)S(1)}, bf16[160,2048]{1,0:T(8,128)(2,1)S(1)}, u32[]{:S(2)}, u32[]{:S(2)}) %collective-permute-start.17) | collective-permute-done | bytes 655392 | tf_op jit(solution)/shard_map/ppermute | solution.py:167
  431.7 24.7 %reduce-scatter.12.cloned.1.call-done = bf16[256,512]{1,0:T(8,128)(2,1)} async-done(((bf16[256,2048]{1,0:T(8,128)(2,1)}), bf16[256,512]{1,0:T(8,128)(2,1)}) %reduce-scatter.12.cloned.1.call-update) | async-done | bytes 262160 | tf_op jit(solution)/shard_map/reduce_scatter | solution.py:334
  459.0 9.3 %psum.37 = f32[256,1]{0,1:T(1,128)S(1)} all-reduce(f32[256,1]{0,1:T(1,128)S(1)} %bitcast.216), channel_id=1, replica_groups=mesh['fsdp'=2,'ctx'=4,'tp'=4] {'tp'}, use_global_device_ids=true, to_apply=%region_22.23 | all-reduce | flops 256 | bytes 2048 | tf_op jit(solution)/shard_map/psum | solution.py:344
  470.7 26.5 %all-gather.17.cloned.1.call-done = bf16[256,2048]{1,0:T(8,128)(2,1)} async-done(((bf16[256,512]{1,0:T(8,128)(2,1)}), bf16[256,2048]{1,0:T(8,128)(2,1)}) %all-gather.17.cloned.1.call-update) | async-done | bytes 1048592 | tf_op jit(solution)/shard_map/all_gather | solution.py:346
  501.5 7.1 attention_backward.1
  513.0 29.8 %reduce-scatter.14.cloned.1.call-done = bf16[256,1024]{1,0:T(8,128)(2,1)} async-done(((bf16[1024,1024]{1,0:T(8,128)(2,1)}), bf16[256,1024]{1,0:T(8,128)(2,1)}) %reduce-scatter.14.cloned.1.call-update) | async-done | bytes 524304 | tf_op jit(solution)/shard_map/reduce_scatter | solution.py:350
  560.9 25.9 %collective-permute-done.7 = bf16[160,2048]{1,0:T(8,128)(2,1)S(1)} collective-permute-done((bf16[160,2048]{1,0:T(8,128)(2,1)S(1)}, bf16[160,2048]{1,0:T(8,128)(2,1)S(1)}, u32[]{:S(2)}, u32[]{:S(2)}) %collective-permute-start.7) | collective-permute-done | bytes 655392 | tf_op jit(solution)/shard_map/ppermute | solution.py:167
  602.9 8.5 pad_maximum_fusion
  611.4 6.2 convolution_convert_fusion.1
  629.2 53.5 %collective-permute-done.30 = bf16[1024,1408]{1,0:T(8,128)(2,1)} collective-permute-done((bf16[1024,1408]{1,0:T(8,128)(2,1)}, bf16[1024,1408]{1,0:T(8,128)(2,1)}, u32[]{:S(2)}, u32[]{:S(2)}) %collective-permute-start.30) | collective-permute-done | bytes 2883616 | tf_op jit(solution)/shard_map/ppermute | solution.py:170
  682.6 5.6 add_convert_fusion
  691.8 86.3 %collective-permute-done.26 = bf16[1024,1408]{1,0:T(8,128)(2,1)} collective-permute-done((bf16[1024,1408]{1,0:T(8,128)(2,1)}, bf16[1024,1408]{1,0:T(8,128)(2,1)}, u32[]{:S(2)}, u32[]{:S(2)}) %collective-permute-start.26) | collective-permute-done | bytes 2883616 | tf_op jit(solution)/shard_map/ppermute | solution.py:170
  784.3 55.6 %collective-permute-done.22 = bf16[1024,1408]{1,0:T(8,128)(2,1)} collective-permute-done((bf16[1024,1408]{1,0:T(8,128)(2,1)}, bf16[1024,1408]{1,0:T(8,128)(2,1)}, u32[]{:S(2)}, u32[]{:S(2)}) %collective-permute-start.22) | collective-permute-done | bytes 2883616 | tf_op jit(solution)/shard_map/ppermute | solution.py:170
  859.3 9.9 %collective-permute-done.28 = bf16[256,1408]{1,0:T(8,128)(2,1)S(1)} collective-permute-done((bf16[256,1408]{1,0:T(8,128)(2,1)S(1)}, bf16[256,1408]{1,0:T(8,128)(2,1)S(1)}, u32[]{:S(2)}, u32[]{:S(2)}) %collective-permute-start.28) | collective-permute-done | bytes 720928 | tf_op jit(solution)/shard_map/ppermute | solution.py:167
  869.2 5.2 collective-permute-start.29
  874.4 10.2 %collective-permute-done.24 = bf16[256,1408]{1,0:T(8,128)(2,1)S(1)} collective-permute-done((bf16[256,1408]{1,0:T(8,128)(2,1)S(1)}, bf16[256,1408]{1,0:T(8,128)(2,1)S(1)}, u32[]{:S(2)}, u32[]{:S(2)}) %collective-permute-start.24) | collective-permute-done | bytes 720928 | tf_op jit(solution)/shard_map/ppermute | solution.py:167
  893.5 7.6 collective-permute-done.25
  905.8 12.2 %all-reduce = (f32[256,1]{0,1:T(1,128)S(1)}, f32[256,6]{0,1:T(8,128)S(1)}) all-reduce(f32[256,1]{0,1:T(1,128)S(1)} %bitcast.203, f32[256,6]{0,1:T(8,128)} %reduce-scatter.18.cloned.1.call-done), channel_id=1, replica_groups=mesh['fsdp'=2,'ctx'=4,'tp'=4] {'tp'}, use_global_device_ids=true, to_apply=%region_26.27 | all-reduce | flops 1792 | bytes 14336 | tf_op jit(solution)/shard_map/psum | solution.py:369
  (383 shorter events, 239.6 us)
Async XLA Ops:
  7.2 37.6 %all-gather.7.cloned.1.call-start = ((), (), s32[]{:S(2)}) async-start(), calls=%async_computation.7 | async-start | bytes 1310720 | tf_op jit(solution)/shard_map/all_gather | solution.py:203
  7.9 67.9 %all-gather.9.cloned.1.call-start = ((), (), s32[]{:S(2)}) async-start(), calls=%async_computation.8 | async-start | bytes 5242880 | tf_op jit(solution)/shard_map/all_gather | solution.py:209
  35.7 68.7 %all-gather.11.cloned.1.call-start = ((), (), s32[]{:S(2)}) async-start(), calls=%async_computation.9 | async-start | bytes 2621440 | tf_op jit(solution)/shard_map/all_gather | solution.py:235
  81.6 59.7 %reduce-scatter.8.cloned.1.call-start = ((), (), s32[]{:S(2)}) async-start(), calls=%async_computation.10 | async-start | bytes 1310720 | tf_op jit(solution)/shard_map/reduce_scatter | solution.py:237
  114.0 66.3 %all-gather.13.cloned.1.call-start = ((), (), s32[]{:S(2)}) async-start(), calls=%async_computation.11 | async-start | bytes 1310720 | tf_op jit(solution)/shard_map/all_gather | solution.py:245
  153.6 55.6 %all-gather.15.cloned.1.call-start = ((), (), s32[]{:S(2)}) async-start(), calls=%async_computation.13 | async-start | bytes 1310720 | tf_op jit(solution)/shard_map/all_gather | solution.py:273
  157.3 65.7 %collective-permute-start.5 = (bf16[1024,1408]{1,0:T(8,128)(2,1)}, bf16[1024,1408]{1,0:T(8,128)(2,1)}, u32[]{:S(2)}, u32[]{:S(2)}) collective-permute-start(bf16[1024,1408]{1,0:T(8,128)(2,1)} %dynamic-slice_bitcast_fusion.1), channel_id=1, source_target_pairs={{0,16},{16,0},{1,17},{17,1},{2,18},{18,2},{3,19},{19,3},{4,20},{20... | collective-permute-start | bytes 8650760 | tf_op jit(solution)/shard_map/ppermute | solution.py:170
  162.4 122.4 %collective-permute-start.4 = (bf16[1024,1408]{1,0:T(8,128)(2,1)}, bf16[1024,1408]{1,0:T(8,128)(2,1)}, u32[]{:S(2)}, u32[]{:S(2)}) collective-permute-start(bf16[1024,1408]{1,0:T(8,128)(2,1)} %dynamic-slice_bitcast_fusion.2), channel_id=1, source_target_pairs={{0,16},{16,0},{1,17},{17,1},{2,18},{18,2},{3,19},{19,3},{4,20},{20... | collective-permute-start | bytes 8650760 | tf_op jit(solution)/shard_map/ppermute | solution.py:170
  163.0 293.4 %reduce-scatter.12.cloned.1.call-start = ((), (), s32[]{:S(2)}) async-start(), calls=%async_computation.14 | async-start | bytes 1310720 | tf_op jit(solution)/shard_map/reduce_scatter | solution.py:334
  186.8 30.5 %collective-permute-start.2 = (bf16[160,2048]{1,0:T(8,128)(2,1)}, bf16[160,2048]{1,0:T(8,128)(2,1)}, u32[]{:S(2)}, u32[]{:S(2)}) collective-permute-start(bf16[160,2048]{1,0:T(8,128)(2,1)} %get-tuple-element.95), channel_id=1, source_target_pairs={{0,8},{4,12},{8,0},{12,4},{1,9},{5,13},{9,1},{13,5},{2,10},{6,14},... | collective-permute-start | bytes 1966088 | tf_op jit(solution)/shard_map/ppermute | solution.py:167
  187.5 30.1 %collective-permute-start.1 = (bf16[160,2048]{1,0:T(8,128)(2,1)}, bf16[160,2048]{1,0:T(8,128)(2,1)}, u32[]{:S(2)}, u32[]{:S(2)}) collective-permute-start(bf16[160,2048]{1,0:T(8,128)(2,1)} %get-tuple-element.96), channel_id=1, source_target_pairs={{0,4},{4,8},{8,12},{12,0},{1,5},{5,9},{9,13},{13,1},{2,6},{6,10},{... | collective-permute-start | bytes 1966088 | tf_op jit(solution)/shard_map/ppermute | solution.py:167
  214.0 129.4 %collective-permute-start.6 = (bf16[1024,1408]{1,0:T(8,128)(2,1)S(1)}, bf16[1024,1408]{1,0:T(8,128)(2,1)S(1)}, u32[]{:S(2)}, u32[]{:S(2)}) collective-permute-start(bf16[1024,1408]{1,0:T(8,128)(2,1)S(1)} %copy-done.13), channel_id=1, source_target_pairs={{0,16},{16,0},{1,17},{17,1},{2,18},{18,2},{3,19},{19,3},{4,20},{20... | collective-permute-start | bytes 8650760 | tf_op jit(solution)/shard_map/ppermute | solution.py:170
  217.4 128.2 %collective-permute-start.15 = (bf16[160,2048]{1,0:T(8,128)(2,1)S(1)}, bf16[160,2048]{1,0:T(8,128)(2,1)S(1)}, u32[]{:S(2)}, u32[]{:S(2)}) collective-permute-start(bf16[160,2048]{1,0:T(8,128)(2,1)S(1)} %get-tuple-element.90), channel_id=1, source_target_pairs={{0,12},{4,0},{8,4},{12,8},{1,13},{5,1},{9,5},{13,9},{2,14},{6,2},{... | collective-permute-start | bytes 1966088 | tf_op jit(solution)/shard_map/ppermute | solution.py:167
  217.6 128.0 %collective-permute-start.14 = (bf16[160,2048]{1,0:T(8,128)(2,1)S(1)}, bf16[160,2048]{1,0:T(8,128)(2,1)S(1)}, u32[]{:S(2)}, u32[]{:S(2)}) collective-permute-start(bf16[160,2048]{1,0:T(8,128)(2,1)S(1)} %get-tuple-element.91), channel_id=1, source_target_pairs={{0,8},{4,12},{8,0},{12,4},{1,9},{5,13},{9,1},{13,5},{2,10},{6,14},... | collective-permute-start | bytes 1966088 | tf_op jit(solution)/shard_map/ppermute | solution.py:167
  223.0 122.6 %collective-permute-start.13 = (bf16[160,2048]{1,0:T(8,128)(2,1)S(1)}, bf16[160,2048]{1,0:T(8,128)(2,1)S(1)}, u32[]{:S(2)}, u32[]{:S(2)}) collective-permute-start(bf16[160,2048]{1,0:T(8,128)(2,1)S(1)} %get-tuple-element.92), channel_id=1, source_target_pairs={{0,4},{4,8},{8,12},{12,0},{1,5},{5,9},{9,13},{13,1},{2,6},{6,10},{... | collective-permute-start | bytes 1966088 | tf_op jit(solution)/shard_map/ppermute | solution.py:167
  400.6 29.3 %collective-permute-start.17 = (bf16[160,2048]{1,0:T(8,128)(2,1)S(1)}, bf16[160,2048]{1,0:T(8,128)(2,1)S(1)}, u32[]{:S(2)}, u32[]{:S(2)}) collective-permute-start(bf16[160,2048]{1,0:T(8,128)(2,1)S(1)} %get-tuple-element.81), channel_id=1, source_target_pairs={{0,8},{4,12},{8,0},{12,4},{1,9},{5,13},{9,1},{13,5},{2,10},{6,14},... | collective-permute-start | bytes 1966088 | tf_op jit(solution)/shard_map/ppermute | solution.py:167
  431.5 65.6 %all-gather.17.cloned.1.call-start = ((), (), s32[]{:S(2)}) async-start(), calls=%async_computation.15 | async-start | bytes 1310720 | tf_op jit(solution)/shard_map/all_gather | solution.py:346
  470.4 72.4 %reduce-scatter.14.cloned.1.call-start = ((), (), s32[]{:S(2)}) async-start(), calls=%async_computation.16 | async-start | bytes 2621440 | tf_op jit(solution)/shard_map/reduce_scatter | solution.py:350
  511.7 77.4 %reduce-scatter.16.cloned.1.call-start = ((), (), s32[]{:S(2)}) async-start(), calls=%async_computation.17 | async-start | bytes 1310720 | tf_op jit(solution)/shard_map/reduce_scatter | solution.py:363
  554.9 350.8 %reduce-scatter.18.cloned.1.call-start = ((), (), s32[]{:S(2)}) async-start(), calls=%async_computation.18 | async-start | bytes 73728 | tf_op jit(solution)/shard_map/reduce_scatter | solution.py:386
  558.1 33.2 %collective-permute-start.8 = (bf16[160,2048]{1,0:T(8,128)(2,1)}, bf16[160,2048]{1,0:T(8,128)(2,1)}, u32[]{:S(2)}, u32[]{:S(2)}) collective-permute-start(bf16[160,2048]{1,0:T(8,128)(2,1)} %get-tuple-element.86), channel_id=1, source_target_pairs={{0,8},{4,12},{8,0},{12,4},{1,9},{5,13},{9,1},{13,5},{2,10},{6,14},... | collective-permute-start | bytes 1966088 | tf_op jit(solution)/shard_map/ppermute | solution.py:167
  558.4 30.2 %collective-permute-start.9 = (bf16[160,2048]{1,0:T(8,128)(2,1)S(1)}, bf16[160,2048]{1,0:T(8,128)(2,1)S(1)}, u32[]{:S(2)}, u32[]{:S(2)}) collective-permute-start(bf16[160,2048]{1,0:T(8,128)(2,1)S(1)} %get-tuple-element.87), channel_id=1, source_target_pairs={{0,4},{4,8},{8,12},{12,0},{1,5},{5,9},{9,13},{13,1},{2,6},{6,10},{... | collective-permute-start | bytes 1966088 | tf_op jit(solution)/shard_map/ppermute | solution.py:167
  558.4 28.4 %collective-permute-start.7 = (bf16[160,2048]{1,0:T(8,128)(2,1)S(1)}, bf16[160,2048]{1,0:T(8,128)(2,1)S(1)}, u32[]{:S(2)}, u32[]{:S(2)}) collective-permute-start(bf16[160,2048]{1,0:T(8,128)(2,1)S(1)} %get-tuple-element.88), channel_id=1, source_target_pairs={{0,12},{4,0},{8,4},{12,8},{1,13},{5,1},{9,5},{13,9},{2,14},{6,2},{... | collective-permute-start | bytes 1966088 | tf_op jit(solution)/shard_map/ppermute | solution.py:167
  591.2 328.0 %reduce-scatter.10.cloned.1.call-start = ((), (), s32[]{:S(2)}) async-start(), calls=%async_computation.12 | async-start | bytes 1310720 | tf_op jit(solution)/shard_map/reduce_scatter | solution.py:294
  594.7 326.8 %reduce-scatter.20.cloned.1.call-start = ((), (), s32[]{:S(2)}) async-start(), calls=%async_computation.19 | async-start | bytes 9437184 | tf_op jit(solution)/shard_map/reduce_scatter | solution.py:374
  617.6 65.0 %collective-permute-start.30 = (bf16[1024,1408]{1,0:T(8,128)(2,1)}, bf16[1024,1408]{1,0:T(8,128)(2,1)}, u32[]{:S(2)}, u32[]{:S(2)}) collective-permute-start(bf16[1024,1408]{1,0:T(8,128)(2,1)} %convolution_convert_fusion.1), channel_id=1, source_target_pairs={{0,16},{16,0},{1,17},{17,1},{2,18},{18,2},{3,19},{19,3},{4,20},{20... | collective-permute-start | bytes 8650760 | tf_op jit(solution)/shard_map/ppermute | solution.py:170
  623.2 154.9 %collective-permute-start.26 = (bf16[1024,1408]{1,0:T(8,128)(2,1)}, bf16[1024,1408]{1,0:T(8,128)(2,1)}, u32[]{:S(2)}, u32[]{:S(2)}) collective-permute-start(bf16[1024,1408]{1,0:T(8,128)(2,1)} %convolution_convert_fusion.2), channel_id=1, source_target_pairs={{0,16},{16,0},{1,17},{17,1},{2,18},{18,2},{3,19},{19,3},{4,20},{20... | collective-permute-start | bytes 8650760 | tf_op jit(solution)/shard_map/ppermute | solution.py:170
  627.6 212.3 %collective-permute-start.22 = (bf16[1024,1408]{1,0:T(8,128)(2,1)}, bf16[1024,1408]{1,0:T(8,128)(2,1)}, u32[]{:S(2)}, u32[]{:S(2)}) collective-permute-start(bf16[1024,1408]{1,0:T(8,128)(2,1)} %convolution_convert_fusion.3), channel_id=1, source_target_pairs={{0,16},{16,0},{1,17},{17,1},{2,18},{18,2},{3,19},{19,3},{4,20},{20... | collective-permute-start | bytes 8650760 | tf_op jit(solution)/shard_map/ppermute | solution.py:170
  688.4 215.4 %collective-permute-start.33 = (bf16[256,1408]{1,0:T(8,128)(2,1)S(1)}, bf16[256,1408]{1,0:T(8,128)(2,1)S(1)}, u32[]{:S(2)}, u32[]{:S(2)}) collective-permute-start(bf16[256,1408]{1,0:T(8,128)(2,1)S(1)} %get-tuple-element.72), channel_id=1, source_target_pairs={{0,12},{4,0},{8,4},{12,8},{1,13},{5,1},{9,5},{13,9},{2,14},{6,2},{... | collective-permute-start | bytes 2162696 | tf_op jit(solution)/shard_map/ppermute | solution.py:167
  690.1 212.5 %collective-permute-start.32 = (bf16[256,1408]{1,0:T(8,128)(2,1)S(1)}, bf16[256,1408]{1,0:T(8,128)(2,1)S(1)}, u32[]{:S(2)}, u32[]{:S(2)}) collective-permute-start(bf16[256,1408]{1,0:T(8,128)(2,1)S(1)} %get-tuple-element.73), channel_id=1, source_target_pairs={{0,8},{4,12},{8,0},{12,4},{1,9},{5,13},{9,1},{13,5},{2,10},{6,14},... | collective-permute-start | bytes 2162696 | tf_op jit(solution)/shard_map/ppermute | solution.py:167
  691.6 209.6 %collective-permute-start.31 = (bf16[256,1408]{1,0:T(8,128)(2,1)S(1)}, bf16[256,1408]{1,0:T(8,128)(2,1)S(1)}, u32[]{:S(2)}, u32[]{:S(2)}) collective-permute-start(bf16[256,1408]{1,0:T(8,128)(2,1)S(1)} %get-tuple-element.74), channel_id=1, source_target_pairs={{0,4},{4,8},{8,12},{12,0},{1,5},{5,9},{9,13},{13,1},{2,6},{6,10},{... | collective-permute-start | bytes 2162696 | tf_op jit(solution)/shard_map/ppermute | solution.py:167
  782.5 67.5 %collective-permute-start.27 = (bf16[256,1408]{1,0:T(8,128)(2,1)S(1)}, bf16[256,1408]{1,0:T(8,128)(2,1)S(1)}, u32[]{:S(2)}, u32[]{:S(2)}) collective-permute-start(bf16[256,1408]{1,0:T(8,128)(2,1)S(1)} %get-tuple-element.77), channel_id=1, source_target_pairs={{0,4},{4,8},{8,12},{12,0},{1,5},{5,9},{9,13},{13,1},{2,6},{6,10},{... | collective-permute-start | bytes 2162696 | tf_op jit(solution)/shard_map/ppermute | solution.py:167
  (91 other events, 1910.5 us)
Sparse Core Ops, SparseCore 0:
  9.6 30.6 all-gather.6
  41.8 33.9 all-gather.8
  81.7 22.5 all-gather.10
  114.1 27.1 reduce-scatter.7
  153.7 26.4 all-gather.12
  181.8 27.4 all-gather.14
  431.6 24.6 reduce-scatter.11
  470.6 26.5 all-gather.16
  511.9 30.9 reduce-scatter.13
  555.1 27.1 reduce-scatter.15
  591.3 34.8 reduce-scatter.17
  628.4 27.1 reduce-scatter.9
  659.1 103.6 reduce-scatter.19

commit v2 on v1

v2 whole, which is shorter than its diff:
```python
from functools import partial
import math

import jax
import jax.numpy as jnp
from jax import lax
from jax.experimental import pallas as pl
from jax.experimental.pallas import tpu as pltpu
from jax.sharding import PartitionSpec as P

HD = 128
CAP = 160


EPS = 1e-05
THETA = 10000.0
NEG = -1e30
BF = jnp.bfloat16
F32 = jnp.float32


def mm(left, right):
    return jnp.dot(left, right, preferred_element_type=F32)


def mm_t(left, right):
    return lax.dot_general(left, right, (((1,), (1,)), ((), ())), preferred_element_type=F32)


def t_mm(left, right):
    return lax.dot_general(left, right, (((0,), (0,)), ((), ())), preferred_element_type=F32)


def rotary_tables(positions):
    half_size = HD // 2
    frequency = THETA ** (-(jnp.arange(half_size, dtype=F32) * 2.0 / HD))
    angles = positions.astype(F32)[:, None] * frequency[None, :]
    return (jnp.cos(angles)[:, None, :], jnp.sin(angles)[:, None, :])


def rotate(values, cosine, sine_table):
    half_size = values.shape[-1] // 2
    first_half = values[..., :half_size]
    second_half = values[..., half_size:]
    return jnp.concatenate(
        [
            first_half * cosine - second_half * sine_table,
            second_half * cosine + first_half * sine_table,
        ],
        axis=-1,
    )


MESH = pl.DeviceIdType.MESH
VM = pl.BlockSpec(memory_space=pltpu.VMEM)
DMA = pltpu.SemaphoreType.DMA


def peer(axis, n, k):
    return lax.rem(lax.axis_index(axis) + k, n)


def greet(groups):
    barrier = pltpu.get_barrier_semaphore()
    for axis, n in groups:
        for k in range(1, n):
            pl.semaphore_signal(
                barrier, inc=1, device_id={axis: peer(axis, n, k)}, device_id_type=MESH
            )
    pl.semaphore_wait(barrier, sum(n - 1 for _, n in groups))


def send(source, target, axis, n, k, sems):
    copy = pltpu.make_async_remote_copy(
        src_ref=source,
        dst_ref=target,
        send_sem=sems[0].at[k - 1],
        recv_sem=sems[1].at[k - 1],
        device_id={axis: peer(axis, n, k)},
        device_id_type=MESH,
    )
    copy.start()
    return copy


def columns(n, size):
    return pl.ds(pl.multiple_of(n * size, 128), size)


def gather_columns(own, full, axis, n, sems):
    size = own.shape[1]
    place = full.at[:, columns(lax.axis_index(axis), size)]
    copies = [send(own, place, axis, n, k, sems) for k in range(1, n)]
    place[...] = own[...]
    return copies


def scatter_columns(part, slots, axis, n, sems):
    size = slots.shape[2]
    return [
        send(part.at[:, columns(peer(axis, n, k), size)], slots.at[k - 1], axis, n, k, sems)
        for k in range(1, n)
    ]


def finish(copies):
    for copy in copies:
        copy.wait()


def row_sums(values):
    ones = jnp.ones((8, values.shape[1]), F32)
    return lax.dot_general(
        ones,
        values,
        (((1,), (1,)), ((), ())),
        precision=lax.Precision.HIGHEST,
        preferred_element_type=F32,
    )


def as_column(sums):
    eighth = jnp.full((8, 128), 0.125, F32)
    return lax.dot_general(
        sums,
        eighth,
        (((0,), (0,)), ((), ())),
        precision=lax.Precision.HIGHEST,
        preferred_element_type=F32,
    )


def total_over(sums, mine, slots, axis, n, sems):
    mine[...] = sums
    copies = [send(mine, slots.at[k - 1], axis, n, k, sems) for k in range(1, n)]
    finish(copies)
    total = sums
    for k in range(1, n):
        total = total + slots[k - 1]
    return total


def call(kernel, out_shape, inputs, scratch, collective, name):
    return pl.pallas_call(
        kernel,
        out_shape=out_shape,
        in_specs=[VM] * len(inputs),
        out_specs=jax.tree.map(lambda _: VM, out_shape),
        scratch_shapes=scratch,
        compiler_params=pltpu.CompilerParams(collective_id=collective, has_side_effects=True),
        cost_estimate=pl.CostEstimate(flops=0, bytes_accessed=0, transcendentals=0),
        name=name,
    )(*inputs)


def shape(dims, dtype):
    return jax.ShapeDtypeStruct(dims, dtype)


def pair_of_sems(n):
    return [DMA((n - 1,)), DMA((n - 1,))]


def first_norm(hidden, grad, small, n_tp, n_fsdp):
    rows, size = hidden.shape
    width = size * n_tp

    def kernel(hid, grd, sml, out, scale, grd_full, sml_full, hid_full, *sems):
        greet([("tp", n_tp), ("fsdp", n_fsdp)])
        gains = gather_columns(sml, sml_full, "fsdp", n_fsdp, sems[0:2])
        hids = gather_columns(hid, hid_full, "tp", n_tp, sems[2:4])
        grads = gather_columns(grd, grd_full, "tp", n_tp, sems[4:6])
        finish(gains)
        finish(hids)
        values = hid_full[...].astype(F32)
        mean = jnp.sum(values * values, axis=-1, keepdims=True) * (1.0 / width)
        factor = lax.rsqrt(mean + EPS)
        scale[...] = jnp.broadcast_to(factor, scale.shape)
        out[...] = (values * factor * sml_full[0:1, :]).astype(BF)
        finish(grads)

    return call(
        kernel,
        (
            shape((rows, width), BF),
            shape((rows, 128), F32),
            shape((rows, width), BF),
            shape((8, width), F32),
        ),
        (hidden, grad, small),
        [pltpu.VMEM((rows, width), BF)] + pair_of_sems(n_fsdp) + pair_of_sems(n_tp) * 2,
        1,
        "first_norm",
    )


def gather_rows(value, axis, n, collective):
    rows = value.shape[0]

    def kernel(own, full, *sems):
        greet([(axis, n)])
        place = full.at[pl.ds(pl.multiple_of(lax.axis_index(axis) * rows, 16), rows), :]
        copies = [send(own, place, axis, n, k, sems) for k in range(1, n)]
        place[...] = own[...]
        finish(copies)

    return call(
        kernel,
        shape((rows * n, value.shape[1]), value.dtype),
        (value,),
        pair_of_sems(n),
        collective,
        "gather_" + axis,
    )


def softmax_rows(query, key, first_row):
    scores = mm_t(query, key) * (1.0 / math.sqrt(HD))
    rows = first_row + lax.broadcasted_iota(jnp.int32, scores.shape, 0)
    cols = lax.broadcasted_iota(jnp.int32, scores.shape, 1)
    scores = jnp.where(cols <= rows, scores, NEG)
    top = jnp.max(scores, axis=-1, keepdims=True)
    weights = jnp.exp(scores - top)
    return weights / jnp.sum(weights, axis=-1, keepdims=True)


def attention_forward(query, kv, n_ctx):
    rows, width = query.shape
    heads = width // HD

    def kernel(qry, own, out, full, *sems):
        greet([("ctx", n_ctx)])
        here = lax.axis_index("ctx")
        place = full.at[pl.ds(pl.multiple_of(here * rows, 16), rows), :]
        copies = [send(own, place, "ctx", n_ctx, k, sems) for k in range(1, n_ctx)]
        place[...] = own[...]
        finish(copies)

        @pl.loop(0, heads)
        def _(h):
            probs = softmax_rows(qry[:, columns(h, HD)], full[:, columns(h, HD)], here * rows)
            out[:, columns(h, HD)] = mm(
                probs.astype(BF), full[:, columns(h + heads, HD)]
            ).astype(BF)

    return call(
        kernel,
        (shape((rows, width), BF), shape((rows * n_ctx, 2 * width), BF)),
        (query, kv),
        pair_of_sems(n_ctx),
        2,
        "attention_forward",
    )


def second_norm(part, hidden, gain, n_tp):
    rows, size = hidden.shape
    width = size * n_tp

    def kernel(prt, hid, gn, resid, scale, out, slots, mine, sums, low, *sems):
        greet([("tp", n_tp)])
        here = lax.axis_index("tp")
        copies = scatter_columns(prt, slots, "tp", n_tp, sems[0:2])
        total = prt[:, columns(here, size)].astype(F32)
        finish(copies)
        for k in range(1, n_tp):
            total = total + slots[k - 1].astype(F32)
        total = hid[...].astype(F32) + total
        resid[...] = total
        square = total_over(row_sums(total * total), mine, sums, "tp", n_tp, sems[2:4])
        factor = lax.rsqrt(as_column(square) * (1.0 / width) + EPS)
        scale[...] = factor
        low[...] = (resid[...] * factor[:, 0:1] * gn[0:1, :]).astype(BF)
        finish(gather_columns(low, out, "tp", n_tp, sems[4:6]))

    return call(
        kernel,
        (shape((rows, size), F32), shape((rows, 128), F32), shape((rows, width), BF)),
        (part, hidden, gain),
        [
            pltpu.VMEM((n_tp - 1, rows, size), BF),
            pltpu.VMEM((8, rows), F32),
            pltpu.VMEM((n_tp - 1, 8, rows), F32),
            pltpu.VMEM((rows, size), BF),
        ]
        + pair_of_sems(n_tp) * 3,
        3,
        "second_norm",
    )


def second_norm_back(part, dots, gates, onehot, names, router, resid, scale, gain, grad, n_tp):
    rows, size = resid.shape
    width = size * n_tp

    def kernel(
        prt, dts, gts, one, nms, rtr, rsd, scl, gn, grd,
        d_resid, d_attn, d_gain, d_logits, slots, mine, sums, mine_two, sums_two, low, *sems
    ):
        greet([("tp", n_tp)])
        here = lax.axis_index("tp")
        copies = scatter_columns(prt, slots, "tp", n_tp, sems[0:2])
        gate_grad = total_over(dts[...], mine, sums, "tp", n_tp, sems[2:4])
        both = [jnp.sum(nms[j] * gate_grad, axis=0, keepdims=True) for j in range(2)]
        gate = [gts[j : j + 1, :] for j in range(2)]
        mean = gate[0] * both[0] + gate[1] * both[1]
        logits = sum(gate[j] * (both[j] - mean) * one[j] for j in range(2))
        d_logits[...] = logits
        total = prt[:, columns(here, size)].astype(F32) + lax.dot_general(
            logits.astype(BF),
            rtr[...].astype(BF),
            (((0,), (0,)), ((), ())),
            preferred_element_type=F32,
        )
        finish(copies)
        for k in range(1, n_tp):
            total = total + slots[k - 1].astype(F32)
        factor = scl[:, 0:1]
        unit = rsd[...] * factor
        d_gain[...] = jnp.broadcast_to(jnp.sum(total * unit, axis=0, keepdims=True), d_gain.shape)
        gained = total * gn[0:1, :]
        d_resid[...] = gained
        dot = total_over(row_sums(unit * gained), mine_two, sums_two, "tp", n_tp, sems[4:6])
        dot = as_column(dot)[:, 0:1] * (1.0 / width)
        result = grd[...].astype(F32) + factor * (d_resid[...] - rsd[...] * factor * dot)
        d_resid[...] = result
        low[...] = result.astype(BF)
        finish(gather_columns(low, d_attn, "tp", n_tp, sems[6:8]))

    return call(
        kernel,
        (
            shape((rows, size), F32),
            shape((rows, width), BF),
            shape((8, size), F32),
            shape((8, rows), F32),
        ),
        (part, dots, gates, onehot, names, router, resid, scale, gain, grad),
        [
            pltpu.VMEM((n_tp - 1, rows, size), BF),
            pltpu.VMEM((8, rows), F32),
            pltpu.VMEM((n_tp - 1, 8, rows), F32),
            pltpu.VMEM((8, rows), F32),
            pltpu.VMEM((n_tp - 1, 8, rows), F32),
            pltpu.VMEM((rows, size), BF),
        ]
        + pair_of_sems(n_tp) * 4,
        4,
        "second_norm_back",
    )


def attention_backward(query, kv, dout, n_ctx):
    rows, width = query.shape
    heads = width // HD
    scale = 1.0 / math.sqrt(HD)

    def kernel(qry, full, dot, dq, dkv, low, slots, *sems):
        greet([("ctx", n_ctx)])
        here = lax.axis_index("ctx")

        @pl.loop(0, heads)
        def _(h):
            at, at_v = columns(h, HD), columns(h + heads, HD)
            probs = softmax_rows(qry[:, at], full[:, at], here * rows)
            d_probs = mm_t(dot[:, at], full[:, at_v])
            delta = jnp.sum(probs * d_probs, axis=-1, keepdims=True)
            d_scores = (probs * (d_probs - delta)).astype(BF)
            dq[:, at] = mm(d_scores, full[:, at]) * scale
            low[:, at] = (t_mm(d_scores, qry[:, at]) * scale).astype(BF)
            low[:, at_v] = t_mm(probs.astype(BF), dot[:, at]).astype(BF)

        copies = []
        for k in range(1, n_ctx):
            to = peer("ctx", n_ctx, k) * rows
            copies.append(
                send(
                    low.at[pl.ds(pl.multiple_of(to, 16), rows), :],
                    slots.at[k - 1],
                    "ctx",
                    n_ctx,
                    k,
                    sems,
                )
            )
        total = low[pl.ds(pl.multiple_of(here * rows, 16), rows), :].astype(F32)
        finish(copies)
        for k in range(1, n_ctx):
            total = total + slots[k - 1].astype(F32)
        dkv[...] = total

    return call(
        kernel,
        (shape((rows, width), F32), shape((rows, 2 * width), F32)),
        (query, kv, dout),
        [
            pltpu.VMEM((rows * n_ctx, 2 * width), BF),
            pltpu.VMEM((n_ctx - 1, rows, 2 * width), BF),
        ]
        + pair_of_sems(n_ctx),
        5,
        "attention_backward",
    )


def first_norm_back(part, hidden, scale, gain, d_resid, n_tp):
    rows, size = hidden.shape
    width = size * n_tp

    def kernel(prt, hid, scl, gn, dr, out, d_gain, slots, mine, sums, *sems):
        greet([("tp", n_tp)])
        here = lax.axis_index("tp")
        copies = scatter_columns(prt, slots, "tp", n_tp, sems[0:2])
        total = prt[:, columns(here, size)].astype(F32)
        finish(copies)
        for k in range(1, n_tp):
            total = total + slots[k - 1].astype(F32)
        factor = scl[:, 0:1]
        unit = hid[...].astype(F32) * factor
        d_gain[...] = jnp.broadcast_to(jnp.sum(total * unit, axis=0, keepdims=True), d_gain.shape)
        gained = total * gn[0:1, :]
        out[...] = gained
        dot = total_over(row_sums(unit * gained), mine, sums, "tp", n_tp, sems[2:4])
        dot = as_column(dot)[:, 0:1] * (1.0 / width)
        unit = hid[...].astype(F32) * factor
        out[...] = dr[...] + factor * (out[...] - unit * dot)

    return call(
        kernel,
        (shape((rows, size), F32), shape((8, size), F32)),
        (part, hidden, scale, gain, d_resid),
        [
            pltpu.VMEM((n_tp - 1, rows, size), BF),
            pltpu.VMEM((8, rows), F32),
            pltpu.VMEM((n_tp - 1, 8, rows), F32),
        ]
        + pair_of_sems(n_tp) * 2,
        6,
        "first_norm_back",
    )


def after(value, *needed):
    held = lax.optimization_barrier((value, *needed))
    return held[0]


def shards(
    hidden_in,
    out_grad,
    attn_gain,
    w_query,
    w_key,
    w_value,
    w_output,
    ffn_gain,
    w_router,
    w_gate,
    w_up,
    w_down,
    routes,
):
    rows_here, width_tp = hidden_in.shape
    here_tp = lax.axis_index("tp")
    here_ctx = lax.axis_index("ctx")
    here_fsdp = lax.axis_index("fsdp")
    n_fsdp = lax.axis_size("fsdp")
    n_ctx = lax.axis_size("ctx")
    n_tp = lax.axis_size("tp")
    experts = w_gate.shape[0]
    assert experts == n_ctx
    width = width_tp * n_tp
    part = width // n_fsdp
    pair = n_fsdp == 2
    heads_width = w_query.shape[1]

    def shift_ctx(value, k):
        return lax.ppermute(value, "ctx", [(i, (i + k) % n_ctx) for i in range(n_ctx)])

    def swap_fsdp(value):
        return lax.ppermute(value, "fsdp", [(0, 1), (1, 0)])

    def other_parts(weight):
        if pair:
            return [weight, swap_fsdp(weight)]
        return [lax.all_gather(weight, "fsdp", axis=0, tiled=True)]

    def split(values):
        if pair:
            return [
                lax.dynamic_slice_in_dim(values, here_fsdp * part, part, 1),
                lax.dynamic_slice_in_dim(values, (1 - here_fsdp) * part, part, 1),
            ]
        return [values]

    def join(pieces):
        if pair:
            first = here_fsdp == 0
            return jnp.concatenate(
                [jnp.where(first, pieces[0], pieces[1]), jnp.where(first, pieces[1], pieces[0])],
                axis=1,
            )
        return pieces[0]

    def into(values, weights):
        return sum(mm(x, w) for x, w in zip(split(values), weights))

    def back(values, weights):
        return join([mm_t(values, w) for w in weights])

    def my_features(values):
        return lax.dynamic_slice_in_dim(values, here_tp * width_tp, width_tp, values.ndim - 1)

    attn_w = jnp.concatenate([w_query, w_key, w_value, w_output], axis=1)
    if pair:
        quarter = part // n_ctx
        own_quarter = lax.dynamic_slice_in_dim(attn_w, here_ctx * quarter, quarter, 0)
        other_quarter = swap_fsdp(own_quarter)
    gate_w = other_parts(lax.dynamic_index_in_dim(w_gate, here_ctx, 0, False))
    up_w = other_parts(lax.dynamic_index_in_dim(w_up, here_ctx, 0, False))
    down_w = other_parts(lax.dynamic_index_in_dim(w_down, here_ctx, 0, False))
    small = jnp.concatenate(
        [attn_gain[None], ffn_gain[None], w_router.T, jnp.zeros((2, part), BF)], axis=0
    ).astype(F32)
    normed_one, scale_one, grad_full, small_full = first_norm(
        hidden_in, out_grad, small, n_tp, n_fsdp
    )
    scale_one = scale_one[:, :1]
    if pair:
        attn_parts = [attn_w, gather_rows(other_quarter, "ctx", n_ctx, 7)]
    else:
        attn_parts = [lax.all_gather(attn_w, "fsdp", axis=0, tiled=True)]
    qkv_parts = [w[:, : 3 * heads_width] for w in attn_parts]
    out_parts = [w[:, 3 * heads_width :] for w in attn_parts]
    small_here = my_features(small_full)
    gain_one_here = jnp.broadcast_to(small_here[0:1], small_here.shape)
    gain_two_here = jnp.broadcast_to(small_here[1:2], small_here.shape)
    router_w = small_full[2 : 2 + experts].astype(BF)
    router_here = jnp.concatenate(
        [small_here[2 : 2 + experts], jnp.zeros((8 - experts, width_tp), F32)], axis=0
    )

    heads_here = heads_width // HD
    head_shape = (rows_here, heads_here, HD)
    flat_shape = (rows_here, heads_width)
    positions = here_ctx * rows_here + jnp.arange(rows_here, dtype=jnp.int32)
    cosine, sine_table = rotary_tables(positions)
    qkv = into(normed_one, qkv_parts)
    query_pre = qkv[:, :heads_width].reshape(head_shape)
    key_pre = qkv[:, heads_width : 2 * heads_width].reshape(head_shape)
    query = rotate(query_pre, cosine, sine_table).astype(BF).reshape(flat_shape)
    key = rotate(key_pre, cosine, sine_table).astype(BF).reshape(flat_shape)
    value = qkv[:, 2 * heads_width :].astype(BF)
    attended, kv = attention_forward(query, jnp.concatenate([key, value], axis=1), n_ctx)
    resid, scale_two, normed_two = second_norm(
        back(attended, out_parts).astype(BF), hidden_in, gain_two_here, n_tp
    )

    logits = mm_t(normed_two, router_w)
    route_onehot = (routes[:, :, None] == jnp.arange(experts, dtype=jnp.int32)).astype(F32)
    picked_logits = jnp.sum(route_onehot * logits[:, None, :], axis=-1)
    gate_pair = jax.nn.softmax(picked_logits, axis=-1)
    relative = (jnp.arange(experts, dtype=jnp.int32) + here_ctx) % experts
    names = (routes[:, :, None] == relative).astype(F32)
    mix_gates = jnp.sum(gate_pair[:, :, None] * names, axis=1)
    chosen = jnp.sum(names, axis=1)
    before = jnp.tril(jnp.ones((rows_here, rows_here), BF), -1)
    slot_of = mm(before, chosen.astype(BF)).astype(jnp.int32)
    slots = jnp.arange(CAP, dtype=jnp.int32)
    pick = (slot_of.T[:, None, :] == slots[None, :, None]) & (chosen.T[:, None, :] > 0)
    pick_low = pick.astype(BF)
    pick_flat = pick_low.reshape(experts * CAP, rows_here)

    def dispatch(slabs):
        return jnp.concatenate(
            [slabs[0]] + [shift_ctx(slabs[k], k) for k in range(1, experts)], axis=0
        )

    def give_back(values):
        slabs = values.reshape(experts, CAP, values.shape[-1])
        return [slabs[0]] + [shift_ctx(slabs[k], -k) for k in range(1, experts)]

    grad_rows = dispatch(mm(pick_flat, grad_full).astype(BF).reshape(experts, CAP, width))
    token_rows = dispatch(mm(pick_flat, normed_two).astype(BF).reshape(experts, CAP, width))
    gate_slots = jnp.sum(jnp.where(pick, mix_gates.T[:, None, :], 0.0), axis=-1)
    gate_rows = dispatch(gate_slots[:, :, None])

    gate_act = into(token_rows, gate_w)
    up_act = into(token_rows, up_w)
    sigma_act = jax.nn.sigmoid(gate_act)
    hidden_act = (gate_act * sigma_act * up_act).astype(BF)
    d_result = (gate_rows * grad_rows.astype(F32)).astype(BF)

    def grad_send(left, right):
        halves = split(left)
        if pair:
            away = t_mm(halves[1], right).astype(BF)
            return halves[0], right, away, swap_fsdp(away)
        return halves[0], right, None, None

    def grad_sum(mine, right, away, other):
        if pair:
            return (t_mm(mine, right) + other.astype(F32)).astype(BF)
        return lax.psum_scatter(t_mm(mine, right).astype(BF), "fsdp", scatter_dimension=0, tiled=True)

    def grad_spread(mine):
        cut = part // n_ctx
        out = jnp.zeros((experts, cut, mine.shape[1]), F32)
        for k in range(experts):
            piece = lax.dynamic_slice_in_dim(mine, ((here_ctx + k) % n_ctx) * cut, cut, 0)
            if k:
                piece = shift_ctx(piece, k)
            out = lax.dynamic_update_index_in_dim(
                out, piece.astype(F32), (here_ctx + n_ctx - k) % n_ctx, 0
            )
        return out

    down_sent = grad_send(d_result, hidden_act)
    if pair:
        hidden_act = after(hidden_act, down_sent[2])
    result = back(hidden_act, down_w)
    gate_dot = jnp.sum(result * grad_rows.astype(F32), axis=-1, keepdims=True)
    returned = give_back(result.astype(BF))
    returned_dot = give_back(gate_dot)
    moe_part = sum(
        mix_gates[:, k][:, None] * t_mm(pick_low[k], returned[k]) for k in range(experts)
    )
    moe_share = lax.psum_scatter(moe_part.astype(BF), "tp", scatter_dimension=1, tiled=True)
    block_out = (resid + moe_share.astype(F32)).astype(BF)

    d_hidden = into(d_result, down_w)
    d_gate_act = (d_hidden * up_act * sigma_act * (1.0 + gate_act * (1.0 - sigma_act))).astype(BF)
    d_up_act = (d_hidden * gate_act * sigma_act).astype(BF)
    d_rows = join(
        [mm_t(d_gate_act, wg) + mm_t(d_up_act, wu) for wg, wu in zip(gate_w, up_w)]
    )
    returned_grad = give_back(d_rows.astype(BF))
    gate_sent = grad_send(token_rows, d_gate_act)
    up_sent = grad_send(token_rows, d_up_act)
    d_normed_part = sum(t_mm(pick_low[k], returned_grad[k]) for k in range(experts))
    d_gate_slots = jnp.stack(
        [jnp.sum(jnp.where(pick[k], returned_dot[k], 0.0), axis=0) for k in range(experts)]
    )
    up_rows = [(0, 8 - experts), (0, 0)]
    d_gate_slots = jnp.pad(d_gate_slots, up_rows)

    if pair:
        d_normed_part = after(d_normed_part, gate_sent[2], up_sent[2])
    d_resid, d_attn, gain_two_part, d_logits = second_norm_back(
        d_normed_part.astype(BF),
        d_gate_slots,
        jnp.pad(gate_pair.T, [(0, 6), (0, 0)]),
        jnp.pad(jnp.transpose(route_onehot, (1, 2, 0)), [(0, 0)] + up_rows),
        jnp.pad(jnp.transpose(names, (1, 2, 0)), [(0, 0)] + up_rows),
        router_here,
        resid,
        scale_two,
        gain_two_here,
        out_grad,
        n_tp,
    )
    grad_router_part = mm(d_logits[:experts].astype(BF), normed_two)

    d_attended = into(d_attn, out_parts).astype(BF)
    d_query, kv_grad = attention_backward(query, kv, d_attended, n_ctx)
    grad_down = grad_spread(grad_sum(*down_sent))
    grad_gate = grad_spread(grad_sum(*gate_sent))
    grad_up = grad_spread(grad_sum(*up_sent))
    d_query_pre = rotate(d_query.reshape(head_shape), cosine, -sine_table)
    d_key_pre = rotate(kv_grad[:, :heads_width].reshape(head_shape), cosine, -sine_table)
    d_qkv = jnp.concatenate(
        [
            d_query_pre.astype(BF).reshape(flat_shape),
            d_key_pre.astype(BF).reshape(flat_shape),
            kv_grad[:, heads_width:].astype(BF),
        ],
        axis=1,
    )
    in_grad, gain_one_part = first_norm_back(
        back(d_qkv, qkv_parts).astype(BF), hidden_in, scale_one, gain_one_here, d_resid, n_tp
    )

    grad_qkv_part = t_mm(normed_one, d_qkv)
    grad_output_part = t_mm(d_attn, attended)
    grad_attn = lax.psum_scatter(
        jnp.concatenate([grad_qkv_part, grad_output_part], axis=1).astype(BF),
        ("fsdp", "ctx"),
        scatter_dimension=0,
        tiled=True,
    ).astype(F32)
    gains = jnp.stack([gain_one_part[0], gain_two_part[0]], axis=1)
    gains = lax.dynamic_update_slice_in_dim(
        jnp.zeros((width, 2), F32), gains, here_tp * width_tp, 0
    )
    small_part = jnp.concatenate([gains, grad_router_part.T / n_tp], axis=1)
    small_grad = lax.psum(
        lax.psum_scatter(small_part, ("fsdp", "ctx"), scatter_dimension=0, tiled=True), "tp"
    )
    return (
        block_out,
        in_grad,
        small_grad[:, 0],
        grad_attn[:, :heads_width],
        grad_attn[:, heads_width : 2 * heads_width],
        grad_attn[:, 2 * heads_width : 3 * heads_width],
        grad_attn[:, 3 * heads_width :],
        small_grad[:, 1],
        small_grad[:, 2:],
        grad_gate,
        grad_up,
        grad_down,
    )


def solution(mesh):
    rows = ("fsdp", "ctx")
    placed = (
        P(rows, "tp"),
        P(rows, "tp"),
        P("fsdp"),
        P("fsdp", "tp"),
        P("fsdp", "tp"),
        P("fsdp", "tp"),
        P("fsdp", "tp"),
        P("fsdp"),
        P("fsdp", None),
        P(None, "fsdp", "tp"),
        P(None, "fsdp", "tp"),
        P(None, "fsdp", "tp"),
        P(rows, None),
    )
    return jax.shard_map(
        shards,
        mesh=mesh,
        in_specs=placed,
        out_specs=(
            P(rows, "tp"),
            P(rows, "tp"),
            P(rows),
            P(rows, "tp"),
            P(rows, "tp"),
            P(rows, "tp"),
            P(rows, "tp"),
            P(rows),
            P(rows, None),
            P(None, rows, "tp"),
            P(None, rows, "tp"),
            P(None, rows, "tp"),
        ),
        check_vma=False,
    )
```

time: 944 us -> 968 us (1.025)
  Pallas kernels: 12.4 us -> 341 us
  waiting for transfers between devices: 606 us -> 369 us
  blocking collectives: 45.2 us -> 12.1 us
  other arithmetic: 52.6 us -> 35.9 us
  starting transfers between devices: 43.6 us -> 29.6 us
    pallas_call x2 -> x7, Pallas kernels: 12.4 us -> 341 us  [call(): pl.pallas_call(kernel, out_shape=out_shape, in_specs=[VM] * len(inputs),...]
    all_gather x6 -> x0, waiting for transfers between devices: 108 us -> none  [the longest x1 26.5 us: shards(): d_attn = lax.all_gather(d_resid.astype(BF), 'tp', axis=1, tiled=True)]
    ppermute x7, waiting for transfers between devices: 320 us -> 219 us  [swap_fsdp(): return lax.ppermute(value, 'fsdp', [(0, 1), (1, 0)])]
    reduce_scatter x4 -> x0, waiting for transfers between devices: 81.7 us -> none  [the longest x1 29.8 us: shards(): lax.psum_scatter(jnp.concatenate([key_grad, value_grad], axis=1), 'ctx',...]
    ppermute x27, waiting for transfers between devices: 95.9 us -> 128 us  [shift_ctx(): lax.ppermute(value, 'ctx', [(i, (i + k) % n_ctx) for i in range(n_ctx)])]
    psum x4 -> x1, blocking collectives: 40.7 us -> 12.1 us  [shards(): lax.psum(lax.psum_scatter(small_part, ('fsdp', 'ctx'), scatter_dimension=...]
    reduce_scatter x1, waiting for transfers between devices: 0.01 us -> 16.3 us  [shards(): lax.psum_scatter(moe_part.astype(BF), 'tp', scatter_dimension=1, tiled=True)]
    ppermute x27, starting transfers between devices: 32.6 us -> 21.4 us  [shift_ctx(): lax.ppermute(value, 'ctx', [(i, (i + k) % n_ctx) for i in range(n_ctx)])]
  transfers between devices with their start and end apart: 47 -> 37, of which waited for: 28 -> 19; matrix products, arithmetic and copies ran while one was open for 14% -> 14% of each run, Pallas kernels for 0% -> 36%
where the time goes in v2:
time: 968 us; the launch traced here: 958 us
  waiting for transfers between devices  369 us (38%)
  Pallas kernels  341 us (35%)
  matrix products  113 us (12%)
  local copies, waits for them, and re-layouts  43.2 us (4%)
  other arithmetic  35.9 us (4%)
  starting transfers between devices  29.6 us (3%)
  between operations  15.4 us (2%)
  blocking collectives  12.1 us (1%)
    pallas_call x7, Pallas kernels, call(): pl.pallas_call(kernel, out_shape=out_shape, in_specs=[VM] * len(inputs),...  341 us
    ppermute x7, waiting for transfers between devices, swap_fsdp(): return lax.ppermute(value, 'fsdp', [(0, 1), (1, 0)])  219 us
    ppermute x27, waiting for transfers between devices, shift_ctx(): lax.ppermute(value, 'ctx', [(i, (i + k) % n_ctx) for i in range(n_ctx)])  128 us
    dot_general x16, matrix products, t_mm(): lax.dot_general(left, right, (((0,), (0,)), ((), ())), preferred_element_...  42.7 us
    dot_general x14, matrix products, mm(): return jnp.dot(left, right, preferred_element_type=F32)  42.4 us
    dot_general x11, matrix products, mm_t(): lax.dot_general(left, right, (((1,), (1,)), ((), ())), preferred_element_...  27.6 us
    ppermute x27, starting transfers between devices, shift_ctx(): lax.ppermute(value, 'ctx', [(i, (i + k) % n_ctx) for i in range(n_ctx)])  21.4 us
  transfers between devices with their start and end apart: 37, of which 19 were waited for; matrix products, arithmetic and copies ran while one was open for 14% of the time, Pallas kernels for 36%

profile of v2, /device:TPU:0, one launch (start us, length us, event | category | flops | bytes accessed | tf_op | source)
XLA Modules:
  0.0 958.5 jit_solution(10454325824808546179)
XLA Ops:
  21.1 79.2 %first_norm.1 = (bf16[256,2048]{1,0:T(8,128)(2,1)}, f32[256,128]{1,0:T(8,128)}, bf16[256,2048]{1,0:T(8,128)(2,1)}, f32[8,2048]{1,0:T(8,128)}) custom-call(bf16[256,512]{1,0:T(8,128)(2,1)} %hid.5, bf16[256,512]{1,0:T(8,128)(2,1)} %grd.3, f32[8,1024]{1,0:T(8,128)} %maximum_convert_fusion.sml), custom_call_target="tpu_custom_call" | custom-call | tf_op jit(solution)/shard_map/first_norm/pallas_call | solution.py:144
  112.8 50.6 %gather_ctx.1 = bf16[1024,2048]{1,0:T(8,128)(2,1)} custom-call(bf16[256,2048]{1,0:T(8,128)(2,1)} %collective-permute-done.own), custom_call_target="tpu_custom_call" | custom-call | tf_op jit(solution)/shard_map/gather_ctx/pallas_call | solution.py:144
  170.0 30.2 %attention_forward.1 = (bf16[256,512]{1,0:T(8,128)(2,1)}, bf16[1024,1024]{1,0:T(8,128)(2,1)}) custom-call(bf16[256,512]{1,0:T(8,128)(2,1)} %bitcast.171, bf16[256,1024]{1,0:T(8,128)(2,1)} %pad_maximum_fusion.8.own), custom_call_target="tpu_custom_call" | custom-call | tf_op jit(solution)/shard_map/attention_forward/pallas_call | solution.py:144
  205.1 53.5 %second_norm.1 = (f32[256,512]{1,0:T(8,128)}, f32[256,128]{1,0:T(8,128)}, bf16[256,2048]{1,0:T(8,128)(2,1)}) custom-call(bf16[256,2048]{1,0:T(8,128)(2,1)} %pad_maximum_fusion.4.prt, bf16[256,512]{1,0:T(8,128)(2,1)} %hid.5, f32[8,512]{1,0:T(8,128)} %broadcast_in_dim.176.gn), custom_call_target="tpu_custom_call" | custom-call | tf_op jit(solution)/shard_map/second_norm/pallas_call | solution.py:144
  266.8 4.9 collective-permute-done.8
  277.2 13.7 %collective-permute-done.2 = bf16[160,2048]{1,0:T(8,128)(2,1)S(1)} collective-permute-done((bf16[160,2048]{1,0:T(8,128)(2,1)S(1)}, bf16[160,2048]{1,0:T(8,128)(2,1)S(1)}, u32[]{:S(2)}, u32[]{:S(2)}) %collective-permute-start.2) | collective-permute-done | bytes 655392 | tf_op jit(solution)/shard_map/ppermute | solution.py:478
  292.1 13.1 %collective-permute-done.1 = bf16[160,2048]{1,0:T(8,128)(2,1)S(1)} collective-permute-done((bf16[160,2048]{1,0:T(8,128)(2,1)S(1)}, bf16[160,2048]{1,0:T(8,128)(2,1)S(1)}, u32[]{:S(2)}, u32[]{:S(2)}) %collective-permute-start.1) | collective-permute-done | bytes 655392 | tf_op jit(solution)/shard_map/ppermute | solution.py:478
  305.8 13.2 %collective-permute-done.10 = bf16[160,2048]{1,0:T(8,128)(2,1)S(1)} collective-permute-done((bf16[160,2048]{1,0:T(8,128)(2,1)S(1)}, bf16[160,2048]{1,0:T(8,128)(2,1)S(1)}, u32[]{:S(2)}, u32[]{:S(2)}) %collective-permute-start.10) | collective-permute-done | bytes 655392 | tf_op jit(solution)/shard_map/ppermute | solution.py:478
  319.0 7.1 collective-permute-done.9
  330.3 6.8 fusion.14
  337.1 5.8 fusion.18
  347.4 50.7 %collective-permute-done.4 = bf16[1024,1408]{1,0:T(8,128)(2,1)S(1)} collective-permute-done((bf16[1024,1408]{1,0:T(8,128)(2,1)S(1)}, bf16[1024,1408]{1,0:T(8,128)(2,1)S(1)}, u32[]{:S(2)}, u32[]{:S(2)}) %collective-permute-start.4) | collective-permute-done | bytes 2883616 | tf_op jit(solution)/shard_map/ppermute | solution.py:481
  403.7 8.2 multiply_convert_fusion.1
  411.9 5.9 fusion.95
  455.1 7.3 collective-permute-done.21
  470.0 28.1 %collective-permute-done.17 = bf16[160,2048]{1,0:T(8,128)(2,1)S(1)} collective-permute-done((bf16[160,2048]{1,0:T(8,128)(2,1)S(1)}, bf16[160,2048]{1,0:T(8,128)(2,1)S(1)}, u32[]{:S(2)}, u32[]{:S(2)}) %collective-permute-start.17) | collective-permute-done | bytes 655392 | tf_op jit(solution)/shard_map/ppermute | solution.py:478
  499.6 54.4 %second_norm_back.1 = (f32[256,512]{1,0:T(8,128)}, bf16[256,2048]{1,0:T(8,128)(2,1)}, f32[8,512]{1,0:T(8,128)}, f32[8,256]{1,0:T(8,128)}) custom-call(bf16[256,2048]{1,0:T(8,128)(2,1)} %fusion.6.prt, f32[8,256]{1,0:T(8,128)} %select_maximum_fusion.dts, f32[8,256]{1,0:T(8,128)} %pad.21.gts, f32[2,8,256]{2,1,0:T(8,128)} %get-tuple-element.168.one, ...), custom_call_target="tpu_custom_call" | custom-call | tf_op jit(solution)/shard_map/second_norm_back/pallas_call | solution.py:144
  558.1 34.2 %attention_backward.1 = (f32[256,512]{1,0:T(8,128)}, f32[256,1024]{1,0:T(8,128)}) custom-call(bf16[256,512]{1,0:T(8,128)(2,1)} %bitcast.172, bf16[1024,1024]{1,0:T(8,128)(2,1)} %get-tuple-element.38.full, bf16[256,512]{1,0:T(8,128)(2,1)} %fusion.11.dot), custom_call_target="tpu_custom_call" | custom-call | tf_op jit(solution)/shard_map/attention_backward/pallas_call | solution.py:144
  607.3 38.5 %first_norm_back.1 = (f32[256,512]{1,0:T(8,128)}, f32[8,512]{1,0:T(8,128)}) custom-call(bf16[256,2048]{1,0:T(8,128)(2,1)} %pad_maximum_fusion.5.prt, bf16[256,512]{1,0:T(8,128)(2,1)} %hid.5, f32[256,1]{1,0:T(8,128)} %bitcast.184, f32[8,512]{1,0:T(8,128)} %broadcast_in_dim.190.gn, f32[256,512]{1,0:T(8,128)} %get-tuple-element.45.dr), custom_call_target="tpu_custom_call" | custom-call | tf_op jit(solution)/shard_map/first_norm_back/pallas_call | solution.py:144
  655.4 5.6 convolution_convert_fusion
  661.0 7.7 pad_maximum_fusion
  672.3 5.8 reduce-scatter.6.cloned.1.call-done
  678.1 12.1 %psum.7 = f32[256,6]{0,1:T(8,128)S(1)} all-reduce(f32[256,6]{0,1:T(8,128)} %reduce-scatter.6.cloned.1.call-done), channel_id=1, replica_groups=mesh['fsdp'=2,'ctx'=4,'tp'=4] {'tp'}, use_global_device_ids=true, to_apply=%region_13.14 | all-reduce | flops 1536 | bytes 12288 | tf_op jit(solution)/shard_map/psum | solution.py:696
  691.4 16.3 %reduce-scatter.4.cloned.1.call-done = bf16[256,512]{1,0:T(8,128)(2,1)} async-done(((bf16[256,2048]{1,0:T(8,128)(2,1)}), bf16[256,512]{1,0:T(8,128)(2,1)}) %reduce-scatter.4.cloned.1.call-update) | async-done | bytes 262160 | tf_op jit(solution)/shard_map/reduce_scatter | solution.py:628
  709.4 25.2 %collective-permute-done.22 = bf16[1024,1408]{1,0:T(8,128)(2,1)} collective-permute-done((bf16[1024,1408]{1,0:T(8,128)(2,1)}, bf16[1024,1408]{1,0:T(8,128)(2,1)}, u32[]{:S(2)}, u32[]{:S(2)}) %collective-permute-start.22) | collective-permute-done | bytes 2883616 | tf_op jit(solution)/shard_map/ppermute | solution.py:481
  734.6 5.1 add_convert_fusion.2
  741.8 88.3 %collective-permute-done.26 = bf16[1024,1408]{1,0:T(8,128)(2,1)} collective-permute-done((bf16[1024,1408]{1,0:T(8,128)(2,1)}, bf16[1024,1408]{1,0:T(8,128)(2,1)}, u32[]{:S(2)}, u32[]{:S(2)}) %collective-permute-start.26) | collective-permute-done | bytes 2883616 | tf_op jit(solution)/shard_map/ppermute | solution.py:481
  835.1 54.6 %collective-permute-done.30 = bf16[1024,1408]{1,0:T(8,128)(2,1)} collective-permute-done((bf16[1024,1408]{1,0:T(8,128)(2,1)}, bf16[1024,1408]{1,0:T(8,128)(2,1)}, u32[]{:S(2)}, u32[]{:S(2)}) %collective-permute-start.30) | collective-permute-done | bytes 2883616 | tf_op jit(solution)/shard_map/ppermute | solution.py:481
  901.8 7.1 collective-permute-done.28
  909.1 13.7 %collective-permute-done.29 = bf16[256,1408]{1,0:T(8,128)(2,1)S(1)} collective-permute-done((bf16[256,1408]{1,0:T(8,128)(2,1)S(1)}, bf16[256,1408]{1,0:T(8,128)(2,1)S(1)}, u32[]{:S(2)}, u32[]{:S(2)}) %collective-permute-start.29) | collective-permute-done | bytes 720928 | tf_op jit(solution)/shard_map/ppermute | solution.py:478
  924.2 13.0 %collective-permute-done.32 = bf16[256,1408]{1,0:T(8,128)(2,1)S(1)} collective-permute-done((bf16[256,1408]{1,0:T(8,128)(2,1)S(1)}, bf16[256,1408]{1,0:T(8,128)(2,1)S(1)}, u32[]{:S(2)}, u32[]{:S(2)}) %collective-permute-start.32) | collective-permute-done | bytes 720928 | tf_op jit(solution)/shard_map/ppermute | solution.py:478
  938.4 5.8 collective-permute-done.33
  (276 shorter events, 177.3 us)
Async XLA Ops:
  7.2 670.9 %reduce-scatter.6.cloned.1.call-start = ((), (), s32[]{:S(2)}) async-start(), calls=%async_computation.4 | async-start | bytes 73728 | tf_op jit(solution)/shard_map/reduce_scatter | solution.py:697
  9.5 103.3 %collective-permute-start = (bf16[256,2048]{1,0:T(8,128)(2,1)}, bf16[256,2048]{1,0:T(8,128)(2,1)}, u32[]{:S(2)}, u32[]{:S(2)}) collective-permute-start(bf16[256,2048]{1,0:T(8,128)(2,1)} %fusion.23), channel_id=1, source_target_pairs={{0,16},{16,0},{1,17},{17,1},{2,18},{18,2},{3,19},{19,3},{4,20},{20... | collective-permute-start | bytes 3145736 | tf_op jit(solution)/shard_map/ppermute | solution.py:481
  16.2 320.9 %collective-permute-start.12 = (bf16[1024,1408]{1,0:T(8,128)(2,1)}, bf16[1024,1408]{1,0:T(8,128)(2,1)}, u32[]{:S(2)}, u32[]{:S(2)}) collective-permute-start(bf16[1024,1408]{1,0:T(8,128)(2,1)} %dynamic-slice_bitcast_fusion), channel_id=1, source_target_pairs={{0,16},{16,0},{1,17},{17,1},{2,18},{18,2},{3,19},{19,3},{4,20},{20... | collective-permute-start | bytes 8650760 | tf_op jit(solution)/shard_map/ppermute | solution.py:481
  271.6 71.3 %collective-permute-start.5 = (bf16[1024,1408]{1,0:T(8,128)(2,1)S(1)}, bf16[1024,1408]{1,0:T(8,128)(2,1)S(1)}, u32[]{:S(2)}, u32[]{:S(2)}) collective-permute-start(bf16[1024,1408]{1,0:T(8,128)(2,1)S(1)} %copy-done.12), channel_id=1, source_target_pairs={{0,16},{16,0},{1,17},{17,1},{2,18},{18,2},{3,19},{19,3},{4,20},{20... | collective-permute-start | bytes 8650760 | tf_op jit(solution)/shard_map/ppermute | solution.py:481
  273.4 17.5 %collective-permute-start.2 = (bf16[160,2048]{1,0:T(8,128)(2,1)S(1)}, bf16[160,2048]{1,0:T(8,128)(2,1)S(1)}, u32[]{:S(2)}, u32[]{:S(2)}) collective-permute-start(bf16[160,2048]{1,0:T(8,128)(2,1)S(1)} %get-tuple-element.120), channel_id=1, source_target_pairs={{0,8},{4,12},{8,0},{12,4},{1,9},{5,13},{9,1},{13,5},{2,10},{6,14},... | collective-permute-start | bytes 1966088 | tf_op jit(solution)/shard_map/ppermute | solution.py:478
  274.5 30.7 %collective-permute-start.1 = (bf16[160,2048]{1,0:T(8,128)(2,1)S(1)}, bf16[160,2048]{1,0:T(8,128)(2,1)S(1)}, u32[]{:S(2)}, u32[]{:S(2)}) collective-permute-start(bf16[160,2048]{1,0:T(8,128)(2,1)S(1)} %get-tuple-element.121), channel_id=1, source_target_pairs={{0,4},{4,8},{8,12},{12,0},{1,5},{5,9},{9,13},{13,1},{2,6},{6,10},{... | collective-permute-start | bytes 1966088 | tf_op jit(solution)/shard_map/ppermute | solution.py:478
  275.2 30.2 %collective-permute-start.11 = (bf16[160,2048]{1,0:T(8,128)(2,1)S(1)}, bf16[160,2048]{1,0:T(8,128)(2,1)S(1)}, u32[]{:S(2)}, u32[]{:S(2)}) collective-permute-start(bf16[160,2048]{1,0:T(8,128)(2,1)S(1)} %get-tuple-element.115), channel_id=1, source_target_pairs={{0,12},{4,0},{8,4},{12,8},{1,13},{5,1},{9,5},{13,9},{2,14},{6,2},{... | collective-permute-start | bytes 1966088 | tf_op jit(solution)/shard_map/ppermute | solution.py:478
  290.9 28.1 %collective-permute-start.10 = (bf16[160,2048]{1,0:T(8,128)(2,1)S(1)}, bf16[160,2048]{1,0:T(8,128)(2,1)S(1)}, u32[]{:S(2)}, u32[]{:S(2)}) collective-permute-start(bf16[160,2048]{1,0:T(8,128)(2,1)S(1)} %get-tuple-element.116), channel_id=1, source_target_pairs={{0,8},{4,12},{8,0},{12,4},{1,9},{5,13},{9,1},{13,5},{2,10},{6,14},... | collective-permute-start | bytes 1966088 | tf_op jit(solution)/shard_map/ppermute | solution.py:478
  305.2 21.0 %collective-permute-start.9 = (bf16[160,2048]{1,0:T(8,128)(2,1)S(1)}, bf16[160,2048]{1,0:T(8,128)(2,1)S(1)}, u32[]{:S(2)}, u32[]{:S(2)}) collective-permute-start(bf16[160,2048]{1,0:T(8,128)(2,1)S(1)} %get-tuple-element.117), channel_id=1, source_target_pairs={{0,4},{4,8},{8,12},{12,0},{1,5},{5,9},{9,13},{13,1},{2,6},{6,10},{... | collective-permute-start | bytes 1966088 | tf_op jit(solution)/shard_map/ppermute | solution.py:478
  305.4 92.7 %collective-permute-start.4 = (bf16[1024,1408]{1,0:T(8,128)(2,1)S(1)}, bf16[1024,1408]{1,0:T(8,128)(2,1)S(1)}, u32[]{:S(2)}, u32[]{:S(2)}) collective-permute-start(bf16[1024,1408]{1,0:T(8,128)(2,1)S(1)} %copy-done.13), channel_id=1, source_target_pairs={{0,16},{16,0},{1,17},{17,1},{2,18},{18,2},{3,19},{19,3},{4,20},{20... | collective-permute-start | bytes 8650760 | tf_op jit(solution)/shard_map/ppermute | solution.py:481
  447.6 21.4 %collective-permute-start.18 = (bf16[160,2048]{1,0:T(8,128)(2,1)S(1)}, bf16[160,2048]{1,0:T(8,128)(2,1)S(1)}, u32[]{:S(2)}, u32[]{:S(2)}) collective-permute-start(bf16[160,2048]{1,0:T(8,128)(2,1)S(1)} %get-tuple-element.108), channel_id=1, source_target_pairs={{0,4},{4,8},{8,12},{12,0},{1,5},{5,9},{9,13},{13,1},{2,6},{6,10},{... | collective-permute-start | bytes 1966088 | tf_op jit(solution)/shard_map/ppermute | solution.py:478
  448.1 21.4 %collective-permute-start.16 = (bf16[160,2048]{1,0:T(8,128)(2,1)S(1)}, bf16[160,2048]{1,0:T(8,128)(2,1)S(1)}, u32[]{:S(2)}, u32[]{:S(2)}) collective-permute-start(bf16[160,2048]{1,0:T(8,128)(2,1)S(1)} %get-tuple-element.107), channel_id=1, source_target_pairs={{0,12},{4,0},{8,4},{12,8},{1,13},{5,1},{9,5},{13,9},{2,14},{6,2},{... | collective-permute-start | bytes 1966088 | tf_op jit(solution)/shard_map/ppermute | solution.py:478
  451.0 13.7 %collective-permute-start.20 = (f32[160,1]{0,1:T(1,128)S(1)}, f32[160,1]{0,1:T(1,128)S(1)}, u32[]{:S(2)}, u32[]{:S(2)}) collective-permute-start(f32[160,1]{0,1:T(1,128)S(1)} %bitcast.204), channel_id=1, source_target_pairs={{0,8},{4,12},{8,0},{12,4},{1,9},{5,13},{9,1},{13,5},{2,10},{6,14},... | collective-permute-start | bytes 1928 | tf_op jit(solution)/shard_map/ppermute | solution.py:478
  452.7 13.4 %collective-permute-start.19 = (f32[160,1]{0,1:T(1,128)S(1)}, f32[160,1]{0,1:T(1,128)S(1)}, u32[]{:S(2)}, u32[]{:S(2)}) collective-permute-start(f32[160,1]{0,1:T(1,128)S(1)} %bitcast.203), channel_id=1, source_target_pairs={{0,12},{4,0},{8,4},{12,8},{1,13},{5,1},{9,5},{13,9},{2,14},{6,2},{... | collective-permute-start | bytes 1928 | tf_op jit(solution)/shard_map/ppermute | solution.py:478
  462.4 184.9 %collective-permute-start.15 = (bf16[160,2048]{1,0:T(8,128)(2,1)}, bf16[160,2048]{1,0:T(8,128)(2,1)}, u32[]{:S(2)}, u32[]{:S(2)}) collective-permute-start(bf16[160,2048]{1,0:T(8,128)(2,1)} %get-tuple-element.112), channel_id=1, source_target_pairs={{0,4},{4,8},{8,12},{12,0},{1,5},{5,9},{9,13},{13,1},{2,6},{6,10},{... | collective-permute-start | bytes 1966088 | tf_op jit(solution)/shard_map/ppermute | solution.py:478
  464.7 184.2 %collective-permute-start.13 = (bf16[160,2048]{1,0:T(8,128)(2,1)}, bf16[160,2048]{1,0:T(8,128)(2,1)}, u32[]{:S(2)}, u32[]{:S(2)}) collective-permute-start(bf16[160,2048]{1,0:T(8,128)(2,1)} %get-tuple-element.113), channel_id=1, source_target_pairs={{0,12},{4,0},{8,4},{12,8},{1,13},{5,1},{9,5},{13,9},{2,14},{6,2},{... | collective-permute-start | bytes 1966088 | tf_op jit(solution)/shard_map/ppermute | solution.py:478
  466.1 32.0 %collective-permute-start.17 = (bf16[160,2048]{1,0:T(8,128)(2,1)S(1)}, bf16[160,2048]{1,0:T(8,128)(2,1)S(1)}, u32[]{:S(2)}, u32[]{:S(2)}) collective-permute-start(bf16[160,2048]{1,0:T(8,128)(2,1)S(1)} %get-tuple-element.106), channel_id=1, source_target_pairs={{0,8},{4,12},{8,0},{12,4},{1,9},{5,13},{9,1},{13,5},{2,10},{6,14},... | collective-permute-start | bytes 1966088 | tf_op jit(solution)/shard_map/ppermute | solution.py:478
  468.9 181.5 %collective-permute-start.14 = (bf16[160,2048]{1,0:T(8,128)(2,1)}, bf16[160,2048]{1,0:T(8,128)(2,1)}, u32[]{:S(2)}, u32[]{:S(2)}) collective-permute-start(bf16[160,2048]{1,0:T(8,128)(2,1)} %get-tuple-element.111), channel_id=1, source_target_pairs={{0,8},{4,12},{8,0},{12,4},{1,9},{5,13},{9,1},{13,5},{2,10},{6,14},... | collective-permute-start | bytes 1966088 | tf_op jit(solution)/shard_map/ppermute | solution.py:478
  647.2 60.5 %reduce-scatter.4.cloned.1.call-start = ((), (), s32[]{:S(2)}) async-start(), calls=%async_computation.3 | async-start | bytes 1310720 | tf_op jit(solution)/shard_map/reduce_scatter | solution.py:628
  653.2 292.1 %reduce-scatter.8.cloned.1.call-start = ((), (), s32[]{:S(2)}) async-start(), calls=%async_computation.5 | async-start | bytes 9437184 | tf_op jit(solution)/shard_map/reduce_scatter | solution.py:685
  668.7 65.9 %collective-permute-start.22 = (bf16[1024,1408]{1,0:T(8,128)(2,1)}, bf16[1024,1408]{1,0:T(8,128)(2,1)}, u32[]{:S(2)}, u32[]{:S(2)}) collective-permute-start(bf16[1024,1408]{1,0:T(8,128)(2,1)} %convolution_convert_fusion.2), channel_id=1, source_target_pairs={{0,16},{16,0},{1,17},{17,1},{2,18},{18,2},{3,19},{19,3},{4,20},{20... | collective-permute-start | bytes 8650760 | tf_op jit(solution)/shard_map/ppermute | solution.py:481
  670.3 159.8 %collective-permute-start.26 = (bf16[1024,1408]{1,0:T(8,128)(2,1)}, bf16[1024,1408]{1,0:T(8,128)(2,1)}, u32[]{:S(2)}, u32[]{:S(2)}) collective-permute-start(bf16[1024,1408]{1,0:T(8,128)(2,1)} %convolution_convert_fusion.1), channel_id=1, source_target_pairs={{0,16},{16,0},{1,17},{17,1},{2,18},{18,2},{3,19},{19,3},{4,20},{20... | collective-permute-start | bytes 8650760 | tf_op jit(solution)/shard_map/ppermute | solution.py:481
  670.8 218.9 %collective-permute-start.30 = (bf16[1024,1408]{1,0:T(8,128)(2,1)}, bf16[1024,1408]{1,0:T(8,128)(2,1)}, u32[]{:S(2)}, u32[]{:S(2)}) collective-permute-start(bf16[1024,1408]{1,0:T(8,128)(2,1)} %convolution_convert_fusion.3), channel_id=1, source_target_pairs={{0,16},{16,0},{1,17},{17,1},{2,18},{18,2},{3,19},{19,3},{4,20},{20... | collective-permute-start | bytes 8650760 | tf_op jit(solution)/shard_map/ppermute | solution.py:481
  739.9 159.8 %collective-permute-start.23 = (bf16[256,1408]{1,0:T(8,128)(2,1)S(1)}, bf16[256,1408]{1,0:T(8,128)(2,1)S(1)}, u32[]{:S(2)}, u32[]{:S(2)}) collective-permute-start(bf16[256,1408]{1,0:T(8,128)(2,1)S(1)} %get-tuple-element.105), channel_id=1, source_target_pairs={{0,4},{4,8},{8,12},{12,0},{1,5},{5,9},{9,13},{13,1},{2,6},{6,10},{... | collective-permute-start | bytes 2162696 | tf_op jit(solution)/shard_map/ppermute | solution.py:478
  740.0 160.5 %collective-permute-start.24 = (bf16[256,1408]{1,0:T(8,128)(2,1)S(1)}, bf16[256,1408]{1,0:T(8,128)(2,1)S(1)}, u32[]{:S(2)}, u32[]{:S(2)}) collective-permute-start(bf16[256,1408]{1,0:T(8,128)(2,1)S(1)} %get-tuple-element.104), channel_id=1, source_target_pairs={{0,8},{4,12},{8,0},{12,4},{1,9},{5,13},{9,1},{13,5},{2,10},{6,14},... | collective-permute-start | bytes 2162696 | tf_op jit(solution)/shard_map/ppermute | solution.py:478
  740.1 168.9 %collective-permute-start.25 = (bf16[256,1408]{1,0:T(8,128)(2,1)S(1)}, bf16[256,1408]{1,0:T(8,128)(2,1)S(1)}, u32[]{:S(2)}, u32[]{:S(2)}) collective-permute-start(bf16[256,1408]{1,0:T(8,128)(2,1)S(1)} %get-tuple-element.103), channel_id=1, source_target_pairs={{0,12},{4,0},{8,4},{12,8},{1,13},{5,1},{9,5},{13,9},{2,14},{6,2},{... | collective-permute-start | bytes 2162696 | tf_op jit(solution)/shard_map/ppermute | solution.py:478
  834.6 65.3 %collective-permute-start.27 = (bf16[256,1408]{1,0:T(8,128)(2,1)S(1)}, bf16[256,1408]{1,0:T(8,128)(2,1)S(1)}, u32[]{:S(2)}, u32[]{:S(2)}) collective-permute-start(bf16[256,1408]{1,0:T(8,128)(2,1)S(1)} %get-tuple-element.102), channel_id=1, source_target_pairs={{0,4},{4,8},{8,12},{12,0},{1,5},{5,9},{9,13},{13,1},{2,6},{6,10},{... | collective-permute-start | bytes 2162696 | tf_op jit(solution)/shard_map/ppermute | solution.py:478
  889.8 19.1 %collective-permute-start.28 = (bf16[256,1408]{1,0:T(8,128)(2,1)S(1)}, bf16[256,1408]{1,0:T(8,128)(2,1)S(1)}, u32[]{:S(2)}, u32[]{:S(2)}) collective-permute-start(bf16[256,1408]{1,0:T(8,128)(2,1)S(1)} %get-tuple-element.101), channel_id=1, source_target_pairs={{0,8},{4,12},{8,0},{12,4},{1,9},{5,13},{9,1},{13,5},{2,10},{6,14},... | collective-permute-start | bytes 2162696 | tf_op jit(solution)/shard_map/ppermute | solution.py:478
  899.7 23.0 %collective-permute-start.29 = (bf16[256,1408]{1,0:T(8,128)(2,1)S(1)}, bf16[256,1408]{1,0:T(8,128)(2,1)S(1)}, u32[]{:S(2)}, u32[]{:S(2)}) collective-permute-start(bf16[256,1408]{1,0:T(8,128)(2,1)S(1)} %get-tuple-element.100), channel_id=1, source_target_pairs={{0,12},{4,0},{8,4},{12,8},{1,13},{5,1},{9,5},{13,9},{2,14},{6,2},{... | collective-permute-start | bytes 2162696 | tf_op jit(solution)/shard_map/ppermute | solution.py:478
  899.8 23.0 %collective-permute-start.31 = (bf16[256,1408]{1,0:T(8,128)(2,1)S(1)}, bf16[256,1408]{1,0:T(8,128)(2,1)S(1)}, u32[]{:S(2)}, u32[]{:S(2)}) collective-permute-start(bf16[256,1408]{1,0:T(8,128)(2,1)S(1)} %get-tuple-element.99), channel_id=1, source_target_pairs={{0,4},{4,8},{8,12},{12,0},{1,5},{5,9},{9,13},{13,1},{2,6},{6,10},{... | collective-permute-start | bytes 2162696 | tf_op jit(solution)/shard_map/ppermute | solution.py:478
  900.5 36.7 %collective-permute-start.32 = (bf16[256,1408]{1,0:T(8,128)(2,1)S(1)}, bf16[256,1408]{1,0:T(8,128)(2,1)S(1)}, u32[]{:S(2)}, u32[]{:S(2)}) collective-permute-start(bf16[256,1408]{1,0:T(8,128)(2,1)S(1)} %get-tuple-element.98), channel_id=1, source_target_pairs={{0,8},{4,12},{8,0},{12,4},{1,9},{5,13},{9,1},{13,5},{2,10},{6,14},... | collective-permute-start | bytes 2162696 | tf_op jit(solution)/shard_map/ppermute | solution.py:478
  908.8 35.3 %collective-permute-start.33 = (bf16[256,1408]{1,0:T(8,128)(2,1)S(1)}, bf16[256,1408]{1,0:T(8,128)(2,1)S(1)}, u32[]{:S(2)}, u32[]{:S(2)}) collective-permute-start(bf16[256,1408]{1,0:T(8,128)(2,1)S(1)} %get-tuple-element.97), channel_id=1, source_target_pairs={{0,12},{4,0},{8,4},{12,8},{1,13},{5,1},{9,5},{13,9},{2,14},{6,2},{... | collective-permute-start | bytes 2162696 | tf_op jit(solution)/shard_map/ppermute | solution.py:478
  (44 other events, 974.8 us)
Sparse Core Ops, SparseCore 0:
  647.3 30.7 reduce-scatter.5
  680.5 27.1 reduce-scatter.3
  711.2 103.6 reduce-scatter.7

commit v3 on v2

v3 whole, which is shorter than its diff:
```python
from functools import partial
import math

import jax
import jax.numpy as jnp
from jax import lax
from jax.experimental import pallas as pl
from jax.experimental.pallas import tpu as pltpu
from jax.sharding import PartitionSpec as P

HD = 128
CAP = 160


EPS = 1e-05
THETA = 10000.0
NEG = -1e30
BF = jnp.bfloat16
F32 = jnp.float32


def mm(left, right):
    return jnp.dot(left, right, preferred_element_type=F32)


def mm_t(left, right):
    return lax.dot_general(left, right, (((1,), (1,)), ((), ())), preferred_element_type=F32)


def t_mm(left, right):
    return lax.dot_general(left, right, (((0,), (0,)), ((), ())), preferred_element_type=F32)


def rotary_tables(positions):
    half_size = HD // 2
    frequency = THETA ** (-(jnp.arange(half_size, dtype=F32) * 2.0 / HD))
    angles = positions.astype(F32)[:, None] * frequency[None, :]
    return (jnp.cos(angles)[:, None, :], jnp.sin(angles)[:, None, :])


def rotate(values, cosine, sine_table):
    half_size = values.shape[-1] // 2
    first_half = values[..., :half_size]
    second_half = values[..., half_size:]
    return jnp.concatenate(
        [
            first_half * cosine - second_half * sine_table,
            second_half * cosine + first_half * sine_table,
        ],
        axis=-1,
    )


MESH = pl.DeviceIdType.MESH
VM = pl.BlockSpec(memory_space=pltpu.VMEM)
DMA = pltpu.SemaphoreType.DMA


def peer(axis, n, k):
    return lax.rem(lax.axis_index(axis) + k, n)


def greet(groups):
    barrier = pltpu.get_barrier_semaphore()
    for axis, n in groups:
        for k in range(1, n):
            pl.semaphore_signal(
                barrier, inc=1, device_id={axis: peer(axis, n, k)}, device_id_type=MESH
            )
    pl.semaphore_wait(barrier, sum(n - 1 for _, n in groups))


def remote(source, target, sems, i, to):
    copy = pltpu.make_async_remote_copy(
        src_ref=source,
        dst_ref=target,
        send_sem=sems[0].at[i],
        recv_sem=sems[1].at[i],
        device_id=to,
        device_id_type=MESH,
    )
    copy.start()
    return copy


def send(source, target, axis, n, k, sems):
    return remote(source, target, sems, k - 1, {axis: peer(axis, n, k)})


def columns(n, size):
    return pl.ds(pl.multiple_of(n * size, 128), size)


def stretch(n, size):
    return pl.ds(pl.multiple_of(n * size, 16), size)


def gather_columns(own, full, axis, n, sems):
    size = own.shape[1]
    place = full.at[:, columns(lax.axis_index(axis), size)]
    copies = [send(own, place, axis, n, k, sems) for k in range(1, n)]
    place[...] = own[...]
    return copies


def scatter_columns(part, slots, axis, n, sems):
    size = slots.shape[2]
    return [
        send(part.at[:, columns(peer(axis, n, k), size)], slots.at[k - 1], axis, n, k, sems)
        for k in range(1, n)
    ]


def finish(copies):
    for copy in copies:
        copy.wait()


def quad():
    here = lax.axis_index("ctx")
    return here, here + 1 - 2 * lax.rem(here, 2), lax.rem(here + 2, 4)


def gather_square(own, full, sems, between):
    rows = own.shape[0]
    here, beside, across = quad()
    place = full.at[stretch(here, rows), :]
    first = remote(own, place, sems, 0, {"ctx": across})
    second = remote(own, place, sems, 1, {"ctx": beside})
    place[...] = own[...]
    between()
    first.wait()
    come = full.at[stretch(across, rows), :]
    third = remote(come, come, sems, 2, {"ctx": beside})
    second.wait()
    third.wait()


def row_sums(values):
    ones = jnp.ones((8, values.shape[1]), F32)
    return lax.dot_general(
        ones,
        values,
        (((1,), (1,)), ((), ())),
        precision=lax.Precision.HIGHEST,
        preferred_element_type=F32,
    )


def as_column(rows, weight):
    return lax.dot_general(
        rows,
        weight,
        (((0,), (0,)), ((), ())),
        precision=lax.Precision.HIGHEST,
        preferred_element_type=F32,
    )


def eighth():
    return jnp.full((8, 128), 0.125, F32)


def total_over(sums, mine, slots, axis, n, sems):
    mine[...] = sums
    copies = [send(mine, slots.at[k - 1], axis, n, k, sems) for k in range(1, n)]
    finish(copies)
    total = sums
    for k in range(1, n):
        total = total + slots[k - 1]
    return total


def call(kernel, out_shape, inputs, scratch, collective, name):
    return pl.pallas_call(
        kernel,
        out_shape=out_shape,
        in_specs=[VM] * len(inputs),
        out_specs=jax.tree.map(lambda _: VM, out_shape),
        scratch_shapes=scratch,
        compiler_params=pltpu.CompilerParams(collective_id=collective, has_side_effects=True),
        cost_estimate=pl.CostEstimate(flops=0, bytes_accessed=0, transcendentals=0),
        name=name,
    )(*inputs)


def shape(dims, dtype):
    return jax.ShapeDtypeStruct(dims, dtype)


def pair_of_sems(n):
    return [DMA((n,)), DMA((n,))]


def gather_tp(value, n_tp):
    rows, size = value.shape

    def kernel(own, full, *sems):
        greet([("tp", n_tp)])
        finish(gather_columns(own, full, "tp", n_tp, sems))

    return call(
        kernel, shape((rows, size * n_tp), value.dtype), (value,), pair_of_sems(n_tp), 1, "gather_tp"
    )


def first_norm(full, grad, gain, quarter, n_tp, n_ctx):
    rows, width = full.shape
    with_quarter = quarter is not None

    def kernel(*refs):
        hid, grd, gn = refs[:3]
        refs = refs[3:]
        if with_quarter:
            qrt, out, scale, grd_full, qrt_full = refs[:5]
            sems = refs[5:]
            greet([("tp", n_tp), ("ctx", n_ctx)])
        else:
            out, scale, grd_full = refs[:3]
            sems = refs[3:]
            greet([("tp", n_tp)])
        grads = gather_columns(grd, grd_full, "tp", n_tp, sems[0:2])

        def norm():
            values = hid[...].astype(F32)
            mean = jnp.sum(values * values, axis=-1, keepdims=True) * (1.0 / width)
            factor = lax.rsqrt(mean + EPS)
            scale[...] = jnp.broadcast_to(factor, scale.shape)
            out[...] = (values * factor * gn[0:1, :]).astype(BF)

        if with_quarter:
            gather_square(qrt, qrt_full, sems[2:4], norm)
        else:
            norm()
        finish(grads)

    outs = [shape((rows, width), BF), shape((rows, 128), F32), shape((rows, width), BF)]
    inputs = [full, grad, gain]
    if with_quarter:
        outs.append(shape((quarter.shape[0] * n_ctx, quarter.shape[1]), BF))
        inputs.append(quarter)
    return call(
        kernel, tuple(outs), inputs, pair_of_sems(n_tp) + pair_of_sems(3), 7, "first_norm"
    )


def softmax_rows(query, key, first_row):
    scores = mm_t(query, key) * (1.0 / math.sqrt(HD))
    rows = first_row + lax.broadcasted_iota(jnp.int32, scores.shape, 0)
    cols = lax.broadcasted_iota(jnp.int32, scores.shape, 1)
    scores = jnp.where(cols <= rows, scores, NEG)
    top = jnp.max(scores, axis=-1, keepdims=True)
    weights = jnp.exp(scores - top)
    return weights / jnp.sum(weights, axis=-1, keepdims=True)


def attention_forward(query, kv, n_ctx):
    rows, width = query.shape
    heads = width // HD

    def kernel(qry, own, out, full, *sems):
        greet([("ctx", n_ctx)])
        here = lax.axis_index("ctx")
        gather_square(own, full, sems, lambda: None)

        @pl.loop(0, heads)
        def _(h):
            probs = softmax_rows(qry[:, columns(h, HD)], full[:, columns(h, HD)], here * rows)
            out[:, columns(h, HD)] = mm(
                probs.astype(BF), full[:, columns(h + heads, HD)]
            ).astype(BF)

    return call(
        kernel,
        (shape((rows, width), BF), shape((rows * n_ctx, 2 * width), BF)),
        (query, kv),
        pair_of_sems(3),
        2,
        "attention_forward",
    )


def second_norm(part, hidden, gain, slabs, n_tp, n_ctx):
    rows, size = hidden.shape
    width = size * n_tp

    def kernel(prt, hid, gn, slb, resid, scale, out, rowsout, slots, mine, sums, low, *sems):
        greet([("tp", n_tp), ("ctx", n_ctx)])
        here = lax.axis_index("tp")
        copies = scatter_columns(prt, slots, "tp", n_tp, sems[0:2])
        moved = [
            send(
                slb.at[pl.ds(k * CAP, CAP)], rowsout.at[pl.ds(k * CAP, CAP)],
                "ctx", n_ctx, k, sems[6:8],
            )
            for k in range(1, n_ctx)
        ]
        rowsout[0:CAP] = slb[0:CAP]
        total = prt[:, columns(here, size)].astype(F32)
        finish(copies)
        for k in range(1, n_tp):
            total = total + slots[k - 1].astype(F32)
        total = hid[...].astype(F32) + total
        resid[...] = total
        square = total_over(row_sums(total * total), mine, sums, "tp", n_tp, sems[2:4])
        factor = lax.rsqrt(as_column(square, eighth()) * (1.0 / width) + EPS)
        scale[...] = factor
        low[...] = (resid[...] * factor[:, 0:1] * gn[0:1, :]).astype(BF)
        finish(gather_columns(low, out, "tp", n_tp, sems[4:6]))
        finish(moved)

    return call(
        kernel,
        (
            shape((rows, size), F32),
            shape((rows, 128), F32),
            shape((rows, width), BF),
            shape(slabs.shape, BF),
        ),
        (part, hidden, gain, slabs),
        [
            pltpu.VMEM((n_tp - 1, rows, size), BF),
            pltpu.VMEM((8, rows), F32),
            pltpu.VMEM((n_tp - 1, 8, rows), F32),
            pltpu.VMEM((rows, size), BF),
        ]
        + pair_of_sems(n_tp) * 3
        + pair_of_sems(n_ctx),
        3,
        "second_norm",
    )


def dispatch_rows(normed, picks, router, onehot, names, n_ctx):
    rows, width = normed.shape
    experts = n_ctx

    def kernel(
        nrm, pck, rtr, one, nms, tokens, slot_gates, gates, mix, slabs, own_gates, *sems
    ):
        greet([("ctx", n_ctx)])
        copies = []
        for k in (2, 3, 1, 0):
            slab = mm(pck[k * CAP : (k + 1) * CAP], nrm[...]).astype(BF)
            if k == 0:
                tokens[0:CAP] = slab
            else:
                slabs[k - 1] = slab
                copies.append(
                    send(
                        slabs.at[k - 1], tokens.at[pl.ds(k * CAP, CAP)],
                        "ctx", n_ctx, k, sems[0:2],
                    )
                )
        logits = mm_t(rtr[...].astype(BF), nrm[...])
        named = [jnp.sum(one[j] * logits, axis=0, keepdims=True) for j in range(2)]
        top = jnp.maximum(named[0], named[1])
        powers = [jnp.exp(value - top) for value in named]
        both = powers[0] + powers[1]
        gate = [value / both for value in powers]
        mixed = gate[0] * nms[0] + gate[1] * nms[1]
        mix[...] = mixed
        order = lax.broadcasted_iota(jnp.int32, (8, rows), 0)
        gates[...] = jnp.where(order == 0, gate[0], jnp.where(order == 1, gate[1], 0.0))
        own_gates[...] = jnp.zeros(own_gates.shape, F32)
        for k in range(experts):
            own_gates[k, :, 0:CAP] = lax.dot_general(
                jnp.broadcast_to(mixed[k : k + 1], (8, rows)),
                pck[k * CAP : (k + 1) * CAP].astype(F32),
                (((1,), (1,)), ((), ())),
                precision=lax.Precision.HIGHEST,
                preferred_element_type=F32,
            )
        slot_gates[0] = own_gates[0]
        for k in range(1, n_ctx):
            copies.append(
                send(own_gates.at[k], slot_gates.at[k], "ctx", n_ctx, k, sems[2:4])
            )
        finish(copies)

    return call(
        kernel,
        (
            shape((experts * CAP, width), BF),
            shape((experts, 8, rows), F32),
            shape((8, rows), F32),
            shape((8, rows), F32),
        ),
        (normed, picks, router, onehot, names),
        [pltpu.VMEM((n_ctx - 1, CAP, width), BF), pltpu.VMEM((experts, 8, rows), F32)]
        + pair_of_sems(n_ctx) * 2,
        8,
        "dispatch_rows",
    )


def second_norm_back(
    d_rows, dots, picks, gates, onehot, names, router, resid, scale, gain, grad, n_tp, n_ctx
):
    rows, size = resid.shape
    width = size * n_tp
    experts = n_ctx

    def kernel(
        drw, dts, pck, gts, one, nms, rtr, rsd, scl, gn, grd,
        d_resid, d_attn, d_gain, d_logits,
        back, back_dots, part, slots, mine, sums, mine_two, sums_two, low, *sems
    ):
        greet([("tp", n_tp), ("ctx", n_ctx)])
        here = lax.axis_index("tp")
        small = []
        large = []
        for k in range(1, n_ctx):
            small.append(
                send(dts.at[k], back_dots.at[k - 1], "ctx", n_ctx, n_ctx - k, sems[0:2])
            )
        for k in range(1, n_ctx):
            large.append(
                send(
                    drw.at[pl.ds(k * CAP, CAP)], back.at[k - 1],
                    "ctx", n_ctx, n_ctx - k, sems[2:4],
                )
            )
        finish(small)
        order = lax.broadcasted_iota(jnp.int32, (8, rows), 0)
        own = jnp.zeros((8, rows), F32)
        for k in range(experts):
            by_slot = dts[0] if k == 0 else back_dots[k - 1]
            by_row = lax.dot_general(
                by_slot[:, 0:CAP],
                pck[k * CAP : (k + 1) * CAP].astype(F32),
                (((1,), (0,)), ((), ())),
                precision=lax.Precision.HIGHEST,
                preferred_element_type=F32,
            )
            own = own + jnp.where(order == k, by_row, 0.0)
        gate_grad = total_over(own, mine, sums, "tp", n_tp, sems[4:6])
        both = [jnp.sum(nms[j] * gate_grad, axis=0, keepdims=True) for j in range(2)]
        gate = [gts[j : j + 1, :] for j in range(2)]
        mean = gate[0] * both[0] + gate[1] * both[1]
        logits = sum(gate[j] * (both[j] - mean) * one[j] for j in range(2))
        d_logits[...] = logits
        finish(large)
        copies = []
        for step in range(1, n_tp + 1):
            at = columns(peer("tp", n_tp, step), size)
            block = t_mm(pck[0:CAP], drw[0:CAP, at])
            for k in range(1, experts):
                block = block + t_mm(pck[k * CAP : (k + 1) * CAP], back[k - 1, :, at])
            if step < n_tp:
                part[step - 1] = block.astype(BF)
                copies.append(
                    send(part.at[step - 1], slots.at[step - 1], "tp", n_tp, step, sems[6:8])
                )
            else:
                total = block
        total = total + lax.dot_general(
            logits.astype(BF),
            rtr[...].astype(BF),
            (((0,), (0,)), ((), ())),
            preferred_element_type=F32,
        )
        finish(copies)
        for k in range(1, n_tp):
            total = total + slots[k - 1].astype(F32)
        factor = scl[:, 0:1]
        unit = rsd[...] * factor
        d_gain[...] = jnp.broadcast_to(jnp.sum(total * unit, axis=0, keepdims=True), d_gain.shape)
        gained = total * gn[0:1, :]
        d_resid[...] = gained
        dot = total_over(row_sums(unit * gained), mine_two, sums_two, "tp", n_tp, sems[8:10])
        dot = as_column(dot, eighth())[:, 0:1] * (1.0 / width)
        result = grd[...].astype(F32) + factor * (d_resid[...] - rsd[...] * factor * dot)
        d_resid[...] = result
        low[...] = result.astype(BF)
        finish(gather_columns(low, d_attn, "tp", n_tp, sems[10:12]))

    return call(
        kernel,
        (
            shape((rows, size), F32),
            shape((rows, width), BF),
            shape((8, size), F32),
            shape((8, rows), F32),
        ),
        (d_rows, dots, picks, gates, onehot, names, router, resid, scale, gain, grad),
        [
            pltpu.VMEM((n_ctx - 1, CAP, width), BF),
            pltpu.VMEM((n_ctx - 1, 8, rows), F32),
            pltpu.VMEM((n_tp - 1, rows, size), BF),
            pltpu.VMEM((n_tp - 1, rows, size), BF),
            pltpu.VMEM((8, rows), F32),
            pltpu.VMEM((n_tp - 1, 8, rows), F32),
            pltpu.VMEM((8, rows), F32),
            pltpu.VMEM((n_tp - 1, 8, rows), F32),
            pltpu.VMEM((rows, size), BF),
        ]
        + pair_of_sems(n_ctx) * 2
        + pair_of_sems(n_tp) * 4,
        4,
        "second_norm_back",
    )


def attention_backward(query, kv, dout, n_ctx):
    rows, width = query.shape
    heads = width // HD
    scale = 1.0 / math.sqrt(HD)

    def kernel(qry, full, dot, dq, dkv, low, slots, last, both, *sems):
        greet([("ctx", n_ctx)])
        here, beside, across = quad()
        beyond = lax.rem(beside + 2, 4)

        @pl.loop(0, heads)
        def _(h):
            at, at_v = columns(h, HD), columns(h + heads, HD)
            probs = softmax_rows(qry[:, at], full[:, at], here * rows)
            d_probs = mm_t(dot[:, at], full[:, at_v])
            delta = jnp.sum(probs * d_probs, axis=-1, keepdims=True)
            d_scores = (probs * (d_probs - delta)).astype(BF)
            dq[:, at] = mm(d_scores, full[:, at]) * scale
            low[:, at] = (t_mm(d_scores, qry[:, at]) * scale).astype(BF)
            low[:, at_v] = t_mm(probs.astype(BF), dot[:, at]).astype(BF)

        first = remote(low.at[stretch(beyond, rows), :], slots.at[0], sems, 0, {"ctx": beside})
        second = remote(low.at[stretch(beside, rows), :], slots.at[1], sems, 1, {"ctx": beside})
        first.wait()
        both[...] = (
            low[stretch(across, rows), :].astype(F32) + slots[0].astype(F32)
        ).astype(BF)
        third = remote(both, last, sems, 2, {"ctx": across})
        second.wait()
        dkv[...] = low[stretch(here, rows), :].astype(F32) + slots[1].astype(F32)
        third.wait()
        dkv[...] = dkv[...] + last[...].astype(F32)

    return call(
        kernel,
        (shape((rows, width), F32), shape((rows, 2 * width), F32)),
        (query, kv, dout),
        [
            pltpu.VMEM((rows * n_ctx, 2 * width), BF),
            pltpu.VMEM((2, rows, 2 * width), BF),
            pltpu.VMEM((rows, 2 * width), BF),
            pltpu.VMEM((rows, 2 * width), BF),
        ]
        + pair_of_sems(3),
        5,
        "attention_backward",
    )


def first_norm_back(part, hidden, scale, gain, d_resid, result, n_tp, n_ctx):
    rows, size = hidden.shape
    width = size * n_tp

    def kernel(prt, hid, scl, gn, dr, rst, out, d_gain, back, slots, mine, sums, *sems):
        greet([("tp", n_tp), ("ctx", n_ctx)])
        here = lax.axis_index("tp")
        copies = scatter_columns(prt, slots, "tp", n_tp, sems[0:2])
        moved = [
            send(
                rst.at[pl.ds(k * CAP, CAP)], back.at[pl.ds(k * CAP, CAP)],
                "ctx", n_ctx, n_ctx - k, sems[4:6],
            )
            for k in range(1, n_ctx)
        ]
        back[0:CAP] = rst[0:CAP]
        total = prt[:, columns(here, size)].astype(F32)
        finish(copies)
        for k in range(1, n_tp):
            total = total + slots[k - 1].astype(F32)
        factor = scl[:, 0:1]
        unit = hid[...].astype(F32) * factor
        d_gain[...] = jnp.broadcast_to(jnp.sum(total * unit, axis=0, keepdims=True), d_gain.shape)
        gained = total * gn[0:1, :]
        out[...] = gained
        dot = total_over(row_sums(unit * gained), mine, sums, "tp", n_tp, sems[2:4])
        dot = as_column(dot, eighth())[:, 0:1] * (1.0 / width)
        unit = hid[...].astype(F32) * factor
        out[...] = dr[...] + factor * (out[...] - unit * dot)
        finish(moved)

    return call(
        kernel,
        (shape((rows, size), F32), shape((8, size), F32), shape(result.shape, BF)),
        (part, hidden, scale, gain, d_resid, result),
        [
            pltpu.VMEM((n_tp - 1, rows, size), BF),
            pltpu.VMEM((8, rows), F32),
            pltpu.VMEM((n_tp - 1, 8, rows), F32),
        ]
        + pair_of_sems(n_tp) * 2
        + pair_of_sems(n_ctx),
        6,
        "first_norm_back",
    )


def experts_out(back, picks, mix, resid, n_tp):
    rows, size = resid.shape
    experts = back.shape[0] // CAP

    def kernel(bck, pck, mx, rsd, out, part, slots, gate, *sems):
        greet([("tp", n_tp)])
        order = lax.broadcasted_iota(jnp.int32, (8, 128), 0)
        for k in range(experts):
            gate[k] = as_column(mx[...], jnp.where(order == k, 1.0, 0.0))
        copies = []
        for step in range(1, n_tp + 1):
            at = columns(peer("tp", n_tp, step), size)
            block = jnp.zeros((rows, size), F32)
            for k in range(experts):
                block = block + gate[k][:, 0:1] * t_mm(
                    pck[k * CAP : (k + 1) * CAP], bck[k * CAP : (k + 1) * CAP, at]
                )
            if step < n_tp:
                part[step - 1] = block.astype(BF)
                copies.append(
                    send(part.at[step - 1], slots.at[step - 1], "tp", n_tp, step, sems)
                )
            else:
                total = block
        finish(copies)
        for k in range(1, n_tp):
            total = total + slots[k - 1].astype(F32)
        out[...] = (rsd[...] + total).astype(BF)

    return call(
        kernel,
        shape((rows, size), BF),
        (back, picks, mix, resid),
        [
            pltpu.VMEM((n_tp - 1, rows, size), BF),
            pltpu.VMEM((n_tp - 1, rows, size), BF),
            pltpu.VMEM((experts, rows, 128), F32),
        ]
        + pair_of_sems(n_tp),
        9,
        "experts_out",
    )


def weight_grads(part, n_ctx):
    rows, size = part.shape[2:]

    def kernel(prt, out, near, two, far, one, last, *sems):
        greet([("fsdp", 2), ("ctx", n_ctx)])
        here, beside, across = quad()
        beyond = lax.rem(beside + 2, 4)
        mine = lax.axis_index("fsdp")
        other = 1 - mine
        steps = []
        for i, (half, column) in enumerate(
            [(other, beyond), (mine, beyond), (other, beside), (mine, beside)]
        ):
            steps.append(
                remote(prt.at[half, column], near.at[i], sems[0:2], i, {"ctx": beside})
            )
        cross = []
        for i, half in enumerate((other, mine)):
            steps[i].wait()
            two[i] = (prt[half, across].astype(F32) + near[i].astype(F32)).astype(BF)
            cross.append(remote(two.at[i], far.at[i], sems[2:4], i, {"ctx": across}))
        steps[2].wait()
        cross[0].wait()
        one[...] = (
            prt[other, here].astype(F32) + near[2].astype(F32) + far[0].astype(F32)
        ).astype(BF)
        final = remote(one, last, sems[4:6], 0, {"fsdp": other})
        steps[3].wait()
        cross[1].wait()
        out[...] = prt[mine, here].astype(F32) + near[3].astype(F32) + far[1].astype(F32)
        final.wait()
        out[...] = out[...] + last[...].astype(F32)

    return call(
        kernel,
        shape((rows, size), F32),
        (part,),
        [
            pltpu.VMEM((4, rows, size), BF),
            pltpu.VMEM((2, rows, size), BF),
            pltpu.VMEM((2, rows, size), BF),
            pltpu.VMEM((rows, size), BF),
            pltpu.VMEM((rows, size), BF),
        ]
        + pair_of_sems(4)
        + pair_of_sems(2)
        + pair_of_sems(1),
        10,
        "weight_grads",
    )


def small_grads(part, n_tp, n_ctx):
    size = part.shape[1]
    width = size * n_tp
    places = 2 * n_ctx
    cut = width // places

    def kernel(prt, out, full, slots, *sems):
        barrier = pltpu.get_barrier_semaphore()
        place = lax.axis_index("fsdp") * n_ctx + lax.axis_index("ctx")
        others = []
        for i in range(1, places):
            to = lax.rem(place + i, places)
            others.append((to, {"fsdp": to // n_ctx, "ctx": lax.rem(to, n_ctx)}))
        ahead = [{"tp": peer("tp", n_tp, k)} for k in range(1, n_tp)]
        for device in ahead + [device for _, device in others]:
            pl.semaphore_signal(barrier, inc=1, device_id=device, device_id_type=MESH)
        pl.semaphore_wait(barrier, n_tp - 1 + places - 1)
        finish(gather_columns(prt, full, "tp", n_tp, sems[0:2]))
        copies = [
            remote(full.at[:, columns(to, cut)], slots.at[i], sems[2:4], i, device)
            for i, (to, device) in enumerate(others)
        ]
        total = full[:, columns(place, cut)]
        finish(copies)
        for i in range(places - 1):
            total = total + slots[i]
        out[...] = total

    return call(
        kernel,
        shape((8, cut), F32),
        (part,),
        [pltpu.VMEM((8, width), F32), pltpu.VMEM((places - 1, 8, cut), F32)]
        + pair_of_sems(n_tp)
        + pair_of_sems(places),
        11,
        "small_grads",
    )


def after(value, *needed):
    return lax.optimization_barrier((value, *needed))[0]


def shards(
    hidden_in,
    out_grad,
    attn_gain,
    w_query,
    w_key,
    w_value,
    w_output,
    ffn_gain,
    w_router,
    w_gate,
    w_up,
    w_down,
    routes,
):
    rows_here, width_tp = hidden_in.shape
    here_tp = lax.axis_index("tp")
    here_ctx = lax.axis_index("ctx")
    here_fsdp = lax.axis_index("fsdp")
    n_fsdp = lax.axis_size("fsdp")
    n_ctx = lax.axis_size("ctx")
    n_tp = lax.axis_size("tp")
    experts = w_gate.shape[0]
    assert experts == n_ctx == 4
    width = width_tp * n_tp
    part = width // n_fsdp
    pair = n_fsdp == 2
    heads_width = w_query.shape[1]

    def shift_ctx(value, k):
        return lax.ppermute(value, "ctx", [(i, (i + k) % n_ctx) for i in range(n_ctx)])

    def swap_fsdp(value):
        return lax.ppermute(value, "fsdp", [(0, 1), (1, 0)])

    def other_parts(weight):
        if pair:
            return [weight, swap_fsdp(weight)]
        return [lax.all_gather(weight, "fsdp", axis=0, tiled=True)]

    def split(values):
        if pair:
            return [
                lax.dynamic_slice_in_dim(values, here_fsdp * part, part, 1),
                lax.dynamic_slice_in_dim(values, (1 - here_fsdp) * part, part, 1),
            ]
        return [values]

    def join(pieces):
        if pair:
            first = here_fsdp == 0
            return jnp.concatenate(
                [jnp.where(first, pieces[0], pieces[1]), jnp.where(first, pieces[1], pieces[0])],
                axis=1,
            )
        return pieces[0]

    def into(values, weights):
        return sum(mm(x, w) for x, w in zip(split(values), weights))

    def back(values, weights):
        return join([mm_t(values, w) for w in weights])

    def my_features(values):
        return lax.dynamic_slice_in_dim(values, here_tp * width_tp, width_tp, values.ndim - 1)

    attn_w = jnp.concatenate([w_query, w_key, w_value, w_output], axis=1)
    small = jnp.concatenate(
        [attn_gain[None], ffn_gain[None], w_router.T, jnp.zeros((2, part), BF)], axis=0
    )
    if pair:
        quarter = part // n_ctx
        own_quarter = lax.dynamic_slice_in_dim(attn_w, here_ctx * quarter, quarter, 0)
        other_quarter = swap_fsdp(own_quarter)
        other_small = swap_fsdp(small)
        small_full = join([small, other_small]).astype(F32)
    else:
        other_quarter = None
        small_full = lax.all_gather(small, "fsdp", axis=1, tiled=True).astype(F32)
    gate_w = other_parts(lax.dynamic_index_in_dim(w_gate, here_ctx, 0, False))
    up_w = other_parts(lax.dynamic_index_in_dim(w_up, here_ctx, 0, False))
    down_w = other_parts(lax.dynamic_index_in_dim(w_down, here_ctx, 0, False))
    small_here = my_features(small_full)
    gain_one_here = jnp.broadcast_to(small_here[0:1], small_here.shape)
    gain_two_here = jnp.broadcast_to(small_here[1:2], small_here.shape)
    nothing = [(0, 8 - experts), (0, 0)]
    router_full = jnp.pad(small_full[2 : 2 + experts], nothing)
    router_here = jnp.pad(small_here[2 : 2 + experts], nothing)

    relative = (jnp.arange(experts, dtype=jnp.int32) + here_ctx) % experts
    numbers = jnp.arange(8, dtype=jnp.int32)
    onehot = (routes.T[:, None, :] == numbers[None, :, None]).astype(F32)
    named = (routes.T[:, None, :] == relative[None, :, None]).astype(F32)
    names = jnp.pad(named, [(0, 0)] + nothing)
    chosen = jnp.sum(named, axis=0)
    earlier = jnp.triu(jnp.ones((rows_here, rows_here), BF), 1)
    slot_of = mm(chosen.astype(BF), earlier).astype(jnp.int32)
    slots = jnp.arange(CAP, dtype=jnp.int32)
    picks = (slot_of[:, None, :] == slots[None, :, None]) & (chosen[:, None, :] > 0)
    picks = picks.astype(BF).reshape(experts * CAP, rows_here)

    inputs_full = gather_tp(hidden_in, n_tp)
    gathered = first_norm(inputs_full, out_grad, small_full, other_quarter, n_tp, n_ctx)
    normed_one, scale_one, grad_full = gathered[:3]
    if pair:
        attn_parts = [attn_w, gathered[3]]
    else:
        attn_parts = [lax.all_gather(attn_w, "fsdp", axis=0, tiled=True)]
    qkv_parts = [w[:, : 3 * heads_width] for w in attn_parts]
    out_parts = [w[:, 3 * heads_width :] for w in attn_parts]
    heads_here = heads_width // HD
    head_shape = (rows_here, heads_here, HD)
    flat_shape = (rows_here, heads_width)
    positions = here_ctx * rows_here + jnp.arange(rows_here, dtype=jnp.int32)
    cosine, sine_table = rotary_tables(positions)
    qkv = into(normed_one, qkv_parts)
    query_pre = qkv[:, :heads_width].reshape(head_shape)
    key_pre = qkv[:, heads_width : 2 * heads_width].reshape(head_shape)
    query = rotate(query_pre, cosine, sine_table).astype(BF).reshape(flat_shape)
    key = rotate(key_pre, cosine, sine_table).astype(BF).reshape(flat_shape)
    value = qkv[:, 2 * heads_width :].astype(BF)
    attended, kv = attention_forward(query, jnp.concatenate([key, value], axis=1), n_ctx)
    resid, scale_two, normed_two, grad_rows = second_norm(
        back(attended, out_parts).astype(BF),
        hidden_in,
        gain_two_here,
        mm(picks, grad_full).astype(BF),
        n_tp,
        n_ctx,
    )
    token_rows, slot_gates, gates, mix = dispatch_rows(
        normed_two, picks, router_full, onehot, names, n_ctx
    )
    gate_rows = slot_gates[:, 0, :CAP].reshape(experts * CAP, 1)

    gate_act = into(token_rows, gate_w)
    up_act = into(token_rows, up_w)
    sigma_act = jax.nn.sigmoid(gate_act)
    hidden_act = (gate_act * sigma_act * up_act).astype(BF)
    d_result = (gate_rows * grad_rows.astype(F32)).astype(BF)

    def grad_send(left, right):
        halves = split(left)
        if pair:
            away = t_mm(halves[1], right).astype(BF)
            return halves[0], right, away, swap_fsdp(away)
        return halves[0], right, None, None

    def grad_sum(mine, right, away, other):
        if pair:
            return (t_mm(mine, right) + other.astype(F32)).astype(BF)
        return lax.psum_scatter(
            t_mm(mine, right).astype(BF), "fsdp", scatter_dimension=0, tiled=True
        )

    def grad_spread(mine):
        cut = part // n_ctx
        out = jnp.zeros((experts, cut, mine.shape[1]), F32)
        for k in range(experts):
            piece = lax.dynamic_slice_in_dim(mine, ((here_ctx + k) % n_ctx) * cut, cut, 0)
            if k:
                piece = shift_ctx(piece, k)
            out = lax.dynamic_update_index_in_dim(
                out, piece.astype(F32), (here_ctx + n_ctx - k) % n_ctx, 0
            )
        return out

    down_sent = grad_send(d_result, hidden_act)
    if pair:
        hidden_act = after(hidden_act, down_sent[2])
    result = back(hidden_act, down_w)
    gate_dot = jnp.sum(result * grad_rows.astype(F32), axis=-1).reshape(experts, CAP)
    gate_dot = jnp.broadcast_to(
        jnp.pad(gate_dot, [(0, 0), (0, rows_here - CAP)])[:, None, :], (experts, 8, rows_here)
    )
    d_hidden = into(d_result, down_w)
    d_gate_act = (d_hidden * up_act * sigma_act * (1.0 + gate_act * (1.0 - sigma_act))).astype(BF)
    d_up_act = (d_hidden * gate_act * sigma_act).astype(BF)
    gate_sent = grad_send(token_rows, d_gate_act)
    up_sent = grad_send(token_rows, d_up_act)
    d_rows = join(
        [mm_t(d_gate_act, wg) + mm_t(d_up_act, wu) for wg, wu in zip(gate_w, up_w)]
    ).astype(BF)
    if pair:
        d_rows = after(d_rows, gate_sent[2], up_sent[2])

    d_resid, d_attn, gain_two_part, d_logits = second_norm_back(
        d_rows,
        gate_dot,
        picks,
        gates,
        onehot,
        names,
        router_here,
        resid,
        scale_two,
        gain_two_here,
        out_grad,
        n_tp,
        n_ctx,
    )
    if pair:
        d_attn = after(d_attn, down_sent[3])
    grad_down = grad_spread(grad_sum(*down_sent))

    d_attended = into(d_attn, out_parts).astype(BF)
    d_query, kv_grad = attention_backward(query, kv, d_attended, n_ctx)
    if pair:
        kv_grad = after(kv_grad, gate_sent[3], grad_down)
    grad_gate = grad_spread(grad_sum(*gate_sent))
    d_query_pre = rotate(d_query.reshape(head_shape), cosine, -sine_table)
    d_key_pre = rotate(kv_grad[:, :heads_width].reshape(head_shape), cosine, -sine_table)
    d_qkv = jnp.concatenate(
        [
            d_query_pre.astype(BF).reshape(flat_shape),
            d_key_pre.astype(BF).reshape(flat_shape),
            kv_grad[:, heads_width:].astype(BF),
        ],
        axis=1,
    )
    in_grad, gain_one_part, returned = first_norm_back(
        back(d_qkv, qkv_parts).astype(BF),
        hidden_in,
        scale_one,
        gain_one_here,
        d_resid,
        result.astype(BF),
        n_tp,
        n_ctx,
    )
    if pair:
        in_grad, up_sent_there, grad_gate = lax.optimization_barrier(
            (in_grad, up_sent[3], grad_gate)
        )
        up_sent = (*up_sent[:3], up_sent_there)
    grad_up = grad_spread(grad_sum(*up_sent))
    block_out = experts_out(returned, picks, mix, resid, n_tp)

    grad_attn = jnp.concatenate([t_mm(normed_one, d_qkv), t_mm(d_attn, attended)], axis=1).astype(
        BF
    )
    small_part = jnp.concatenate(
        [
            gain_one_part[:1],
            gain_two_part[:1],
            mm(d_logits[:experts].astype(BF), my_features(normed_two)),
            jnp.zeros((6 - experts, width_tp), F32),
        ],
        axis=0,
    )
    if pair:
        grad_attn = weight_grads(grad_attn.reshape(n_fsdp, n_ctx, quarter, -1), n_ctx)
        small_grad = small_grads(small_part, n_tp, n_ctx)
    else:
        scatter = partial(
            lax.psum_scatter, axis_name=("fsdp", "ctx"), scatter_dimension=0, tiled=True
        )
        grad_attn = scatter(grad_attn).astype(F32)
        small_grad = lax.all_gather(small_part, "tp", axis=1, tiled=True)
        small_grad = scatter(small_grad.T).T
    return (
        block_out,
        in_grad,
        small_grad[0],
        grad_attn[:, :heads_width],
        grad_attn[:, heads_width : 2 * heads_width],
        grad_attn[:, 2 * heads_width : 3 * heads_width],
        grad_attn[:, 3 * heads_width :],
        small_grad[1],
        small_grad[2 : 2 + experts].T,
        grad_gate,
        grad_up,
        grad_down,
    )


def solution(mesh):
    rows = ("fsdp", "ctx")
    placed = (
        P(rows, "tp"),
        P(rows, "tp"),
        P("fsdp"),
        P("fsdp", "tp"),
        P("fsdp", "tp"),
        P("fsdp", "tp"),
        P("fsdp", "tp"),
        P("fsdp"),
        P("fsdp", None),
        P(None, "fsdp", "tp"),
        P(None, "fsdp", "tp"),
        P(None, "fsdp", "tp"),
        P(rows, None),
    )
    return jax.shard_map(
        shards,
        mesh=mesh,
        in_specs=placed,
        out_specs=(
            P(rows, "tp"),
            P(rows, "tp"),
            P(rows),
            P(rows, "tp"),
            P(rows, "tp"),
            P(rows, "tp"),
            P(rows, "tp"),
            P(rows),
            P(rows, None),
            P(None, rows, "tp"),
            P(None, rows, "tp"),
            P(None, rows, "tp"),
        ),
        check_vma=False,
    )
```

time: 968 us -> 753 us (0.78)
  waiting for transfers between devices: 369 us -> 68.3 us
  Pallas kernels: 341 us -> 456 us
  other arithmetic: 35.9 us -> 53.3 us
  starting transfers between devices: 29.6 us -> 15.2 us
  between operations: 15.4 us -> 1.86 us
  blocking collectives: 12.1 us -> 0 us
    ppermute x7 -> x8, waiting for transfers between devices: 219 us -> 59.7 us  [swap_fsdp(): return lax.ppermute(value, 'fsdp', [(0, 1), (1, 0)])]
    ppermute x27 -> x9, waiting for transfers between devices: 128 us -> 8.63 us  [shift_ctx(): lax.ppermute(value, 'ctx', [(i, (i + k) % n_ctx) for i in range(n_ctx)])]
    pallas_call x7 -> x11, Pallas kernels: 341 us -> 456 us  [call(): pl.pallas_call(kernel, out_shape=out_shape, in_specs=[VM] * len(inputs),...]
    reduce_scatter x3 -> x0, waiting for transfers between devices: 22.1 us -> none  [the longest x1 16.3 us: shards(): lax.psum_scatter(moe_part.astype(BF), 'tp', scatter_dimension=1, tiled=True)]
    ppermute x27 -> x9, starting transfers between devices: 21.4 us -> 5.62 us  [shift_ctx(): lax.ppermute(value, 'ctx', [(i, (i + k) % n_ctx) for i in range(n_ctx)])]
    dynamic_update_slice x12, other arithmetic: 5.66 us -> 21.4 us  [grad_spread(): lax.dynamic_update_index_in_dim(out, piece.astype(F32), (here_ctx + n_ctx...]
    psum x1 -> x0, blocking collectives: 12.1 us -> none  [shards(): lax.psum(lax.psum_scatter(small_part, ('fsdp', 'ctx'), scatter_dimension=...]
    dot_general x16 -> x8, matrix products: 42.7 us -> 32.3 us  [t_mm(): lax.dot_general(left, right, (((0,), (0,)), ((), ())), preferred_element_...]
  transfers between devices with their start and end apart: 37 -> 17, of which waited for: 19 -> 2; matrix products, arithmetic and copies ran while one was open for 14% -> 22% of each run, Pallas kernels for 36% -> 59%
where the time goes in v3:
time: 753 us; the launch traced here: 745 us
  Pallas kernels  456 us (61%)
  matrix products  106 us (14%)
  waiting for transfers between devices  68.3 us (9%)
  other arithmetic  53.3 us (7%)
  local copies, waits for them, and re-layouts  44.9 us (6%)
  starting transfers between devices  15.2 us (2%)
    pallas_call x11, Pallas kernels, call(): pl.pallas_call(kernel, out_shape=out_shape, in_specs=[VM] * len(inputs),...  456 us
    ppermute x8, waiting for transfers between devices, swap_fsdp(): return lax.ppermute(value, 'fsdp', [(0, 1), (1, 0)])  59.7 us
    dot_general x13, matrix products, mm(): return jnp.dot(left, right, preferred_element_type=F32)  41 us
    dot_general x10, matrix products, mm_t(): lax.dot_general(left, right, (((1,), (1,)), ((), ())), preferred_element_...  32.5 us
    dot_general x8, matrix products, t_mm(): lax.dot_general(left, right, (((0,), (0,)), ((), ())), preferred_element_...  32.3 us
    dynamic_update_slice x12, other arithmetic, grad_spread(): lax.dynamic_update_index_in_dim(out, piece.astype(F32), (here_ctx + n_ctx...  21.4 us
  transfers between devices with their start and end apart: 17, of which 2 were waited for; matrix products, arithmetic and copies ran while one was open for 22% of the time, Pallas kernels for 59%

profile of v3, /device:TPU:0, one launch (start us, length us, event | category | flops | bytes accessed | tf_op | source)
XLA Modules:
  0.0 745.4 jit_solution(8110425981995473255)
XLA Ops:
  25.6 22.2 %gather_tp.1.refs_0_ = bf16[256,2048]{1,0:T(8,128)(2,1)} custom-call(bf16[256,512]{1,0:T(8,128)(2,1)} %hid.3), custom_call_target="tpu_custom_call" | custom-call | tf_op jit(solution)/shard_map/gather_tp/pallas_call | solution.py:175
  51.6 37.6 %first_norm.1 = (bf16[256,2048]{1,0:T(8,128)(2,1)}, f32[256,128]{1,0:T(8,128)}, bf16[256,2048]{1,0:T(8,128)(2,1)}, bf16[1024,2048]{1,0:T(8,128)(2,1)}) custom-call(bf16[256,2048]{1,0:T(8,128)(2,1)} %gather_tp.1.refs_0_, bf16[256,512]{1,0:T(8,128)(2,1)} %grd.1, f32[8,2048]{1,0:T(8,128)} %copy-done.26, bf16[256,2048]{1,0:T(8,128)(2,1)} %collective-permute-done.1.refs_3_), custom_call_target="tpu_custom_call" | custom-call | tf_op jit(solution)/shard_map/first_norm/pallas_call | solution.py:175
  97.4 21.7 %attention_forward.1 = (bf16[256,512]{1,0:T(8,128)(2,1)}, bf16[1024,1024]{1,0:T(8,128)(2,1)}) custom-call(bf16[256,512]{1,0:T(8,128)(2,1)} %bitcast.115, bf16[256,1024]{1,0:T(8,128)(2,1)} %pad_maximum_fusion.6.own), custom_call_target="tpu_custom_call" | custom-call | tf_op jit(solution)/shard_map/attention_forward/pallas_call | solution.py:175
  126.3 53.7 %second_norm.1 = (f32[256,512]{1,0:T(8,128)}, f32[256,128]{1,0:T(8,128)}, bf16[256,2048]{1,0:T(8,128)(2,1)}, bf16[640,2048]{1,0:T(8,128)(2,1)}) custom-call(bf16[256,2048]{1,0:T(8,128)(2,1)} %pad_maximum_fusion.3.prt, bf16[256,512]{1,0:T(8,128)(2,1)} %hid.3, f32[8,512]{1,0:T(8,128)} %broadcast_in_dim.127.gn, bf16[640,2048]{1,0:T(8,128)(2,1)} %convolution_convert_fusion.4.slb), custom_call_target="tpu_custom_call" | custom-call | tf_op jit(solution)/shard_map/second_norm/pallas_call | solution.py:175
  180.0 35.0 %dispatch_rows.1 = (bf16[640,2048]{1,0:T(8,128)(2,1)}, f32[4,8,256]{2,1,0:T(8,128)}, f32[8,256]{1,0:T(8,128)}, f32[8,256]{1,0:T(8,128)}) custom-call(bf16[256,2048]{1,0:T(8,128)(2,1)} %get-tuple-element.47.nrm, bf16[640,256]{1,0:T(8,128)(2,1)} %get-tuple-element.114.pck, f32[8,2048]{1,0:T(8,128)} %pad.16.rtr, f32[2,8,256]{2,1,0:T(8,128)} %fusion.49.one, ...), custom_call_target="tpu_custom_call" | custom-call | tf_op jit(solution)/shard_map/dispatch_rows/pallas_call | solution.py:175
  215.1 6.4 fusion.31
  222.3 4.2 fusion.33
  227.0 5.0 fusion.12
  232.0 4.2 convolution_add_fusion.2
  236.2 4.3 convolution_add_fusion
  240.5 6.5 multiply_convert_fusion
  247.0 6.8 fusion.78
  262.4 4.0 fusion.80
  266.4 4.1 broadcast_select_fusion.1
  272.7 6.2 convolution_convert_fusion.2
  281.0 4.0 convolution_add_fusion.5
  285.0 4.2 fusion.79
  289.2 4.1 select_convert_fusion.1
  295.6 84.9 %second_norm_back.1 = (f32[256,512]{1,0:T(8,128)}, bf16[256,2048]{1,0:T(8,128)(2,1)}, f32[8,512]{1,0:T(8,128)}, f32[8,256]{1,0:T(8,128)}) custom-call(bf16[640,2048]{1,0:T(8,128)(2,1)} %pad_maximum_fusion.2.drw, f32[4,8,256]{2,1,0:T(8,128)} %broadcast_in_dim.130.dts, bf16[640,256]{1,0:T(8,128)(2,1)} %get-tuple-element.114.pck, ...), custom_call_target="tpu_custom_call" | custom-call | tf_op jit(solution)/shard_map/second_norm_back/pallas_call | solution.py:175
  386.2 4.4 fusion.27
  390.7 59.7 %collective-permute-done.6 = bf16[1024,1408]{1,0:T(8,128)(2,1)} collective-permute-done((bf16[1024,1408]{1,0:T(8,128)(2,1)}, bf16[1024,1408]{1,0:T(8,128)(2,1)}, u32[]{:S(2)}, u32[]{:S(2)}) %collective-permute-start.6) | collective-permute-done | bytes 2883616 | tf_op jit(solution)/shard_map/ppermute | solution.py:774
  450.3 4.2 add_convert_fusion.1
  459.4 4.2 add_convert_fusion.2
  471.5 46.7 %attention_backward.1 = (f32[256,512]{1,0:T(8,128)}, f32[256,1024]{1,0:T(8,128)}) custom-call(bf16[256,512]{1,0:T(8,128)(2,1)} %bitcast.116, bf16[1024,1024]{1,0:T(8,128)(2,1)} %get-tuple-element.44.full, bf16[256,512]{1,0:T(8,128)(2,1)} %fusion.7.dot), custom_call_target="tpu_custom_call" | custom-call | tf_op jit(solution)/shard_map/attention_backward/pallas_call | solution.py:175
  531.7 8.6 %collective-permute-done.9 = bf16[256,1408]{1,0:T(8,128)(2,1)S(1)} collective-permute-done((bf16[256,1408]{1,0:T(8,128)(2,1)S(1)}, bf16[256,1408]{1,0:T(8,128)(2,1)S(1)}, u32[]{:S(2)}, u32[]{:S(2)}) %collective-permute-start.9) | collective-permute-done | bytes 720928 | tf_op jit(solution)/shard_map/ppermute | solution.py:771
  549.3 4.5 convolution_convert_fusion
  557.9 42.7 %first_norm_back.1 = (f32[256,512]{1,0:T(8,128)}, f32[8,512]{1,0:T(8,128)}, bf16[640,2048]{1,0:T(8,128)(2,1)}) custom-call(bf16[256,2048]{1,0:T(8,128)(2,1)} %pad_maximum_fusion.4.prt, bf16[256,512]{1,0:T(8,128)(2,1)} %hid.3, f32[256,128]{1,0:T(8,128)} %get-tuple-element.61.scl, f32[8,512]{1,0:T(8,128)} %broadcast_in_dim.140.gn, ...), custom_call_target="tpu_custom_call" | custom-call | tf_op jit(solution)/shard_map/first_norm_back/pallas_call | solution.py:175
  600.6 24.3 %experts_out.1 = bf16[256,512]{1,0:T(8,128)(2,1)} custom-call(bf16[640,2048]{1,0:T(8,128)(2,1)} %get-tuple-element.63.bck, bf16[640,256]{1,0:T(8,128)(2,1)} %get-tuple-element.114.pck, f32[8,256]{1,0:T(8,128)} %get-tuple-element.64.mx, f32[256,512]{1,0:T(8,128)} %get-tuple-element.54.rsd), custom_call_target="tpu_custom_call" | custom-call | tf_op jit(solution)/shard_map/experts_out/pallas_call | solution.py:175
  630.9 13.8 %small_grads.1 = f32[8,256]{1,0:T(8,128)} custom-call(f32[8,512]{1,0:T(8,128)} %maximum_maximum_fusion.1.prt), custom_call_target="tpu_custom_call" | custom-call | tf_op jit(solution)/shard_map/small_grads/pallas_call | solution.py:175
  644.7 4.1 add_convert_fusion
  653.3 7.4 pad_maximum_fusion.prt
  660.8 73.6 %weight_grads.1 = f32[256,2048]{1,0:T(8,128)} custom-call(bf16[2,4,256,2048]{3,2,1,0:T(8,128)(2,1)} %pad_maximum_fusion.prt), custom_call_target="tpu_custom_call" | custom-call | tf_op jit(solution)/shard_map/weight_grads/pallas_call | solution.py:175
  (222 shorter events, 126.4 us)
Async XLA Ops:
  2.9 47.2 %collective-permute-start = (bf16[8,1024]{1,0:T(8,128)(2,1)S(1)}, bf16[8,1024]{1,0:T(8,128)(2,1)S(1)}, u32[]{:S(2)}, u32[]{:S(2)}) collective-permute-start(bf16[8,1024]{1,0:T(8,128)(2,1)S(1)} %maximum_maximum_fusion), channel_id=1, source_target_pairs={{0,16},{16,0},{1,17},{17,1},{2,18},{18,2},{3,19},{19,3},{4,20},{20... | collective-permute-start | bytes 49160 | tf_op jit(solution)/shard_map/ppermute | solution.py:774
  8.1 43.4 %collective-permute-start.1 = (bf16[256,2048]{1,0:T(8,128)(2,1)}, bf16[256,2048]{1,0:T(8,128)(2,1)}, u32[]{:S(2)}, u32[]{:S(2)}) collective-permute-start(bf16[256,2048]{1,0:T(8,128)(2,1)} %fusion.18), channel_id=1, source_target_pairs={{0,16},{16,0},{1,17},{17,1},{2,18},{18,2},{3,19},{19,3},{4,20},{20... | collective-permute-start | bytes 3145736 | tf_op jit(solution)/shard_map/ppermute | solution.py:774
  11.7 220.3 %collective-permute-start.2 = (bf16[1024,1408]{1,0:T(8,128)(2,1)}, bf16[1024,1408]{1,0:T(8,128)(2,1)}, u32[]{:S(2)}, u32[]{:S(2)}) collective-permute-start(bf16[1024,1408]{1,0:T(8,128)(2,1)} %dynamic-slice_bitcast_fusion.2), channel_id=1, source_target_pairs={{0,16},{16,0},{1,17},{17,1},{2,18},{18,2},{3,19},{19,3},{4,20},{20... | collective-permute-start | bytes 8650760 | tf_op jit(solution)/shard_map/ppermute | solution.py:774
  17.3 6.7 copy-start.12
  17.3 223.2 %collective-permute-start.3 = (bf16[1024,1408]{1,0:T(8,128)(2,1)}, bf16[1024,1408]{1,0:T(8,128)(2,1)}, u32[]{:S(2)}, u32[]{:S(2)}) collective-permute-start(bf16[1024,1408]{1,0:T(8,128)(2,1)} %dynamic-slice_bitcast_fusion.1), channel_id=1, source_target_pairs={{0,16},{16,0},{1,17},{17,1},{2,18},{18,2},{3,19},{19,3},{4,20},{20... | collective-permute-start | bytes 8650760 | tf_op jit(solution)/shard_map/ppermute | solution.py:774
  21.1 215.1 %collective-permute-start.4 = (bf16[1024,1408]{1,0:T(8,128)(2,1)}, bf16[1024,1408]{1,0:T(8,128)(2,1)}, u32[]{:S(2)}, u32[]{:S(2)}) collective-permute-start(bf16[1024,1408]{1,0:T(8,128)(2,1)} %dynamic-slice_bitcast_fusion), channel_id=1, source_target_pairs={{0,16},{16,0},{1,17},{17,1},{2,18},{18,2},{3,19},{19,3},{4,20},{20... | collective-permute-start | bytes 8650760 | tf_op jit(solution)/shard_map/ppermute | solution.py:774
  24.0 26.0 %copy-start.27 = (bf16[1024,4]{0,1:T(4,128)(2,1)S(1)}, bf16[1024,4]{0,1:T(4,128)(2,1)}, u32[]{:S(2)}) copy-start(bf16[1024,4]{0,1:T(4,128)(2,1)} %param.21) | copy-start | bytes 24580
  25.4 66.9 %copy-start.8 = (bf16[1024,1536]{1,0:T(8,128)(2,1)}, bf16[1024,1536]{1,0:T(8,128)(2,1)S(1)}, u32[]{:S(2)}) copy-start(bf16[1024,1536]{1,0:T(8,128)(2,1)S(1)} %constant_dynamic-update-slice_fusion) | copy-start | bytes 9437188
  95.0 24.1 %copy-start.3 = (bf16[1024,512]{1,0:T(8,128)(2,1)S(1)}, bf16[1024,512]{1,0:T(8,128)(2,1)}, u32[]{:S(2)}) copy-start(bf16[1024,512]{1,0:T(8,128)(2,1)} %param.19) | copy-start | bytes 3145732
  97.4 24.9 %copy-start.21 = (bf16[256,2048]{1,0:T(8,128)(2,1)S(1)}, bf16[256,2048]{1,0:T(8,128)(2,1)}, u32[]{:S(2)}) copy-start(bf16[256,2048]{1,0:T(8,128)(2,1)} %get-tuple-element.46) | copy-start | bytes 3145732
  215.1 7.3 copy-start.32
  227.0 30.8 %copy-start.17 = (bf16[640,2048]{1,0:T(8,128)(2,1)}, bf16[640,2048]{1,0:T(8,128)(2,1)S(1)}, u32[]{:S(2)}) copy-start(bf16[640,2048]{1,0:T(8,128)(2,1)S(1)} %fusion) | copy-start | bytes 7864324
  247.0 6.8 copy-start.39
  247.0 19.5 %copy-start.34 = (bf16[640,1408]{1,0:T(8,128)(2,1)}, bf16[640,1408]{1,0:T(8,128)(2,1)S(1)}, u32[]{:S(2)}) copy-start(bf16[640,1408]{1,0:T(8,128)(2,1)S(1)} %get-tuple-element.52) | copy-start | bytes 5406724
  261.7 195.9 %collective-permute-start.5 = (bf16[1024,1408]{1,0:T(8,128)(2,1)}, bf16[1024,1408]{1,0:T(8,128)(2,1)}, u32[]{:S(2)}, u32[]{:S(2)}) collective-permute-start(bf16[1024,1408]{1,0:T(8,128)(2,1)} %convolution_convert_fusion.1), channel_id=1, source_target_pairs={{0,16},{16,0},{1,17},{17,1},{2,18},{18,2},{3,19},{19,3},{4,20},{20... | collective-permute-start | bytes 8650760 | tf_op jit(solution)/shard_map/ppermute | solution.py:774
  272.7 8.2 %copy-start.37 = (bf16[640,1408]{1,0:T(8,128)(2,1)S(1)}, bf16[640,1408]{1,0:T(8,128)(2,1)}, u32[]{:S(2)}) copy-start(bf16[640,1408]{1,0:T(8,128)(2,1)} %get-tuple-element.74) | copy-start | bytes 5406724
  272.7 8.2 %copy-start.42 = (f32[640,1024]{1,0:T(8,128)S(1)}, f32[640,1024]{1,0:T(8,128)}, u32[]{:S(2)}) copy-start(f32[640,1024]{1,0:T(8,128)} %fusion.78) | copy-start | bytes 7864324
  278.9 350.6 %collective-permute-start.10 = (bf16[1024,1408]{1,0:T(8,128)(2,1)}, bf16[1024,1408]{1,0:T(8,128)(2,1)}, u32[]{:S(2)}, u32[]{:S(2)}) collective-permute-start(bf16[1024,1408]{1,0:T(8,128)(2,1)} %convolution_convert_fusion.2), channel_id=1, source_target_pairs={{0,16},{16,0},{1,17},{17,1},{2,18},{18,2},{3,19},{19,3},{4,20},{20... | collective-permute-start | bytes 8650760 | tf_op jit(solution)/shard_map/ppermute | solution.py:774
  280.3 170.0 %collective-permute-start.6 = (bf16[1024,1408]{1,0:T(8,128)(2,1)}, bf16[1024,1408]{1,0:T(8,128)(2,1)}, u32[]{:S(2)}, u32[]{:S(2)}) collective-permute-start(bf16[1024,1408]{1,0:T(8,128)(2,1)} %convolution_convert_fusion.3), channel_id=1, source_target_pairs={{0,16},{16,0},{1,17},{17,1},{2,18},{18,2},{3,19},{19,3},{4,20},{20... | collective-permute-start | bytes 8650760 | tf_op jit(solution)/shard_map/ppermute | solution.py:774
  386.2 64.1 %copy-start.41 = (bf16[640,1408]{1,0:T(8,128)(2,1)S(1)}, bf16[640,1408]{1,0:T(8,128)(2,1)}, u32[]{:S(2)}) copy-start(bf16[640,1408]{1,0:T(8,128)(2,1)} %copy-done.39) | copy-start | bytes 5406724
  456.0 171.2 %collective-permute-start.13 = (bf16[256,1408]{1,0:T(8,128)(2,1)}, bf16[256,1408]{1,0:T(8,128)(2,1)}, u32[]{:S(2)}, u32[]{:S(2)}) collective-permute-start(bf16[256,1408]{1,0:T(8,128)(2,1)} %get-tuple-element.80), channel_id=1, source_target_pairs={{0,12},{4,0},{8,4},{12,8},{1,13},{5,1},{9,5},{13,9},{2,14},{6,2},{... | collective-permute-start | bytes 2162696 | tf_op jit(solution)/shard_map/ppermute | solution.py:771
  456.8 168.1 %collective-permute-start.12 = (bf16[256,1408]{1,0:T(8,128)(2,1)}, bf16[256,1408]{1,0:T(8,128)(2,1)}, u32[]{:S(2)}, u32[]{:S(2)}) collective-permute-start(bf16[256,1408]{1,0:T(8,128)(2,1)} %get-tuple-element.81), channel_id=1, source_target_pairs={{0,8},{4,12},{8,0},{12,4},{1,9},{5,13},{9,1},{13,5},{2,10},{6,14},... | collective-permute-start | bytes 2162696 | tf_op jit(solution)/shard_map/ppermute | solution.py:771
  465.1 64.1 %collective-permute-start.8 = (bf16[256,1408]{1,0:T(8,128)(2,1)}, bf16[256,1408]{1,0:T(8,128)(2,1)}, u32[]{:S(2)}, u32[]{:S(2)}) collective-permute-start(bf16[256,1408]{1,0:T(8,128)(2,1)} %get-tuple-element.84), channel_id=1, source_target_pairs={{0,8},{4,12},{8,0},{12,4},{1,9},{5,13},{9,1},{13,5},{2,10},{6,14},... | collective-permute-start | bytes 2162696 | tf_op jit(solution)/shard_map/ppermute | solution.py:771
  466.2 59.9 %collective-permute-start.7 = (bf16[256,1408]{1,0:T(8,128)(2,1)}, bf16[256,1408]{1,0:T(8,128)(2,1)}, u32[]{:S(2)}, u32[]{:S(2)}) collective-permute-start(bf16[256,1408]{1,0:T(8,128)(2,1)} %get-tuple-element.85), channel_id=1, source_target_pairs={{0,4},{4,8},{8,12},{12,0},{1,5},{5,9},{9,13},{13,1},{2,6},{6,10},{... | collective-permute-start | bytes 2162696 | tf_op jit(solution)/shard_map/ppermute | solution.py:771
  470.4 49.8 %copy-start.20 = (bf16[256,512]{1,0:T(8,128)(2,1)S(1)}, bf16[256,512]{1,0:T(8,128)(2,1)}, u32[]{:S(2)}) copy-start(bf16[256,512]{1,0:T(8,128)(2,1)} %get-tuple-element.45) | copy-start | bytes 786436
  526.1 15.3 %copy-start.23 = (f32[256,1024]{1,0:T(8,128)S(1)}, f32[256,1024]{1,0:T(8,128)}, u32[]{:S(2)}) copy-start(f32[256,1024]{1,0:T(8,128)} %get-tuple-element.60) | copy-start | bytes 3145732
  526.2 14.1 %collective-permute-start.9 = (bf16[256,1408]{1,0:T(8,128)(2,1)S(1)}, bf16[256,1408]{1,0:T(8,128)(2,1)S(1)}, u32[]{:S(2)}, u32[]{:S(2)}) collective-permute-start(bf16[256,1408]{1,0:T(8,128)(2,1)S(1)} %copy-done.22), channel_id=1, source_target_pairs={{0,12},{4,0},{8,4},{12,8},{1,13},{5,1},{9,5},{13,9},{2,14},{6,2},{... | collective-permute-start | bytes 2162696 | tf_op jit(solution)/shard_map/ppermute | solution.py:771
  529.2 24.7 %collective-permute-start.11 = (bf16[256,1408]{1,0:T(8,128)(2,1)}, bf16[256,1408]{1,0:T(8,128)(2,1)}, u32[]{:S(2)}, u32[]{:S(2)}) collective-permute-start(bf16[256,1408]{1,0:T(8,128)(2,1)} %get-tuple-element.82), channel_id=1, source_target_pairs={{0,4},{4,8},{8,12},{12,0},{1,5},{5,9},{9,13},{13,1},{2,6},{6,10},{... | collective-permute-start | bytes 2162696 | tf_op jit(solution)/shard_map/ppermute | solution.py:771
  531.6 11.9 %copy-start.10 = (f32[256,4,128]{2,1,0:T(4,128)S(1)}, f32[256,4,128]{2,1,0:T(4,128)}, u32[]{:S(2)}) copy-start(f32[256,4,128]{2,1,0:T(4,128)} %reshape.171) | copy-start | bytes 1572868
  651.4 89.8 %collective-permute-start.16 = (bf16[256,1408]{1,0:T(8,128)(2,1)S(1)}, bf16[256,1408]{1,0:T(8,128)(2,1)}, u32[]{:S(2)}, u32[]{:S(2)}) collective-permute-start(bf16[256,1408]{1,0:T(8,128)(2,1)S(1)} %get-tuple-element.77), channel_id=1, source_target_pairs={{0,12},{4,0},{8,4},{12,8},{1,13},{5,1},{9,5},{13,9},{2,14},{6,2},{... | collective-permute-start | bytes 2162696 | tf_op jit(solution)/shard_map/ppermute | solution.py:771
  652.3 87.6 %collective-permute-start.15 = (bf16[256,1408]{1,0:T(8,128)(2,1)S(1)}, bf16[256,1408]{1,0:T(8,128)(2,1)}, u32[]{:S(2)}, u32[]{:S(2)}) collective-permute-start(bf16[256,1408]{1,0:T(8,128)(2,1)S(1)} %get-tuple-element.78), channel_id=1, source_target_pairs={{0,8},{4,12},{8,0},{12,4},{1,9},{5,13},{9,1},{13,5},{2,10},{6,14},... | collective-permute-start | bytes 2162696 | tf_op jit(solution)/shard_map/ppermute | solution.py:771
  653.1 85.5 %collective-permute-start.14 = (bf16[256,1408]{1,0:T(8,128)(2,1)}, bf16[256,1408]{1,0:T(8,128)(2,1)}, u32[]{:S(2)}, u32[]{:S(2)}) collective-permute-start(bf16[256,1408]{1,0:T(8,128)(2,1)} %get-tuple-element.79), channel_id=1, source_target_pairs={{0,4},{4,8},{8,12},{12,0},{1,5},{5,9},{9,13},{13,1},{2,6},{6,10},{... | collective-permute-start | bytes 2162696 | tf_op jit(solution)/shard_map/ppermute | solution.py:771
  (28 other events, 98.1 us)

commit v4 on v3

v4 whole, which is shorter than its diff:
```python
from functools import partial
import math

import jax
import jax.numpy as jnp
from jax import lax
from jax.experimental import pallas as pl
from jax.experimental.pallas import tpu as pltpu
from jax.sharding import PartitionSpec as P

HD = 128
CAP = 160


EPS = 1e-05
THETA = 10000.0
NEG = -1e30
BF = jnp.bfloat16
F32 = jnp.float32


def mm(left, right):
    return jnp.dot(left, right, preferred_element_type=F32)


def mm_t(left, right):
    return lax.dot_general(left, right, (((1,), (1,)), ((), ())), preferred_element_type=F32)


def t_mm(left, right):
    return lax.dot_general(left, right, (((0,), (0,)), ((), ())), preferred_element_type=F32)


def rotary_tables(positions):
    half_size = HD // 2
    frequency = THETA ** (-(jnp.arange(half_size, dtype=F32) * 2.0 / HD))
    angles = positions.astype(F32)[:, None] * frequency[None, :]
    cosine, sine = jnp.cos(angles), jnp.sin(angles)
    return jnp.concatenate([cosine, cosine], axis=1), jnp.concatenate([-sine, sine], axis=1)


MESH = pl.DeviceIdType.MESH
VM = pl.BlockSpec(memory_space=pltpu.VMEM)
DMA = pltpu.SemaphoreType.DMA


def peer(axis, n, k):
    return lax.rem(lax.axis_index(axis) + k, n)


def greet(groups):
    barrier = pltpu.get_barrier_semaphore()
    for axis, n in groups:
        for k in range(1, n):
            pl.semaphore_signal(
                barrier, inc=1, device_id={axis: peer(axis, n, k)}, device_id_type=MESH
            )
    pl.semaphore_wait(barrier, sum(n - 1 for _, n in groups))


def remote(source, target, sems, i, to):
    copy = pltpu.make_async_remote_copy(
        src_ref=source,
        dst_ref=target,
        send_sem=sems[0].at[i],
        recv_sem=sems[1].at[i],
        device_id=to,
        device_id_type=MESH,
    )
    copy.start()
    return copy


def send(source, target, axis, n, k, sems):
    return remote(source, target, sems, k - 1, {axis: peer(axis, n, k)})


def columns(n, size):
    return pl.ds(pl.multiple_of(n * size, 128), size)


def stretch(n, size):
    return pl.ds(pl.multiple_of(n * size, 16), size)


def gather_columns(own, full, axis, n, sems):
    size = own.shape[1]
    place = full.at[:, columns(lax.axis_index(axis), size)]
    copies = [send(own, place, axis, n, k, sems) for k in range(1, n)]
    place[...] = own[...]
    return copies


def scatter_columns(part, slots, axis, n, sems):
    size = slots.shape[2]
    return [
        send(part.at[:, columns(peer(axis, n, k), size)], slots.at[k - 1], axis, n, k, sems)
        for k in range(1, n)
    ]


def finish(copies):
    for copy in copies:
        copy.wait()


def quad():
    here = lax.axis_index("ctx")
    return here, here + 1 - 2 * lax.rem(here, 2), lax.rem(here + 2, 4)


def gather_square(own, full, first_row, sems, between):
    rows = own.shape[0]
    here, beside, across = quad()

    def place(rank):
        return full.at[pl.ds(pl.multiple_of(first_row + rank * rows, 16), rows), :]

    first = remote(own, place(here), sems, 0, {"ctx": across})
    second = remote(own, place(here), sems, 1, {"ctx": beside})
    full[pl.ds(pl.multiple_of(first_row + here * rows, 16), rows), :] = own[...]
    between()
    first.wait()
    third = remote(place(across), place(across), sems, 2, {"ctx": beside})
    second.wait()
    third.wait()


def row_sums(values):
    ones = jnp.ones((8, values.shape[1]), F32)
    return lax.dot_general(
        ones,
        values,
        (((1,), (1,)), ((), ())),
        precision=lax.Precision.HIGHEST,
        preferred_element_type=F32,
    )


def as_column(rows, weight):
    return lax.dot_general(
        rows,
        weight,
        (((0,), (0,)), ((), ())),
        precision=lax.Precision.HIGHEST,
        preferred_element_type=F32,
    )


def eighth():
    return jnp.full((8, 128), 0.125, F32)


def total_over(sums, mine, slots, axis, n, sems):
    mine[...] = sums
    copies = [send(mine, slots.at[k - 1], axis, n, k, sems) for k in range(1, n)]
    finish(copies)
    total = sums
    for k in range(1, n):
        total = total + slots[k - 1]
    return total


def call(kernel, out_shape, inputs, scratch, collective, name):
    return pl.pallas_call(
        kernel,
        out_shape=out_shape,
        in_specs=[VM] * len(inputs),
        out_specs=jax.tree.map(lambda _: VM, out_shape),
        scratch_shapes=scratch,
        compiler_params=pltpu.CompilerParams(collective_id=collective, has_side_effects=True),
        cost_estimate=pl.CostEstimate(flops=0, bytes_accessed=0, transcendentals=0),
        name=name,
    )(*inputs)


def shape(dims, dtype):
    return jax.ShapeDtypeStruct(dims, dtype)


def pair_of_sems(n):
    return [DMA((n,)), DMA((n,))]


def gather_tp(value, n_tp):
    rows, size = value.shape

    def kernel(own, full, *sems):
        greet([("tp", n_tp)])
        finish(gather_columns(own, full, "tp", n_tp, sems))

    return call(
        kernel, shape((rows, size * n_tp), value.dtype), (value,), pair_of_sems(n_tp), 1, "gather_tp"
    )


def first_norm(full, grad, gain, weights, quarter, n_tp, n_ctx):
    rows, width = full.shape
    with_quarter = quarter is not None

    def kernel(*refs):
        hid, grd, gn = refs[:3]
        refs = refs[3:]
        if with_quarter:
            wgt, qrt, out, scale, grd_full, wgt_full = refs[:6]
            sems = refs[6:]
            greet([("tp", n_tp), ("ctx", n_ctx)])
        else:
            out, scale, grd_full = refs[:3]
            sems = refs[3:]
            greet([("tp", n_tp)])
        grads = gather_columns(grd, grd_full, "tp", n_tp, sems[0:2])

        def norm():
            values = hid[...].astype(F32)
            mean = jnp.sum(values * values, axis=-1, keepdims=True) * (1.0 / width)
            factor = lax.rsqrt(mean + EPS)
            scale[...] = jnp.broadcast_to(factor, scale.shape)
            out[...] = (values * factor * gn[0:1, :]).astype(BF)

        if with_quarter:
            half = wgt.shape[0]
            mine = lax.axis_index("fsdp")

            def work():
                norm()
                wgt_full[pl.ds(pl.multiple_of(mine * half, 16), half), :] = wgt[...]

            gather_square(qrt, wgt_full, (1 - mine) * half, sems[2:4], work)
        else:
            norm()
        finish(grads)

    outs = [shape((rows, width), BF), shape((rows, 128), F32), shape((rows, width), BF)]
    inputs = [full, grad, gain]
    if with_quarter:
        outs.append(shape((2 * weights.shape[0], weights.shape[1]), BF))
        inputs += [weights, quarter]
    return call(
        kernel, tuple(outs), inputs, pair_of_sems(n_tp) + pair_of_sems(3), 7, "first_norm"
    )


def turn(values, cosine, sine):
    return values * cosine + pltpu.roll(values, HD // 2, axis=1) * sine


def softmax_rows(query, key, first_row):
    scores = mm_t(query, key) * (1.0 / math.sqrt(HD))
    rows = first_row + lax.broadcasted_iota(jnp.int32, scores.shape, 0)
    cols = lax.broadcasted_iota(jnp.int32, scores.shape, 1)
    scores = jnp.where(cols <= rows, scores, NEG)
    top = jnp.max(scores, axis=-1, keepdims=True)
    weights = jnp.exp(scores - top)
    return weights / jnp.sum(weights, axis=-1, keepdims=True)


def attention_forward(qkv, cosine, sine, n_ctx):
    rows = qkv.shape[0]
    width = qkv.shape[1] // 3
    heads = width // HD

    def kernel(prj, cs, sn, out, qry, full, own, *sems):
        greet([("ctx", n_ctx)])
        here = lax.axis_index("ctx")

        @pl.loop(0, heads)
        def _(h):
            own[:, columns(h, HD)] = turn(
                prj[:, columns(h + heads, HD)], cs[...], sn[...]
            ).astype(BF)
            own[:, columns(h + heads, HD)] = prj[:, columns(h + 2 * heads, HD)].astype(BF)

        def queries():
            @pl.loop(0, heads)
            def _(h):
                qry[:, columns(h, HD)] = turn(prj[:, columns(h, HD)], cs[...], sn[...]).astype(BF)

        gather_square(own, full, 0, sems, queries)

        @pl.loop(0, heads)
        def _(h):
            probs = softmax_rows(qry[:, columns(h, HD)], full[:, columns(h, HD)], here * rows)
            out[:, columns(h, HD)] = mm(
                probs.astype(BF), full[:, columns(h + heads, HD)]
            ).astype(BF)

    return call(
        kernel,
        (
            shape((rows, width), BF),
            shape((rows, width), BF),
            shape((rows * n_ctx, 2 * width), BF),
        ),
        (qkv, cosine, sine),
        [pltpu.VMEM((rows, 2 * width), BF)] + pair_of_sems(3),
        2,
        "attention_forward",
    )


def second_norm(part, hidden, gain, slabs, picks, router, onehot, names, n_tp, n_ctx):
    rows, size = hidden.shape
    width = size * n_tp
    experts = n_ctx

    def kernel(
        prt, hid, gn, slb, pck, rtr, one, nms,
        resid, scale, out, moved, tokens, slot_gates, gates, mix,
        slots, mine, sums, low, sent, own_gates, *sems
    ):
        greet([("tp", n_tp), ("ctx", n_ctx)])
        here = lax.axis_index("tp")
        copies = scatter_columns(prt, slots, "tp", n_tp, sems[0:2])
        others = [
            send(
                slb.at[pl.ds(k * CAP, CAP)], moved.at[pl.ds(k * CAP, CAP)],
                "ctx", n_ctx, k, sems[6:8],
            )
            for k in range(1, n_ctx)
        ]
        moved[0:CAP] = slb[0:CAP]
        total = prt[:, columns(here, size)].astype(F32)
        finish(copies)
        for k in range(1, n_tp):
            total = total + slots[k - 1].astype(F32)
        total = hid[...].astype(F32) + total
        resid[...] = total
        square = total_over(row_sums(total * total), mine, sums, "tp", n_tp, sems[2:4])
        factor = lax.rsqrt(as_column(square, eighth()) * (1.0 / width) + EPS)
        scale[...] = factor
        low[...] = (resid[...] * factor[:, 0:1] * gn[0:1, :]).astype(BF)
        copies = gather_columns(low, out, "tp", n_tp, sems[4:6])
        for step in range(n_tp):
            at = columns(peer("tp", n_tp, n_tp - step), size)
            if step:
                copies[step - 1].wait()
                block = out[:, at]
            else:
                block = low[...]
            sent[step] = mm(pck[...], block).astype(BF)
            tokens[0:CAP, at] = sent[step, 0:CAP]
            for k in (2, 3, 1):
                others.append(
                    remote(
                        sent.at[step, pl.ds(k * CAP, CAP)], tokens.at[pl.ds(k * CAP, CAP), at],
                        sems[8:10], step * n_ctx + k, {"ctx": peer("ctx", n_ctx, k)},
                    )
                )
        logits = mm_t(rtr[...].astype(BF), out[...])
        named = [jnp.sum(one[j] * logits, axis=0, keepdims=True) for j in range(2)]
        top = jnp.maximum(named[0], named[1])
        powers = [jnp.exp(value - top) for value in named]
        both = powers[0] + powers[1]
        gate = [value / both for value in powers]
        mixed = gate[0] * nms[0] + gate[1] * nms[1]
        mix[...] = mixed
        order = lax.broadcasted_iota(jnp.int32, (8, rows), 0)
        gates[...] = jnp.where(order == 0, gate[0], jnp.where(order == 1, gate[1], 0.0))
        own_gates[...] = jnp.zeros(own_gates.shape, F32)
        for k in range(experts):
            own_gates[k, :, 0:CAP] = lax.dot_general(
                jnp.broadcast_to(mixed[k : k + 1], (8, rows)),
                pck[k * CAP : (k + 1) * CAP].astype(F32),
                (((1,), (1,)), ((), ())),
                precision=lax.Precision.HIGHEST,
                preferred_element_type=F32,
            )
        slot_gates[0] = own_gates[0]
        for k in range(1, n_ctx):
            others.append(
                send(own_gates.at[k], slot_gates.at[k], "ctx", n_ctx, k, sems[10:12])
            )
        finish(others)

    return call(
        kernel,
        (
            shape((rows, size), F32),
            shape((rows, 128), F32),
            shape((rows, width), BF),
            shape(slabs.shape, BF),
            shape(slabs.shape, BF),
            shape((experts, 8, rows), F32),
            shape((8, rows), F32),
            shape((8, rows), F32),
        ),
        (part, hidden, gain, slabs, picks, router, onehot, names),
        [
            pltpu.VMEM((n_tp - 1, rows, size), BF),
            pltpu.VMEM((8, rows), F32),
            pltpu.VMEM((n_tp - 1, 8, rows), F32),
            pltpu.VMEM((rows, size), BF),
            pltpu.VMEM((n_tp, experts * CAP, size), BF),
            pltpu.VMEM((experts, 8, rows), F32),
        ]
        + pair_of_sems(n_tp) * 3
        + pair_of_sems(n_ctx)
        + pair_of_sems(n_tp * n_ctx)
        + pair_of_sems(n_ctx),
        3,
        "second_norm",
    )


def second_norm_back(
    d_rows, dots, picks, gates, onehot, names, router, resid, scale, gain, grad, n_tp, n_ctx
):
    rows, size = resid.shape
    width = size * n_tp
    experts = n_ctx

    def kernel(
        drw, dts, pck, gts, one, nms, rtr, rsd, scl, gn, grd,
        d_resid, low, d_gain, d_logits,
        back, back_dots, part, slots, mine, sums, mine_two, sums_two, *sems
    ):
        greet([("tp", n_tp), ("ctx", n_ctx)])
        here = lax.axis_index("tp")
        small = []
        large = []
        for k in range(1, n_ctx):
            small.append(
                send(dts.at[k], back_dots.at[k - 1], "ctx", n_ctx, n_ctx - k, sems[0:2])
            )
        for step in range(1, n_tp + 1):
            at = columns(peer("tp", n_tp, step), size)
            for k in (2, 3, 1):
                large.append(
                    remote(
                        drw.at[pl.ds(k * CAP, CAP), at], back.at[k - 1, :, at],
                        sems[2:4], step * n_ctx - k, {"ctx": peer("ctx", n_ctx, n_ctx - k)},
                    )
                )
        finish(small)
        order = lax.broadcasted_iota(jnp.int32, (8, rows), 0)
        own = jnp.zeros((8, rows), F32)
        for k in range(experts):
            by_slot = dts[0] if k == 0 else back_dots[k - 1]
            by_row = lax.dot_general(
                by_slot[:, 0:CAP],
                pck[k * CAP : (k + 1) * CAP].astype(F32),
                (((1,), (0,)), ((), ())),
                precision=lax.Precision.HIGHEST,
                preferred_element_type=F32,
            )
            own = own + jnp.where(order == k, by_row, 0.0)
        gate_grad = total_over(own, mine, sums, "tp", n_tp, sems[4:6])
        both = [jnp.sum(nms[j] * gate_grad, axis=0, keepdims=True) for j in range(2)]
        gate = [gts[j : j + 1, :] for j in range(2)]
        mean = gate[0] * both[0] + gate[1] * both[1]
        logits = sum(gate[j] * (both[j] - mean) * one[j] for j in range(2))
        d_logits[...] = logits
        copies = []
        for step in range(1, n_tp + 1):
            at = columns(peer("tp", n_tp, step), size)
            finish(large[3 * step - 3 : 3 * step])
            block = t_mm(pck[0:CAP], drw[0:CAP, at])
            for k in range(1, experts):
                block = block + t_mm(pck[k * CAP : (k + 1) * CAP], back[k - 1, :, at])
            if step < n_tp:
                part[step - 1] = block.astype(BF)
                copies.append(
                    send(part.at[step - 1], slots.at[step - 1], "tp", n_tp, step, sems[6:8])
                )
            else:
                total = block
        total = total + lax.dot_general(
            logits.astype(BF),
            rtr[...].astype(BF),
            (((0,), (0,)), ((), ())),
            preferred_element_type=F32,
        )
        finish(copies)
        for k in range(1, n_tp):
            total = total + slots[k - 1].astype(F32)
        factor = scl[:, 0:1]
        unit = rsd[...] * factor
        d_gain[...] = jnp.broadcast_to(jnp.sum(total * unit, axis=0, keepdims=True), d_gain.shape)
        gained = total * gn[0:1, :]
        d_resid[...] = gained
        dot = total_over(row_sums(unit * gained), mine_two, sums_two, "tp", n_tp, sems[8:10])
        dot = as_column(dot, eighth())[:, 0:1] * (1.0 / width)
        result = grd[...].astype(F32) + factor * (d_resid[...] - rsd[...] * factor * dot)
        d_resid[...] = result
        low[...] = result.astype(BF)

    return call(
        kernel,
        (
            shape((rows, size), F32),
            shape((rows, size), BF),
            shape((8, size), F32),
            shape((8, rows), F32),
        ),
        (d_rows, dots, picks, gates, onehot, names, router, resid, scale, gain, grad),
        [
            pltpu.VMEM((n_ctx - 1, CAP, width), BF),
            pltpu.VMEM((n_ctx - 1, 8, rows), F32),
            pltpu.VMEM((n_tp - 1, rows, size), BF),
            pltpu.VMEM((n_tp - 1, rows, size), BF),
            pltpu.VMEM((8, rows), F32),
            pltpu.VMEM((n_tp - 1, 8, rows), F32),
            pltpu.VMEM((8, rows), F32),
            pltpu.VMEM((n_tp - 1, 8, rows), F32),
        ]
        + pair_of_sems(n_ctx)
        + pair_of_sems(n_tp * n_ctx)
        + pair_of_sems(n_tp) * 3,
        4,
        "second_norm_back",
    )


def attention_backward(low, output_w, query, kv, cosine, sine, n_tp, n_ctx):
    rows, size = low.shape
    width = size * n_tp
    inner = query.shape[1]
    heads = inner // HD
    scale = 1.0 / math.sqrt(HD)

    def kernel(
        lw, wgt, qry, full, cs, sn, d_attn, d_qkv, dot, dqs, dkv, slots, last, both, total, *sems
    ):
        greet([("tp", n_tp), ("ctx", n_ctx)])
        here, beside, across = quad()
        beyond = lax.rem(beside + 2, 4)
        copies = gather_columns(lw, d_attn, "tp", n_tp, sems[2:4])
        for step in range(n_tp):
            rank = peer("tp", n_tp, n_tp - step)
            weights = wgt[pl.ds(pl.multiple_of(rank * size, 16), size), :]
            if step:
                copies[step - 1].wait()
                total[...] += mm(d_attn[:, columns(rank, size)], weights)
            else:
                total[...] = mm(lw[...], weights)
        dot[...] = total[...].astype(BF)

        @pl.loop(0, heads)
        def _(h):
            at, at_v = columns(h, HD), columns(h + heads, HD)
            probs = softmax_rows(qry[:, at], full[:, at], here * rows)
            d_probs = mm_t(dot[:, at], full[:, at_v])
            delta = jnp.sum(probs * d_probs, axis=-1, keepdims=True)
            d_scores = (probs * (d_probs - delta)).astype(BF)
            dqs[:, at] = mm(d_scores, full[:, at]) * scale
            dkv[:, at] = (t_mm(d_scores, qry[:, at]) * scale).astype(BF)
            dkv[:, at_v] = t_mm(probs.astype(BF), dot[:, at]).astype(BF)

        first = remote(dkv.at[stretch(beyond, rows), :], slots.at[0], sems, 0, {"ctx": beside})
        second = remote(dkv.at[stretch(beside, rows), :], slots.at[1], sems, 1, {"ctx": beside})
        first.wait()
        both[...] = (
            dkv[stretch(across, rows), :].astype(F32) + slots[0].astype(F32)
        ).astype(BF)
        third = remote(both, last, sems, 2, {"ctx": across})

        @pl.loop(0, heads)
        def _(h):
            d_qkv[:, columns(h, HD)] = turn(dqs[:, columns(h, HD)], cs[...], sn[...]).astype(BF)

        second.wait()
        third.wait()

        @pl.loop(0, heads)
        def _(h):
            at, at_v = columns(h, HD), columns(h + heads, HD)
            mine = stretch(here, rows)
            d_key = dkv[mine, at].astype(F32) + slots[1, :, at].astype(F32)
            d_key = d_key + last[:, at].astype(F32)
            d_qkv[:, columns(h + heads, HD)] = turn(d_key, cs[...], sn[...]).astype(BF)
            d_value = dkv[mine, at_v].astype(F32) + slots[1, :, at_v].astype(F32)
            d_value = d_value + last[:, at_v].astype(F32)
            d_qkv[:, columns(h + 2 * heads, HD)] = d_value.astype(BF)

    return call(
        kernel,
        (shape((rows, width), BF), shape((rows, 3 * inner), BF)),
        (low, output_w, query, kv, cosine, sine),
        [
            pltpu.VMEM((rows, inner), BF),
            pltpu.VMEM((rows, inner), F32),
            pltpu.VMEM((rows * n_ctx, 2 * inner), BF),
            pltpu.VMEM((2, rows, 2 * inner), BF),
            pltpu.VMEM((rows, 2 * inner), BF),
            pltpu.VMEM((rows, 2 * inner), BF),
            pltpu.VMEM((rows, inner), F32),
        ]
        + pair_of_sems(3)
        + pair_of_sems(n_tp),
        5,
        "attention_backward",
    )


def first_norm_back(part, hidden, scale, gain, d_resid, n_tp):
    rows, size = hidden.shape
    width = size * n_tp

    def kernel(prt, hid, scl, gn, dr, out, d_gain, slots, mine, sums, *sems):
        greet([("tp", n_tp)])
        here = lax.axis_index("tp")
        copies = scatter_columns(prt, slots, "tp", n_tp, sems[0:2])
        total = prt[:, columns(here, size)].astype(F32)
        finish(copies)
        for k in range(1, n_tp):
            total = total + slots[k - 1].astype(F32)
        factor = scl[:, 0:1]
        unit = hid[...].astype(F32) * factor
        d_gain[...] = jnp.broadcast_to(jnp.sum(total * unit, axis=0, keepdims=True), d_gain.shape)
        gained = total * gn[0:1, :]
        out[...] = gained
        dot = total_over(row_sums(unit * gained), mine, sums, "tp", n_tp, sems[2:4])
        dot = as_column(dot, eighth())[:, 0:1] * (1.0 / width)
        unit = hid[...].astype(F32) * factor
        out[...] = dr[...] + factor * (out[...] - unit * dot)

    return call(
        kernel,
        (shape((rows, size), F32), shape((8, size), F32)),
        (part, hidden, scale, gain, d_resid),
        [
            pltpu.VMEM((n_tp - 1, rows, size), BF),
            pltpu.VMEM((8, rows), F32),
            pltpu.VMEM((n_tp - 1, 8, rows), F32),
        ]
        + pair_of_sems(n_tp) * 2,
        6,
        "first_norm_back",
    )


def weight_grads(part, small, n_tp, n_ctx):
    rows, size = part.shape[2:]
    half = size // 2
    width = small.shape[1] * n_tp
    places = 2 * n_ctx
    cut = width // places

    def kernel(
        prt, sml, out, small_out, near, two, far, one, last, sml_full, sml_slots, *sems
    ):
        barrier = pltpu.get_barrier_semaphore()
        here, beside, across = quad()
        beyond = lax.rem(beside + 2, 4)
        mine = lax.axis_index("fsdp")
        other = 1 - mine
        place = mine * n_ctx + here
        others = []
        for i in range(1, places):
            to = lax.rem(place + i, places)
            others.append((to, {"fsdp": to // n_ctx, "ctx": lax.rem(to, n_ctx)}))
        ahead = [{"tp": peer("tp", n_tp, k)} for k in range(1, n_tp)]
        for device in ahead + [device for _, device in others]:
            pl.semaphore_signal(barrier, inc=1, device_id=device, device_id_type=MESH)
        pl.semaphore_wait(barrier, n_tp - 1 + places - 1)
        gathers = gather_columns(sml, sml_full, "tp", n_tp, sems[6:8])
        left, right = pl.ds(0, half), pl.ds(half, half)
        blocks = [
            (other, beyond, left), (mine, beyond, left), (other, beyond, right),
            (other, beside, right), (other, beside, left), (mine, beside, left),
            (mine, beyond, right), (mine, beside, right),
        ]
        steps = []
        for i, (rank, column, at) in enumerate(blocks):
            steps.append(
                remote(prt.at[rank, column, :, at], near.at[i], sems[0:2], i, {"ctx": beside})
            )
        finish(gathers)
        totals = [
            remote(
                sml_full.at[:, columns(to, cut)], sml_slots.at[i], sems[8:10], i, device
            )
            for i, (to, device) in enumerate(others)
        ]

        def chip(i, rank, column, at):
            steps[i].wait()
            return prt[rank, column, :, at].astype(F32) + near[i].astype(F32)

        first_hop = []
        for slot, (i, rank, column, at, to) in enumerate(
            [
                (0, other, across, left, {"ctx": across}),
                (1, mine, across, left, {"ctx": across}),
                (2, other, across, right, {"fsdp": other}),
                (3, other, here, right, {"fsdp": other}),
            ]
        ):
            two[slot] = chip(i, rank, column, at).astype(BF)
            first_hop.append(remote(two.at[slot], far.at[slot], sems[2:4], slot, to))
        value = chip(4, other, here, left)
        first_hop[0].wait()
        one[0] = (value + far[0].astype(F32)).astype(BF)
        second_hop = [remote(one.at[0], last.at[0], sems[4:6], 0, {"fsdp": other})]
        value = chip(6, mine, across, right)
        first_hop[2].wait()
        one[1] = (value + far[2].astype(F32)).astype(BF)
        second_hop.append(remote(one.at[1], last.at[1], sems[4:6], 1, {"ctx": across}))
        value = chip(5, mine, here, left)
        first_hop[1].wait()
        out[:, left] = value + far[1].astype(F32)
        value = chip(7, mine, here, right)
        first_hop[3].wait()
        out[:, right] = value + far[3].astype(F32)
        finish(totals)
        sums = sml_full[:, columns(place, cut)]
        for i in range(places - 1):
            sums = sums + sml_slots[i]
        small_out[...] = sums
        second_hop[0].wait()
        out[:, left] = out[:, left] + last[0].astype(F32)
        second_hop[1].wait()
        out[:, right] = out[:, right] + last[1].astype(F32)

    return call(
        kernel,
        (shape((rows, size), F32), shape((8, cut), F32)),
        (part, small),
        [
            pltpu.VMEM((8, rows, half), BF),
            pltpu.VMEM((4, rows, half), BF),
            pltpu.VMEM((4, rows, half), BF),
            pltpu.VMEM((2, rows, half), BF),
            pltpu.VMEM((2, rows, half), BF),
            pltpu.VMEM((8, width), F32),
            pltpu.VMEM((places - 1, 8, cut), F32),
        ]
        + pair_of_sems(8)
        + pair_of_sems(4)
        + pair_of_sems(2)
        + pair_of_sems(n_tp)
        + pair_of_sems(places),
        10,
        "weight_grads",
    )


def place_pieces(pieces, n_ctx):
    rows, size = pieces[0].shape
    tile = 64 if rows % 64 == 0 else rows

    def kernel(*refs):
        here = lax.axis_index("ctx")
        for k in range(n_ctx):
            refs[-1][lax.rem(here + n_ctx - k, n_ctx)] = refs[k][...].astype(F32)

    return pl.pallas_call(
        kernel,
        grid=(rows // tile,),
        out_shape=shape((n_ctx, rows, size), F32),
        in_specs=[pl.BlockSpec((tile, size), lambda i: (i, 0))] * n_ctx,
        out_specs=pl.BlockSpec((n_ctx, tile, size), lambda i: (0, i, 0)),
        cost_estimate=pl.CostEstimate(
            flops=0, bytes_accessed=6 * n_ctx * rows * size, transcendentals=0
        ),
        name="place_pieces",
    )(*pieces)


def after(value, *needed):
    return lax.optimization_barrier((value, *needed))[0]


def shards(
    hidden_in,
    out_grad,
    attn_gain,
    w_query,
    w_key,
    w_value,
    w_output,
    ffn_gain,
    w_router,
    w_gate,
    w_up,
    w_down,
    routes,
):
    rows_here, width_tp = hidden_in.shape
    here_tp = lax.axis_index("tp")
    here_ctx = lax.axis_index("ctx")
    here_fsdp = lax.axis_index("fsdp")
    n_fsdp = lax.axis_size("fsdp")
    n_ctx = lax.axis_size("ctx")
    n_tp = lax.axis_size("tp")
    experts = w_gate.shape[0]
    assert experts == n_ctx == 4
    width = width_tp * n_tp
    part = width // n_fsdp
    pair = n_fsdp == 2
    heads_width = w_query.shape[1]

    def shift_ctx(value, k):
        return lax.ppermute(value, "ctx", [(i, (i + k) % n_ctx) for i in range(n_ctx)])

    def swap_fsdp(value):
        return lax.ppermute(value, "fsdp", [(0, 1), (1, 0)])

    def other_parts(weight):
        if pair:
            return [weight, swap_fsdp(weight)]
        return [lax.all_gather(weight, "fsdp", axis=0, tiled=True)]

    def split(values):
        if pair:
            return [
                lax.dynamic_slice_in_dim(values, here_fsdp * part, part, 1),
                lax.dynamic_slice_in_dim(values, (1 - here_fsdp) * part, part, 1),
            ]
        return [values]

    def join(pieces):
        if pair:
            first = here_fsdp == 0
            return jnp.concatenate(
                [jnp.where(first, pieces[0], pieces[1]), jnp.where(first, pieces[1], pieces[0])],
                axis=1,
            )
        return pieces[0]

    def into(values, weights):
        return sum(mm(x, w) for x, w in zip(split(values), weights))

    def back(values, weights):
        return join([mm_t(values, w) for w in weights])

    def my_features(values):
        return lax.dynamic_slice_in_dim(values, here_tp * width_tp, width_tp, values.ndim - 1)

    attn_w = jnp.concatenate([w_query, w_key, w_value, w_output], axis=1)
    small = jnp.concatenate(
        [attn_gain[None], ffn_gain[None], w_router.T, jnp.zeros((2, part), BF)], axis=0
    )
    if pair:
        quarter = part // n_ctx
        own_quarter = lax.dynamic_slice_in_dim(attn_w, here_ctx * quarter, quarter, 0)
        other_quarter = swap_fsdp(own_quarter)
        other_small = swap_fsdp(small)
        small_full = join([small, other_small]).astype(F32)
    else:
        other_quarter = None
        small_full = lax.all_gather(small, "fsdp", axis=1, tiled=True).astype(F32)
    inputs_full = gather_tp(hidden_in, n_tp)

    def expert_parts(weights, ready):
        rank, _ = lax.optimization_barrier((here_ctx, ready))
        return other_parts(lax.dynamic_index_in_dim(weights, rank, 0, False))

    gate_w = expert_parts(w_gate, small)
    up_w = expert_parts(w_up, inputs_full)
    down_w = expert_parts(w_down, inputs_full)
    small_here = my_features(small_full)
    gain_one_here = jnp.broadcast_to(small_here[0:1], small_here.shape)
    gain_two_here = jnp.broadcast_to(small_here[1:2], small_here.shape)
    nothing = [(0, 8 - experts), (0, 0)]
    router_full = jnp.pad(small_full[2 : 2 + experts], nothing)
    router_here = jnp.pad(small_here[2 : 2 + experts], nothing)

    relative = (jnp.arange(experts, dtype=jnp.int32) + here_ctx) % experts
    numbers = jnp.arange(8, dtype=jnp.int32)
    onehot = (routes.T[:, None, :] == numbers[None, :, None]).astype(F32)
    named = (routes.T[:, None, :] == relative[None, :, None]).astype(F32)
    names = jnp.pad(named, [(0, 0)] + nothing)
    chosen = jnp.sum(named, axis=0)
    earlier = jnp.triu(jnp.ones((rows_here, rows_here), BF), 1)
    slot_of = mm(chosen.astype(BF), earlier).astype(jnp.int32)
    slots = jnp.arange(CAP, dtype=jnp.int32)
    picks = (slot_of[:, None, :] == slots[None, :, None]) & (chosen[:, None, :] > 0)
    picks = picks.astype(BF).reshape(experts * CAP, rows_here)

    gathered = first_norm(
        inputs_full, out_grad, small_full, attn_w, other_quarter, n_tp, n_ctx
    )
    normed_one, scale_one, grad_full = gathered[:3]
    if pair:
        attn_full = gathered[3]
    else:
        attn_full = lax.all_gather(attn_w, "fsdp", axis=0, tiled=True)
    qkv_w = attn_full[:, : 3 * heads_width]
    output_w = attn_full[:, 3 * heads_width :]
    positions = here_ctx * rows_here + jnp.arange(rows_here, dtype=jnp.int32)
    cosine, sine = rotary_tables(positions)
    attended, query, kv = attention_forward(mm(normed_one, qkv_w), cosine, sine, n_ctx)
    resid, scale_two, normed_two, grad_rows, token_rows, slot_gates, gates, mix = second_norm(
        mm_t(attended, output_w).astype(BF),
        hidden_in,
        gain_two_here,
        mm(picks, grad_full).astype(BF),
        picks,
        router_full,
        onehot,
        names,
        n_tp,
        n_ctx,
    )
    gate_rows = slot_gates[:, 0, :CAP].reshape(experts * CAP, 1)

    gate_act = into(token_rows, gate_w)
    up_act = into(token_rows, up_w)
    sigma_act = jax.nn.sigmoid(gate_act)
    hidden_act = (gate_act * sigma_act * up_act).astype(BF)
    d_result = (gate_rows * grad_rows.astype(F32)).astype(BF)

    def grad_send(left, right):
        halves = split(left)
        if pair:
            away = t_mm(halves[1], right).astype(BF)
            return halves[0], right, away, swap_fsdp(away)
        return halves[0], right, None, None

    def grad_sum(mine, right, away, other):
        if pair:
            return (t_mm(mine, right) + other.astype(F32)).astype(BF)
        return lax.psum_scatter(
            t_mm(mine, right).astype(BF), "fsdp", scatter_dimension=0, tiled=True
        )

    def grad_spread(mine):
        cut = part // n_ctx
        pieces = []
        for k in range(experts):
            piece = lax.dynamic_slice_in_dim(mine, ((here_ctx + k) % n_ctx) * cut, cut, 0)
            pieces.append(shift_ctx(piece, k) if k else piece)
        return pieces

    down_sent = grad_send(d_result, hidden_act)
    if pair:
        grad_rows = after(grad_rows, down_sent[2])
    d_hidden = into(grad_rows, down_w)
    gate_dot = jnp.sum(hidden_act.astype(F32) * d_hidden, axis=-1).reshape(experts, CAP)
    gate_dot = jnp.broadcast_to(
        jnp.pad(gate_dot, [(0, 0), (0, rows_here - CAP)])[:, None, :], (experts, 8, rows_here)
    )
    d_hidden = gate_rows * d_hidden
    d_gate_act = (d_hidden * up_act * sigma_act * (1.0 + gate_act * (1.0 - sigma_act))).astype(BF)
    d_up_act = (d_hidden * gate_act * sigma_act).astype(BF)
    gate_sent = grad_send(token_rows, d_gate_act)
    up_sent = grad_send(token_rows, d_up_act)
    d_rows = join(
        [mm_t(d_gate_act, wg) + mm_t(d_up_act, wu) for wg, wu in zip(gate_w, up_w)]
    ).astype(BF)
    if pair:
        d_rows = after(d_rows, gate_sent[2], up_sent[2])
    result = back(after(hidden_act, d_rows), down_w)

    d_resid, d_attn_here, gain_two_part, d_logits = second_norm_back(
        d_rows,
        gate_dot,
        picks,
        gates,
        onehot,
        names,
        router_here,
        resid,
        scale_two,
        gain_two_here,
        out_grad,
        n_tp,
        n_ctx,
    )
    if pair:
        d_attn_here = after(d_attn_here, down_sent[3])
    down_pieces = grad_spread(grad_sum(*down_sent))

    if pair:
        d_attn_here = after(d_attn_here, down_pieces[0])
    d_attn, d_qkv = attention_backward(
        d_attn_here, output_w, query, kv, cosine, -sine, n_tp, n_ctx
    )
    if pair:
        d_qkv = after(d_qkv, gate_sent[3], *down_pieces)
    gate_pieces = grad_spread(grad_sum(*gate_sent))
    if pair:
        d_qkv = after(d_qkv, gate_pieces[0])
    in_grad, gain_one_part = first_norm_back(
        mm_t(d_qkv, qkv_w).astype(BF), hidden_in, scale_one, gain_one_here, d_resid, n_tp
    )

    share = my_features(result)
    for k in range(1, n_tp):
        piece = lax.dynamic_slice_in_dim(
            result, ((here_tp + k) % n_tp) * width_tp, width_tp, 1
        ).astype(BF)
        piece = lax.ppermute(piece, "tp", [(i, (i + k) % n_tp) for i in range(n_tp)])
        share = share + piece.astype(F32)
    shares = share.astype(BF).reshape(experts, CAP, width_tp)
    moe_part = jnp.zeros(resid.shape, F32)
    for k in range(experts):
        piece = shift_ctx(shares[k], -k) if k else shares[k]
        pick = picks[k * CAP : (k + 1) * CAP]
        moe_part = moe_part + mix[k][:, None] * t_mm(pick, piece)
    block_out = (resid + moe_part).astype(BF)

    grad_attn = jnp.concatenate([t_mm(normed_one, d_qkv), t_mm(d_attn, attended)], axis=1).astype(
        BF
    )
    small_part = jnp.concatenate(
        [
            gain_one_part[:1],
            gain_two_part[:1],
            mm(d_logits[:experts].astype(BF), my_features(normed_two)),
            jnp.zeros((6 - experts, width_tp), F32),
        ],
        axis=0,
    )
    if pair:
        in_grad, small_part = lax.optimization_barrier((in_grad, small_part))
        grad_attn, small_grad = weight_grads(
            grad_attn.reshape(n_fsdp, n_ctx, quarter, -1), small_part, n_tp, n_ctx
        )
        up_there, grad_attn = lax.optimization_barrier((up_sent[3], grad_attn))
        up_sent = (*up_sent[:3], up_there)
    else:
        scatter = partial(
            lax.psum_scatter, axis_name=("fsdp", "ctx"), scatter_dimension=0, tiled=True
        )
        grad_attn = scatter(grad_attn).astype(F32)
        small_grad = lax.all_gather(small_part, "tp", axis=1, tiled=True)
        small_grad = scatter(small_grad.T).T
    up_pieces = grad_spread(grad_sum(*up_sent))
    grad_gate, grad_up, grad_down = (
        place_pieces(pieces, n_ctx) for pieces in (gate_pieces, up_pieces, down_pieces)
    )
    return (
        block_out,
        in_grad,
        small_grad[0],
        grad_attn[:, :heads_width],
        grad_attn[:, heads_width : 2 * heads_width],
        grad_attn[:, 2 * heads_width : 3 * heads_width],
        grad_attn[:, 3 * heads_width :],
        small_grad[1],
        small_grad[2 : 2 + experts].T,
        grad_gate,
        grad_up,
        grad_down,
    )


def solution(mesh):
    rows = ("fsdp", "ctx")
    placed = (
        P(rows, "tp"),
        P(rows, "tp"),
        P("fsdp"),
        P("fsdp", "tp"),
        P("fsdp", "tp"),
        P("fsdp", "tp"),
        P("fsdp", "tp"),
        P("fsdp"),
        P("fsdp", None),
        P(None, "fsdp", "tp"),
        P(None, "fsdp", "tp"),
        P(None, "fsdp", "tp"),
        P(rows, None),
    )
    return jax.shard_map(
        shards,
        mesh=mesh,
        in_specs=placed,
        out_specs=(
            P(rows, "tp"),
            P(rows, "tp"),
            P(rows),
            P(rows, "tp"),
            P(rows, "tp"),
            P(rows, "tp"),
            P(rows, "tp"),
            P(rows),
            P(rows, None),
            P(None, rows, "tp"),
            P(None, rows, "tp"),
            P(None, rows, "tp"),
        ),
        check_vma=False,
    )
```

time: 753 us -> 611 us (0.81)
  Pallas kernels: 456 us -> 386 us
  waiting for transfers between devices: 68.3 us -> 23.8 us
  other arithmetic: 53.3 us -> 24.2 us
  starting transfers between devices: 15.2 us -> 25.1 us
    pallas_call x11 -> x8, Pallas kernels: 456 us -> 372 us  [call(): pl.pallas_call(kernel, out_shape=out_shape, in_specs=[VM] * len(inputs),...]
    ppermute x8, waiting for transfers between devices: 59.7 us -> 0.02 us  [swap_fsdp(): return lax.ppermute(value, 'fsdp', [(0, 1), (1, 0)])]
    dynamic_update_slice x12 -> x0, other arithmetic: 21.4 us -> none  [grad_spread(): lax.dynamic_update_index_in_dim(out, piece.astype(F32), (here_ctx + n_ctx...]
    ppermute x9 -> x12, waiting for transfers between devices: 8.63 us -> 23.8 us  [shift_ctx(): lax.ppermute(value, 'ctx', [(i, (i + k) % n_ctx) for i in range(n_ctx)])]
    pallas_call x0 -> x3, Pallas kernels: none -> 14.9 us  [place_pieces(): pl.pallas_call(kernel, grid=(rows // tile,), out_shape=shape((n_ctx, rows...]
    dot_general x13 -> x10, matrix products: 41 us -> 35.2 us  [mm(): return jnp.dot(left, right, preferred_element_type=F32)]
    dot_general x8 -> x12, matrix products: 32.3 us -> 35.2 us  [t_mm(): lax.dot_general(left, right, (((0,), (0,)), ((), ())), preferred_element_...]
    dot_general x10 -> x8, matrix products: 32.5 us -> 32.2 us  [mm_t(): lax.dot_general(left, right, (((1,), (1,)), ((), ())), preferred_element_...]
  transfers between devices with their start and end apart: 17 -> 23, of which waited for: 2 -> 5; matrix products, arithmetic and copies ran while one was open for 22% -> 24% of each run, Pallas kernels for 59% -> 63%
where the time goes in v4:
time: 611 us; the launch traced here: 603 us
  Pallas kernels  386 us (63%)
  matrix products  103 us (17%)
  local copies, waits for them, and re-layouts  39.9 us (7%)
  starting transfers between devices  25.1 us (4%)
  other arithmetic  24.2 us (4%)
  waiting for transfers between devices  23.8 us (4%)
    pallas_call x8, Pallas kernels, call(): pl.pallas_call(kernel, out_shape=out_shape, in_specs=[VM] * len(inputs),...  372 us
    dot_general x10, matrix products, mm(): return jnp.dot(left, right, preferred_element_type=F32)  35.2 us
    dot_general x12, matrix products, t_mm(): lax.dot_general(left, right, (((0,), (0,)), ((), ())), preferred_element_...  35.2 us
    dot_general x8, matrix products, mm_t(): lax.dot_general(left, right, (((1,), (1,)), ((), ())), preferred_element_...  32.2 us
    ppermute x12, waiting for transfers between devices, shift_ctx(): lax.ppermute(value, 'ctx', [(i, (i + k) % n_ctx) for i in range(n_ctx)])  23.8 us
    pallas_call x3, Pallas kernels, place_pieces(): pl.pallas_call(kernel, grid=(rows // tile,), out_shape=shape((n_ctx, rows...  14.9 us
  transfers between devices with their start and end apart: 23, of which 5 were waited for; matrix products, arithmetic and copies ran while one was open for 24% of the time, Pallas kernels for 63%

profile of v4, /device:TPU:0, one launch (start us, length us, event | category | flops | bytes accessed | tf_op | source)
XLA Modules:
  0.0 603.5 jit_solution(17410279348507728896)
XLA Ops:
  20.5 22.6 %gather_tp.1.refs_0_ = bf16[256,2048]{1,0:T(8,128)(2,1)} custom-call(bf16[256,512]{1,0:T(8,128)(2,1)} %hid.3), custom_call_target="tpu_custom_call" | custom-call | tf_op jit(solution)/shard_map/gather_tp/pallas_call | solution.py:165
  57.8 39.6 %first_norm.1 = (bf16[256,2048]{1,0:T(8,128)(2,1)}, f32[256,128]{1,0:T(8,128)}, bf16[256,2048]{1,0:T(8,128)(2,1)}, bf16[2048,2048]{1,0:T(8,128)(2,1)}) custom-call(bf16[256,2048]{1,0:T(8,128)(2,1)} %gather_tp.1.refs_0_, bf16[256,512]{1,0:T(8,128)(2,1)} %grd.1, f32[8,2048]{1,0:T(8,128)} %copy-done.15, ...), custom_call_target="tpu_custom_call" | custom-call | tf_op jit(solution)/shard_map/first_norm/pallas_call | solution.py:165
  100.5 5.7 fusion.2.prj
  106.3 22.1 %attention_forward.1 = (bf16[256,512]{1,0:T(8,128)(2,1)}, bf16[256,512]{1,0:T(8,128)(2,1)}, bf16[1024,1024]{1,0:T(8,128)(2,1)}) custom-call(f32[256,1536]{1,0:T(8,128)} %fusion.2.prj, f32[256,128]{1,0:T(8,128)} %pad_maximum_fusion.2.cs, f32[256,128]{1,0:T(8,128)} %get-tuple-element.89.sn), custom_call_target="tpu_custom_call" | custom-call | tf_op jit(solution)/shard_map/attention_forward/pallas_call | solution.py:165
  134.9 73.1 %second_norm.1 = (f32[256,512]{1,0:T(8,128)}, f32[256,128]{1,0:T(8,128)}, bf16[256,2048]{1,0:T(8,128)(2,1)}, bf16[640,2048]{1,0:T(8,128)(2,1)}, bf16[640,2048]{1...) custom-call(bf16[256,2048]{1,0:T(8,128)(2,1)} %convolution_convert_fusion.6.prt, ...), custom_call_target="tpu_custom_call" | custom-call | tf_op jit(solution)/shard_map/second_norm/pallas_call | solution.py:165
  208.9 4.6 fusion.41
  215.2 5.0 fusion.39
  224.2 4.4 multiply_convert_fusion.3
  228.6 4.2 convolution_convert_fusion.3
  235.0 5.6 multiply_convert_fusion.2
  240.7 4.7 fusion.81
  249.9 4.4 convolution_convert_fusion.1
  254.3 4.1 convolution_add_fusion.4
  258.4 4.0 fusion.82
  262.4 4.1 select_convert_fusion.1
  270.4 4.1 broadcast_select_fusion
  276.6 5.7 collective-permute-start.7
  285.3 4.6 fusion.35
  290.6 82.3 %second_norm_back.1 = (f32[256,512]{1,0:T(8,128)}, bf16[256,512]{1,0:T(8,128)(2,1)}, f32[8,512]{1,0:T(8,128)}, f32[8,256]{1,0:T(8,128)}) custom-call(bf16[640,2048]{1,0:T(8,128)(2,1)} %pad_maximum_fusion.1.drw, f32[4,8,256]{2,1,0:T(8,128)} %broadcast_in_dim.55.dts, bf16[640,256]{1,0:T(8,128)(2,1)} %get-tuple-element.123.pck, ...), custom_call_target="tpu_custom_call" | custom-call | tf_op jit(solution)/shard_map/second_norm_back/pallas_call | solution.py:165
  387.5 4.2 add_convert_fusion.2
  396.5 4.2 add_convert_fusion.1
  402.6 47.0 %attention_backward.1 = (bf16[256,2048]{1,0:T(8,128)(2,1)}, bf16[256,1536]{1,0:T(8,128)(2,1)}) custom-call(bf16[256,512]{1,0:T(8,128)(2,1)} %get-tuple-element.68.lw, bf16[2048,512]{1,0:T(8,128)(2,1)} %slice.105.wgt, bf16[256,512]{1,0:T(8,128)(2,1)} %get-tuple-element.69.qry, bf16[1024,1024]{1,0:T(8,128)(2,1)} %get-tuple-element.70.full, ...), custom_call_target="tpu_custom_call" | custom-call | tf_op jit(solution)/shard_map/attention_backward/pallas_call | solution.py:165
  453.7 5.6 fusion.4.prt
  459.9 38.3 %first_norm_back.1 = (f32[256,512]{1,0:T(8,128)}, f32[8,512]{1,0:T(8,128)}) custom-call(bf16[256,2048]{1,0:T(8,128)(2,1)} %fusion.4.prt, bf16[256,512]{1,0:T(8,128)(2,1)} %hid.3, f32[256,128]{1,0:T(8,128)} %get-tuple-element.74.scl, f32[8,512]{1,0:T(8,128)} %broadcast_in_dim.57.gn, f32[256,512]{1,0:T(8,128)} %get-tuple-element.75.dr), custom_call_target="tpu_custom_call" | custom-call | tf_op jit(solution)/shard_map/first_norm_back/pallas_call | solution.py:165
  500.2 5.6 convolution_convert_fusion
  505.8 7.4 %pad_maximum_fusion.prt = bf16[2,4,256,2048]{3,2,1,0:T(8,128)(2,1)} fusion(bf16[2,4,256,512]{3,2,1,0:T(8,128)(2,1)S(1)} %bitcast.79, bf16[2,4,256,1536]{3,2,1,0:T(8,128)(2,1)} %bitcast.78), kind=kLoop, calls=%fused_computation | loop fusion | flops 16777216 | bytes 16777216 | tf_op jit(solution)/shard_map/concatenate | solution.py:995
  513.2 46.6 %weight_grads.1 = (f32[256,2048]{1,0:T(8,128)}, f32[8,256]{1,0:T(8,128)}) custom-call(bf16[2,4,256,2048]{3,2,1,0:T(8,128)(2,1)} %pad_maximum_fusion.prt, f32[8,512]{1,0:T(8,128)} %maximum_maximum_fusion.1.sml), custom_call_target="tpu_custom_call" | custom-call | tf_op jit(solution)/shard_map/weight_grads/pallas_call | solution.py:165
  559.7 4.1 add_convert_fusion
  565.9 4.9 place_pieces.5
  572.3 4.9 place_pieces.3
  584.2 13.3 %collective-permute-done.22.refs_3_ = bf16[256,1408]{1,0:T(8,128)(2,1)} collective-permute-done((bf16[256,1408]{1,0:T(8,128)(2,1)S(1)}, bf16[256,1408]{1,0:T(8,128)(2,1)}, u32[]{:S(2)}, u32[]{:S(2)}) %collective-permute-start.22) | collective-permute-done | bytes 720928 | tf_op jit(solution)/shard_map/ppermute | solution.py:795
  597.5 5.0 place_pieces.4
  (172 shorter events, 106.3 us)
Async XLA Ops:
  0.6 9.9 %copy-start.8 = (bf16[1024,512]{1,0:T(8,128)(2,1)S(1)}, bf16[1024,512]{1,0:T(8,128)(2,1)}, u32[]{:S(2)}) copy-start(bf16[1024,512]{1,0:T(8,128)(2,1)} %param.18) | copy-start | bytes 3145732
  3.0 53.3 %collective-permute-start = (bf16[8,1024]{1,0:T(8,128)(2,1)S(1)}, bf16[8,1024]{1,0:T(8,128)(2,1)S(1)}, u32[]{:S(2)}, u32[]{:S(2)}) collective-permute-start(bf16[8,1024]{1,0:T(8,128)(2,1)S(1)} %maximum_maximum_fusion), channel_id=1, source_target_pairs={{0,16},{16,0},{1,17},{17,1},{2,18},{18,2},{3,19},{19,3},{4,20},{20... | collective-permute-start | bytes 49160 | tf_op jit(solution)/shard_map/ppermute | solution.py:798
  14.9 42.9 %collective-permute-start.1 = (bf16[256,2048]{1,0:T(8,128)(2,1)}, bf16[256,2048]{1,0:T(8,128)(2,1)}, u32[]{:S(2)}, u32[]{:S(2)}) collective-permute-start(bf16[256,2048]{1,0:T(8,128)(2,1)} %constant_dynamic-slice_fusion.13), channel_id=1, source_target_pairs={{0,16},{16,0},{1,17},{17,1},{2,18},{18,2},{3,19},{19,3},{4,20},{20... | collective-permute-start | bytes 3145736 | tf_op jit(solution)/shard_map/ppermute | solution.py:798
  18.5 201.6 %collective-permute-start.2 = (bf16[1024,1408]{1,0:T(8,128)(2,1)}, bf16[1024,1408]{1,0:T(8,128)(2,1)}, u32[]{:S(2)}, u32[]{:S(2)}) collective-permute-start(bf16[1024,1408]{1,0:T(8,128)(2,1)} %dynamic-slice_bitcast_fusion.2), channel_id=1, source_target_pairs={{0,16},{16,0},{1,17},{17,1},{2,18},{18,2},{3,19},{19,3},{4,20},{20... | collective-permute-start | bytes 8650760 | tf_op jit(solution)/shard_map/ppermute | solution.py:798
  46.8 9.5 %copy-start.16 = (bf16[1024,4]{0,1:T(4,128)(2,1)S(1)}, bf16[1024,4]{0,1:T(4,128)(2,1)}, u32[]{:S(2)}) copy-start(bf16[1024,4]{0,1:T(4,128)(2,1)} %param.21) | copy-start | bytes 24580
  46.8 177.5 %collective-permute-start.3 = (bf16[1024,1408]{1,0:T(8,128)(2,1)}, bf16[1024,1408]{1,0:T(8,128)(2,1)}, u32[]{:S(2)}, u32[]{:S(2)}) collective-permute-start(bf16[1024,1408]{1,0:T(8,128)(2,1)} %dynamic-slice_bitcast_fusion.1), channel_id=1, source_target_pairs={{0,16},{16,0},{1,17},{17,1},{2,18},{18,2},{3,19},{19,3},{4,20},{20... | collective-permute-start | bytes 8650760 | tf_op jit(solution)/shard_map/ppermute | solution.py:798
  49.3 185.7 %collective-permute-start.4 = (bf16[1024,1408]{1,0:T(8,128)(2,1)S(1)}, bf16[1024,1408]{1,0:T(8,128)(2,1)}, u32[]{:S(2)}, u32[]{:S(2)}) collective-permute-start(bf16[1024,1408]{1,0:T(8,128)(2,1)S(1)} %dynamic-slice_bitcast_fusion), channel_id=1, source_target_pairs={{0,16},{16,0},{1,17},{17,1},{2,18},{18,2},{3,19},{19,3},{4,20},{20... | collective-permute-start | bytes 8650760 | tf_op jit(solution)/shard_map/ppermute | solution.py:798
  215.2 13.4 %copy-start.1 = (bf16[640,2048]{1,0:T(8,128)(2,1)}, bf16[640,2048]{1,0:T(8,128)(2,1)S(1)}, u32[]{:S(2)}) copy-start(bf16[640,2048]{1,0:T(8,128)(2,1)S(1)} %multiply_convert_fusion) | copy-start | bytes 7864324
  228.6 41.8 %copy-start.23 = (bf16[640,1408]{1,0:T(8,128)(2,1)}, bf16[640,1408]{1,0:T(8,128)(2,1)S(1)}, u32[]{:S(2)}) copy-start(bf16[640,1408]{1,0:T(8,128)(2,1)S(1)} %get-tuple-element.63) | copy-start | bytes 5406724
  240.7 21.7 %copy-start.25 = (bf16[640,1408]{1,0:T(8,128)(2,1)}, bf16[640,1408]{1,0:T(8,128)(2,1)S(1)}, u32[]{:S(2)}) copy-start(bf16[640,1408]{1,0:T(8,128)(2,1)S(1)} %get-tuple-element.90) | copy-start | bytes 5406724
  249.4 138.1 %collective-permute-start.11 = (bf16[1024,1408]{1,0:T(8,128)(2,1)}, bf16[1024,1408]{1,0:T(8,128)(2,1)}, u32[]{:S(2)}, u32[]{:S(2)}) collective-permute-start(bf16[1024,1408]{1,0:T(8,128)(2,1)} %convolution_convert_fusion.3), channel_id=1, source_target_pairs={{0,16},{16,0},{1,17},{17,1},{2,18},{18,2},{3,19},{19,3},{4,20},{20... | collective-permute-start | bytes 8650760 | tf_op jit(solution)/shard_map/ppermute | solution.py:798
  274.5 9.3 %copy-start.20 = (f32[8,256]{1,0:T(8,128)S(1)}, f32[8,256]{1,0:T(8,128)}, u32[]{:S(2)}) copy-start(f32[8,256]{1,0:T(8,128)} %get-tuple-element.55) | copy-start | bytes 24580
  276.6 97.0 %collective-permute-start.7 = (bf16[640,512]{1,0:T(8,128)(2,1)}, bf16[640,512]{1,0:T(8,128)(2,1)}, u32[]{:S(2)}, u32[]{:S(2)}) collective-permute-start(bf16[640,512]{1,0:T(8,128)(2,1)} %get-tuple-element.94), channel_id=1, source_target_pairs={{0,3},{1,0},{2,1},{3,2},{4,7},{5,4},{6,5},{7,6},{8,11},{9,8},{10,9... | collective-permute-start | bytes 1966088 | tf_op jit(solution)/shard_map/ppermute | solution.py:985
  282.4 92.8 %collective-permute-start.6 = (bf16[640,512]{1,0:T(8,128)(2,1)}, bf16[640,512]{1,0:T(8,128)(2,1)}, u32[]{:S(2)}, u32[]{:S(2)}) collective-permute-start(bf16[640,512]{1,0:T(8,128)(2,1)} %get-tuple-element.93), channel_id=1, source_target_pairs={{0,2},{1,3},{2,0},{3,1},{4,6},{5,7},{6,4},{7,5},{8,10},{9,11},{10,... | collective-permute-start | bytes 1966088 | tf_op jit(solution)/shard_map/ppermute | solution.py:985
  283.8 91.4 %collective-permute-start.5 = (bf16[640,512]{1,0:T(8,128)(2,1)}, bf16[640,512]{1,0:T(8,128)(2,1)}, u32[]{:S(2)}, u32[]{:S(2)}) collective-permute-start(bf16[640,512]{1,0:T(8,128)(2,1)} %get-tuple-element.92), channel_id=1, source_target_pairs={{0,1},{1,2},{2,3},{3,0},{4,5},{5,6},{6,7},{7,4},{8,9},{9,10},{10,1... | collective-permute-start | bytes 1966088 | tf_op jit(solution)/shard_map/ppermute | solution.py:985
  283.8 112.7 %collective-permute-start.12 = (bf16[1024,1408]{1,0:T(8,128)(2,1)}, bf16[1024,1408]{1,0:T(8,128)(2,1)}, u32[]{:S(2)}, u32[]{:S(2)}) collective-permute-start(bf16[1024,1408]{1,0:T(8,128)(2,1)} %convolution_convert_fusion.2), channel_id=1, source_target_pairs={{0,16},{16,0},{1,17},{17,1},{2,18},{18,2},{3,19},{19,3},{4,20},{20... | collective-permute-start | bytes 8650760 | tf_op jit(solution)/shard_map/ppermute | solution.py:798
  373.6 186.1 %collective-permute-start.16 = (bf16[1024,1408]{1,0:T(8,128)(2,1)}, bf16[1024,1408]{1,0:T(8,128)(2,1)}, u32[]{:S(2)}, u32[]{:S(2)}) collective-permute-start(bf16[1024,1408]{1,0:T(8,128)(2,1)} %convolution_convert_fusion.1), channel_id=1, source_target_pairs={{0,16},{16,0},{1,17},{17,1},{2,18},{18,2},{3,19},{19,3},{4,20},{20... | collective-permute-start | bytes 8650760 | tf_op jit(solution)/shard_map/ppermute | solution.py:798
  377.5 10.0 %copy-start.2 = (bf16[640,2048]{1,0:T(8,128)(2,1)S(1)}, bf16[640,2048]{1,0:T(8,128)(2,1)}, u32[]{:S(2)}) copy-start(bf16[640,2048]{1,0:T(8,128)(2,1)} %copy-done.1) | copy-start | bytes 7864324
  377.5 10.0 %copy-start.24 = (bf16[640,1408]{1,0:T(8,128)(2,1)S(1)}, bf16[640,1408]{1,0:T(8,128)(2,1)}, u32[]{:S(2)}) copy-start(bf16[640,1408]{1,0:T(8,128)(2,1)} %copy-done.23) | copy-start | bytes 5406724
  377.6 4.8 collective-permute-start.10
  378.9 7.0 %collective-permute-start.9 = (bf16[160,512]{1,0:T(8,128)(2,1)S(1)}, bf16[160,512]{1,0:T(8,128)(2,1)S(1)}, u32[]{:S(2)}, u32[]{:S(2)}) collective-permute-start(bf16[160,512]{1,0:T(8,128)(2,1)S(1)} %get-tuple-element.118), channel_id=1, source_target_pairs={{0,8},{4,12},{8,0},{12,4},{1,9},{5,13},{9,1},{13,5},{2,10},{6,14},... | collective-permute-start | bytes 491528 | tf_op jit(solution)/shard_map/ppermute | solution.py:795
  382.4 3.8 collective-permute-start.8
  393.4 58.3 %collective-permute-start.13 = (bf16[256,1408]{1,0:T(8,128)(2,1)}, bf16[256,1408]{1,0:T(8,128)(2,1)S(1)}, u32[]{:S(2)}, u32[]{:S(2)}) collective-permute-start(bf16[256,1408]{1,0:T(8,128)(2,1)} %get-tuple-element.108), channel_id=1, source_target_pairs={{0,4},{4,8},{8,12},{12,0},{1,5},{5,9},{9,13},{13,1},{2,6},{6,10},{... | collective-permute-start | bytes 2162696 | tf_op jit(solution)/shard_map/ppermute | solution.py:795
  395.1 57.7 %collective-permute-start.14 = (bf16[256,1408]{1,0:T(8,128)(2,1)}, bf16[256,1408]{1,0:T(8,128)(2,1)S(1)}, u32[]{:S(2)}, u32[]{:S(2)}) collective-permute-start(bf16[256,1408]{1,0:T(8,128)(2,1)} %get-tuple-element.107), channel_id=1, source_target_pairs={{0,8},{4,12},{8,0},{12,4},{1,9},{5,13},{9,1},{13,5},{2,10},{6,14},... | collective-permute-start | bytes 2162696 | tf_op jit(solution)/shard_map/ppermute | solution.py:795
  395.7 57.2 %collective-permute-start.15 = (bf16[256,1408]{1,0:T(8,128)(2,1)}, bf16[256,1408]{1,0:T(8,128)(2,1)}, u32[]{:S(2)}, u32[]{:S(2)}) collective-permute-start(bf16[256,1408]{1,0:T(8,128)(2,1)} %get-tuple-element.106), channel_id=1, source_target_pairs={{0,12},{4,0},{8,4},{12,8},{1,13},{5,1},{9,5},{13,9},{2,14},{6,2},{... | collective-permute-start | bytes 2162696 | tf_op jit(solution)/shard_map/ppermute | solution.py:795
  402.3 168.5 %collective-permute-start.17 = (bf16[256,1408]{1,0:T(8,128)(2,1)}, bf16[256,1408]{1,0:T(8,128)(2,1)}, u32[]{:S(2)}, u32[]{:S(2)}) collective-permute-start(bf16[256,1408]{1,0:T(8,128)(2,1)} %get-tuple-element.104), channel_id=1, source_target_pairs={{0,4},{4,8},{8,12},{12,0},{1,5},{5,9},{9,13},{13,1},{2,6},{6,10},{... | collective-permute-start | bytes 2162696 | tf_op jit(solution)/shard_map/ppermute | solution.py:795
  451.7 120.6 %collective-permute-start.18 = (bf16[256,1408]{1,0:T(8,128)(2,1)}, bf16[256,1408]{1,0:T(8,128)(2,1)}, u32[]{:S(2)}, u32[]{:S(2)}) collective-permute-start(bf16[256,1408]{1,0:T(8,128)(2,1)} %get-tuple-element.103), channel_id=1, source_target_pairs={{0,8},{4,12},{8,0},{12,4},{1,9},{5,13},{9,1},{13,5},{2,10},{6,14},... | collective-permute-start | bytes 2162696 | tf_op jit(solution)/shard_map/ppermute | solution.py:795
  452.8 119.5 %collective-permute-start.19 = (bf16[256,1408]{1,0:T(8,128)(2,1)}, bf16[256,1408]{1,0:T(8,128)(2,1)}, u32[]{:S(2)}, u32[]{:S(2)}) collective-permute-start(bf16[256,1408]{1,0:T(8,128)(2,1)} %get-tuple-element.102), channel_id=1, source_target_pairs={{0,12},{4,0},{8,4},{12,8},{1,13},{5,1},{9,5},{13,9},{2,14},{6,2},{... | collective-permute-start | bytes 2162696 | tf_op jit(solution)/shard_map/ppermute | solution.py:795
  459.2 40.9 %copy-start.7 = (bf16[256,2048]{1,0:T(8,128)(2,1)S(1)}, bf16[256,2048]{1,0:T(8,128)(2,1)}, u32[]{:S(2)}) copy-start(bf16[256,2048]{1,0:T(8,128)(2,1)} %get-tuple-element.50) | copy-start | bytes 3145732
  565.2 18.4 %collective-permute-start.20 = (bf16[256,1408]{1,0:T(8,128)(2,1)}, bf16[256,1408]{1,0:T(8,128)(2,1)}, u32[]{:S(2)}, u32[]{:S(2)}) collective-permute-start(bf16[256,1408]{1,0:T(8,128)(2,1)} %get-tuple-element.100), channel_id=1, source_target_pairs={{0,4},{4,8},{8,12},{12,0},{1,5},{5,9},{9,13},{13,1},{2,6},{6,10},{... | collective-permute-start | bytes 2162696 | tf_op jit(solution)/shard_map/ppermute | solution.py:795
  565.2 19.1 %collective-permute-start.21 = (bf16[256,1408]{1,0:T(8,128)(2,1)S(1)}, bf16[256,1408]{1,0:T(8,128)(2,1)}, u32[]{:S(2)}, u32[]{:S(2)}) collective-permute-start(bf16[256,1408]{1,0:T(8,128)(2,1)S(1)} %get-tuple-element.99), channel_id=1, source_target_pairs={{0,8},{4,12},{8,0},{12,4},{1,9},{5,13},{9,1},{13,5},{2,10},{6,14},... | collective-permute-start | bytes 2162696 | tf_op jit(solution)/shard_map/ppermute | solution.py:795
  570.9 26.6 %collective-permute-start.22 = (bf16[256,1408]{1,0:T(8,128)(2,1)S(1)}, bf16[256,1408]{1,0:T(8,128)(2,1)}, u32[]{:S(2)}, u32[]{:S(2)}) collective-permute-start(bf16[256,1408]{1,0:T(8,128)(2,1)S(1)} %get-tuple-element.98), channel_id=1, source_target_pairs={{0,12},{4,0},{8,4},{12,8},{1,13},{5,1},{9,5},{13,9},{2,14},{6,2},{... | collective-permute-start | bytes 2162696 | tf_op jit(solution)/shard_map/ppermute | solution.py:795
  (18 other events, 73.9 us)

commit v5 on v4

--- a/solution.py
+++ b/solution.py
@@ -58,8 +58,8 @@
     pl.semaphore_wait(barrier, sum(n - 1 for _, n in groups))
 
 
-def remote(source, target, sems, i, to):
-    copy = pltpu.make_async_remote_copy(
+def described(source, target, sems, i, to):
+    return pltpu.make_async_remote_copy(
         src_ref=source,
         dst_ref=target,
         send_sem=sems[0].at[i],
@@ -67,6 +67,10 @@
         device_id=to,
         device_id_type=MESH,
     )
+
+
+def remote(source, target, sems, i, to):
+    copy = described(source, target, sems, i, to)
     copy.start()
     return copy
 
@@ -104,6 +108,14 @@
         copy.wait()
 
 
+def spread(mine, out, n_ctx, sems, order=(2, 1, 3)):
+    cut = mine.shape[0] // n_ctx
+    return [
+        send(mine.at[stretch(peer("ctx", n_ctx, k), cut), :], out.at[k - 1], "ctx", n_ctx, k, sems)
+        for k in order
+    ]
+
+
 def quad():
     here = lax.axis_index("ctx")
     return here, here + 1 - 2 * lax.rem(here, 2), lax.rem(here + 2, 4)
@@ -111,19 +123,28 @@
 
 def gather_square(own, full, first_row, sems, between):
     rows = own.shape[0]
+    cuts = own.shape[1] // 512
     here, beside, across = quad()
 
-    def place(rank):
-        return full.at[pl.ds(pl.multiple_of(first_row + rank * rows, 16), rows), :]
-
-    first = remote(own, place(here), sems, 0, {"ctx": across})
-    second = remote(own, place(here), sems, 1, {"ctx": beside})
+    def place(rank, i):
+        return full.at[
+            pl.ds(pl.multiple_of(first_row + rank * rows, 16), rows), pl.ds(i * 512, 512)
+        ]
+
+    first, second, third = [], [], []
+    for i in range(cuts):
+        piece = own.at[:, pl.ds(i * 512, 512)]
+        first.append(remote(piece, place(here, i), sems, 3 * i, {"ctx": across}))
+        second.append(remote(piece, place(here, i), sems, 3 * i + 1, {"ctx": beside}))
     full[pl.ds(pl.multiple_of(first_row + here * rows, 16), rows), :] = own[...]
     between()
-    first.wait()
-    third = remote(place(across), place(across), sems, 2, {"ctx": beside})
-    second.wait()
-    third.wait()
+    for i in range(cuts):
+        first[i].wait()
+        third.append(
+            remote(place(across, i), place(across, i), sems, 3 * i + 2, {"ctx": beside})
+        )
+    finish(second)
+    finish(third)
 
 
 def row_sums(values):
@@ -161,12 +182,15 @@
     return total
 
 
-def call(kernel, out_shape, inputs, scratch, collective, name):
+def call(kernel, out_shape, inputs, scratch, collective, name, left=()):
+    anywhere = pl.BlockSpec(memory_space=pl.ANY)
+    outs = out_shape if isinstance(out_shape, tuple) else (out_shape,)
+    specs = [anywhere if i - len(outs) in left else VM for i in range(len(outs))]
     return pl.pallas_call(
         kernel,
         out_shape=out_shape,
-        in_specs=[VM] * len(inputs),
-        out_specs=jax.tree.map(lambda _: VM, out_shape),
+        in_specs=[anywhere if i in left else VM for i in range(len(inputs))],
+        out_specs=tuple(specs) if isinstance(out_shape, tuple) else specs[0],
         scratch_shapes=scratch,
         compiler_params=pltpu.CompilerParams(collective_id=collective, has_side_effects=True),
         cost_estimate=pl.CostEstimate(flops=0, bytes_accessed=0, transcendentals=0),
@@ -178,6 +202,10 @@
     return jax.ShapeDtypeStruct(dims, dtype)
 
 
+def came_shape(payload, n_ctx):
+    return shape((n_ctx - 1, payload.shape[0] // n_ctx, payload.shape[1]), payload.dtype)
+
+
 def pair_of_sems(n):
     return [DMA((n,)), DMA((n,))]
 
@@ -202,8 +230,9 @@
         hid, grd, gn = refs[:3]
         refs = refs[3:]
         if with_quarter:
-            wgt, qrt, out, scale, grd_full, wgt_full = refs[:6]
-            sems = refs[6:]
+            wgts, refs = refs[: len(weights)], refs[len(weights) :]
+            qrt, out, scale, grd_full, wgt_full = refs[:5]
+            sems = refs[5:]
             greet([("tp", n_tp), ("ctx", n_ctx)])
         else:
             out, scale, grd_full = refs[:3]
@@ -219,12 +248,15 @@
             out[...] = (values * factor * gn[0:1, :]).astype(BF)
 
         if with_quarter:
-            half = wgt.shape[0]
+            half, inner = wgts[0].shape
             mine = lax.axis_index("fsdp")
 
             def work():
                 norm()
-                wgt_full[pl.ds(pl.multiple_of(mine * half, 16), half), :] = wgt[...]
+                for i, wgt in enumerate(wgts):
+                    wgt_full[
+                        pl.ds(pl.multiple_of(mine * half, 16), half), pl.ds(i * inner, inner)
+                    ] = wgt[...]
 
             gather_square(qrt, wgt_full, (1 - mine) * half, sems[2:4], work)
         else:
@@ -234,10 +266,10 @@
     outs = [shape((rows, width), BF), shape((rows, 128), F32), shape((rows, width), BF)]
     inputs = [full, grad, gain]
     if with_quarter:
-        outs.append(shape((2 * weights.shape[0], weights.shape[1]), BF))
-        inputs += [weights, quarter]
+        outs.append(shape((2 * weights[0].shape[0], quarter.shape[1]), BF))
+        inputs += [*weights, quarter]
     return call(
-        kernel, tuple(outs), inputs, pair_of_sems(n_tp) + pair_of_sems(3), 7, "first_norm"
+        kernel, tuple(outs), inputs, pair_of_sems(n_tp) + pair_of_sems(12), 7, "first_norm"
     )
 
 
@@ -293,7 +325,7 @@
             shape((rows * n_ctx, 2 * width), BF),
         ),
         (qkv, cosine, sine),
-        [pltpu.VMEM((rows, 2 * width), BF)] + pair_of_sems(3),
+        [pltpu.VMEM((rows, 2 * width), BF)] + pair_of_sems(6 * width // 512),
         2,
         "attention_forward",
     )
@@ -404,34 +436,111 @@
 
 
 def second_norm_back(
-    d_rows, dots, picks, gates, onehot, names, router, resid, scale, gain, grad, n_tp, n_ctx
+    acts, weights, dots, picks, gates, onehot, names, router, resid, scale, gain, grad, n_tp, n_ctx
 ):
     rows, size = resid.shape
     width = size * n_tp
     experts = n_ctx
-
-    def kernel(
-        drw, dts, pck, gts, one, nms, rtr, rsd, scl, gn, grd,
-        d_resid, low, d_gain, d_logits,
-        back, back_dots, part, slots, mine, sums, mine_two, sums_two, *sems
-    ):
+    hidden = acts[0].shape[1]
+    count = len(weights[0])
+    part = weights[0][0].shape[0]
+
+    def kernel(*refs):
+        dga, dup, hid = refs[:3]
+        wgt = [refs[3 + i * count : 3 + (i + 1) * count] for i in range(3)]
+        refs = refs[3 + 3 * count :]
+        dts, pck, gts, one, nms, rtr, rsd, scl, gn, grd = refs[:10]
+        d_resid, low, d_gain, d_logits, out_back = refs[10:15]
+        (
+            drw, eo, buffer, back, back_dots, parts, slots, mine, sums, mine_two, sums_two, loads,
+        ) = refs[15:27]
+        sems = refs[27:]
+        here = lax.axis_index("tp")
+        first = lax.axis_index("fsdp")
+
+        def load(which, rank, slot, lane):
+            feature = rank * size
+            inside = pl.ds(pl.multiple_of(lax.rem(feature, part), 16), size)
+            target = buffer.at[slot, lane]
+            if count == 1:
+                pltpu.make_async_copy(
+                    wgt[which][0].at[inside], target, loads.at[slot, lane]
+                ).start()
+                return
+            own = feature // part == first
+
+            @pl.when(own)
+            def _():
+                pltpu.make_async_copy(
+                    wgt[which][0].at[inside], target, loads.at[slot, lane]
+                ).start()
+
+            @pl.when(jnp.logical_not(own))
+            def _():
+                pltpu.make_async_copy(
+                    wgt[which][1].at[inside], target, loads.at[slot, lane]
+                ).start()
+
+        def loaded(which, slot, lane):
+            pltpu.make_async_copy(
+                wgt[which][0].at[pl.ds(0, size)], buffer.at[slot, lane], loads.at[slot, lane]
+            ).wait()
+
+        load(0, peer("tp", n_tp, 1), 0, 0)
+        load(1, peer("tp", n_tp, 1), 0, 1)
         greet([("tp", n_tp), ("ctx", n_ctx)])
-        here = lax.axis_index("tp")
         small = []
-        large = []
         for k in range(1, n_ctx):
             small.append(
                 send(dts.at[k], back_dots.at[k - 1], "ctx", n_ctx, n_ctx - k, sems[0:2])
             )
-        for step in range(1, n_tp + 1):
-            at = columns(peer("tp", n_tp, step), size)
+
+        def slab(k, rank, step):
+            at = columns(rank, size)
+            return described(
+                drw.at[pl.ds(k * CAP, CAP), at], back.at[k - 1, :, at],
+                sems[2:4], step * n_ctx + k - 1, {"ctx": peer("ctx", n_ctx, n_ctx - k)},
+            )
+
+        @pl.loop(0, n_tp)
+        def _(step):
+            rank = peer("tp", n_tp, step + 1)
+            slot = lax.rem(step, 2)
+            loaded(0, slot, 0)
+            loaded(1, slot, 1)
+
+            @pl.when(step + 1 < n_tp)
+            def _():
+                load(0, peer("tp", n_tp, step + 2), 1 - slot, 0)
+                load(1, peer("tp", n_tp, step + 2), 1 - slot, 1)
+
+            drw[:, columns(rank, size)] = (
+                mm_t(dga[...], buffer[slot, 0]) + mm_t(dup[...], buffer[slot, 1])
+            ).astype(BF)
             for k in (2, 3, 1):
-                large.append(
-                    remote(
-                        drw.at[pl.ds(k * CAP, CAP), at], back.at[k - 1, :, at],
-                        sems[2:4], step * n_ctx - k, {"ctx": peer("ctx", n_ctx, n_ctx - k)},
-                    )
-                )
+                slab(k, rank, step).start()
+
+        load(2, 0, 0, 0)
+
+        @pl.loop(0, n_tp)
+        def _(rank):
+            slot = lax.rem(rank, 2)
+            loaded(2, slot, 0)
+
+            @pl.when(rank + 1 < n_tp)
+            def _():
+                load(2, rank + 1, 1 - slot, 0)
+
+            eo[:, columns(rank, size)] = mm_t(hid[...], buffer[slot, 0]).astype(BF)
+
+        moved = [
+            send(
+                eo.at[pl.ds(k * CAP, CAP)], out_back.at[pl.ds(k * CAP, CAP)],
+                "ctx", n_ctx, n_ctx - k, sems[10:12],
+            )
+            for k in range(1, n_ctx)
+        ]
+        out_back[0:CAP] = eo[0:CAP]
         finish(small)
         order = lax.broadcasted_iota(jnp.int32, (8, rows), 0)
         own = jnp.zeros((8, rows), F32)
@@ -453,15 +562,17 @@
         d_logits[...] = logits
         copies = []
         for step in range(1, n_tp + 1):
-            at = columns(peer("tp", n_tp, step), size)
-            finish(large[3 * step - 3 : 3 * step])
+            rank = peer("tp", n_tp, step)
+            at = columns(rank, size)
+            for k in (2, 3, 1):
+                slab(k, rank, step - 1).wait()
             block = t_mm(pck[0:CAP], drw[0:CAP, at])
             for k in range(1, experts):
                 block = block + t_mm(pck[k * CAP : (k + 1) * CAP], back[k - 1, :, at])
             if step < n_tp:
-                part[step - 1] = block.astype(BF)
+                parts[step - 1] = block.astype(BF)
                 copies.append(
-                    send(part.at[step - 1], slots.at[step - 1], "tp", n_tp, step, sems[6:8])
+                    send(parts.at[step - 1], slots.at[step - 1], "tp", n_tp, step, sems[6:8])
                 )
             else:
                 total = block
@@ -484,7 +595,9 @@
         result = grd[...].astype(F32) + factor * (d_resid[...] - rsd[...] * factor * dot)
         d_resid[...] = result
         low[...] = result.astype(BF)
-
+        finish(moved)
+
+    flat = [array for group in weights for array in group]
     return call(
         kernel,
         (
@@ -492,9 +605,13 @@
             shape((rows, size), BF),
             shape((8, size), F32),
             shape((8, rows), F32),
+            shape((experts * CAP, width), BF),
         ),
-        (d_rows, dots, picks, gates, onehot, names, router, resid, scale, gain, grad),
+        (*acts, *flat, dots, picks, gates, onehot, names, router, resid, scale, gain, grad),
         [
+            pltpu.VMEM((experts * CAP, width), BF),
+            pltpu.VMEM((experts * CAP, width), BF),
+            pltpu.VMEM((2, 2, size, hidden), BF),
             pltpu.VMEM((n_ctx - 1, CAP, width), BF),
             pltpu.VMEM((n_ctx - 1, 8, rows), F32),
             pltpu.VMEM((n_tp - 1, rows, size), BF),
@@ -503,16 +620,19 @@
             pltpu.VMEM((n_tp - 1, 8, rows), F32),
             pltpu.VMEM((8, rows), F32),
             pltpu.VMEM((n_tp - 1, 8, rows), F32),
+            DMA((2, 2)),
         ]
         + pair_of_sems(n_ctx)
         + pair_of_sems(n_tp * n_ctx)
-        + pair_of_sems(n_tp) * 3,
+        + pair_of_sems(n_tp) * 3
+        + pair_of_sems(n_ctx),
         4,
         "second_norm_back",
-    )
-
-
-def attention_backward(low, output_w, query, kv, cosine, sine, n_tp, n_ctx):
+        left=tuple(range(3, 3 + 3 * count)),
+    )
+
+
+def attention_backward(low, output_w, query, kv, cosine, sine, payload, n_tp, n_ctx):
     rows, size = low.shape
     width = size * n_tp
     inner = query.shape[1]
@@ -520,12 +640,13 @@
     scale = 1.0 / math.sqrt(HD)
 
     def kernel(
-        lw, wgt, qry, full, cs, sn, d_attn, d_qkv, dot, dqs, dkv, slots, last, both, total, *sems
+        lw, wgt, qry, full, cs, sn, pay, d_attn, d_qkv, came, dot, dqs, dkv, slots, last, both, total, *sems
     ):
         greet([("tp", n_tp), ("ctx", n_ctx)])
         here, beside, across = quad()
         beyond = lax.rem(beside + 2, 4)
         copies = gather_columns(lw, d_attn, "tp", n_tp, sems[2:4])
+        moved = spread(pay, came, n_ctx, sems[4:6])
         for step in range(n_tp):
             rank = peer("tp", n_tp, n_tp - step)
             weights = wgt[pl.ds(pl.multiple_of(rank * size, 16), size), :]
@@ -573,10 +694,12 @@
             d_value = d_value + last[:, at_v].astype(F32)
             d_qkv[:, columns(h + 2 * heads, HD)] = d_value.astype(BF)
 
+        finish(moved)
+
     return call(
         kernel,
-        (shape((rows, width), BF), shape((rows, 3 * inner), BF)),
-        (low, output_w, query, kv, cosine, sine),
+        (shape((rows, width), BF), shape((rows, 3 * inner), BF), came_shape(payload, n_ctx)),
+        (low, output_w, query, kv, cosine, sine, payload),
         [
             pltpu.VMEM((rows, inner), BF),
             pltpu.VMEM((rows, inner), F32),
@@ -587,20 +710,23 @@
             pltpu.VMEM((rows, inner), F32),
         ]
         + pair_of_sems(3)
-        + pair_of_sems(n_tp),
+        + pair_of_sems(n_tp)
+        + pair_of_sems(n_ctx),
         5,
         "attention_backward",
-    )
-
-
-def first_norm_back(part, hidden, scale, gain, d_resid, n_tp):
+        left=(6, -1),
+    )
+
+
+def first_norm_back(part, hidden, scale, gain, d_resid, payload, n_tp, n_ctx):
     rows, size = hidden.shape
     width = size * n_tp
 
-    def kernel(prt, hid, scl, gn, dr, out, d_gain, slots, mine, sums, *sems):
-        greet([("tp", n_tp)])
+    def kernel(prt, hid, scl, gn, dr, pay, out, d_gain, came, slots, mine, sums, *sems):
+        greet([("tp", n_tp), ("ctx", n_ctx)])
         here = lax.axis_index("tp")
         copies = scatter_columns(prt, slots, "tp", n_tp, sems[0:2])
+        moved = spread(pay, came, n_ctx, sems[4:6])
         total = prt[:, columns(here, size)].astype(F32)
         finish(copies)
         for k in range(1, n_tp):
@@ -614,32 +740,40 @@
         dot = as_column(dot, eighth())[:, 0:1] * (1.0 / width)
         unit = hid[...].astype(F32) * factor
         out[...] = dr[...] + factor * (out[...] - unit * dot)
+        finish(moved)
 
     return call(
         kernel,
-        (shape((rows, size), F32), shape((8, size), F32)),
-        (part, hidden, scale, gain, d_resid),
+        (shape((rows, size), F32), shape((8, size), F32), came_shape(payload, n_ctx)),
+        (part, hidden, scale, gain, d_resid, payload),
         [
             pltpu.VMEM((n_tp - 1, rows, size), BF),
             pltpu.VMEM((8, rows), F32),
             pltpu.VMEM((n_tp - 1, 8, rows), F32),
         ]
-        + pair_of_sems(n_tp) * 2,
+        + pair_of_sems(n_tp) * 2
+        + pair_of_sems(n_ctx),
         6,
         "first_norm_back",
-    )
-
-
-def weight_grads(part, small, n_tp, n_ctx):
-    rows, size = part.shape[2:]
-    half = size // 2
+        left=(5, -1),
+    )
+
+
+def weight_grads(parts, groups, small, payload, back, picks, mix, resid, n_tp, n_ctx):
+    tokens, block_size = resid.shape
+    experts = n_ctx
+    rows = parts[0].shape[2]
     width = small.shape[1] * n_tp
     places = 2 * n_ctx
     cut = width // places
-
-    def kernel(
-        prt, sml, out, small_out, near, two, far, one, last, sml_full, sml_slots, *sems
-    ):
+    total_columns = sum(size for _, _, size, _ in groups)
+
+    def kernel(*refs):
+        prts, refs = refs[: len(parts)], refs[len(parts) :]
+        sml, pay, bck, pck, mx, rsd, out, small_out, block_out, came = refs[:10]
+        sml_full, sml_slots, mixed, shares, share_slots = refs[10:15]
+        refs = refs[15:]
+        scratch, sems = refs[: 5 * len(groups)], refs[5 * len(groups) :]
         barrier = pltpu.get_barrier_semaphore()
         here, beside, across = quad()
         beyond = lax.rem(beside + 2, 4)
@@ -654,108 +788,202 @@
         for device in ahead + [device for _, device in others]:
             pl.semaphore_signal(barrier, inc=1, device_id=device, device_id_type=MESH)
         pl.semaphore_wait(barrier, n_tp - 1 + places - 1)
-        gathers = gather_columns(sml, sml_full, "tp", n_tp, sems[6:8])
-        left, right = pl.ds(0, half), pl.ds(half, half)
-        blocks = [
-            (other, beyond, left), (mine, beyond, left), (other, beyond, right),
-            (other, beside, right), (other, beside, left), (mine, beside, left),
-            (mine, beyond, right), (mine, beside, right),
-        ]
-        steps = []
-        for i, (rank, column, at) in enumerate(blocks):
-            steps.append(
-                remote(prt.at[rank, column, :, at], near.at[i], sems[0:2], i, {"ctx": beside})
+        gathers = gather_columns(sml, sml_full, "tp", n_tp, sems[0:2])
+        moved = spread(pay, came, n_ctx, sems[4:6], (2,))
+        moves = []
+        for g, (which, first, size, ctx_first) in enumerate(groups):
+            near = scratch[5 * g]
+            at = pl.ds(first, size)
+            far_here = (mine, beyond) if ctx_first else (other, beside)
+            blocks = [(other, beyond), far_here]
+            blocks += [(other, beside) if ctx_first else (mine, beyond), (mine, beside)]
+            moves.append(
+                [
+                    remote(
+                        prts[which].at[rank, column, :, at], near.at[i],
+                        sems[8 + 6 * g : 10 + 6 * g], i, {"ctx": beside},
+                    )
+                    for i, (rank, column) in enumerate(blocks)
+                ]
             )
         finish(gathers)
         totals = [
-            remote(
-                sml_full.at[:, columns(to, cut)], sml_slots.at[i], sems[8:10], i, device
-            )
+            remote(sml_full.at[:, columns(to, cut)], sml_slots.at[i], sems[2:4], i, device)
             for i, (to, device) in enumerate(others)
         ]
 
-        def chip(i, rank, column, at):
-            steps[i].wait()
-            return prt[rank, column, :, at].astype(F32) + near[i].astype(F32)
-
-        first_hop = []
-        for slot, (i, rank, column, at, to) in enumerate(
-            [
-                (0, other, across, left, {"ctx": across}),
-                (1, mine, across, left, {"ctx": across}),
-                (2, other, across, right, {"fsdp": other}),
-                (3, other, here, right, {"fsdp": other}),
-            ]
-        ):
-            two[slot] = chip(i, rank, column, at).astype(BF)
-            first_hop.append(remote(two.at[slot], far.at[slot], sems[2:4], slot, to))
-        value = chip(4, other, here, left)
-        first_hop[0].wait()
-        one[0] = (value + far[0].astype(F32)).astype(BF)
-        second_hop = [remote(one.at[0], last.at[0], sems[4:6], 0, {"fsdp": other})]
-        value = chip(6, mine, across, right)
-        first_hop[2].wait()
-        one[1] = (value + far[2].astype(F32)).astype(BF)
-        second_hop.append(remote(one.at[1], last.at[1], sems[4:6], 1, {"ctx": across}))
-        value = chip(5, mine, here, left)
-        first_hop[1].wait()
-        out[:, left] = value + far[1].astype(F32)
-        value = chip(7, mine, here, right)
-        first_hop[3].wait()
-        out[:, right] = value + far[3].astype(F32)
+        def chip(g, i, rank, column):
+            which, first, size, _ = groups[g]
+            moves[g][i].wait()
+            value = prts[which][rank, column, :, first : first + size].astype(F32)
+            return value + scratch[5 * g][i].astype(F32)
+
+        hops = []
+        for g, (_, _, _, ctx_first) in enumerate(groups):
+            two, far = scratch[5 * g + 1 : 5 * g + 3]
+            to = {"ctx": across} if ctx_first else {"fsdp": other}
+            pair = [(other, across), (mine, across) if ctx_first else (other, here)]
+            sent = []
+            for i, (rank, column) in enumerate(pair):
+                two[i] = chip(g, i, rank, column).astype(BF)
+                sent.append(
+                    remote(two.at[i], far.at[i], sems[10 + 6 * g : 12 + 6 * g], i, to)
+                )
+            hops.append(sent)
+        moved += spread(pay, came, n_ctx, sems[4:6], (1, 3))
+        order = lax.broadcasted_iota(jnp.int32, (8, 128), 0)
+        for k in range(experts):
+            mixed[k] = as_column(mx[...], jnp.where(order == k, 1.0, 0.0))
+        given = []
+        for step in range(1, n_tp + 1):
+            at = columns(peer("tp", n_tp, step), block_size)
+            block = jnp.zeros((tokens, block_size), F32)
+            for k in range(experts):
+                block = block + mixed[k][:, 0:1] * t_mm(
+                    pck[k * CAP : (k + 1) * CAP], bck[k * CAP : (k + 1) * CAP, at]
+                )
+            if step < n_tp:
+                shares[step - 1] = block.astype(BF)
+                given.append(
+                    send(shares.at[step - 1], share_slots.at[step - 1], "tp", n_tp, step, sems[6:8])
+                )
+            else:
+                moe = rsd[...] + block
+        lasts = []
+        for g, (_, _, _, ctx_first) in enumerate(groups):
+            far, one, last = scratch[5 * g + 2], scratch[5 * g + 3], scratch[5 * g + 4]
+            value = chip(g, 2, *((other, here) if ctx_first else (mine, across)))
+            hops[g][0].wait()
+            one[...] = (value + far[0].astype(F32)).astype(BF)
+            to = {"fsdp": other} if ctx_first else {"ctx": across}
+            lasts.append(remote(one, last, sems[12 + 6 * g : 14 + 6 * g], 0, to))
+        start = 0
+        for g, (_, _, size, _) in enumerate(groups):
+            far = scratch[5 * g + 2]
+            value = chip(g, 3, mine, here)
+            hops[g][1].wait()
+            out[:, start : start + size] = value + far[1].astype(F32)
+            start += size
         finish(totals)
         sums = sml_full[:, columns(place, cut)]
         for i in range(places - 1):
             sums = sums + sml_slots[i]
         small_out[...] = sums
-        second_hop[0].wait()
-        out[:, left] = out[:, left] + last[0].astype(F32)
-        second_hop[1].wait()
-        out[:, right] = out[:, right] + last[1].astype(F32)
-
+        finish(given)
+        for k in range(1, n_tp):
+            moe = moe + share_slots[k - 1].astype(F32)
+        block_out[...] = moe.astype(BF)
+        start = 0
+        for g, (_, _, size, _) in enumerate(groups):
+            lasts[g].wait()
+            at = pl.ds(start, size)
+            out[:, at] = out[:, at] + scratch[5 * g + 4][...].astype(F32)
+            start += size
+        finish(moved)
+
+    buffers = [
+        pltpu.VMEM((8, width), F32),
+        pltpu.VMEM((places - 1, 8, cut), F32),
+        pltpu.VMEM((experts, tokens, 128), F32),
+        pltpu.VMEM((n_tp - 1, tokens, block_size), BF),
+        pltpu.VMEM((n_tp - 1, tokens, block_size), BF),
+    ]
+    sems = pair_of_sems(n_tp) + pair_of_sems(places) + pair_of_sems(n_ctx) + pair_of_sems(n_tp)
+    for _, _, size, _ in groups:
+        buffers += [
+            pltpu.VMEM((4, rows, size), BF),
+            pltpu.VMEM((2, rows, size), BF),
+            pltpu.VMEM((2, rows, size), BF),
+            pltpu.VMEM((rows, size), BF),
+            pltpu.VMEM((rows, size), BF),
+        ]
+        sems += pair_of_sems(4) + pair_of_sems(2) + pair_of_sems(1)
     return call(
         kernel,
-        (shape((rows, size), F32), shape((8, cut), F32)),
-        (part, small),
-        [
-            pltpu.VMEM((8, rows, half), BF),
-            pltpu.VMEM((4, rows, half), BF),
-            pltpu.VMEM((4, rows, half), BF),
-            pltpu.VMEM((2, rows, half), BF),
-            pltpu.VMEM((2, rows, half), BF),
-            pltpu.VMEM((8, width), F32),
-            pltpu.VMEM((places - 1, 8, cut), F32),
-        ]
-        + pair_of_sems(8)
-        + pair_of_sems(4)
-        + pair_of_sems(2)
-        + pair_of_sems(n_tp)
-        + pair_of_sems(places),
+        (
+            shape((rows, total_columns), F32),
+            shape((8, cut), F32),
+            shape((tokens, block_size), BF),
+            came_shape(payload, n_ctx),
+        ),
+        (*parts, small, payload, back, picks, mix, resid),
+        buffers + sems,
         10,
         "weight_grads",
-    )
-
-
-def place_pieces(pieces, n_ctx):
-    rows, size = pieces[0].shape
+        left=(len(parts) + 1, -1),
+    )
+
+
+def experts_out(back, picks, mix, resid, payload, n_tp, n_ctx):
+    rows, size = resid.shape
+    experts = n_ctx
+
+    def kernel(bck, pck, mx, rsd, pay, out, came, part, slots, *sems):
+        greet([("tp", n_tp), ("ctx", n_ctx)])
+        moved = spread(pay, came, n_ctx, sems[2:4])
+        order = lax.broadcasted_iota(jnp.int32, (8, 128), 0)
+        gate = [as_column(mx[...], jnp.where(order == k, 1.0, 0.0)) for k in range(experts)]
+        copies = []
+        for step in range(1, n_tp + 1):
+            at = columns(peer("tp", n_tp, step), size)
+            block = jnp.zeros((rows, size), F32)
+            for k in range(experts):
+                block = block + gate[k][:, 0:1] * t_mm(
+                    pck[k * CAP : (k + 1) * CAP], bck[k * CAP : (k + 1) * CAP, at]
+                )
+            if step < n_tp:
+                part[step - 1] = block.astype(BF)
+                copies.append(
+                    send(part.at[step - 1], slots.at[step - 1], "tp", n_tp, step, sems[0:2])
+                )
+            else:
+                total = rsd[...] + block
+        finish(copies)
+        for k in range(1, n_tp):
+            total = total + slots[k - 1].astype(F32)
+        out[...] = total.astype(BF)
+        finish(moved)
+
+    return call(
+        kernel,
+        (shape((rows, size), BF), came_shape(payload, n_ctx)),
+        (back, picks, mix, resid, payload),
+        [
+            pltpu.VMEM((n_tp - 1, rows, size), BF),
+            pltpu.VMEM((n_tp - 1, rows, size), BF),
+        ]
+        + pair_of_sems(n_tp)
+        + pair_of_sems(n_ctx),
+        9,
+        "experts_out",
+        left=(4, -1),
+    )
+
+
+def place_pieces(own, came, n_ctx):
+    rows, size = own.shape
     tile = 64 if rows % 64 == 0 else rows
 
-    def kernel(*refs):
+    def kernel(mine, others, out):
         here = lax.axis_index("ctx")
-        for k in range(n_ctx):
-            refs[-1][lax.rem(here + n_ctx - k, n_ctx)] = refs[k][...].astype(F32)
+        out[here] = mine[...].astype(F32)
+        for k in range(1, n_ctx):
+            out[lax.rem(here + n_ctx - k, n_ctx)] = others[k - 1].astype(F32)
 
     return pl.pallas_call(
         kernel,
         grid=(rows // tile,),
         out_shape=shape((n_ctx, rows, size), F32),
-        in_specs=[pl.BlockSpec((tile, size), lambda i: (i, 0))] * n_ctx,
+        in_specs=[
+            pl.BlockSpec((tile, size), lambda i: (i, 0)),
+            pl.BlockSpec((n_ctx - 1, tile, size), lambda i: (0, i, 0)),
+        ],
         out_specs=pl.BlockSpec((n_ctx, tile, size), lambda i: (0, i, 0)),
         cost_estimate=pl.CostEstimate(
             flops=0, bytes_accessed=6 * n_ctx * rows * size, transcendentals=0
         ),
         name="place_pieces",
-    )(*pieces)
+    )(own, came)
 
 
 def after(value, *needed):
@@ -791,9 +1019,6 @@
     pair = n_fsdp == 2
     heads_width = w_query.shape[1]
 
-    def shift_ctx(value, k):
-        return lax.ppermute(value, "ctx", [(i, (i + k) % n_ctx) for i in range(n_ctx)])
-
     def swap_fsdp(value):
         return lax.ppermute(value, "fsdp", [(0, 1), (1, 0)])
 
@@ -828,13 +1053,15 @@
     def my_features(values):
         return lax.dynamic_slice_in_dim(values, here_tp * width_tp, width_tp, values.ndim - 1)
 
-    attn_w = jnp.concatenate([w_query, w_key, w_value, w_output], axis=1)
+    attn_w = (w_query, w_key, w_value, w_output)
     small = jnp.concatenate(
         [attn_gain[None], ffn_gain[None], w_router.T, jnp.zeros((2, part), BF)], axis=0
     )
     if pair:
         quarter = part // n_ctx
-        own_quarter = lax.dynamic_slice_in_dim(attn_w, here_ctx * quarter, quarter, 0)
+        own_quarter = jnp.concatenate(
+            [lax.dynamic_slice_in_dim(w, here_ctx * quarter, quarter, 0) for w in attn_w], axis=1
+        )
         other_quarter = swap_fsdp(own_quarter)
         other_small = swap_fsdp(small)
         small_full = join([small, other_small]).astype(F32)
@@ -876,7 +1103,9 @@
     if pair:
         attn_full = gathered[3]
     else:
-        attn_full = lax.all_gather(attn_w, "fsdp", axis=0, tiled=True)
+        attn_full = lax.all_gather(
+            jnp.concatenate(attn_w, axis=1), "fsdp", axis=0, tiled=True
+        )
     qkv_w = attn_full[:, : 3 * heads_width]
     output_w = attn_full[:, 3 * heads_width :]
     positions = here_ctx * rows_here + jnp.arange(rows_here, dtype=jnp.int32)
@@ -916,13 +1145,10 @@
             t_mm(mine, right).astype(BF), "fsdp", scatter_dimension=0, tiled=True
         )
 
-    def grad_spread(mine):
+    def grad_place(mine, came):
         cut = part // n_ctx
-        pieces = []
-        for k in range(experts):
-            piece = lax.dynamic_slice_in_dim(mine, ((here_ctx + k) % n_ctx) * cut, cut, 0)
-            pieces.append(shift_ctx(piece, k) if k else piece)
-        return pieces
+        own = lax.dynamic_slice_in_dim(mine, here_ctx * cut, cut, 0)
+        return place_pieces(own, came, n_ctx)
 
     down_sent = grad_send(d_result, hidden_act)
     if pair:
@@ -936,16 +1162,13 @@
     d_gate_act = (d_hidden * up_act * sigma_act * (1.0 + gate_act * (1.0 - sigma_act))).astype(BF)
     d_up_act = (d_hidden * gate_act * sigma_act).astype(BF)
     gate_sent = grad_send(token_rows, d_gate_act)
-    up_sent = grad_send(token_rows, d_up_act)
-    d_rows = join(
-        [mm_t(d_gate_act, wg) + mm_t(d_up_act, wu) for wg, wu in zip(gate_w, up_w)]
-    ).astype(BF)
+
+    acts = (d_gate_act, d_up_act, hidden_act)
     if pair:
-        d_rows = after(d_rows, gate_sent[2], up_sent[2])
-    result = back(after(hidden_act, d_rows), down_w)
-
-    d_resid, d_attn_here, gain_two_part, d_logits = second_norm_back(
-        d_rows,
+        acts = lax.optimization_barrier((*acts, gate_sent[2]))[:3]
+    d_resid, d_attn_here, gain_two_part, d_logits, returned = second_norm_back(
+        acts,
+        (gate_w, up_w, down_w),
         gate_dot,
         picks,
         gates,
@@ -960,41 +1183,35 @@
         n_ctx,
     )
     if pair:
-        d_attn_here = after(d_attn_here, down_sent[3])
-    down_pieces = grad_spread(grad_sum(*down_sent))
-
+        up_sent = grad_send(token_rows, after(d_up_act, d_resid))
+        d_attn_here, *down_sent = lax.optimization_barrier((d_attn_here, *down_sent))
+        d_attn_here = after(d_attn_here, up_sent[2])
+    else:
+        up_sent = grad_send(token_rows, d_up_act)
+    grad_down = grad_sum(*down_sent)
+
+    d_attn, d_qkv, down_came = attention_backward(
+        d_attn_here, output_w, query, kv, cosine, -sine, grad_down, n_tp, n_ctx
+    )
     if pair:
-        d_attn_here = after(d_attn_here, down_pieces[0])
-    d_attn, d_qkv = attention_backward(
-        d_attn_here, output_w, query, kv, cosine, -sine, n_tp, n_ctx
+        d_qkv, *gate_sent = lax.optimization_barrier((d_qkv, *gate_sent))
+    grad_gate = grad_sum(*gate_sent)
+    in_grad, gain_one_part, gate_came = first_norm_back(
+        mm_t(d_qkv, qkv_w).astype(BF),
+        hidden_in,
+        scale_one,
+        gain_one_here,
+        d_resid,
+        grad_gate,
+        n_tp,
+        n_ctx,
     )
     if pair:
-        d_qkv = after(d_qkv, gate_sent[3], *down_pieces)
-    gate_pieces = grad_spread(grad_sum(*gate_sent))
-    if pair:
-        d_qkv = after(d_qkv, gate_pieces[0])
-    in_grad, gain_one_part = first_norm_back(
-        mm_t(d_qkv, qkv_w).astype(BF), hidden_in, scale_one, gain_one_here, d_resid, n_tp
-    )
-
-    share = my_features(result)
-    for k in range(1, n_tp):
-        piece = lax.dynamic_slice_in_dim(
-            result, ((here_tp + k) % n_tp) * width_tp, width_tp, 1
-        ).astype(BF)
-        piece = lax.ppermute(piece, "tp", [(i, (i + k) % n_tp) for i in range(n_tp)])
-        share = share + piece.astype(F32)
-    shares = share.astype(BF).reshape(experts, CAP, width_tp)
-    moe_part = jnp.zeros(resid.shape, F32)
-    for k in range(experts):
-        piece = shift_ctx(shares[k], -k) if k else shares[k]
-        pick = picks[k * CAP : (k + 1) * CAP]
-        moe_part = moe_part + mix[k][:, None] * t_mm(pick, piece)
-    block_out = (resid + moe_part).astype(BF)
-
-    grad_attn = jnp.concatenate([t_mm(normed_one, d_qkv), t_mm(d_attn, attended)], axis=1).astype(
-        BF
-    )
+        in_grad, *up_sent = lax.optimization_barrier((in_grad, *up_sent))
+    grad_up = grad_sum(*up_sent)
+
+    grad_qkv = t_mm(normed_one, d_qkv).astype(BF)
+    grad_output = t_mm(d_attn, attended).astype(BF)
     small_part = jnp.concatenate(
         [
             gain_one_part[:1],
@@ -1004,24 +1221,32 @@
         ],
         axis=0,
     )
+    mixing = (returned, picks, mix, resid)
     if pair:
-        in_grad, small_part = lax.optimization_barrier((in_grad, small_part))
-        grad_attn, small_grad = weight_grads(
-            grad_attn.reshape(n_fsdp, n_ctx, quarter, -1), small_part, n_tp, n_ctx
+        grad_attn, small_grad, block_out, up_came = weight_grads(
+            [value.reshape(n_fsdp, n_ctx, quarter, -1) for value in (grad_qkv, grad_output)],
+            [
+                (0, 0, 2 * heads_width, True),
+                (0, 2 * heads_width, heads_width, False),
+                (1, 0, heads_width, False),
+            ],
+            small_part,
+            grad_up,
+            *mixing,
+            n_tp,
+            n_ctx,
         )
-        up_there, grad_attn = lax.optimization_barrier((up_sent[3], grad_attn))
-        up_sent = (*up_sent[:3], up_there)
     else:
         scatter = partial(
             lax.psum_scatter, axis_name=("fsdp", "ctx"), scatter_dimension=0, tiled=True
         )
-        grad_attn = scatter(grad_attn).astype(F32)
+        grad_attn = scatter(jnp.concatenate([grad_qkv, grad_output], axis=1)).astype(F32)
         small_grad = lax.all_gather(small_part, "tp", axis=1, tiled=True)
         small_grad = scatter(small_grad.T).T
-    up_pieces = grad_spread(grad_sum(*up_sent))
-    grad_gate, grad_up, grad_down = (
-        place_pieces(pieces, n_ctx) for pieces in (gate_pieces, up_pieces, down_pieces)
-    )
+        block_out, up_came = experts_out(*mixing, grad_up, n_tp, n_ctx)
+    grad_down = grad_place(grad_down, down_came)
+    grad_gate = grad_place(grad_gate, gate_came)
+    grad_up = grad_place(grad_up, up_came)
     return (
         block_out,
         in_grad,

time: 611 us -> 548 us (0.90)
  waiting for transfers between devices: 23.8 us -> 0.02 us
  matrix products: 103 us -> 81.1 us
  Pallas kernels: 386 us -> 407 us
  other arithmetic: 24.2 us -> 6.37 us
  starting transfers between devices: 25.1 us -> 9.83 us
    ppermute x15 -> x0, waiting for transfers between devices: 23.8 us -> none  [the longest x12 23.8 us: shift_ctx(): lax.ppermute(value, 'ctx', [(i, (i + k) % n_ctx) for i in range(n_ctx)])]
    dot_general x8 -> x2, matrix products: 32.2 us -> 9.49 us  [mm_t(): lax.dot_general(left, right, (((1,), (1,)), ((), ())), preferred_element_...]
    pallas_call x8, Pallas kernels: 372 us -> 392 us  [call(): pl.pallas_call(kernel, out_shape=out_shape, in_specs=[anywhere if i in le...]
    ppermute x15 -> x0, starting transfers between devices: 14.5 us -> none  [the longest x12 7.36 us: shift_ctx(): lax.ppermute(value, 'ctx', [(i, (i + k) % n_ctx) for i in range(n_ctx)])]
    convert_element_type x3 -> x0, other arithmetic: 8.54 us -> none  [the longest x1 4.06 us: grad_sum(): return (t_mm(mine, right) + other.astype(F32)).astype(BF)]
    concatenate x2 -> x1, other arithmetic: 9.08 us -> 1.11 us  [shards(): jnp.concatenate([lax.dynamic_slice_in_dim(w, here_ctx * quarter, quarter,...]
    unnamed x58, local copies, waits for them, and re-layouts: 8.51 us -> 1.79 us
    dot_general x12 -> x8, matrix products: 35.2 us -> 35.5 us  [t_mm(): lax.dot_general(left, right, (((0,), (0,)), ((), ())), preferred_element_...]
  transfers between devices with their start and end apart: 23 -> 8, of which waited for: 5 -> 0; matrix products, arithmetic and copies ran while one was open for 24% -> 19% of each run, Pallas kernels for 63% -> 58%
where the time goes in v5:
time: 548 us; the launch traced here: 542 us
  Pallas kernels  407 us (74%)
  matrix products  81.1 us (15%)
  local copies, waits for them, and re-layouts  35.8 us (7%)
  starting transfers between devices  9.83 us (2%)
  other arithmetic  6.37 us (1%)
    pallas_call x8, Pallas kernels, call(): pl.pallas_call(kernel, out_shape=out_shape, in_specs=[anywhere if i in le...  392 us
    dot_general x10, matrix products, mm(): return jnp.dot(left, right, preferred_element_type=F32)  36.2 us
    dot_general x8, matrix products, t_mm(): lax.dot_general(left, right, (((0,), (0,)), ((), ())), preferred_element_...  35.5 us
    pallas_call x3, Pallas kernels, place_pieces(): pl.pallas_call(kernel, grid=(rows // tile,), out_shape=shape((n_ctx, rows...  14.6 us
  transfers between devices with their start and end apart: 8, of which 0 were waited for; matrix products, arithmetic and copies ran while one was open for 19% of the time, Pallas kernels for 58%

profile of v5, /device:TPU:0, one launch (start us, length us, event | category | flops | bytes accessed | tf_op | source)
XLA Modules:
  0.0 541.7 jit_solution(6992211179738703558)
XLA Ops:
  5.7 2.9 collective-permute-start.1
  13.0 22.6 %gather_tp.1.refs_0_ = bf16[256,2048]{1,0:T(8,128)(2,1)} custom-call(bf16[256,512]{1,0:T(8,128)(2,1)} %hid.3), custom_call_target="tpu_custom_call" | custom-call | tf_op jit(solution)/shard_map/gather_tp/pallas_call | solution.py:189
  35.6 3.6 dynamic-slice_bitcast_fusion.1.refs_5_
  40.0 3.6 dynamic-slice_bitcast_fusion.refs_7_
  50.4 38.6 %first_norm.1 = (bf16[256,2048]{1,0:T(8,128)(2,1)}, f32[256,128]{1,0:T(8,128)}, bf16[256,2048]{1,0:T(8,128)(2,1)}, bf16[2048,2048]{1,0:T(8,128)(2,1)}) custom-call(bf16[256,2048]{1,0:T(8,128)(2,1)} %gather_tp.1.refs_0_, bf16[256,512]{1,0:T(8,128)(2,1)} %refs_18_.1, f32[8,2048]{1,0:T(8,128)} %copy-done.20, bf16[1024,512]{1,0:T(8,128)(2,1)} %refs_3_.1, ...), custom_call_target="tpu_custom_call" | custom-call | tf_op jit(solution)/shard_map/first_norm/pallas_call | solution.py:189
  88.9 6.1 %fusion.2.prj = f32[256,1536]{1,0:T(8,128)} fusion(bf16[256,2048]{1,0:T(8,128)(2,1)} %get-tuple-element.62, bf16[2048,2048]{1,0:T(8,128)(2,1)} %get-tuple-element.63), kind=kOutput, calls=%fused_computation.6 | convolution fusion | flops 1610612736 | bytes 8912896 | tf_op jit(solution)/shard_map/dot_general | solution.py:23
  95.0 22.1 %attention_forward.1 = (bf16[256,512]{1,0:T(8,128)(2,1)}, bf16[256,512]{1,0:T(8,128)(2,1)}, bf16[1024,1024]{1,0:T(8,128)(2,1)}) custom-call(f32[256,1536]{1,0:T(8,128)} %fusion.2.prj, f32[256,128]{1,0:T(8,128)} %pad_maximum_fusion.1.cs, f32[256,128]{1,0:T(8,128)} %get-tuple-element.113.sn), custom_call_target="tpu_custom_call" | custom-call | tf_op jit(solution)/shard_map/attention_forward/pallas_call | solution.py:189
  117.2 3.5 convolution_convert_fusion.6.prt
  123.6 73.0 %second_norm.1 = (f32[256,512]{1,0:T(8,128)}, f32[256,128]{1,0:T(8,128)}, bf16[256,2048]{1,0:T(8,128)(2,1)}, bf16[640,2048]{1,0:T(8,128)(2,1)}, bf16[640,2048]{1...) custom-call(bf16[256,2048]{1,0:T(8,128)(2,1)} %convolution_convert_fusion.6.prt, ...), custom_call_target="tpu_custom_call" | custom-call | tf_op jit(solution)/shard_map/second_norm/pallas_call | solution.py:189
  201.7 5.0 fusion.43
  206.7 4.1 convolution_add_fusion.2
  210.8 4.4 multiply_convert_fusion.3
  215.2 4.1 convolution_convert_fusion.3
  220.1 4.0 fusion.8
  224.1 6.8 %multiply_convert_fusion.1 = (bf16[640,1408]{1,0:T(8,128)(2,1)}, bf16[640,1408]{1,0:T(8,128)(2,1)S(1)}, f32[640]{0:T(1024)S(1)}) fusion(f32[640,1408]{1,0:T(8,128)S(1)} %convolution_add_fusion.2, f32[640]{0:T(1024)S(1)} %mul.96, f32[640,1408]{1,0:T(8,128)S(1)} %get-tuple-element.133, bf16[640,1408]{1,0:T(8,128)(2,1)S(1)} %get-tuple-element.86.refs_2_, ...), kind=kOutput, calls=%fused_computation.13 | convolution fusion | flops 1861713280 | bytes 20421124 | tf_op jit(solution)/shard_map/dot_general | solution.py:23
  231.0 4.0 convolution_convert_fusion.2
  237.8 3.0 slice.53.wgt
  241.5 70.5 %second_norm_back.1 = (f32[256,512]{1,0:T(8,128)}, bf16[256,512]{1,0:T(8,128)(2,1)}, f32[8,512]{1,0:T(8,128)}, f32[8,256]{1,0:T(8,128)}, bf16[640,2048]{1,0:T(8,128)(2,1)}) custom-call(bf16[640,1408]{1,0:T(8,128)(2,1)} %copy-done.9, bf16[640,1408]{1,0:T(8,128)(2,1)} %get-tuple-element.101.refs_1_, bf16[640,1408]{1,0:T(8,128)(2,1)} %copy-done.11, ...), custom_call_target="tpu_custom_call" | custom-call | tf_op jit(solution)/shard_map/second_norm_back/pallas_call | solution.py:189
  312.0 5.7 %convolution_convert_fusion.1 = bf16[1024,1408]{1,0:T(8,128)(2,1)} fusion(bf16[640,1408]{1,0:T(8,128)(2,1)S(1)} %copy-done.7, bf16[640,2048]{1,0:T(8,128)(2,1)} %get-tuple-element.68, s32[]{:T(128)S(6)} %select_n.71), kind=kOutput, calls=%fused_computation.9 | convolution fusion | flops 1846935552 | bytes 5996548 | tf_op jit(solution)/shard_map/dot_general | solution.py:31
  320.3 5.3 add_convert_fusion.2.pay
  325.7 49.8 %attention_backward.1 = (bf16[256,2048]{1,0:T(8,128)(2,1)}, bf16[256,1536]{1,0:T(8,128)(2,1)}, bf16[3,256,1408]{2,1,0:T(8,128)(2,1)}) custom-call(bf16[256,512]{1,0:T(8,128)(2,1)} %get-tuple-element.82.lw, bf16[2048,512]{1,0:T(8,128)(2,1)} %slice.53.wgt, bf16[256,512]{1,0:T(8,128)(2,1)} %get-tuple-element.83.qry, bf16[1024,1024]{1,0:T(8,128)(2,1)} %get-tuple-element.84.full, ...), custom_call_target="tpu_custom_call" | custom-call | tf_op jit(solution)/shard_map/attention_backward/pallas_call | solution.py:189
  375.5 6.0 %fusion.4.prt = bf16[256,2048]{1,0:T(8,128)(2,1)} fusion(bf16[256,1536]{1,0:T(8,128)(2,1)} %get-tuple-element.89, bf16[2048,2048]{1,0:T(8,128)(2,1)} %get-tuple-element.63), kind=kOutput, calls=%fused_computation.26 | convolution fusion | flops 1611137024 | bytes 8126464 | tf_op jit(solution)/shard_map/dot_general | solution.py:27
  381.5 5.5 %add_convert_fusion.1.pay = bf16[1024,1408]{1,0:T(8,128)(2,1)} fusion(bf16[1024,1408]{1,0:T(8,128)(2,1)} %collective-permute-done.6, bf16[640,1024]{1,0:T(8,128)(2,1)S(1)} %copy-done.14, bf16[640,1408]{1,0:T(8,128)(2,1)S(1)} %copy-done.10), kind=kOutput, calls=%fused_computation.2 | convolution fusion | flops 1849819136 | bytes 8880128 | tf_op jit(solution)/shard_map/dot_general | solution.py:31
  387.7 39.5 %first_norm_back.1 = (f32[256,512]{1,0:T(8,128)}, f32[8,512]{1,0:T(8,128)}, bf16[3,256,1408]{2,1,0:T(8,128)(2,1)}) custom-call(bf16[256,2048]{1,0:T(8,128)(2,1)} %fusion.4.prt, bf16[256,512]{1,0:T(8,128)(2,1)} %hid.3, f32[256,128]{1,0:T(8,128)} %get-tuple-element.91.scl, f32[8,512]{1,0:T(8,128)} %broadcast_in_dim.57.gn, f32[256,512]{1,0:T(8,128)} %get-tuple-element.80.dr, ...), custom_call_target="tpu_custom_call" | custom-call | tf_op jit(solution)/shard_map/first_norm_back/pallas_call | solution.py:189
  427.2 2.6 constant_dynamic-slice_fusion
  429.8 4.5 convolution_convert_fusion
  437.3 4.2 add_convert_fusion.refs_3_
  443.3 76.4 %weight_grads.1 = (f32[256,2048]{1,0:T(8,128)}, f32[8,256]{1,0:T(8,128)}, bf16[256,512]{1,0:T(8,128)(2,1)}, bf16[3,256,1408]{2,1,0:T(8,128)(2,1)}) custom-call(bf16[2,4,256,1536]{3,2,1,0:T(8,128)(2,1)} %bitcast.52, bf16[2,4,256,512]{3,2,1,0:T(8,128)(2,1)} %bitcast.53, f32[8,512]{1,0:T(8,128)} %maximum_maximum_fusion.1.refs_2_, bf16[1024,1408]{1,0:T(8,128)(2,1)} %copy-done.3, ...), custom_call_target="tpu_custom_call" | custom-call | tf_op jit(solution)/shard_map/weight_grads/pallas_call | solution.py:189
  522.3 2.9 fusion.40
  525.2 4.8 place_pieces.5
  530.0 4.8 place_pieces.4
  534.9 4.9 place_pieces.3
  (128 shorter events, 41.2 us)
Async XLA Ops:
  0.6 8.0 %copy-start.26 = (bf16[1024]{0:T(1024)(128)(2,1)S(1)}, bf16[1024]{0:T(1024)(128)(2,1)}, u32[]{:S(2)}) copy-start(bf16[1024]{0:T(1024)(128)(2,1)} %param.15) | copy-start | bytes 6148
  0.7 8.0 %copy-start.27 = (bf16[1024]{0:T(1024)(128)(2,1)S(1)}, bf16[1024]{0:T(1024)(128)(2,1)}, u32[]{:S(2)}) copy-start(bf16[1024]{0:T(1024)(128)(2,1)} %param.20) | copy-start | bytes 6148
  0.7 8.1 %copy-start.23 = (bf16[1024,4]{0,1:T(4,128)(2,1)S(1)}, bf16[1024,4]{0,1:T(4,128)(2,1)}, u32[]{:S(2)}) copy-start(bf16[1024,4]{0,1:T(4,128)(2,1)} %param.21) | copy-start | bytes 24580
  5.7 44.7 %collective-permute-start.1 = (bf16[256,2048]{1,0:T(8,128)(2,1)}, bf16[256,2048]{1,0:T(8,128)(2,1)}, u32[]{:S(2)}, u32[]{:S(2)}) collective-permute-start(bf16[256,2048]{1,0:T(8,128)(2,1)} %pad_maximum_fusion), channel_id=1, source_target_pairs={{0,16},{16,0},{1,17},{17,1},{2,18},{18,2},{3,19},{19,3},{4,20},{20... | collective-permute-start | bytes 3145736 | tf_op jit(solution)/shard_map/ppermute | solution.py:1023
  8.8 40.7 %collective-permute-start = (bf16[8,1024]{1,0:T(8,128)(2,1)S(1)}, bf16[8,1024]{1,0:T(8,128)(2,1)S(1)}, u32[]{:S(2)}, u32[]{:S(2)}) collective-permute-start(bf16[8,1024]{1,0:T(8,128)(2,1)S(1)} %maximum_maximum_fusion), channel_id=1, source_target_pairs={{0,16},{16,0},{1,17},{17,1},{2,18},{18,2},{3,19},{19,3},{4,20},{20... | collective-permute-start | bytes 49160 | tf_op jit(solution)/shard_map/ppermute | solution.py:1023
  10.9 188.0 %copy-start = (bf16[1024,1408]{1,0:T(8,128)(2,1)}, bf16[1024,1408]{1,0:T(8,128)(2,1)S(1)}, u32[]{:S(2)}) copy-start(bf16[1024,1408]{1,0:T(8,128)(2,1)S(1)} %dynamic-slice_bitcast_fusion.2.refs_3_) | copy-start | bytes 8650756
  10.9 195.8 %collective-permute-start.2 = (bf16[1024,1408]{1,0:T(8,128)(2,1)S(1)}, bf16[1024,1408]{1,0:T(8,128)(2,1)}, u32[]{:S(2)}, u32[]{:S(2)}) collective-permute-start(bf16[1024,1408]{1,0:T(8,128)(2,1)S(1)} %dynamic-slice_bitcast_fusion.2.refs_3_), channel_id=1, source_target_pairs={{0,16},{16,0},{1,17},{17,1},{2,18},{18,2},{3,19},{19,3},{4,20},{20... | collective-permute-start | bytes 8650760 | tf_op jit(solution)/shard_map/ppermute | solution.py:1023
  39.2 5.7 %copy-start.24 = (s32[256,2]{0,1:T(2,128)S(1)}, s32[256,2]{0,1:T(2,128)}, u32[]{:S(2)}) copy-start(s32[256,2]{0,1:T(2,128)} %param.25) | copy-start | bytes 6148
  39.2 171.6 %collective-permute-start.3 = (bf16[1024,1408]{1,0:T(8,128)(2,1)}, bf16[1024,1408]{1,0:T(8,128)(2,1)}, u32[]{:S(2)}, u32[]{:S(2)}) collective-permute-start(bf16[1024,1408]{1,0:T(8,128)(2,1)} %dynamic-slice_bitcast_fusion.1.refs_5_), channel_id=1, source_target_pairs={{0,16},{16,0},{1,17},{17,1},{2,18},{18,2},{3,19},{19,3},{4,20},{20... | collective-permute-start | bytes 8650760 | tf_op jit(solution)/shard_map/ppermute | solution.py:1023
  43.6 180.6 %collective-permute-start.4 = (bf16[1024,1408]{1,0:T(8,128)(2,1)}, bf16[1024,1408]{1,0:T(8,128)(2,1)}, u32[]{:S(2)}, u32[]{:S(2)}) collective-permute-start(bf16[1024,1408]{1,0:T(8,128)(2,1)} %dynamic-slice_bitcast_fusion.refs_7_), channel_id=1, source_target_pairs={{0,16},{16,0},{1,17},{17,1},{2,18},{18,2},{3,19},{19,3},{4,20},{20... | collective-permute-start | bytes 8650760 | tf_op jit(solution)/shard_map/ppermute | solution.py:1023
  117.2 3.5 copy-start.16
  198.9 2.7 copy-start.13
  201.7 13.6 %copy-start.1 = (bf16[640,2048]{1,0:T(8,128)(2,1)}, bf16[640,2048]{1,0:T(8,128)(2,1)S(1)}, u32[]{:S(2)}) copy-start(bf16[640,2048]{1,0:T(8,128)(2,1)S(1)} %multiply_convert_fusion) | copy-start | bytes 7864324
  201.7 5.0 copy-start.18
  215.2 8.9 %copy-start.11 = (bf16[640,1408]{1,0:T(8,128)(2,1)}, bf16[640,1408]{1,0:T(8,128)(2,1)S(1)}, u32[]{:S(2)}) copy-start(bf16[640,1408]{1,0:T(8,128)(2,1)S(1)} %get-tuple-element.86.refs_2_) | copy-start | bytes 5406724
  219.4 101.0 %collective-permute-start.5 = (bf16[1024,1408]{1,0:T(8,128)(2,1)}, bf16[1024,1408]{1,0:T(8,128)(2,1)}, u32[]{:S(2)}, u32[]{:S(2)}) collective-permute-start(bf16[1024,1408]{1,0:T(8,128)(2,1)} %convolution_convert_fusion.3), channel_id=1, source_target_pairs={{0,16},{16,0},{1,17},{17,1},{2,18},{18,2},{3,19},{19,3},{4,20},{20... | collective-permute-start | bytes 8650760 | tf_op jit(solution)/shard_map/ppermute | solution.py:1023
  231.0 4.0 copy-start.9
  235.0 140.5 %collective-permute-start.6 = (bf16[1024,1408]{1,0:T(8,128)(2,1)}, bf16[1024,1408]{1,0:T(8,128)(2,1)}, u32[]{:S(2)}, u32[]{:S(2)}) collective-permute-start(bf16[1024,1408]{1,0:T(8,128)(2,1)} %convolution_convert_fusion.2), channel_id=1, source_target_pairs={{0,16},{16,0},{1,17},{17,1},{2,18},{18,2},{3,19},{19,3},{4,20},{20... | collective-permute-start | bytes 8650760 | tf_op jit(solution)/shard_map/ppermute | solution.py:1023
  241.5 70.5 %copy-start.7 = (bf16[640,1408]{1,0:T(8,128)(2,1)S(1)}, bf16[640,1408]{1,0:T(8,128)(2,1)}, u32[]{:S(2)}) copy-start(bf16[640,1408]{1,0:T(8,128)(2,1)} %get-tuple-element.101.refs_1_) | copy-start | bytes 5406724
  312.0 6.4 %copy-start.2 = (bf16[640,2048]{1,0:T(8,128)(2,1)S(1)}, bf16[640,2048]{1,0:T(8,128)(2,1)}, u32[]{:S(2)}) copy-start(bf16[640,2048]{1,0:T(8,128)(2,1)} %copy-done.1) | copy-start | bytes 7864324
  312.0 7.3 %copy-start.25 = (f32[8,256]{1,0:T(8,128)S(1)}, f32[8,256]{1,0:T(8,128)}, u32[]{:S(2)}) copy-start(f32[8,256]{1,0:T(8,128)} %get-tuple-element.97) | copy-start | bytes 24580
  317.7 2.7 copy-start.12
  317.7 116.6 %collective-permute-start.7 = (bf16[1024,1408]{1,0:T(8,128)(2,1)}, bf16[1024,1408]{1,0:T(8,128)(2,1)}, u32[]{:S(2)}, u32[]{:S(2)}) collective-permute-start(bf16[1024,1408]{1,0:T(8,128)(2,1)} %convolution_convert_fusion.1), channel_id=1, source_target_pairs={{0,16},{16,0},{1,17},{17,1},{2,18},{18,2},{3,19},{19,3},{4,20},{20... | collective-permute-start | bytes 8650760 | tf_op jit(solution)/shard_map/ppermute | solution.py:1023
  375.5 6.0 %copy-start.10 = (bf16[640,1408]{1,0:T(8,128)(2,1)S(1)}, bf16[640,1408]{1,0:T(8,128)(2,1)}, u32[]{:S(2)}) copy-start(bf16[640,1408]{1,0:T(8,128)(2,1)} %copy-done.9) | copy-start | bytes 5406724
  375.5 6.0 %copy-start.14 = (bf16[640,1024]{1,0:T(8,128)(2,1)S(1)}, bf16[640,1024]{1,0:T(8,128)(2,1)}, u32[]{:S(2)}) copy-start(bf16[640,1024]{1,0:T(8,128)(2,1)} %copy-done.13) | copy-start | bytes 3932164
  387.6 42.1 %copy-start.6 = (bf16[256,2048]{1,0:T(8,128)(2,1)S(1)}, bf16[256,2048]{1,0:T(8,128)(2,1)}, u32[]{:S(2)}) copy-start(bf16[256,2048]{1,0:T(8,128)(2,1)} %get-tuple-element.62) | copy-start | bytes 3145732
  387.7 42.1 %copy-start.17 = (bf16[256,1536]{1,0:T(8,128)(2,1)S(1)}, bf16[256,1536]{1,0:T(8,128)(2,1)}, u32[]{:S(2)}) copy-start(bf16[256,1536]{1,0:T(8,128)(2,1)} %get-tuple-element.89) | copy-start | bytes 2359300
  429.8 5.3 copy-start.4
  429.8 5.3 copy-start.21
  435.0 2.2 copy-start.15
  534.9 4.9 copy-start.22
  534.9 5.6 %copy-start.19 = (f32[256,512]{1,0:T(8,128)S(1)}, f32[256,512]{1,0:T(8,128)}, u32[]{:S(2)}) copy-start(f32[256,512]{1,0:T(8,128)} %get-tuple-element.149) | copy-start | bytes 1572868
  (4 other events, 6.9 us)

commit v6 on v5

--- a/solution.py
+++ b/solution.py
@@ -121,30 +121,30 @@
     return here, here + 1 - 2 * lax.rem(here, 2), lax.rem(here + 2, 4)
 
 
-def gather_square(own, full, first_row, sems, between):
-    rows = own.shape[0]
+def gather_square(own, places, sems, between, local=None):
     cuts = own.shape[1] // 512
     here, beside, across = quad()
-
-    def place(rank, i):
-        return full.at[
-            pl.ds(pl.multiple_of(first_row + rank * rows, 16), rows), pl.ds(i * 512, 512)
-        ]
-
     first, second, third = [], [], []
     for i in range(cuts):
         piece = own.at[:, pl.ds(i * 512, 512)]
-        first.append(remote(piece, place(here, i), sems, 3 * i, {"ctx": across}))
-        second.append(remote(piece, place(here, i), sems, 3 * i + 1, {"ctx": beside}))
-    full[pl.ds(pl.multiple_of(first_row + here * rows, 16), rows), :] = own[...]
+        first.append(remote(piece, places(here, i), sems, 3 * i, {"ctx": across}))
+        second.append(remote(piece, places(here, i), sems, 3 * i + 1, {"ctx": beside}))
+        if local is None:
+            places(here, i)[...] = piece[...]
+        else:
+            pltpu.make_async_copy(piece, places(here, i), local.at[i]).start()
     between()
     for i in range(cuts):
         first[i].wait()
         third.append(
-            remote(place(across, i), place(across, i), sems, 3 * i + 2, {"ctx": beside})
+            remote(places(across, i), places(across, i), sems, 3 * i + 2, {"ctx": beside})
         )
     finish(second)
     finish(third)
+    if local is not None:
+        for i in range(cuts):
+            piece = own.at[:, pl.ds(i * 512, 512)]
+            pltpu.make_async_copy(piece, places(here, i), local.at[i]).wait()
 
 
 def row_sums(values):
@@ -210,15 +210,41 @@
     return [DMA((n,)), DMA((n,))]
 
 
-def gather_tp(value, n_tp):
+def gather_tp(value, stacks, n_tp):
     rows, size = value.shape
-
-    def kernel(own, full, *sems):
+    many = len(stacks)
+    member = stacks[0].shape[1:]
+
+    def kernel(own, *refs):
+        stk, full, outs = refs[:many], refs[many], refs[many + 1 : 2 * many + 1]
+        held, loads, stores = refs[2 * many + 1 : 2 * many + 4]
+        sems = refs[2 * many + 4 :]
+        here = lax.axis_index("ctx")
+        into = [
+            pltpu.make_async_copy(stk[i].at[here], held.at[i], loads.at[i]) for i in range(many)
+        ]
+        away = [pltpu.make_async_copy(held.at[i], outs[i], stores.at[i]) for i in range(many)]
+        for copy in into:
+            copy.start()
         greet([("tp", n_tp)])
-        finish(gather_columns(own, full, "tp", n_tp, sems))
+        copies = gather_columns(own, full, "tp", n_tp, sems)
+        for i in range(many):
+            into[i].wait()
+            away[i].start()
+        finish(copies)
+        finish(away)
 
     return call(
-        kernel, shape((rows, size * n_tp), value.dtype), (value,), pair_of_sems(n_tp), 1, "gather_tp"
+        kernel,
+        (
+            shape((rows, size * n_tp), value.dtype),
+            *(shape(member, stack.dtype) for stack in stacks),
+        ),
+        (value, *stacks),
+        [pltpu.VMEM((many, *member), BF), DMA((many,)), DMA((many,))] + pair_of_sems(n_tp),
+        1,
+        "gather_tp",
+        left=tuple(range(1, many + 1)) + tuple(range(-many, 0)),
     )
 
 
@@ -231,8 +257,27 @@
         refs = refs[3:]
         if with_quarter:
             wgts, refs = refs[: len(weights)], refs[len(weights) :]
-            qrt, out, scale, grd_full, wgt_full = refs[:5]
-            sems = refs[5:]
+            qrt, out, scale, grd_full, many_full, last_full, held, local, loads, stores = refs[:10]
+            sems = refs[10:]
+            half, inner = wgts[0].shape
+            last = len(wgts) - 1
+            mine = lax.axis_index("fsdp")
+
+            def target(i, first_row, count):
+                at = pl.ds(pl.multiple_of(first_row, 16), count)
+                if i == last:
+                    return last_full.at[at, :]
+                return many_full.at[at, pl.ds(i * inner, inner)]
+
+            into = [
+                pltpu.make_async_copy(wgts[i], held.at[i], loads.at[i]) for i in range(len(wgts))
+            ]
+            away = [
+                pltpu.make_async_copy(held.at[i], target(i, mine * half, half), stores.at[i])
+                for i in range(len(wgts))
+            ]
+            for copy in into:
+                copy.start()
             greet([("tp", n_tp), ("ctx", n_ctx)])
         else:
             out, scale, grd_full = refs[:3]
@@ -248,28 +293,43 @@
             out[...] = (values * factor * gn[0:1, :]).astype(BF)
 
         if with_quarter:
-            half, inner = wgts[0].shape
-            mine = lax.axis_index("fsdp")
+            count = qrt.shape[0]
 
             def work():
+                for i in range(len(wgts)):
+                    into[i].wait()
+                    away[i].start()
                 norm()
-                for i, wgt in enumerate(wgts):
-                    wgt_full[
-                        pl.ds(pl.multiple_of(mine * half, 16), half), pl.ds(i * inner, inner)
-                    ] = wgt[...]
-
-            gather_square(qrt, wgt_full, (1 - mine) * half, sems[2:4], work)
+
+            def places(rank, i):
+                return target(i, (1 - mine) * half + rank * count, count)
+
+            gather_square(qrt, places, sems[2:4], work, local)
+            finish(away)
         else:
             norm()
         finish(grads)
 
     outs = [shape((rows, width), BF), shape((rows, 128), F32), shape((rows, width), BF)]
     inputs = [full, grad, gain]
+    scratch, left = [], ()
     if with_quarter:
-        outs.append(shape((2 * weights[0].shape[0], quarter.shape[1]), BF))
+        half, inner = weights[0].shape
+        many = len(weights)
+        assert inner == 512
+        outs.append(shape((2 * half, (many - 1) * inner), BF))
+        outs.append(shape((2 * half, inner), BF))
         inputs += [*weights, quarter]
+        scratch = [pltpu.VMEM((many, half, inner), BF), DMA((many,)), DMA((many,)), DMA((many,))]
+        left = tuple(range(3, 3 + many)) + (-2, -1)
     return call(
-        kernel, tuple(outs), inputs, pair_of_sems(n_tp) + pair_of_sems(12), 7, "first_norm"
+        kernel,
+        tuple(outs),
+        inputs,
+        scratch + pair_of_sems(n_tp) + pair_of_sems(12),
+        7,
+        "first_norm",
+        left=left,
     )
 
 
@@ -308,7 +368,10 @@
             def _(h):
                 qry[:, columns(h, HD)] = turn(prj[:, columns(h, HD)], cs[...], sn[...]).astype(BF)
 
-        gather_square(own, full, 0, sems, queries)
+        def places(rank, i):
+            return full.at[stretch(rank, rows), pl.ds(i * 512, 512)]
+
+        gather_square(own, places, sems, queries)
 
         @pl.loop(0, heads)
         def _(h):
@@ -339,7 +402,7 @@
     def kernel(
         prt, hid, gn, slb, pck, rtr, one, nms,
         resid, scale, out, moved, tokens, slot_gates, gates, mix,
-        slots, mine, sums, low, sent, own_gates, *sems
+        slots, mine, sums, mine_two, sums_two, low, sent, own_gates, *sems
     ):
         greet([("tp", n_tp), ("ctx", n_ctx)])
         here = lax.axis_index("tp")
@@ -362,7 +425,42 @@
         factor = lax.rsqrt(as_column(square, eighth()) * (1.0 / width) + EPS)
         scale[...] = factor
         low[...] = (resid[...] * factor[:, 0:1] * gn[0:1, :]).astype(BF)
+        partial_logits = mm_t(rtr[...].astype(BF), low[...])
+        mine_two[...] = partial_logits
+        logit_copies = [
+            send(mine_two, sums_two.at[k - 1], "tp", n_tp, k, sems[12:14]) for k in range(1, n_tp)
+        ]
         copies = gather_columns(low, out, "tp", n_tp, sems[4:6])
+
+        def route():
+            finish(logit_copies)
+            logits = partial_logits
+            for k in range(1, n_tp):
+                logits = logits + sums_two[k - 1]
+            named = [jnp.sum(one[j] * logits, axis=0, keepdims=True) for j in range(2)]
+            top = jnp.maximum(named[0], named[1])
+            powers = [jnp.exp(value - top) for value in named]
+            both = powers[0] + powers[1]
+            gate = [value / both for value in powers]
+            mixed = gate[0] * nms[0] + gate[1] * nms[1]
+            mix[...] = mixed
+            order = lax.broadcasted_iota(jnp.int32, (8, rows), 0)
+            gates[...] = jnp.where(order == 0, gate[0], jnp.where(order == 1, gate[1], 0.0))
+            own_gates[...] = jnp.zeros(own_gates.shape, F32)
+            for k in range(experts):
+                own_gates[k, :, 0:CAP] = lax.dot_general(
+                    jnp.broadcast_to(mixed[k : k + 1], (8, rows)),
+                    pck[k * CAP : (k + 1) * CAP].astype(F32),
+                    (((1,), (1,)), ((), ())),
+                    precision=lax.Precision.HIGHEST,
+                    preferred_element_type=F32,
+                )
+            slot_gates[0] = own_gates[0]
+            for k in range(1, n_ctx):
+                others.append(
+                    send(own_gates.at[k], slot_gates.at[k], "ctx", n_ctx, k, sems[10:12])
+                )
+
         for step in range(n_tp):
             at = columns(peer("tp", n_tp, n_tp - step), size)
             if step:
@@ -379,30 +477,8 @@
                         sems[8:10], step * n_ctx + k, {"ctx": peer("ctx", n_ctx, k)},
                     )
                 )
-        logits = mm_t(rtr[...].astype(BF), out[...])
-        named = [jnp.sum(one[j] * logits, axis=0, keepdims=True) for j in range(2)]
-        top = jnp.maximum(named[0], named[1])
-        powers = [jnp.exp(value - top) for value in named]
-        both = powers[0] + powers[1]
-        gate = [value / both for value in powers]
-        mixed = gate[0] * nms[0] + gate[1] * nms[1]
-        mix[...] = mixed
-        order = lax.broadcasted_iota(jnp.int32, (8, rows), 0)
-        gates[...] = jnp.where(order == 0, gate[0], jnp.where(order == 1, gate[1], 0.0))
-        own_gates[...] = jnp.zeros(own_gates.shape, F32)
-        for k in range(experts):
-            own_gates[k, :, 0:CAP] = lax.dot_general(
-                jnp.broadcast_to(mixed[k : k + 1], (8, rows)),
-                pck[k * CAP : (k + 1) * CAP].astype(F32),
-                (((1,), (1,)), ((), ())),
-                precision=lax.Precision.HIGHEST,
-                preferred_element_type=F32,
-            )
-        slot_gates[0] = own_gates[0]
-        for k in range(1, n_ctx):
-            others.append(
-                send(own_gates.at[k], slot_gates.at[k], "ctx", n_ctx, k, sems[10:12])
-            )
+            if step == 0:
+                route()
         finish(others)
 
     return call(
@@ -422,6 +498,8 @@
             pltpu.VMEM((n_tp - 1, rows, size), BF),
             pltpu.VMEM((8, rows), F32),
             pltpu.VMEM((n_tp - 1, 8, rows), F32),
+            pltpu.VMEM((8, rows), F32),
+            pltpu.VMEM((n_tp - 1, 8, rows), F32),
             pltpu.VMEM((rows, size), BF),
             pltpu.VMEM((n_tp, experts * CAP, size), BF),
             pltpu.VMEM((experts, 8, rows), F32),
@@ -429,14 +507,16 @@
         + pair_of_sems(n_tp) * 3
         + pair_of_sems(n_ctx)
         + pair_of_sems(n_tp * n_ctx)
-        + pair_of_sems(n_ctx),
+        + pair_of_sems(n_ctx)
+        + pair_of_sems(n_tp),
         3,
         "second_norm",
     )
 
 
 def second_norm_back(
-    acts, weights, dots, picks, gates, onehot, names, router, resid, scale, gain, grad, n_tp, n_ctx
+    acts, weights, tokens, dots, picks, gates, onehot, names, router, resid, scale, gain, grad,
+    n_tp, n_ctx,
 ):
     rows, size = resid.shape
     width = size * n_tp
@@ -449,12 +529,16 @@
         dga, dup, hid = refs[:3]
         wgt = [refs[3 + i * count : 3 + (i + 1) * count] for i in range(3)]
         refs = refs[3 + 3 * count :]
-        dts, pck, gts, one, nms, rtr, rsd, scl, gn, grd = refs[:10]
-        d_resid, low, d_gain, d_logits, out_back = refs[10:15]
+        tok, dts, pck, gts, one, nms, rtr, rsd, scl, gn, grd = refs[:11]
+        d_resid, low, d_gain, d_logits, out_back = refs[11:16]
+        refs = refs[16:]
+        if count == 2:
+            up_away, up_held, up_sem = refs[:1] + refs[1:3]
+            refs = refs[3:]
         (
             drw, eo, buffer, back, back_dots, parts, slots, mine, sums, mine_two, sums_two, loads,
-        ) = refs[15:27]
-        sems = refs[27:]
+        ) = refs[:12]
+        sems = refs[12:]
         here = lax.axis_index("tp")
         first = lax.axis_index("fsdp")
 
@@ -541,6 +625,14 @@
             for k in range(1, n_ctx)
         ]
         out_back[0:CAP] = eo[0:CAP]
+        if count == 2:
+
+            @pl.loop(0, part // 256)
+            def _(i):
+                at = pl.ds(pl.multiple_of((1 - first) * part + i * 256, 128), 256)
+                up_held[stretch(i, 256), :] = t_mm(tok[:, at], dup[...]).astype(BF)
+
+            pltpu.make_async_copy(up_held, up_away, up_sem).start()
         finish(small)
         order = lax.broadcasted_iota(jnp.int32, (8, rows), 0)
         own = jnp.zeros((8, rows), F32)
@@ -596,19 +688,27 @@
         d_resid[...] = result
         low[...] = result.astype(BF)
         finish(moved)
-
+        if count == 2:
+            pltpu.make_async_copy(up_held, up_away, up_sem).wait()
+
+    outs = [
+        shape((rows, size), F32),
+        shape((rows, size), BF),
+        shape((8, size), F32),
+        shape((8, rows), F32),
+        shape((experts * CAP, width), BF),
+    ]
+    held = []
+    if count == 2:
+        outs.append(shape((part, hidden), BF))
+        held = [pltpu.VMEM((part, hidden), BF), DMA]
     flat = [array for group in weights for array in group]
     return call(
         kernel,
-        (
-            shape((rows, size), F32),
-            shape((rows, size), BF),
-            shape((8, size), F32),
-            shape((8, rows), F32),
-            shape((experts * CAP, width), BF),
-        ),
-        (*acts, *flat, dots, picks, gates, onehot, names, router, resid, scale, gain, grad),
-        [
+        tuple(outs),
+        (*acts, *flat, tokens, dots, picks, gates, onehot, names, router, resid, scale, gain, grad),
+        held
+        + [
             pltpu.VMEM((experts * CAP, width), BF),
             pltpu.VMEM((experts * CAP, width), BF),
             pltpu.VMEM((2, 2, size, hidden), BF),
@@ -628,7 +728,7 @@
         + pair_of_sems(n_ctx),
         4,
         "second_norm_back",
-        left=tuple(range(3, 3 + 3 * count)),
+        left=tuple(range(3, 3 + 3 * count)) + ((-1,) if count == 2 else ()),
     )
 
 
@@ -640,13 +740,19 @@
     scale = 1.0 / math.sqrt(HD)
 
     def kernel(
-        lw, wgt, qry, full, cs, sn, pay, d_attn, d_qkv, came, dot, dqs, dkv, slots, last, both, total, *sems
+        lw, wgt, qry, full, cs, sn, pay, d_attn, d_qkv, came, dot, dqs, dkv, slots, last, both, total, kept, *sems
     ):
         greet([("tp", n_tp), ("ctx", n_ctx)])
         here, beside, across = quad()
         beyond = lax.rem(beside + 2, 4)
         copies = gather_columns(lw, d_attn, "tp", n_tp, sems[2:4])
         moved = spread(pay, came, n_ctx, sems[4:6])
+
+        @pl.loop(0, heads)
+        def _(h):
+            at = columns(h, HD)
+            kept[h] = softmax_rows(qry[:, at], full[:, at], here * rows)
+
         for step in range(n_tp):
             rank = peer("tp", n_tp, n_tp - step)
             weights = wgt[pl.ds(pl.multiple_of(rank * size, 16), size), :]
@@ -660,7 +766,7 @@
         @pl.loop(0, heads)
         def _(h):
             at, at_v = columns(h, HD), columns(h + heads, HD)
-            probs = softmax_rows(qry[:, at], full[:, at], here * rows)
+            probs = kept[h]
             d_probs = mm_t(dot[:, at], full[:, at_v])
             delta = jnp.sum(probs * d_probs, axis=-1, keepdims=True)
             d_scores = (probs * (d_probs - delta)).astype(BF)
@@ -708,6 +814,7 @@
             pltpu.VMEM((rows, 2 * inner), BF),
             pltpu.VMEM((rows, 2 * inner), BF),
             pltpu.VMEM((rows, inner), F32),
+            pltpu.VMEM((heads, rows, rows * n_ctx), F32),
         ]
         + pair_of_sems(3)
         + pair_of_sems(n_tp)
@@ -960,30 +1067,52 @@
     )
 
 
-def place_pieces(own, came, n_ctx):
-    rows, size = own.shape
-    tile = 64 if rows % 64 == 0 else rows
-
-    def kernel(mine, others, out):
-        here = lax.axis_index("ctx")
-        out[here] = mine[...].astype(F32)
-        for k in range(1, n_ctx):
-            out[lax.rem(here + n_ctx - k, n_ctx)] = others[k - 1].astype(F32)
-
+def write_out(experts_grads, attn_grad, plain, n_ctx):
+    _, rows, size = experts_grads[0][1].shape
+    steps = max(1, rows // 32)
+    tile = rows // steps
+    many, block = len(experts_grads), attn_grad.shape[1] // 4
+
+    def kernel(rank, *refs):
+        here = rank[0]
+        ins, outs = refs[: 2 * many + 1 + len(plain)], refs[2 * many + 1 + len(plain) :]
+        for i in range(many):
+            mine, came = ins[2 * i : 2 * i + 2]
+            outs[i][here] = mine[...].astype(F32)
+            for k in range(1, n_ctx):
+                outs[i][lax.rem(here + n_ctx - k, n_ctx)] = came[k - 1].astype(F32)
+        for i in range(4):
+            outs[many + i][...] = ins[2 * many][:, i * block : (i + 1) * block]
+        for i in range(len(plain)):
+            outs[many + 4 + i][...] = ins[2 * many + 1 + i][...]
+
+    def flat(array):
+        return pl.BlockSpec((array.shape[0] // steps, array.shape[1]), lambda i, rank: (i, 0))
+
+    in_specs, out_specs, out_shape = [], [], []
+    for _ in experts_grads:
+        in_specs.append(pl.BlockSpec((tile, size), lambda i, rank: (rank[0] * steps + i, 0)))
+        in_specs.append(pl.BlockSpec((n_ctx - 1, tile, size), lambda i, rank: (0, i, 0)))
+        out_specs.append(pl.BlockSpec((n_ctx, tile, size), lambda i, rank: (0, i, 0)))
+        out_shape.append(shape((n_ctx, rows, size), F32))
+    in_specs.append(flat(attn_grad))
+    quarter = jax.ShapeDtypeStruct((attn_grad.shape[0], block), F32)
+    for array in [quarter] * 4 + list(plain):
+        out_specs.append(flat(array))
+        out_shape.append(shape(array.shape, array.dtype))
+    in_specs += [flat(array) for array in plain]
+    inputs = [array for pair in experts_grads for array in pair] + [attn_grad, *plain]
     return pl.pallas_call(
         kernel,
-        grid=(rows // tile,),
-        out_shape=shape((n_ctx, rows, size), F32),
-        in_specs=[
-            pl.BlockSpec((tile, size), lambda i: (i, 0)),
-            pl.BlockSpec((n_ctx - 1, tile, size), lambda i: (0, i, 0)),
-        ],
-        out_specs=pl.BlockSpec((n_ctx, tile, size), lambda i: (0, i, 0)),
+        grid_spec=pltpu.PrefetchScalarGridSpec(
+            num_scalar_prefetch=1, grid=(steps,), in_specs=in_specs, out_specs=out_specs
+        ),
+        out_shape=out_shape,
         cost_estimate=pl.CostEstimate(
-            flops=0, bytes_accessed=6 * n_ctx * rows * size, transcendentals=0
+            flops=0, bytes_accessed=6 * many * n_ctx * rows * size, transcendentals=0
         ),
-        name="place_pieces",
-    )(own, came)
+        name="write_out",
+    )(lax.axis_index("ctx").reshape(1), *inputs)
 
 
 def after(value, *needed):
@@ -1068,20 +1197,14 @@
     else:
         other_quarter = None
         small_full = lax.all_gather(small, "fsdp", axis=1, tiled=True).astype(F32)
-    inputs_full = gather_tp(hidden_in, n_tp)
-
-    def expert_parts(weights, ready):
-        rank, _ = lax.optimization_barrier((here_ctx, ready))
-        return other_parts(lax.dynamic_index_in_dim(weights, rank, 0, False))
-
-    gate_w = expert_parts(w_gate, small)
-    up_w = expert_parts(w_up, inputs_full)
-    down_w = expert_parts(w_down, inputs_full)
+    inputs_full, up_mine, down_mine = gather_tp(hidden_in, (w_up, w_down), n_tp)
+    gate_w = other_parts(lax.dynamic_index_in_dim(w_gate, here_ctx, 0, False))
+    up_w = other_parts(up_mine)
+    down_w = other_parts(down_mine)
     small_here = my_features(small_full)
     gain_one_here = jnp.broadcast_to(small_here[0:1], small_here.shape)
     gain_two_here = jnp.broadcast_to(small_here[1:2], small_here.shape)
     nothing = [(0, 8 - experts), (0, 0)]
-    router_full = jnp.pad(small_full[2 : 2 + experts], nothing)
     router_here = jnp.pad(small_here[2 : 2 + experts], nothing)
 
     relative = (jnp.arange(experts, dtype=jnp.int32) + here_ctx) % experts
@@ -1101,13 +1224,12 @@
     )
     normed_one, scale_one, grad_full = gathered[:3]
     if pair:
-        attn_full = gathered[3]
+        qkv_w, output_w = gathered[3:]
     else:
-        attn_full = lax.all_gather(
-            jnp.concatenate(attn_w, axis=1), "fsdp", axis=0, tiled=True
+        qkv_w, output_w = (
+            lax.all_gather(w, "fsdp", axis=0, tiled=True)
+            for w in (jnp.concatenate(attn_w[:3], axis=1), w_output)
         )
-    qkv_w = attn_full[:, : 3 * heads_width]
-    output_w = attn_full[:, 3 * heads_width :]
     positions = here_ctx * rows_here + jnp.arange(rows_here, dtype=jnp.int32)
     cosine, sine = rotary_tables(positions)
     attended, query, kv = attention_forward(mm(normed_one, qkv_w), cosine, sine, n_ctx)
@@ -1117,7 +1239,7 @@
         gain_two_here,
         mm(picks, grad_full).astype(BF),
         picks,
-        router_full,
+        router_here,
         onehot,
         names,
         n_tp,
@@ -1144,11 +1266,6 @@
         return lax.psum_scatter(
             t_mm(mine, right).astype(BF), "fsdp", scatter_dimension=0, tiled=True
         )
-
-    def grad_place(mine, came):
-        cut = part // n_ctx
-        own = lax.dynamic_slice_in_dim(mine, here_ctx * cut, cut, 0)
-        return place_pieces(own, came, n_ctx)
 
     down_sent = grad_send(d_result, hidden_act)
     if pair:
@@ -1166,9 +1283,10 @@
     acts = (d_gate_act, d_up_act, hidden_act)
     if pair:
         acts = lax.optimization_barrier((*acts, gate_sent[2]))[:3]
-    d_resid, d_attn_here, gain_two_part, d_logits, returned = second_norm_back(
+    d_resid, d_attn_here, gain_two_part, d_logits, returned, *up_away = second_norm_back(
         acts,
         (gate_w, up_w, down_w),
+        token_rows,
         gate_dot,
         picks,
         gates,
@@ -1183,9 +1301,8 @@
         n_ctx,
     )
     if pair:
-        up_sent = grad_send(token_rows, after(d_up_act, d_resid))
+        up_sent = (split(token_rows)[0], d_up_act, up_away[0], swap_fsdp(up_away[0]))
         d_attn_here, *down_sent = lax.optimization_barrier((d_attn_here, *down_sent))
-        d_attn_here = after(d_attn_here, up_sent[2])
     else:
         up_sent = grad_send(token_rows, d_up_act)
     grad_down = grad_sum(*down_sent)
@@ -1226,9 +1343,9 @@
         grad_attn, small_grad, block_out, up_came = weight_grads(
             [value.reshape(n_fsdp, n_ctx, quarter, -1) for value in (grad_qkv, grad_output)],
             [
-                (0, 0, 2 * heads_width, True),
+                (1, 0, heads_width, False),
+                (0, 0, 2 * heads_width, False),
                 (0, 2 * heads_width, heads_width, False),
-                (1, 0, heads_width, False),
             ],
             small_part,
             grad_up,
@@ -1240,21 +1357,23 @@
         scatter = partial(
             lax.psum_scatter, axis_name=("fsdp", "ctx"), scatter_dimension=0, tiled=True
         )
-        grad_attn = scatter(jnp.concatenate([grad_qkv, grad_output], axis=1)).astype(F32)
+        grad_attn = scatter(jnp.concatenate([grad_output, grad_qkv], axis=1)).astype(F32)
         small_grad = lax.all_gather(small_part, "tp", axis=1, tiled=True)
         small_grad = scatter(small_grad.T).T
         block_out, up_came = experts_out(*mixing, grad_up, n_tp, n_ctx)
-    grad_down = grad_place(grad_down, down_came)
-    grad_gate = grad_place(grad_gate, gate_came)
-    grad_up = grad_place(grad_up, up_came)
+    pieces = [(grad_gate, gate_came), (grad_up, up_came), (grad_down, down_came)]
+    (
+        grad_gate, grad_up, grad_down, grad_output, grad_query, grad_key, grad_value,
+        block_out, in_grad,
+    ) = write_out(pieces, grad_attn, (block_out, in_grad), n_ctx)
     return (
         block_out,
         in_grad,
         small_grad[0],
-        grad_attn[:, :heads_width],
-        grad_attn[:, heads_width : 2 * heads_width],
-        grad_attn[:, 2 * heads_width : 3 * heads_width],
-        grad_attn[:, 3 * heads_width :],
+        grad_query,
+        grad_key,
+        grad_value,
+        grad_output,
         small_grad[1],
         small_grad[2 : 2 + experts].T,
         grad_gate,

time: 548 us -> 505 us (0.922)
  Pallas kernels: 407 us -> 386 us
  local copies, waits for them, and re-layouts: 35.8 us -> 16.1 us
  matrix products: 81.1 us -> 71.9 us
  waiting for transfers between devices: 0.02 us -> 7.99 us
    pallas_call x8, Pallas kernels: 392 us -> 374 us  [call(): pl.pallas_call(kernel, out_shape=out_shape, in_specs=[anywhere if i in le...]
    ppermute x8, waiting for transfers between devices: 0.02 us -> 7.99 us  [swap_fsdp(): return lax.ppermute(value, 'fsdp', [(0, 1), (1, 0)])]
    squeeze x3 -> x1, local copies, waits for them, and re-layouts: 9.25 us -> 2.03 us  [shards(): gate_w = other_parts(lax.dynamic_index_in_dim(w_gate, here_ctx, 0, False))]
    slice x3 -> x0, local copies, waits for them, and re-layouts: 5.9 us -> none  [the longest x1 3.02 us: shards(): output_w = attn_full[:, 3 * heads_width:]]
    dot_general x8 -> x7, matrix products: 35.5 us -> 31 us  [t_mm(): lax.dot_general(left, right, (((0,), (0,)), ((), ())), preferred_element_...]
    pallas_call x3 -> x1, Pallas kernels: 14.6 us -> 12.1 us  [write_out(): pl.pallas_call(kernel, grid_spec=pltpu.PrefetchScalarGridSpec(num_scalar_...]
  transfers between devices with their start and end apart: 8 -> 8, of which waited for: 0 -> 1; matrix products, arithmetic and copies ran while one was open for 19% -> 16% of each run, Pallas kernels for 58% -> 62%
where the time goes in v6:
time: 505 us; the launch traced here: 500 us
  Pallas kernels  386 us (76%)
  matrix products  71.9 us (14%)
  local copies, waits for them, and re-layouts  16.1 us (3%)
  starting transfers between devices  10.5 us (2%)
  waiting for transfers between devices  7.99 us (2%)
  other arithmetic  6.24 us (1%)
    pallas_call x8, Pallas kernels, call(): pl.pallas_call(kernel, out_shape=out_shape, in_specs=[anywhere if i in le...  374 us
    dot_general x10, matrix products, mm(): return jnp.dot(left, right, preferred_element_type=F32)  31.5 us
    dot_general x7, matrix products, t_mm(): lax.dot_general(left, right, (((0,), (0,)), ((), ())), preferred_element_...  31 us
    pallas_call x1, Pallas kernels, write_out(): pl.pallas_call(kernel, grid_spec=pltpu.PrefetchScalarGridSpec(num_scalar_...  12.1 us
    ppermute x8, starting transfers between devices, swap_fsdp(): return lax.ppermute(value, 'fsdp', [(0, 1), (1, 0)])  10.5 us
  transfers between devices with their start and end apart: 8, of which 1 were waited for; matrix products, arithmetic and copies ran while one was open for 16% of the time, Pallas kernels for 62%

profile of v6, /device:TPU:0, one launch (start us, length us, event | category | flops | bytes accessed | tf_op | source)
XLA Modules:
  0.0 499.8 jit_solution(12759163154436965393)
XLA Ops:
  3.9 2.9 collective-permute-start.1
  7.1 2.0 dynamic-slice_bitcast_fusion.refs_3_
  9.1 2.1 collective-permute-start.2
  11.2 22.7 %gather_tp.1 = (bf16[256,2048]{1,0:T(8,128)(2,1)}, bf16[1024,1408]{1,0:T(8,128)(2,1)}, bf16[1024,1408]{1,0:T(8,128)(2,1)}) custom-call(bf16[256,512]{1,0:T(8,128)(2,1)} %hid.3, bf16[4,1024,1408]{2,1,0:T(8,128)(2,1)} %refs_0_.1, bf16[4,1024,1408]{2,1,0:T(8,128)(2,1)} %refs_1_.2), custom_call_target="tpu_custom_call" | custom-call | tf_op jit(solution)/shard_map/gather_tp/pallas_call | solution.py:189
  41.7 35.3 %first_norm.1 = (bf16[256,2048]{1,0:T(8,128)(2,1)}, f32[256,128]{1,0:T(8,128)}, bf16[256,2048]{1,0:T(8,128)(2,1)}, bf16[2048,1536]{1,0:T(8,128)(2,1)}, bf16[2048,512]{1,0:T(8,128)(2,1)}) custom-call(bf16[256,2048]{1,0:T(8,128)(2,1)} %get-tuple-element.72.refs_0_, bf16[256,512]{1,0:T(8,128)(2,1)} %refs_19_.1, f32[8,2048]{1,0:T(8,128)} %copy-done.19, ...), custom_call_target="tpu_custom_call" | custom-call | tf_op jit(solution)/shard_map/first_norm/pallas_call | solution.py:189
  76.9 6.1 %fusion.31.prj = f32[256,1536]{1,0:T(8,128)} fusion(bf16[256,2048]{1,0:T(8,128)(2,1)} %get-tuple-element.73, bf16[2048,1536]{1,0:T(8,128)(2,1)} %get-tuple-element.74), kind=kOutput, calls=%fused_computation.81 | convolution fusion | flops 1610612736 | bytes 8912896 | tf_op jit(solution)/shard_map/dot_general | solution.py:23
  83.0 21.8 %attention_forward.1 = (bf16[256,512]{1,0:T(8,128)(2,1)}, bf16[256,512]{1,0:T(8,128)(2,1)}, bf16[1024,1024]{1,0:T(8,128)(2,1)}) custom-call(f32[256,1536]{1,0:T(8,128)} %fusion.31.prj, f32[256,128]{1,0:T(8,128)} %pad_maximum_fusion.1.cs, f32[256,128]{1,0:T(8,128)} %get-tuple-element.133.sn), custom_call_target="tpu_custom_call" | custom-call | tf_op jit(solution)/shard_map/attention_forward/pallas_call | solution.py:189
  104.8 3.5 convolution_convert_fusion.5.prt
  108.3 2.3 convolution_convert_fusion.3.slb
  111.2 73.1 %second_norm.1 = (f32[256,512]{1,0:T(8,128)}, f32[256,128]{1,0:T(8,128)}, bf16[256,2048]{1,0:T(8,128)(2,1)}, bf16[640,2048]{1,0:T(8,128)(2,1)}, bf16[640,2048]{1...) custom-call(bf16[256,2048]{1,0:T(8,128)(2,1)} %convolution_convert_fusion.5.prt, ...), custom_call_target="tpu_custom_call" | custom-call | tf_op jit(solution)/shard_map/second_norm/pallas_call | solution.py:189
  185.2 1.4 constant_dynamic-slice_fusion.1
  186.6 2.2 fusion.32
  190.6 2.2 fusion.33
  193.3 4.0 convolution_add_fusion.2
  197.4 4.4 multiply_convert_fusion.3
  201.8 4.2 convolution_convert_fusion.2
  206.7 2.2 fusion.1
  208.9 8.0 %collective-permute-done.4.refs_8_ = bf16[1024,1408]{1,0:T(8,128)(2,1)} collective-permute-done((bf16[1024,1408]{1,0:T(8,128)(2,1)}, bf16[1024,1408]{1,0:T(8,128)(2,1)}, u32[]{:S(2)}, u32[]{:S(2)}) %collective-permute-start.4) | collective-permute-done | bytes 2883616 | tf_op jit(solution)/shard_map/ppermute | solution.py:1152
  216.9 6.8 %multiply_convert_fusion.1 = (bf16[640,1408]{1,0:T(8,128)(2,1)}, bf16[640,1408]{1,0:T(8,128)(2,1)S(1)}, f32[640]{0:T(1024)S(1)}) fusion(f32[640,1408]{1,0:T(8,128)S(1)} %convolution_add_fusion.2, f32[640]{0:T(1024)S(1)} %mul.92, f32[640,1408]{1,0:T(8,128)S(1)} %get-tuple-element.149, bf16[640,1408]{1,0:T(8,128)(2,1)S(1)} %get-tuple-element.95.refs_2_, ...), kind=kOutput, calls=%fused_computation.8 | convolution fusion | flops 1861713280 | bytes 20421124 | tf_op jit(solution)/shard_map/dot_general | solution.py:23
  223.7 4.0 convolution_convert_fusion.1
  227.7 2.1 collective-permute-start.6
  230.5 68.0 %second_norm_back.1 = (f32[256,512]{1,0:T(8,128)}, bf16[256,512]{1,0:T(8,128)(2,1)}, f32[8,512]{1,0:T(8,128)}, f32[8,256]{1,0:T(8,128)}, bf16[640,2048]{1,0:T(8,128)(2,1)}, /*index=5*/bf16[1024,1408]{1,0:T(8,128)(2,1)}) custom-call(bf16[640,1408]{1,0:T(8,128)(2,1)} %copy-done.10, bf16[640,1408]{1,0:T(8,128)(2,1)} %get-tuple-element.108.refs_1_, ...), custom_call_target="tpu_custom_call" | custom-call | tf_op jit(solution)/shard_map/second_norm_back/pallas_call | solution.py:189
  301.1 5.4 %add_convert_fusion.2.pay.refs_4_ = bf16[1024,1408]{1,0:T(8,128)(2,1)} fusion(bf16[1024,1408]{1,0:T(8,128)(2,1)} %collective-permute-done.5, bf16[640,1024]{1,0:T(8,128)(2,1)S(1)} %constant_dynamic-slice_fusion, bf16[640,1408]{1,0:T(8,128)(2,1)S(1)} %copy-done.13), kind=kOutput, calls=%fused_computation.3 | convolution fusion | flops 1849819136 | bytes 8880128 | tf_op jit(solution)/shard_map/dot_general | solution.py:31
  306.5 49.8 %attention_backward.1 = (bf16[256,2048]{1,0:T(8,128)(2,1)}, bf16[256,1536]{1,0:T(8,128)(2,1)}, bf16[3,256,1408]{2,1,0:T(8,128)(2,1)}) custom-call(bf16[256,512]{1,0:T(8,128)(2,1)} %get-tuple-element.91.lw, bf16[2048,512]{1,0:T(8,128)(2,1)} %get-tuple-element.76.wgt, bf16[256,512]{1,0:T(8,128)(2,1)} %get-tuple-element.92.qry, ...), custom_call_target="tpu_custom_call" | custom-call | tf_op jit(solution)/shard_map/attention_backward/pallas_call | solution.py:189
  356.3 6.0 %convolution_convert_fusion.6.prt = bf16[256,2048]{1,0:T(8,128)(2,1)} fusion(bf16[256,1536]{1,0:T(8,128)(2,1)} %get-tuple-element.101, bf16[2048,1536]{1,0:T(8,128)(2,1)} %get-tuple-element.74), kind=kOutput, calls=%fused_computation.19 | convolution fusion | flops 1611137024 | bytes 8126464 | tf_op jit(solution)/shard_map/dot_general | solution.py:27
  362.3 5.5 %add_convert_fusion.1.pay.refs_0_ = bf16[1024,1408]{1,0:T(8,128)(2,1)} fusion(bf16[1024,1408]{1,0:T(8,128)(2,1)} %collective-permute-done.6, bf16[640,1024]{1,0:T(8,128)(2,1)S(1)} %copy-done.15, bf16[640,1408]{1,0:T(8,128)(2,1)S(1)} %copy-done.11), kind=kOutput, calls=%fused_computation.2 | convolution fusion | flops 1849819136 | bytes 8880128 | tf_op jit(solution)/shard_map/dot_general | solution.py:31
  368.4 37.6 %first_norm_back.1 = (f32[256,512]{1,0:T(8,128)}, f32[8,512]{1,0:T(8,128)}, bf16[3,256,1408]{2,1,0:T(8,128)(2,1)}) custom-call(bf16[256,2048]{1,0:T(8,128)(2,1)} %convolution_convert_fusion.6.prt, bf16[256,512]{1,0:T(8,128)(2,1)} %hid.3, f32[256,128]{1,0:T(8,128)} %get-tuple-element.102.scl, f32[8,512]{1,0:T(8,128)} %broadcast_in_dim.57.gn, ...), custom_call_target="tpu_custom_call" | custom-call | tf_op jit(solution)/shard_map/first_norm_back/pallas_call | solution.py:189
  406.7 2.1 convolution_convert_fusion.4
  408.7 4.5 convolution_convert_fusion
  413.2 5.4 %add_convert_fusion.refs_3_.refs_2_ = bf16[1024,1408]{1,0:T(8,128)(2,1)} fusion(bf16[1024,1408]{1,0:T(8,128)(2,1)} %collective-permute-done.7, bf16[640,1024]{1,0:T(8,128)(2,1)S(1)} %copy-done.15, bf16[640,1408]{1,0:T(8,128)(2,1)S(1)} %copy-done.9), kind=kOutput, calls=%fused_computation.1 | convolution fusion | flops 1849819136 | bytes 8880128 | tf_op jit(solution)/shard_map/dot_general | solution.py:31
  419.3 65.5 %weight_grads.1 = (f32[256,2048]{1,0:T(8,128)}, f32[8,256]{1,0:T(8,128)}, bf16[256,512]{1,0:T(8,128)(2,1)}, bf16[3,256,1408]{2,1,0:T(8,128)(2,1)}) custom-call(bf16[2,4,256,1536]{3,2,1,0:T(8,128)(2,1)} %bitcast.51, bf16[2,4,256,512]{3,2,1,0:T(8,128)(2,1)} %bitcast.52, f32[8,512]{1,0:T(8,128)} %maximum_maximum_fusion.1.refs_2_, ...), custom_call_target="tpu_custom_call" | custom-call | tf_op jit(solution)/shard_map/weight_grads/pallas_call | solution.py:189
  487.5 12.1 %write_out.1 = (f32[4,256,1408]{2,1,0:T(8,128)}, f32[4,256,1408]{2,1,0:T(8,128)}, f32[4,256,1408]{2,1,0:T(8,128)}, f32[256,512]{1,0:T(8,128)}, f32[256,512]{1,0:...) custom-call(s32[1]{0:T(128)} %bitcast.rank, ...), custom_call_target="tpu_custom_call" | custom-call | bytes 25952256 | tf_op jit(solution)/shard_map/write_out/pallas_call | solution.py:1105
  (105 shorter events, 23.6 us)
Async XLA Ops:
  0.6 6.2 %copy-start.22 = (bf16[1024]{0:T(1024)(128)(2,1)S(1)}, bf16[1024]{0:T(1024)(128)(2,1)}, u32[]{:S(2)}) copy-start(bf16[1024]{0:T(1024)(128)(2,1)} %param.15) | copy-start | bytes 6148
  0.7 6.2 %copy-start.23 = (bf16[1024]{0:T(1024)(128)(2,1)S(1)}, bf16[1024]{0:T(1024)(128)(2,1)}, u32[]{:S(2)}) copy-start(bf16[1024]{0:T(1024)(128)(2,1)} %param.20) | copy-start | bytes 6148
  0.7 6.3 %copy-start.20 = (bf16[1024,4]{0,1:T(4,128)(2,1)S(1)}, bf16[1024,4]{0,1:T(4,128)(2,1)}, u32[]{:S(2)}) copy-start(bf16[1024,4]{0,1:T(4,128)(2,1)} %param.21) | copy-start | bytes 24580
  3.9 37.7 %collective-permute-start.1 = (bf16[256,2048]{1,0:T(8,128)(2,1)}, bf16[256,2048]{1,0:T(8,128)(2,1)}, u32[]{:S(2)}, u32[]{:S(2)}) collective-permute-start(bf16[256,2048]{1,0:T(8,128)(2,1)} %pad_maximum_fusion), channel_id=1, source_target_pairs={{0,16},{16,0},{1,17},{17,1},{2,18},{18,2},{3,19},{19,3},{4,20},{20... | collective-permute-start | bytes 3145736 | tf_op jit(solution)/shard_map/ppermute | solution.py:1152
  7.1 33.7 %collective-permute-start = (bf16[8,1024]{1,0:T(8,128)(2,1)S(1)}, bf16[8,1024]{1,0:T(8,128)(2,1)S(1)}, u32[]{:S(2)}, u32[]{:S(2)}) collective-permute-start(bf16[8,1024]{1,0:T(8,128)(2,1)S(1)} %maximum_maximum_fusion), channel_id=1, source_target_pairs={{0,16},{16,0},{1,17},{17,1},{2,18},{18,2},{3,19},{19,3},{4,20},{20... | collective-permute-start | bytes 49160 | tf_op jit(solution)/shard_map/ppermute | solution.py:1152
  9.1 177.5 %copy-start = (bf16[1024,1408]{1,0:T(8,128)(2,1)}, bf16[1024,1408]{1,0:T(8,128)(2,1)S(1)}, u32[]{:S(2)}) copy-start(bf16[1024,1408]{1,0:T(8,128)(2,1)S(1)} %dynamic-slice_bitcast_fusion.refs_3_) | copy-start | bytes 8650756
  9.1 27.0 %copy-start.21 = (s32[256,2]{0,1:T(2,128)S(1)}, s32[256,2]{0,1:T(2,128)}, u32[]{:S(2)}) copy-start(s32[256,2]{0,1:T(2,128)} %param.25) | copy-start | bytes 6148
  9.1 183.7 %collective-permute-start.2 = (bf16[1024,1408]{1,0:T(8,128)(2,1)S(1)}, bf16[1024,1408]{1,0:T(8,128)(2,1)}, u32[]{:S(2)}, u32[]{:S(2)}) collective-permute-start(bf16[1024,1408]{1,0:T(8,128)(2,1)S(1)} %dynamic-slice_bitcast_fusion.refs_3_), channel_id=1, source_target_pairs={{0,16},{16,0},{1,17},{17,1},{2,18},{18,2},{3,19},{19,3},{4,20},{20... | collective-permute-start | bytes 8650760 | tf_op jit(solution)/shard_map/ppermute | solution.py:1152
  34.0 163.4 %collective-permute-start.3 = (bf16[1024,1408]{1,0:T(8,128)(2,1)}, bf16[1024,1408]{1,0:T(8,128)(2,1)}, u32[]{:S(2)}, u32[]{:S(2)}) collective-permute-start(bf16[1024,1408]{1,0:T(8,128)(2,1)} %get-tuple-element.81.refs_5_), channel_id=1, source_target_pairs={{0,16},{16,0},{1,17},{17,1},{2,18},{18,2},{3,19},{19,3},{4,20},{20... | collective-permute-start | bytes 8650760 | tf_op jit(solution)/shard_map/ppermute | solution.py:1152
  34.8 182.1 %collective-permute-start.4 = (bf16[1024,1408]{1,0:T(8,128)(2,1)}, bf16[1024,1408]{1,0:T(8,128)(2,1)}, u32[]{:S(2)}, u32[]{:S(2)}) collective-permute-start(bf16[1024,1408]{1,0:T(8,128)(2,1)} %get-tuple-element.83.refs_7_), channel_id=1, source_target_pairs={{0,16},{16,0},{1,17},{17,1},{2,18},{18,2},{3,19},{19,3},{4,20},{20... | collective-permute-start | bytes 8650760 | tf_op jit(solution)/shard_map/ppermute | solution.py:1152
  40.9 0.8 copy-start.19
  104.8 3.5 copy-start.16
  186.6 2.7 copy-start.14
  186.6 2.2 copy-start.7
  188.8 1.8 copy-start.5
  190.6 11.2 %copy-start.2 = (bf16[640,2048]{1,0:T(8,128)(2,1)}, bf16[640,2048]{1,0:T(8,128)(2,1)S(1)}, u32[]{:S(2)}) copy-start(bf16[640,2048]{1,0:T(8,128)(2,1)S(1)} %multiply_convert_fusion) | copy-start | bytes 7864324
  190.6 2.7 copy-start.1
  201.8 15.1 %copy-start.12 = (bf16[640,1408]{1,0:T(8,128)(2,1)}, bf16[640,1408]{1,0:T(8,128)(2,1)S(1)}, u32[]{:S(2)}) copy-start(bf16[640,1408]{1,0:T(8,128)(2,1)S(1)} %get-tuple-element.95.refs_2_) | copy-start | bytes 5406724
  201.8 4.9 copy-start.6
  206.0 95.1 %collective-permute-start.5 = (bf16[1024,1408]{1,0:T(8,128)(2,1)}, bf16[1024,1408]{1,0:T(8,128)(2,1)}, u32[]{:S(2)}, u32[]{:S(2)}) collective-permute-start(bf16[1024,1408]{1,0:T(8,128)(2,1)} %convolution_convert_fusion.2), channel_id=1, source_target_pairs={{0,16},{16,0},{1,17},{17,1},{2,18},{18,2},{3,19},{19,3},{4,20},{20... | collective-permute-start | bytes 8650760 | tf_op jit(solution)/shard_map/ppermute | solution.py:1152
  223.7 4.0 copy-start.10
  227.7 128.6 %collective-permute-start.6 = (bf16[1024,1408]{1,0:T(8,128)(2,1)}, bf16[1024,1408]{1,0:T(8,128)(2,1)}, u32[]{:S(2)}, u32[]{:S(2)}) collective-permute-start(bf16[1024,1408]{1,0:T(8,128)(2,1)} %convolution_convert_fusion.1), channel_id=1, source_target_pairs={{0,16},{16,0},{1,17},{17,1},{2,18},{18,2},{3,19},{19,3},{4,20},{20... | collective-permute-start | bytes 8650760 | tf_op jit(solution)/shard_map/ppermute | solution.py:1152
  230.5 68.6 %copy-start.3 = (bf16[640,2048]{1,0:T(8,128)(2,1)S(1)}, bf16[640,2048]{1,0:T(8,128)(2,1)}, u32[]{:S(2)}) copy-start(bf16[640,2048]{1,0:T(8,128)(2,1)} %copy-done.2) | copy-start | bytes 7864324
  298.5 2.6 copy-start.13
  298.6 114.7 %collective-permute-start.7 = (bf16[1024,1408]{1,0:T(8,128)(2,1)}, bf16[1024,1408]{1,0:T(8,128)(2,1)}, u32[]{:S(2)}, u32[]{:S(2)}) collective-permute-start(bf16[1024,1408]{1,0:T(8,128)(2,1)} %get-tuple-element.106), channel_id=1, source_target_pairs={{0,16},{16,0},{1,17},{17,1},{2,18},{18,2},{3,19},{19,3},{4,20},{20... | collective-permute-start | bytes 8650760 | tf_op jit(solution)/shard_map/ppermute | solution.py:1152
  356.3 6.0 %copy-start.11 = (bf16[640,1408]{1,0:T(8,128)(2,1)S(1)}, bf16[640,1408]{1,0:T(8,128)(2,1)}, u32[]{:S(2)}) copy-start(bf16[640,1408]{1,0:T(8,128)(2,1)} %copy-done.10) | copy-start | bytes 5406724
  356.3 6.0 %copy-start.15 = (bf16[640,1024]{1,0:T(8,128)(2,1)S(1)}, bf16[640,1024]{1,0:T(8,128)(2,1)}, u32[]{:S(2)}) copy-start(bf16[640,1024]{1,0:T(8,128)(2,1)} %copy-done.14) | copy-start | bytes 3932164
  367.7 38.9 %copy-start.4 = (bf16[256,2048]{1,0:T(8,128)(2,1)S(1)}, bf16[256,2048]{1,0:T(8,128)(2,1)}, u32[]{:S(2)}) copy-start(bf16[256,2048]{1,0:T(8,128)(2,1)} %get-tuple-element.110) | copy-start | bytes 3145732
  367.8 38.9 %copy-start.17 = (bf16[256,512]{1,0:T(8,128)(2,1)S(1)}, bf16[256,512]{1,0:T(8,128)(2,1)}, u32[]{:S(2)}) copy-start(bf16[256,512]{1,0:T(8,128)(2,1)} %get-tuple-element.75) | copy-start | bytes 786436
  406.7 2.1 copy-start.8
  406.7 2.1 copy-start.18
  408.7 4.5 copy-start.9

commit v7 on v6

--- a/solution.py
+++ b/solution.py
@@ -108,12 +108,108 @@
         copy.wait()
 
 
-def spread(mine, out, n_ctx, sems, order=(2, 1, 3)):
-    cut = mine.shape[0] // n_ctx
-    return [
-        send(mine.at[stretch(peer("ctx", n_ctx, k), cut), :], out.at[k - 1], "ctx", n_ctx, k, sems)
-        for k in order
-    ]
+class Payload:
+
+    def __init__(self, n_ctx, rows=None, product=None):
+        self.n_ctx = n_ctx
+        self.product = product is not None
+        self.inputs = list(product) if self.product else [rows]
+        last = self.inputs[-1]
+        self.rows, self.hidden = last.shape
+        self.cut = self.rows // n_ctx
+        self.outs = [shape((n_ctx - 1, self.cut, self.hidden), BF)]
+        self.scratch = pair_of_sems(n_ctx)
+        if self.product:
+            self.outs.append(shape((self.cut, self.hidden), BF))
+            self.scratch += [
+                pltpu.VMEM((self.rows, self.hidden), BF),
+                pltpu.VMEM((self.rows, self.hidden), BF),
+                DMA,
+            ]
+
+    def take(self, ins, outs, scratch):
+        self.ins, self.out_refs, self.held = ins, outs, scratch
+
+    def load(self):
+        if self.product:
+            pltpu.make_async_copy(self.ins[2], self.held[2], self.held[4]).start()
+
+    def copy(self, k):
+        to = peer("ctx", self.n_ctx, k)
+        source = self.held[3] if self.product else self.ins[0]
+        return described(
+            source.at[stretch(to, self.cut), :], self.out_refs[0].at[k - 1],
+            self.held[0:2], k - 1, {"ctx": to},
+        )
+
+    def go(self, first=0, last=4):
+        n_ctx, cut = self.n_ctx, self.cut
+        if not self.product:
+            for j in range(first, last):
+                if (j + 2) % n_ctx:
+                    self.copy((j + 2) % n_ctx).start()
+            return
+        left, right, other = self.ins
+        if first == 0:
+            pltpu.make_async_copy(other, self.held[2], self.held[4]).wait()
+        base = lax.axis_index("fsdp") * self.rows
+
+        @pl.loop(first, last)
+        def _(j):
+            k = lax.rem(j + 2, n_ctx)
+            to = peer("ctx", n_ctx, k)
+            value = t_mm(left[:, pl.ds(pl.multiple_of(base + to * cut, 128), cut)], right[...])
+            value = value + self.held[2][stretch(to, cut), :].astype(F32)
+            self.held[3][stretch(to, cut), :] = value.astype(BF)
+
+            @pl.when(j != n_ctx - 2)
+            def _():
+                self.copy(k).start()
+
+    def wait(self):
+        if self.product:
+            self.out_refs[1][...] = self.held[3][stretch(lax.axis_index("ctx"), self.cut), :]
+        for k in range(1, self.n_ctx):
+            self.copy(k).wait()
+
+
+class RowSums:
+
+    def __init__(self, made, first, count, n_tp):
+        self.n_tp, self.first = n_tp, first
+        self.shape = (count, made.shape[1] // n_tp)
+        self.scratch = [
+            pltpu.VMEM((n_tp - 1, *self.shape), BF),
+            pltpu.VMEM(self.shape, BF),
+            DMA,
+        ] + pair_of_sems(n_tp)
+
+    def take(self, made, scratch):
+        self.made, self.held = made, scratch
+
+    def rows(self, rank):
+        return self.made.at[pl.ds(self.first, self.shape[0]), columns(rank, self.shape[1])]
+
+    def mine(self):
+        return pltpu.make_async_copy(
+            self.rows(lax.axis_index("tp")), self.held[1], self.held[2]
+        )
+
+    def start(self):
+        self.mine().start()
+        n = self.n_tp
+        self.copies = [
+            send(self.rows(peer("tp", n, k)), self.held[0].at[k - 1], "tp", n, k, self.held[3:5])
+            for k in range(1, n)
+        ]
+
+    def total(self):
+        self.mine().wait()
+        finish(self.copies)
+        value = self.held[1][...].astype(F32)
+        for k in range(1, self.n_tp):
+            value = value + self.held[0][k - 1].astype(F32)
+        return value
 
 
 def quad():
@@ -200,10 +296,6 @@
 
 def shape(dims, dtype):
     return jax.ShapeDtypeStruct(dims, dtype)
-
-
-def came_shape(payload, n_ctx):
-    return shape((n_ctx - 1, payload.shape[0] // n_ctx, payload.shape[1]), payload.dtype)
 
 
 def pair_of_sems(n):
@@ -430,7 +522,7 @@
         logit_copies = [
             send(mine_two, sums_two.at[k - 1], "tp", n_tp, k, sems[12:14]) for k in range(1, n_tp)
         ]
-        copies = gather_columns(low, out, "tp", n_tp, sems[4:6])
+        gather_columns(low, out, "tp", n_tp, sems[4:6])
 
         def route():
             finish(logit_copies)
@@ -461,24 +553,34 @@
                     send(own_gates.at[k], slot_gates.at[k], "ctx", n_ctx, k, sems[10:12])
                 )
 
+
+        def slab(k, step):
+            at = columns(peer("tp", n_tp, n_tp - step), size)
+            return described(
+                sent.at[step, pl.ds(k * CAP, CAP)], tokens.at[pl.ds(k * CAP, CAP), at],
+                sems[8:10], step * n_ctx + k, {"ctx": peer("ctx", n_ctx, k)},
+            )
+
+        def dispatch(step, block):
+            sent[step] = mm(pck[...], block).astype(BF)
+            tokens[0:CAP, columns(peer("tp", n_tp, n_tp - step), size)] = sent[step, 0:CAP]
+            for k in (2, 3, 1):
+                slab(k, step).start()
+
+        dispatch(0, low[...])
+        route()
+
+        @pl.loop(1, n_tp)
+        def _(step):
+            place = out.at[:, columns(here, size)]
+            described(
+                low, place, sems[4:6], step - 1, {"tp": peer("tp", n_tp, step)}
+            ).wait()
+            dispatch(step, out[:, columns(peer("tp", n_tp, n_tp - step), size)])
+
         for step in range(n_tp):
-            at = columns(peer("tp", n_tp, n_tp - step), size)
-            if step:
-                copies[step - 1].wait()
-                block = out[:, at]
-            else:
-                block = low[...]
-            sent[step] = mm(pck[...], block).astype(BF)
-            tokens[0:CAP, at] = sent[step, 0:CAP]
             for k in (2, 3, 1):
-                others.append(
-                    remote(
-                        sent.at[step, pl.ds(k * CAP, CAP)], tokens.at[pl.ds(k * CAP, CAP), at],
-                        sems[8:10], step * n_ctx + k, {"ctx": peer("ctx", n_ctx, k)},
-                    )
-                )
-            if step == 0:
-                route()
+                slab(k, step).wait()
         finish(others)
 
     return call(
@@ -530,15 +632,16 @@
         wgt = [refs[3 + i * count : 3 + (i + 1) * count] for i in range(3)]
         refs = refs[3 + 3 * count :]
         tok, dts, pck, gts, one, nms, rtr, rsd, scl, gn, grd = refs[:11]
-        d_resid, low, d_gain, d_logits, out_back = refs[11:16]
+        d_resid, low, d_gain, d_logits, out_rows = refs[11:16]
         refs = refs[16:]
         if count == 2:
             up_away, up_held, up_sem = refs[:1] + refs[1:3]
             refs = refs[3:]
         (
             drw, eo, buffer, back, back_dots, parts, slots, mine, sums, mine_two, sums_two, loads,
-        ) = refs[:12]
-        sems = refs[12:]
+            out_sem,
+        ) = refs[:13]
+        sems = refs[13:]
         here = lax.axis_index("tp")
         first = lax.axis_index("fsdp")
 
@@ -617,14 +720,7 @@
 
             eo[:, columns(rank, size)] = mm_t(hid[...], buffer[slot, 0]).astype(BF)
 
-        moved = [
-            send(
-                eo.at[pl.ds(k * CAP, CAP)], out_back.at[pl.ds(k * CAP, CAP)],
-                "ctx", n_ctx, n_ctx - k, sems[10:12],
-            )
-            for k in range(1, n_ctx)
-        ]
-        out_back[0:CAP] = eo[0:CAP]
+        pltpu.make_async_copy(eo, out_rows, out_sem).start()
         if count == 2:
 
             @pl.loop(0, part // 256)
@@ -652,8 +748,8 @@
         mean = gate[0] * both[0] + gate[1] * both[1]
         logits = sum(gate[j] * (both[j] - mean) * one[j] for j in range(2))
         d_logits[...] = logits
-        copies = []
-        for step in range(1, n_tp + 1):
+
+        def combined(step):
             rank = peer("tp", n_tp, step)
             at = columns(rank, size)
             for k in (2, 3, 1):
@@ -661,13 +757,21 @@
             block = t_mm(pck[0:CAP], drw[0:CAP, at])
             for k in range(1, experts):
                 block = block + t_mm(pck[k * CAP : (k + 1) * CAP], back[k - 1, :, at])
-            if step < n_tp:
-                parts[step - 1] = block.astype(BF)
-                copies.append(
-                    send(parts.at[step - 1], slots.at[step - 1], "tp", n_tp, step, sems[6:8])
-                )
-            else:
-                total = block
+            return block
+
+        def give(step):
+            return described(
+                parts.at[step - 1], slots.at[step - 1], sems[6:8], step - 1,
+                {"tp": peer("tp", n_tp, step)},
+            )
+
+        @pl.loop(1, n_tp)
+        def _(step):
+            parts[step - 1] = combined(step).astype(BF)
+            give(step).start()
+
+        copies = [give(step) for step in range(1, n_tp)]
+        total = combined(n_tp)
         total = total + lax.dot_general(
             logits.astype(BF),
             rtr[...].astype(BF),
@@ -687,7 +791,7 @@
         result = grd[...].astype(F32) + factor * (d_resid[...] - rsd[...] * factor * dot)
         d_resid[...] = result
         low[...] = result.astype(BF)
-        finish(moved)
+        pltpu.make_async_copy(eo, out_rows, out_sem).wait()
         if count == 2:
             pltpu.make_async_copy(up_held, up_away, up_sem).wait()
 
@@ -721,32 +825,48 @@
             pltpu.VMEM((8, rows), F32),
             pltpu.VMEM((n_tp - 1, 8, rows), F32),
             DMA((2, 2)),
+            DMA,
         ]
         + pair_of_sems(n_ctx)
         + pair_of_sems(n_tp * n_ctx)
-        + pair_of_sems(n_tp) * 3
-        + pair_of_sems(n_ctx),
+        + pair_of_sems(n_tp) * 3,
         4,
         "second_norm_back",
-        left=tuple(range(3, 3 + 3 * count)) + ((-1,) if count == 2 else ()),
-    )
-
-
-def attention_backward(low, output_w, query, kv, cosine, sine, payload, n_tp, n_ctx):
+        left=tuple(range(3, 3 + 3 * count)) + ((-2, -1) if count == 2 else (-1,)),
+    )
+
+
+def attention_backward(
+    low, output_w, query, kv, cosine, sine, sums, payload, n_tp, n_ctx
+):
     rows, size = low.shape
     width = size * n_tp
     inner = query.shape[1]
     heads = inner // HD
     scale = 1.0 / math.sqrt(HD)
 
-    def kernel(
-        lw, wgt, qry, full, cs, sn, pay, d_attn, d_qkv, came, dot, dqs, dkv, slots, last, both, total, kept, *sems
-    ):
+    half = heads // 2
+    sums, sums_input = sums
+    lane = 2 * half * HD
+
+    def kernel(*refs):
+        lw, wgt, qry, full, cs, sn, made = refs[:7]
+        n_in, n_out = 7 + len(payload.inputs), len(payload.outs)
+        d_attn, d_qkv, summed = refs[n_in : n_in + 3]
+        scratch = refs[n_in + 3 + n_out :]
+        dot, dqs, dkv, slots, last, both, total, kept = scratch[:8]
+        sems = scratch[8:12]
+        sums.take(made, scratch[12 : 12 + len(sums.scratch)])
+        payload.take(
+            refs[7:n_in], refs[n_in + 3 : n_in + 3 + n_out], scratch[12 + len(sums.scratch) :]
+        )
+        payload.load()
         greet([("tp", n_tp), ("ctx", n_ctx)])
         here, beside, across = quad()
         beyond = lax.rem(beside + 2, 4)
         copies = gather_columns(lw, d_attn, "tp", n_tp, sems[2:4])
-        moved = spread(pay, came, n_ctx, sems[4:6])
+        sums.start()
+        payload.go()
 
         @pl.loop(0, heads)
         def _(h):
@@ -762,50 +882,79 @@
             else:
                 total[...] = mm(lw[...], weights)
         dot[...] = total[...].astype(BF)
-
-        @pl.loop(0, heads)
-        def _(h):
-            at, at_v = columns(h, HD), columns(h + heads, HD)
-            probs = kept[h]
-            d_probs = mm_t(dot[:, at], full[:, at_v])
-            delta = jnp.sum(probs * d_probs, axis=-1, keepdims=True)
-            d_scores = (probs * (d_probs - delta)).astype(BF)
-            dqs[:, at] = mm(d_scores, full[:, at]) * scale
-            dkv[:, at] = (t_mm(d_scores, qry[:, at]) * scale).astype(BF)
-            dkv[:, at_v] = t_mm(probs.astype(BF), dot[:, at]).astype(BF)
-
-        first = remote(dkv.at[stretch(beyond, rows), :], slots.at[0], sems, 0, {"ctx": beside})
-        second = remote(dkv.at[stretch(beside, rows), :], slots.at[1], sems, 1, {"ctx": beside})
-        first.wait()
-        both[...] = (
-            dkv[stretch(across, rows), :].astype(F32) + slots[0].astype(F32)
-        ).astype(BF)
-        third = remote(both, last, sems, 2, {"ctx": across})
+        first, second, third = [], [], []
+        for j in range(2):
+
+            @pl.loop(0, half)
+            def _(i):
+                h = j * half + i
+                at, at_v = columns(h, HD), columns(h + heads, HD)
+                key_at = pl.ds(pl.multiple_of(j * lane + i * HD, 128), HD)
+                value_at = pl.ds(pl.multiple_of(j * lane + (half + i) * HD, 128), HD)
+                probs = kept[h]
+                d_probs = mm_t(dot[:, at], full[:, at_v])
+                delta = jnp.sum(probs * d_probs, axis=-1, keepdims=True)
+                d_scores = (probs * (d_probs - delta)).astype(BF)
+                dqs[:, at] = mm(d_scores, full[:, at]) * scale
+                dkv[:, key_at] = (t_mm(d_scores, qry[:, at]) * scale).astype(BF)
+                dkv[:, value_at] = t_mm(probs.astype(BF), dot[:, at]).astype(BF)
+
+            at = pl.ds(j * lane, lane)
+            first.append(
+                remote(
+                    dkv.at[stretch(beyond, rows), at], slots.at[0, :, at],
+                    sems, 3 * j, {"ctx": beside},
+                )
+            )
+            second.append(
+                remote(
+                    dkv.at[stretch(beside, rows), at], slots.at[1, :, at],
+                    sems, 3 * j + 1, {"ctx": beside},
+                )
+            )
+        for j in range(2):
+            at = pl.ds(j * lane, lane)
+            first[j].wait()
+            both[:, at] = (
+                dkv[stretch(across, rows), at].astype(F32) + slots[0, :, at].astype(F32)
+            ).astype(BF)
+            third.append(
+                remote(both.at[:, at], last.at[:, at], sems, 3 * j + 2, {"ctx": across})
+            )
 
         @pl.loop(0, heads)
         def _(h):
             d_qkv[:, columns(h, HD)] = turn(dqs[:, columns(h, HD)], cs[...], sn[...]).astype(BF)
 
-        second.wait()
-        third.wait()
-
-        @pl.loop(0, heads)
-        def _(h):
-            at, at_v = columns(h, HD), columns(h + heads, HD)
-            mine = stretch(here, rows)
-            d_key = dkv[mine, at].astype(F32) + slots[1, :, at].astype(F32)
-            d_key = d_key + last[:, at].astype(F32)
-            d_qkv[:, columns(h + heads, HD)] = turn(d_key, cs[...], sn[...]).astype(BF)
-            d_value = dkv[mine, at_v].astype(F32) + slots[1, :, at_v].astype(F32)
-            d_value = d_value + last[:, at_v].astype(F32)
-            d_qkv[:, columns(h + 2 * heads, HD)] = d_value.astype(BF)
-
-        finish(moved)
+        for j in range(2):
+            second[j].wait()
+            third[j].wait()
+
+            @pl.loop(0, half)
+            def _(i):
+                h = j * half + i
+                key_at = pl.ds(pl.multiple_of(j * lane + i * HD, 128), HD)
+                value_at = pl.ds(pl.multiple_of(j * lane + (half + i) * HD, 128), HD)
+                mine = stretch(here, rows)
+                d_key = dkv[mine, key_at].astype(F32) + slots[1, :, key_at].astype(F32)
+                d_key = d_key + last[:, key_at].astype(F32)
+                d_qkv[:, columns(h + heads, HD)] = turn(d_key, cs[...], sn[...]).astype(BF)
+                d_value = dkv[mine, value_at].astype(F32) + slots[1, :, value_at].astype(F32)
+                d_value = d_value + last[:, value_at].astype(F32)
+                d_qkv[:, columns(h + 2 * heads, HD)] = d_value.astype(BF)
+
+        summed[...] = sums.total().astype(BF)
+        payload.wait()
 
     return call(
         kernel,
-        (shape((rows, width), BF), shape((rows, 3 * inner), BF), came_shape(payload, n_ctx)),
-        (low, output_w, query, kv, cosine, sine, payload),
+        (
+            shape((rows, width), BF),
+            shape((rows, 3 * inner), BF),
+            shape(sums.shape, BF),
+            *payload.outs,
+        ),
+        (low, output_w, query, kv, cosine, sine, sums_input, *payload.inputs),
         [
             pltpu.VMEM((rows, inner), BF),
             pltpu.VMEM((rows, inner), F32),
@@ -816,26 +965,58 @@
             pltpu.VMEM((rows, inner), F32),
             pltpu.VMEM((heads, rows, rows * n_ctx), F32),
         ]
-        + pair_of_sems(3)
+        + pair_of_sems(6)
         + pair_of_sems(n_tp)
-        + pair_of_sems(n_ctx),
+        + sums.scratch
+        + payload.scratch,
         5,
         "attention_backward",
-        left=(6, -1),
-    )
-
-
-def first_norm_back(part, hidden, scale, gain, d_resid, payload, n_tp, n_ctx):
+        left=(6, 6 + len(payload.inputs), -len(payload.outs)),
+    )
+
+
+def first_norm_back(d_qkv, weights, hidden, scale, gain, d_resid, payload, n_tp, n_ctx):
     rows, size = hidden.shape
     width = size * n_tp
 
-    def kernel(prt, hid, scl, gn, dr, pay, out, d_gain, came, slots, mine, sums, *sems):
+    def kernel(*refs):
+        dpr, wgt, hid, scl, gn, dr = refs[:6]
+        n_in, n_out = 6 + len(payload.inputs), len(payload.outs)
+        out, d_gain = refs[n_in : n_in + 2]
+        scratch = refs[n_in + 2 + n_out :]
+        held, parts, slots, mine, sums, loads = scratch[:6]
+        sems = scratch[6:10]
+        payload.take(refs[6:n_in], refs[n_in + 2 : n_in + 2 + n_out], scratch[10:])
+
+        def block(step):
+            rank = peer("tp", n_tp, step)
+            return pltpu.make_async_copy(
+                wgt.at[stretch(rank, size), :], held.at[step - 1], loads.at[step - 1]
+            )
+
+        for step in range(1, n_tp + 1):
+            block(step).start()
+        payload.load()
         greet([("tp", n_tp), ("ctx", n_ctx)])
-        here = lax.axis_index("tp")
-        copies = scatter_columns(prt, slots, "tp", n_tp, sems[0:2])
-        moved = spread(pay, came, n_ctx, sems[4:6])
-        total = prt[:, columns(here, size)].astype(F32)
+
+        def give(step):
+            return described(
+                parts.at[step - 1], slots.at[step - 1], sems[0:2], step - 1,
+                {"tp": peer("tp", n_tp, step)},
+            )
+
+        @pl.loop(1, n_tp)
+        def _(step):
+            block(step).wait()
+            parts[step - 1] = mm_t(dpr[...], held[step - 1]).astype(BF)
+            give(step).start()
+
+        copies = [give(step) for step in range(1, n_tp)]
+        block(n_tp).wait()
+        out[...] = mm_t(dpr[...], held[n_tp - 1])
+        payload.go()
         finish(copies)
+        total = out[...]
         for k in range(1, n_tp):
             total = total + slots[k - 1].astype(F32)
         factor = scl[:, 0:1]
@@ -847,40 +1028,97 @@
         dot = as_column(dot, eighth())[:, 0:1] * (1.0 / width)
         unit = hid[...].astype(F32) * factor
         out[...] = dr[...] + factor * (out[...] - unit * dot)
-        finish(moved)
+        payload.wait()
 
     return call(
         kernel,
-        (shape((rows, size), F32), shape((8, size), F32), came_shape(payload, n_ctx)),
-        (part, hidden, scale, gain, d_resid, payload),
+        (shape((rows, size), F32), shape((8, size), F32), *payload.outs),
+        (d_qkv, weights, hidden, scale, gain, d_resid, *payload.inputs),
         [
+            pltpu.VMEM((n_tp, size, d_qkv.shape[1]), BF),
+            pltpu.VMEM((n_tp - 1, rows, size), BF),
             pltpu.VMEM((n_tp - 1, rows, size), BF),
             pltpu.VMEM((8, rows), F32),
             pltpu.VMEM((n_tp - 1, 8, rows), F32),
+            DMA((n_tp,)),
         ]
         + pair_of_sems(n_tp) * 2
-        + pair_of_sems(n_ctx),
+        + payload.scratch,
         6,
         "first_norm_back",
-        left=(5, -1),
-    )
-
-
-def weight_grads(parts, groups, small, payload, back, picks, mix, resid, n_tp, n_ctx):
-    tokens, block_size = resid.shape
-    experts = n_ctx
-    rows = parts[0].shape[2]
-    width = small.shape[1] * n_tp
+        left=(1, 5 + len(payload.inputs), -len(payload.outs)),
+    )
+
+
+class ExpertsOut:
+
+    def __init__(self, made, done, picks, mix, resid, n_tp, n_ctx):
+        self.n_ctx = n_ctx
+        self.sums = RowSums(made, done.shape[0], made.shape[0] - done.shape[0], n_tp)
+        self.inputs = [made, done, picks, mix, resid]
+        self.size = resid.shape[1]
+        self.out = shape(resid.shape, BF)
+        self.scratch = [
+            pltpu.VMEM(self.sums.shape, BF),
+            pltpu.VMEM((n_ctx - 1, CAP, self.size), BF),
+        ]
+        self.scratch += pair_of_sems(n_ctx) + self.sums.scratch
+
+    def take(self, ins, out, scratch):
+        self.ins, self.out_ref, self.held = ins, out, scratch[:4]
+        self.sums.take(ins[0], scratch[4:])
+
+    def block(self, k):
+        done, share = self.ins[1], self.held[0]
+        first = k * CAP
+        if first < done.shape[0]:
+            return done.at[pl.ds(first, CAP)]
+        return share.at[pl.ds(first - done.shape[0], CAP)]
+
+    def give_back(self):
+        share, back = self.held[:2]
+        share[...] = self.sums.total().astype(BF)
+        n_ctx = self.n_ctx
+        self.copies = [
+            send(self.block(k), back.at[k - 1], "ctx", n_ctx, n_ctx - k, self.held[2:4])
+            for k in range(1, n_ctx)
+        ]
+
+    def mix(self):
+        made, done, picks, mix, resid = self.ins
+        back = self.held[1]
+        finish(self.copies)
+        order = lax.broadcasted_iota(jnp.int32, (8, 128), 0)
+        total = resid[...]
+        for k in range(self.n_ctx):
+            gate = as_column(mix[...], jnp.where(order == k, 1.0, 0.0))[:, 0:1]
+            rows = self.block(0)[...] if k == 0 else back[k - 1]
+            total = total + gate * t_mm(picks[k * CAP : (k + 1) * CAP], rows)
+        self.out_ref[...] = total.astype(BF)
+
+
+def weight_grads(products, groups, small, payload, experts_out, n_tp, n_ctx):
+    width = products[0][0].shape[1]
     places = 2 * n_ctx
     cut = width // places
-    total_columns = sum(size for _, _, size, _ in groups)
+    total_columns = sum(size for _, _, size in groups)
+    flat = [array for pair in products for array in pair]
+    inputs = [*flat, small, *experts_out.inputs, *payload.inputs]
 
     def kernel(*refs):
-        prts, refs = refs[: len(parts)], refs[len(parts) :]
-        sml, pay, bck, pck, mx, rsd, out, small_out, block_out, came = refs[:10]
-        sml_full, sml_slots, mixed, shares, share_slots = refs[10:15]
-        refs = refs[15:]
-        scratch, sems = refs[: 5 * len(groups)], refs[5 * len(groups) :]
+        factors, refs = refs[: len(flat)], refs[len(flat) :]
+        sml, refs = refs[0], refs[1:]
+        given, refs = refs[: len(experts_out.inputs)], refs[len(experts_out.inputs) :]
+        paid, refs = refs[: len(payload.inputs)], refs[len(payload.inputs) :]
+        out, small_out, block_out = refs[:3]
+        paid_out, refs = refs[3 : 3 + len(payload.outs)], refs[3 + len(payload.outs) :]
+        sml_full, sml_slots, refs = refs[0], refs[1], refs[2:]
+        scratch, refs = refs[: 6 * len(groups)], refs[6 * len(groups) :]
+        experts_out.take(given, block_out, refs[: len(experts_out.scratch)])
+        refs = refs[len(experts_out.scratch) :]
+        payload.take(paid, paid_out, refs[: len(payload.scratch)])
+        sems = refs[len(payload.scratch) :]
+        payload.load()
         barrier = pltpu.get_barrier_semaphore()
         here, beside, across = quad()
         beyond = lax.rem(beside + 2, 4)
@@ -896,223 +1134,202 @@
             pl.semaphore_signal(barrier, inc=1, device_id=device, device_id_type=MESH)
         pl.semaphore_wait(barrier, n_tp - 1 + places - 1)
         gathers = gather_columns(sml, sml_full, "tp", n_tp, sems[0:2])
-        moved = spread(pay, came, n_ctx, sems[4:6], (2,))
+        experts_out.sums.start()
         moves = []
-        for g, (which, first, size, ctx_first) in enumerate(groups):
-            near = scratch[5 * g]
-            at = pl.ds(first, size)
-            far_here = (mine, beyond) if ctx_first else (other, beside)
-            blocks = [(other, beyond), far_here]
-            blocks += [(other, beside) if ctx_first else (mine, beyond), (mine, beside)]
+
+        def near(g):
+            which, start, size = groups[g]
+            prt, come = scratch[6 * g : 6 * g + 2]
+            left, right = factors[2 * which : 2 * which + 2]
+
+            @pl.loop(0, places)
+            def _(i):
+                prt[i] = t_mm(left[:, columns(i, cut)], right[:, start : start + size]).astype(BF)
+
+            blocks = [(other, beyond), (other, beside), (mine, beyond), (mine, beside)]
             moves.append(
                 [
                     remote(
-                        prts[which].at[rank, column, :, at], near.at[i],
-                        sems[8 + 6 * g : 10 + 6 * g], i, {"ctx": beside},
+                        prt.at[rank * n_ctx + column], come.at[i],
+                        sems[4 + 6 * g : 6 + 6 * g], i, {"ctx": beside},
                     )
                     for i, (rank, column) in enumerate(blocks)
                 ]
             )
+
+        def chip(g, i, rank, column):
+            prt, come = scratch[6 * g : 6 * g + 2]
+            moves[g][i].wait()
+            return prt[rank * n_ctx + column].astype(F32) + come[i].astype(F32)
+
+        hops = []
+
+        def hop(g):
+            two, far = scratch[6 * g + 2 : 6 * g + 4]
+            sent = []
+            for i, column in enumerate((across, here)):
+                two[i] = chip(g, i, other, column).astype(BF)
+                sent.append(
+                    remote(
+                        two.at[i], far.at[i], sems[6 + 6 * g : 8 + 6 * g], i, {"fsdp": other}
+                    )
+                )
+            hops.append(sent)
+
+        near(0)
+        payload.go(0, 1)
         finish(gathers)
         totals = [
             remote(sml_full.at[:, columns(to, cut)], sml_slots.at[i], sems[2:4], i, device)
             for i, (to, device) in enumerate(others)
         ]
-
-        def chip(g, i, rank, column):
-            which, first, size, _ = groups[g]
-            moves[g][i].wait()
-            value = prts[which][rank, column, :, first : first + size].astype(F32)
-            return value + scratch[5 * g][i].astype(F32)
-
-        hops = []
-        for g, (_, _, _, ctx_first) in enumerate(groups):
-            two, far = scratch[5 * g + 1 : 5 * g + 3]
-            to = {"ctx": across} if ctx_first else {"fsdp": other}
-            pair = [(other, across), (mine, across) if ctx_first else (other, here)]
-            sent = []
-            for i, (rank, column) in enumerate(pair):
-                two[i] = chip(g, i, rank, column).astype(BF)
-                sent.append(
-                    remote(two.at[i], far.at[i], sems[10 + 6 * g : 12 + 6 * g], i, to)
-                )
-            hops.append(sent)
-        moved += spread(pay, came, n_ctx, sems[4:6], (1, 3))
-        order = lax.broadcasted_iota(jnp.int32, (8, 128), 0)
-        for k in range(experts):
-            mixed[k] = as_column(mx[...], jnp.where(order == k, 1.0, 0.0))
-        given = []
-        for step in range(1, n_tp + 1):
-            at = columns(peer("tp", n_tp, step), block_size)
-            block = jnp.zeros((tokens, block_size), F32)
-            for k in range(experts):
-                block = block + mixed[k][:, 0:1] * t_mm(
-                    pck[k * CAP : (k + 1) * CAP], bck[k * CAP : (k + 1) * CAP, at]
-                )
-            if step < n_tp:
-                shares[step - 1] = block.astype(BF)
-                given.append(
-                    send(shares.at[step - 1], share_slots.at[step - 1], "tp", n_tp, step, sems[6:8])
-                )
-            else:
-                moe = rsd[...] + block
+        hop(0)
+        for g in range(1, len(groups)):
+            near(g)
+            hop(g)
+            if g == 1:
+                payload.go(1, 4)
         lasts = []
-        for g, (_, _, _, ctx_first) in enumerate(groups):
-            far, one, last = scratch[5 * g + 2], scratch[5 * g + 3], scratch[5 * g + 4]
-            value = chip(g, 2, *((other, here) if ctx_first else (mine, across)))
+        for g in range(len(groups)):
+            far, one, last = scratch[6 * g + 3 : 6 * g + 6]
+            value = chip(g, 2, mine, across)
             hops[g][0].wait()
             one[...] = (value + far[0].astype(F32)).astype(BF)
-            to = {"fsdp": other} if ctx_first else {"ctx": across}
-            lasts.append(remote(one, last, sems[12 + 6 * g : 14 + 6 * g], 0, to))
-        start = 0
-        for g, (_, _, size, _) in enumerate(groups):
-            far = scratch[5 * g + 2]
-            value = chip(g, 3, mine, here)
-            hops[g][1].wait()
-            out[:, start : start + size] = value + far[1].astype(F32)
-            start += size
+            lasts.append(
+                remote(one, last, sems[8 + 6 * g : 10 + 6 * g], 0, {"ctx": across})
+            )
         finish(totals)
         sums = sml_full[:, columns(place, cut)]
         for i in range(places - 1):
             sums = sums + sml_slots[i]
         small_out[...] = sums
-        finish(given)
-        for k in range(1, n_tp):
-            moe = moe + share_slots[k - 1].astype(F32)
-        block_out[...] = moe.astype(BF)
+        experts_out.give_back()
         start = 0
-        for g, (_, _, size, _) in enumerate(groups):
+        for g, (_, _, size) in enumerate(groups):
+            far = scratch[6 * g + 3]
+            value = chip(g, 3, mine, here)
+            hops[g][1].wait()
+            value = value + far[1].astype(F32)
+            out[:, start : start + size] = value
+            start += size
+        experts_out.mix()
+        payload.wait()
+        start = 0
+        for g, (_, _, size) in enumerate(groups):
             lasts[g].wait()
             at = pl.ds(start, size)
-            out[:, at] = out[:, at] + scratch[5 * g + 4][...].astype(F32)
+            out[:, at] = out[:, at] + scratch[6 * g + 5][...].astype(F32)
             start += size
-        finish(moved)
-
-    buffers = [
-        pltpu.VMEM((8, width), F32),
-        pltpu.VMEM((places - 1, 8, cut), F32),
-        pltpu.VMEM((experts, tokens, 128), F32),
-        pltpu.VMEM((n_tp - 1, tokens, block_size), BF),
-        pltpu.VMEM((n_tp - 1, tokens, block_size), BF),
-    ]
-    sems = pair_of_sems(n_tp) + pair_of_sems(places) + pair_of_sems(n_ctx) + pair_of_sems(n_tp)
-    for _, _, size, _ in groups:
+
+    buffers = [pltpu.VMEM((8, width), F32), pltpu.VMEM((places - 1, 8, cut), F32)]
+    sems = pair_of_sems(n_tp) + pair_of_sems(places)
+    for _, _, size in groups:
         buffers += [
-            pltpu.VMEM((4, rows, size), BF),
-            pltpu.VMEM((2, rows, size), BF),
-            pltpu.VMEM((2, rows, size), BF),
-            pltpu.VMEM((rows, size), BF),
-            pltpu.VMEM((rows, size), BF),
+            pltpu.VMEM((places, cut, size), BF),
+            pltpu.VMEM((4, cut, size), BF),
+            pltpu.VMEM((2, cut, size), BF),
+            pltpu.VMEM((2, cut, size), BF),
+            pltpu.VMEM((cut, size), BF),
+            pltpu.VMEM((cut, size), BF),
         ]
         sems += pair_of_sems(4) + pair_of_sems(2) + pair_of_sems(1)
     return call(
         kernel,
         (
-            shape((rows, total_columns), F32),
+            shape((cut, total_columns), F32),
             shape((8, cut), F32),
-            shape((tokens, block_size), BF),
-            came_shape(payload, n_ctx),
+            experts_out.out,
+            *payload.outs,
         ),
-        (*parts, small, payload, back, picks, mix, resid),
-        buffers + sems,
+        inputs,
+        buffers + experts_out.scratch + payload.scratch + sems,
         10,
         "weight_grads",
-        left=(len(parts) + 1, -1),
-    )
-
-
-def experts_out(back, picks, mix, resid, payload, n_tp, n_ctx):
-    rows, size = resid.shape
-    experts = n_ctx
-
-    def kernel(bck, pck, mx, rsd, pay, out, came, part, slots, *sems):
+        left=(
+            len(flat) + 1,
+            len(inputs) - 1,
+            -len(payload.outs),
+        ),
+    )
+
+
+def experts_back(experts_out, payload, n_tp, n_ctx):
+    inputs = [*experts_out.inputs, *payload.inputs]
+    given = len(experts_out.inputs)
+
+    def kernel(*refs):
+        ins, refs = refs[: len(inputs)], refs[len(inputs) :]
+        outs, scratch = refs[: 1 + len(payload.outs)], refs[1 + len(payload.outs) :]
+        experts_out.take(ins[:given], outs[0], scratch[: len(experts_out.scratch)])
+        payload.take(ins[given:], outs[1:], scratch[len(experts_out.scratch) :])
         greet([("tp", n_tp), ("ctx", n_ctx)])
-        moved = spread(pay, came, n_ctx, sems[2:4])
-        order = lax.broadcasted_iota(jnp.int32, (8, 128), 0)
-        gate = [as_column(mx[...], jnp.where(order == k, 1.0, 0.0)) for k in range(experts)]
-        copies = []
-        for step in range(1, n_tp + 1):
-            at = columns(peer("tp", n_tp, step), size)
-            block = jnp.zeros((rows, size), F32)
-            for k in range(experts):
-                block = block + gate[k][:, 0:1] * t_mm(
-                    pck[k * CAP : (k + 1) * CAP], bck[k * CAP : (k + 1) * CAP, at]
-                )
-            if step < n_tp:
-                part[step - 1] = block.astype(BF)
-                copies.append(
-                    send(part.at[step - 1], slots.at[step - 1], "tp", n_tp, step, sems[0:2])
-                )
-            else:
-                total = rsd[...] + block
-        finish(copies)
-        for k in range(1, n_tp):
-            total = total + slots[k - 1].astype(F32)
-        out[...] = total.astype(BF)
-        finish(moved)
+        experts_out.sums.start()
+        payload.go()
+        experts_out.give_back()
+        experts_out.mix()
+        payload.wait()
 
     return call(
         kernel,
-        (shape((rows, size), BF), came_shape(payload, n_ctx)),
-        (back, picks, mix, resid, payload),
-        [
-            pltpu.VMEM((n_tp - 1, rows, size), BF),
-            pltpu.VMEM((n_tp - 1, rows, size), BF),
-        ]
-        + pair_of_sems(n_tp)
-        + pair_of_sems(n_ctx),
+        (experts_out.out, *payload.outs),
+        inputs,
+        experts_out.scratch + payload.scratch,
         9,
-        "experts_out",
-        left=(4, -1),
+        "experts_back",
+        left=(0, len(inputs) - 1, -len(payload.outs)),
     )
 
 
 def write_out(experts_grads, attn_grad, plain, n_ctx):
-    _, rows, size = experts_grads[0][1].shape
+    _, rows, size = experts_grads[0][0].shape
     steps = max(1, rows // 32)
     tile = rows // steps
-    many, block = len(experts_grads), attn_grad.shape[1] // 4
-
-    def kernel(rank, *refs):
-        here = rank[0]
-        ins, outs = refs[: 2 * many + 1 + len(plain)], refs[2 * many + 1 + len(plain) :]
+    many = len(experts_grads)
+    plain = list(plain)
+    blocks = []
+    if attn_grad is not None:
+        block = attn_grad.shape[1] // 4
+        blocks = [shape((attn_grad.shape[0], block), F32)] * 4
+        plain.append(attn_grad)
+
+    def kernel(*refs):
+        here = lax.axis_index("ctx")
+        ins, outs = refs[: 2 * many + len(plain)], refs[2 * many + len(plain) :]
         for i in range(many):
-            mine, came = ins[2 * i : 2 * i + 2]
+            came, mine = ins[2 * i : 2 * i + 2]
             outs[i][here] = mine[...].astype(F32)
             for k in range(1, n_ctx):
                 outs[i][lax.rem(here + n_ctx - k, n_ctx)] = came[k - 1].astype(F32)
-        for i in range(4):
-            outs[many + i][...] = ins[2 * many][:, i * block : (i + 1) * block]
-        for i in range(len(plain)):
-            outs[many + 4 + i][...] = ins[2 * many + 1 + i][...]
+        for i in range(len(plain) - (1 if blocks else 0)):
+            outs[many + i][...] = ins[2 * many + i][...]
+        for i in range(len(blocks)):
+            outs[i - 4][...] = ins[-1][:, i * block : (i + 1) * block]
 
     def flat(array):
-        return pl.BlockSpec((array.shape[0] // steps, array.shape[1]), lambda i, rank: (i, 0))
+        return pl.BlockSpec((array.shape[0] // steps, array.shape[1]), lambda i: (i, 0))
 
     in_specs, out_specs, out_shape = [], [], []
     for _ in experts_grads:
-        in_specs.append(pl.BlockSpec((tile, size), lambda i, rank: (rank[0] * steps + i, 0)))
-        in_specs.append(pl.BlockSpec((n_ctx - 1, tile, size), lambda i, rank: (0, i, 0)))
-        out_specs.append(pl.BlockSpec((n_ctx, tile, size), lambda i, rank: (0, i, 0)))
+        in_specs.append(pl.BlockSpec((n_ctx - 1, tile, size), lambda i: (0, i, 0)))
+        in_specs.append(pl.BlockSpec((tile, size), lambda i: (i, 0)))
+        out_specs.append(pl.BlockSpec((n_ctx, tile, size), lambda i: (0, i, 0)))
         out_shape.append(shape((n_ctx, rows, size), F32))
-    in_specs.append(flat(attn_grad))
-    quarter = jax.ShapeDtypeStruct((attn_grad.shape[0], block), F32)
-    for array in [quarter] * 4 + list(plain):
+    for array in plain[: len(plain) - (1 if blocks else 0)] + blocks:
         out_specs.append(flat(array))
         out_shape.append(shape(array.shape, array.dtype))
     in_specs += [flat(array) for array in plain]
-    inputs = [array for pair in experts_grads for array in pair] + [attn_grad, *plain]
+    inputs = [array for pair in experts_grads for array in pair] + plain
     return pl.pallas_call(
         kernel,
-        grid_spec=pltpu.PrefetchScalarGridSpec(
-            num_scalar_prefetch=1, grid=(steps,), in_specs=in_specs, out_specs=out_specs
-        ),
+        grid=(steps,),
+        in_specs=in_specs,
+        out_specs=out_specs,
         out_shape=out_shape,
         cost_estimate=pl.CostEstimate(
             flops=0, bytes_accessed=6 * many * n_ctx * rows * size, transcendentals=0
         ),
         name="write_out",
-    )(lax.axis_index("ctx").reshape(1), *inputs)
+    )(*inputs)
 
 
 def after(value, *needed):
@@ -1253,23 +1470,30 @@
     hidden_act = (gate_act * sigma_act * up_act).astype(BF)
     d_result = (gate_rows * grad_rows.astype(F32)).astype(BF)
 
-    def grad_send(left, right):
-        halves = split(left)
+    def away(left, right):
+        value = t_mm(split(left)[1], right).astype(BF)
+        return value, swap_fsdp(value)
+
+    def payload_of(left, right, come):
         if pair:
-            away = t_mm(halves[1], right).astype(BF)
-            return halves[0], right, away, swap_fsdp(away)
-        return halves[0], right, None, None
-
-    def grad_sum(mine, right, away, other):
+            return Payload(n_ctx, product=(left, right, come))
+        return Payload(
+            n_ctx,
+            rows=lax.psum_scatter(
+                t_mm(left, right).astype(BF), "fsdp", scatter_dimension=0, tiled=True
+            ),
+        )
+
+    def came_and_own(outs, payload):
         if pair:
-            return (t_mm(mine, right) + other.astype(F32)).astype(BF)
-        return lax.psum_scatter(
-            t_mm(mine, right).astype(BF), "fsdp", scatter_dimension=0, tiled=True
-        )
-
-    down_sent = grad_send(d_result, hidden_act)
+            return tuple(outs)
+        own = lax.dynamic_slice_in_dim(payload.inputs[0], here_ctx * payload.cut, payload.cut, 0)
+        return outs[0], own
+
+    down_come = gate_come = up_come = None
     if pair:
-        grad_rows = after(grad_rows, down_sent[2])
+        down_away, down_come = away(d_result, hidden_act)
+        grad_rows = after(grad_rows, down_away)
     d_hidden = into(grad_rows, down_w)
     gate_dot = jnp.sum(hidden_act.astype(F32) * d_hidden, axis=-1).reshape(experts, CAP)
     gate_dot = jnp.broadcast_to(
@@ -1278,12 +1502,13 @@
     d_hidden = gate_rows * d_hidden
     d_gate_act = (d_hidden * up_act * sigma_act * (1.0 + gate_act * (1.0 - sigma_act))).astype(BF)
     d_up_act = (d_hidden * gate_act * sigma_act).astype(BF)
-    gate_sent = grad_send(token_rows, d_gate_act)
+    if pair:
+        gate_away, gate_come = away(token_rows, d_gate_act)
 
     acts = (d_gate_act, d_up_act, hidden_act)
     if pair:
-        acts = lax.optimization_barrier((*acts, gate_sent[2]))[:3]
-    d_resid, d_attn_here, gain_two_part, d_logits, returned, *up_away = second_norm_back(
+        acts = lax.optimization_barrier((*acts, gate_away))[:3]
+    d_resid, d_attn_here, gain_two_part, d_logits, made, *up_away = second_norm_back(
         acts,
         (gate_w, up_w, down_w),
         token_rows,
@@ -1301,34 +1526,21 @@
         n_ctx,
     )
     if pair:
-        up_sent = (split(token_rows)[0], d_up_act, up_away[0], swap_fsdp(up_away[0]))
-        d_attn_here, *down_sent = lax.optimization_barrier((d_attn_here, *down_sent))
-    else:
-        up_sent = grad_send(token_rows, d_up_act)
-    grad_down = grad_sum(*down_sent)
-
-    d_attn, d_qkv, down_came = attention_backward(
-        d_attn_here, output_w, query, kv, cosine, -sine, grad_down, n_tp, n_ctx
-    )
-    if pair:
-        d_qkv, *gate_sent = lax.optimization_barrier((d_qkv, *gate_sent))
-    grad_gate = grad_sum(*gate_sent)
-    in_grad, gain_one_part, gate_came = first_norm_back(
-        mm_t(d_qkv, qkv_w).astype(BF),
-        hidden_in,
-        scale_one,
-        gain_one_here,
-        d_resid,
-        grad_gate,
-        n_tp,
-        n_ctx,
-    )
-    if pair:
-        in_grad, *up_sent = lax.optimization_barrier((in_grad, *up_sent))
-    grad_up = grad_sum(*up_sent)
-
-    grad_qkv = t_mm(normed_one, d_qkv).astype(BF)
-    grad_output = t_mm(d_attn, attended).astype(BF)
+        up_come = swap_fsdp(up_away[0])
+
+    payload = payload_of(d_result, hidden_act, down_come)
+    early = (RowSums(made, 0, CAP, n_tp), made)
+    d_attn, d_qkv, made_early, *outs = attention_backward(
+        d_attn_here, output_w, query, kv, cosine, -sine, early, payload, n_tp, n_ctx
+    )
+    grad_down = came_and_own(outs, payload)
+    payload = payload_of(token_rows, d_gate_act, gate_come)
+    in_grad, gain_one_part, *outs = first_norm_back(
+        d_qkv, qkv_w, hidden_in, scale_one, gain_one_here, d_resid, payload, n_tp, n_ctx
+    )
+    grad_gate = came_and_own(outs, payload)
+    payload = payload_of(token_rows, d_up_act, up_come)
+
     small_part = jnp.concatenate(
         [
             gain_one_part[:1],
@@ -1338,34 +1550,34 @@
         ],
         axis=0,
     )
-    mixing = (returned, picks, mix, resid)
+    written = write_out([grad_gate, grad_down], None, (), n_ctx)
     if pair:
-        grad_attn, small_grad, block_out, up_came = weight_grads(
-            [value.reshape(n_fsdp, n_ctx, quarter, -1) for value in (grad_qkv, grad_output)],
-            [
-                (1, 0, heads_width, False),
-                (0, 0, 2 * heads_width, False),
-                (0, 2 * heads_width, heads_width, False),
-            ],
+        small_part = after(small_part, *written)
+    grad_gate, grad_down = written
+    experts_out = ExpertsOut(made, made_early, picks, mix, resid, n_tp, n_ctx)
+    if pair:
+        grad_attn, small_grad, block_out, *outs = weight_grads(
+            [(d_attn, attended), (normed_one, d_qkv)],
+            [(0, 0, heads_width), (1, 0, 2 * heads_width), (1, 2 * heads_width, heads_width)],
             small_part,
-            grad_up,
-            *mixing,
+            payload,
+            experts_out,
             n_tp,
             n_ctx,
         )
     else:
+        grad_attn = jnp.concatenate([t_mm(d_attn, attended), t_mm(normed_one, d_qkv)], axis=1)
         scatter = partial(
             lax.psum_scatter, axis_name=("fsdp", "ctx"), scatter_dimension=0, tiled=True
         )
-        grad_attn = scatter(jnp.concatenate([grad_output, grad_qkv], axis=1)).astype(F32)
+        grad_attn = scatter(grad_attn.astype(BF)).astype(F32)
         small_grad = lax.all_gather(small_part, "tp", axis=1, tiled=True)
         small_grad = scatter(small_grad.T).T
-        block_out, up_came = experts_out(*mixing, grad_up, n_tp, n_ctx)
-    pieces = [(grad_gate, gate_came), (grad_up, up_came), (grad_down, down_came)]
-    (
-        grad_gate, grad_up, grad_down, grad_output, grad_query, grad_key, grad_value,
-        block_out, in_grad,
-    ) = write_out(pieces, grad_attn, (block_out, in_grad), n_ctx)
+        block_out, *outs = experts_back(experts_out, payload, n_tp, n_ctx)
+    grad_up = came_and_own(outs, payload)
+    grad_up, block_out, in_grad, grad_output, grad_query, grad_key, grad_value = write_out(
+        [grad_up], grad_attn, (block_out, in_grad), n_ctx
+    )
     return (
         block_out,
         in_grad,

time: 505 us -> 503 us (level)
  matrix products: 71.9 us -> 46.7 us
  Pallas kernels: 386 us -> 411 us
    dot_general x7 -> x2, matrix products: 31 us -> 8.14 us  [t_mm(): lax.dot_general(left, right, (((0,), (0,)), ((), ())), preferred_element_...]
    pallas_call x8, Pallas kernels: 374 us -> 395 us  [call(): pl.pallas_call(kernel, out_shape=out_shape, in_specs=[anywhere if i in le...]
    dot_general x2 -> x1, matrix products: 9.43 us -> 2.66 us  [mm_t(): lax.dot_general(left, right, (((1,), (1,)), ((), ())), preferred_element_...]
    pallas_call x1 -> x2, Pallas kernels: 12.1 us -> 16.4 us  [write_out(): pl.pallas_call(kernel, grid=(steps,), in_specs=in_specs, out_specs=out_sp...]
  transfers between devices with their start and end apart: 8 -> 8, of which waited for: 1 -> 2; matrix products, arithmetic and copies ran while one was open for 16% -> 12% of each run, Pallas kernels for 62% -> 64%
where the time goes in v7:
time: 503 us; the launch traced here: 497 us
  Pallas kernels  411 us (82%)
  matrix products  46.7 us (9%)
  local copies, waits for them, and re-layouts  17.5 us (3%)
  starting transfers between devices  9.8 us (2%)
  other arithmetic  5.26 us (1%)
    pallas_call x8, Pallas kernels, call(): pl.pallas_call(kernel, out_shape=out_shape, in_specs=[anywhere if i in le...  395 us
    dot_general x10, matrix products, mm(): return jnp.dot(left, right, preferred_element_type=F32)  35.9 us
    pallas_call x2, Pallas kernels, write_out(): pl.pallas_call(kernel, grid=(steps,), in_specs=in_specs, out_specs=out_sp...  16.4 us
  transfers between devices with their start and end apart: 8, of which 2 were waited for; matrix products, arithmetic and copies ran while one was open for 12% of the time, Pallas kernels for 64%

profile of v7, /device:TPU:0, one launch (start us, length us, event | category | flops | bytes accessed | tf_op | source)
XLA Modules:
  0.0 496.5 jit_solution(15940042507248206669)
XLA Ops:
  0.7 1.1 constant_dynamic-slice_fusion.1
  3.0 3.0 collective-permute-start.1
  6.2 3.6 dynamic-slice_bitcast_fusion.refs_3_
  9.8 2.0 collective-permute-start.2
  11.8 22.6 %gather_tp.1 = (bf16[256,2048]{1,0:T(8,128)(2,1)}, bf16[1024,1408]{1,0:T(8,128)(2,1)}, bf16[1024,1408]{1,0:T(8,128)(2,1)}) custom-call(bf16[256,512]{1,0:T(8,128)(2,1)} %refs_2_.1, bf16[4,1024,1408]{2,1,0:T(8,128)(2,1)} %refs_0_.1, bf16[4,1024,1408]{2,1,0:T(8,128)(2,1)} %refs_1_.2), custom_call_target="tpu_custom_call" | custom-call | tf_op jit(solution)/shard_map/gather_tp/pallas_call | solution.py:285
  35.1 1.5 collective-permute-start.4
  43.1 35.3 %first_norm.1 = (bf16[256,2048]{1,0:T(8,128)(2,1)}, f32[256,128]{1,0:T(8,128)}, bf16[256,2048]{1,0:T(8,128)(2,1)}, bf16[2048,1536]{1,0:T(8,128)(2,1)}, bf16[2048,512]{1,0:T(8,128)(2,1)}) custom-call(bf16[256,2048]{1,0:T(8,128)(2,1)} %get-tuple-element.65.refs_0_, bf16[256,512]{1,0:T(8,128)(2,1)} %refs_19_.1, f32[8,2048]{1,0:T(8,128)} %copy-done.11, ...), custom_call_target="tpu_custom_call" | custom-call | tf_op jit(solution)/shard_map/first_norm/pallas_call | solution.py:285
  78.4 6.2 %fusion.37.prj = f32[256,1536]{1,0:T(8,128)} fusion(bf16[256,2048]{1,0:T(8,128)(2,1)} %get-tuple-element.66.refs_2_, bf16[2048,1536]{1,0:T(8,128)(2,1)} %get-tuple-element.67.refs_1_), kind=kOutput, calls=%fused_computation.79 | convolution fusion | flops 1610612736 | bytes 8912896 | tf_op jit(solution)/shard_map/dot_general | solution.py:23
  84.6 21.9 %attention_forward.1 = (bf16[256,512]{1,0:T(8,128)(2,1)}, bf16[256,512]{1,0:T(8,128)(2,1)}, bf16[1024,1024]{1,0:T(8,128)(2,1)}) custom-call(f32[256,1536]{1,0:T(8,128)} %fusion.37.prj, f32[256,128]{1,0:T(8,128)} %pad_maximum_fusion.1.cs.refs_4_, f32[256,128]{1,0:T(8,128)} %get-tuple-element.119.sn), custom_call_target="tpu_custom_call" | custom-call | tf_op jit(solution)/shard_map/attention_forward/pallas_call | solution.py:285
  106.5 2.7 convolution_convert_fusion.3.prt
  109.2 2.3 convolution_convert_fusion.2.slb
  112.1 73.3 %second_norm.1 = (f32[256,512]{1,0:T(8,128)}, f32[256,128]{1,0:T(8,128)}, bf16[256,2048]{1,0:T(8,128)(2,1)}, bf16[640,2048]{1,0:T(8,128)(2,1)}, bf16[640,2048]{1...) custom-call(bf16[256,2048]{1,0:T(8,128)(2,1)} %convolution_convert_fusion.3.prt, ...), custom_call_target="tpu_custom_call" | custom-call | tf_op jit(solution)/shard_map/second_norm/pallas_call | solution.py:285
  186.3 3.7 fusion.4
  190.5 1.2 copy-done
  191.7 5.0 fusion.6
  196.7 4.1 convolution_add_fusion.2
  200.7 4.4 multiply_convert_fusion.3
  205.2 4.2 convolution_convert_fusion.1
  209.9 2.2 fusion.1
  212.1 3.7 collective-permute-done.4.refs_8_
  215.8 6.8 %multiply_convert_fusion.1 = (bf16[640,1408]{1,0:T(8,128)(2,1)}, bf16[640,1408]{1,0:T(8,128)(2,1)S(1)}, f32[640]{0:T(1024)S(1)}) fusion(f32[640,1408]{1,0:T(8,128)S(1)} %convolution_add_fusion.2, f32[640]{0:T(1024)S(1)} %mul.89, f32[640,1408]{1,0:T(8,128)S(1)} %get-tuple-element.135, bf16[640,1408]{1,0:T(8,128)(2,1)S(1)} %get-tuple-element.79.refs_2_.refs_8_, ...), kind=kOutput, calls=%fused_computation.4 | convolution fusion | flops 1861713280 | bytes 20421124 | tf_op jit(solution)/shard_map/dot_general | solution.py:23
  222.6 3.9 convolution_convert_fusion
  226.6 2.1 collective-permute-start.6
  229.3 61.1 %second_norm_back.1 = (f32[256,512]{1,0:T(8,128)}, bf16[256,512]{1,0:T(8,128)(2,1)}, f32[8,512]{1,0:T(8,128)}, f32[8,256]{1,0:T(8,128)}, bf16[640,2048]{1,0:T(8,128)(2,1)}, /*index=5*/bf16[1024,1408]{1,0:T(8,128)(2,1)}) custom-call(bf16[640,1408]{1,0:T(8,128)(2,1)} %copy-done.4, bf16[640,1408]{1,0:T(8,128)(2,1)} %get-tuple-element.78.refs_1_.refs_11_, ...), custom_call_target="tpu_custom_call" | custom-call | tf_op jit(solution)/shard_map/second_norm_back/pallas_call | solution.py:285
  291.3 1.1 fusion.12
  292.4 52.0 %attention_backward.1 = (bf16[256,2048]{1,0:T(8,128)(2,1)}, bf16[256,1536]{1,0:T(8,128)(2,1)}, bf16[160,512]{1,0:T(8,128)(2,1)}, bf16[3,256,1408]{2,1,0:T(8,128)(2,1)}, bf16[256,1408]{1,0:T(8,128)(2,1)}) custom-call(bf16[256,512]{1,0:T(8,128)(2,1)} %get-tuple-element.83.refs_0_, bf16[2048,512]{1,0:T(8,128)(2,1)} %get-tuple-element.69.refs_1_, ...), custom_call_target="tpu_custom_call" | custom-call | tf_op jit(solution)/shard_map/attention_backward/pallas_call | solution.py:285
  346.0 43.6 %first_norm_back.1 = (f32[256,512]{1,0:T(8,128)}, f32[8,512]{1,0:T(8,128)}, bf16[3,256,1408]{2,1,0:T(8,128)(2,1)}, bf16[256,1408]{1,0:T(8,128)(2,1)}) custom-call(bf16[256,1536]{1,0:T(8,128)(2,1)} %get-tuple-element.88.refs_0_.refs_3_, bf16[2048,1536]{1,0:T(8,128)(2,1)} %get-tuple-element.67.refs_1_, bf16[256,512]{1,0:T(8,128)(2,1)} %refs_2_.1, ...), custom_call_target="tpu_custom_call" | custom-call | tf_op jit(solution)/shard_map/first_norm_back/pallas_call | solution.py:285
  390.3 8.4 %write_out.2 = (f32[4,256,1408]{2,1,0:T(8,128)}, f32[4,256,1408]{2,1,0:T(8,128)}) custom-call(bf16[3,256,1408]{2,1,0:T(8,128)(2,1)} %get-tuple-element.95.refs_0_, bf16[256,1408]{1,0:T(8,128)(2,1)} %get-tuple-element.96.refs_1_, bf16[3,256,1408]{2,1,0:T(8,128)(2,1)} %get-tuple-element.97.refs_2_, bf16[256,1408]{1,0:T(8,128)(2,1)} %get-tuple-element.98.refs_3_), custom_call_target="tpu_custom_call" | custom-call | bytes 17301504 | tf_op jit(solution)/shard_map/write_out/pallas_call | solution.py:1322
  400.3 85.3 %weight_grads.1 = (f32[256,2048]{1,0:T(8,128)}, f32[8,256]{1,0:T(8,128)}, bf16[256,512]{1,0:T(8,128)(2,1)}, bf16[3,256,1408]{2,1,0:T(8,128)(2,1)}, bf16[256,1408]{1,0:T(8,128)(2,1)}) custom-call(bf16[256,2048]{1,0:T(8,128)(2,1)} %get-tuple-element.87.refs_0_, bf16[256,512]{1,0:T(8,128)(2,1)} %get-tuple-element.68.refs_1_, ...), custom_call_target="tpu_custom_call" | custom-call | tf_op jit(solution)/shard_map/weight_grads/pallas_call | solution.py:285
  485.6 1.3 slice_bitcast_fusion
  486.9 1.3 fusion.36
  488.3 8.0 %write_out.3 = (f32[4,256,1408]{2,1,0:T(8,128)}, bf16[256,512]{1,0:T(8,128)(2,1)}, f32[256,512]{1,0:T(8,128)}, f32[256,512]{1,0:T(8,128)}, f32[256,512]{1,0:T(8,...) custom-call(bf16[3,256,1408]{2,1,0:T(8,128)(2,1)} %get-tuple-element.105.refs_0_, ...), custom_call_target="tpu_custom_call" | custom-call | bytes 8650752 | tf_op jit(solution)/shard_map/write_out/pallas_call | solution.py:1322
  (82 shorter events, 16.5 us)
Async XLA Ops:
  0.6 5.3 %copy-start.14 = (bf16[1024]{0:T(1024)(128)(2,1)S(1)}, bf16[1024]{0:T(1024)(128)(2,1)}, u32[]{:S(2)}) copy-start(bf16[1024]{0:T(1024)(128)(2,1)} %param.15) | copy-start | bytes 6148
  0.7 5.3 %copy-start.15 = (bf16[1024]{0:T(1024)(128)(2,1)S(1)}, bf16[1024]{0:T(1024)(128)(2,1)}, u32[]{:S(2)}) copy-start(bf16[1024]{0:T(1024)(128)(2,1)} %param.20) | copy-start | bytes 6148
  0.7 5.4 %copy-start.12 = (bf16[1024,4]{0,1:T(4,128)(2,1)S(1)}, bf16[1024,4]{0,1:T(4,128)(2,1)}, u32[]{:S(2)}) copy-start(bf16[1024,4]{0,1:T(4,128)(2,1)} %param.21) | copy-start | bytes 24580
  3.0 39.2 %collective-permute-start.1 = (bf16[256,2048]{1,0:T(8,128)(2,1)S(1)}, bf16[256,2048]{1,0:T(8,128)(2,1)S(1)}, u32[]{:S(2)}, u32[]{:S(2)}) collective-permute-start(bf16[256,2048]{1,0:T(8,128)(2,1)S(1)} %pad_maximum_fusion), channel_id=1, source_target_pairs={{0,16},{16,0},{1,17},{17,1},{2,18},{18,2},{3,19},{19,3},{4,20},{20... | collective-permute-start | bytes 3145736 | tf_op jit(solution)/shard_map/ppermute | solution.py:1369
  6.2 35.1 %collective-permute-start = (bf16[8,1024]{1,0:T(8,128)(2,1)S(1)}, bf16[8,1024]{1,0:T(8,128)(2,1)S(1)}, u32[]{:S(2)}, u32[]{:S(2)}) collective-permute-start(bf16[8,1024]{1,0:T(8,128)(2,1)S(1)} %maximum_maximum_fusion), channel_id=1, source_target_pairs={{0,16},{16,0},{1,17},{17,1},{2,18},{18,2},{3,19},{19,3},{4,20},{20... | collective-permute-start | bytes 49160 | tf_op jit(solution)/shard_map/ppermute | solution.py:1369
  9.8 26.8 %copy-start.13 = (s32[256,2]{0,1:T(2,128)S(1)}, s32[256,2]{0,1:T(2,128)}, u32[]{:S(2)}) copy-start(s32[256,2]{0,1:T(2,128)} %param.25) | copy-start | bytes 6148
  9.8 186.8 %collective-permute-start.2 = (bf16[1024,1408]{1,0:T(8,128)(2,1)}, bf16[1024,1408]{1,0:T(8,128)(2,1)}, u32[]{:S(2)}, u32[]{:S(2)}) collective-permute-start(bf16[1024,1408]{1,0:T(8,128)(2,1)} %dynamic-slice_bitcast_fusion.refs_3_), channel_id=1, source_target_pairs={{0,16},{16,0},{1,17},{17,1},{2,18},{18,2},{3,19},{19,3},{4,20},{20... | collective-permute-start | bytes 8650760 | tf_op jit(solution)/shard_map/ppermute | solution.py:1369
  34.5 166.3 %collective-permute-start.3 = (bf16[1024,1408]{1,0:T(8,128)(2,1)}, bf16[1024,1408]{1,0:T(8,128)(2,1)}, u32[]{:S(2)}, u32[]{:S(2)}) collective-permute-start(bf16[1024,1408]{1,0:T(8,128)(2,1)} %get-tuple-element.74.refs_5_), channel_id=1, source_target_pairs={{0,16},{16,0},{1,17},{17,1},{2,18},{18,2},{3,19},{19,3},{4,20},{20... | collective-permute-start | bytes 8650760 | tf_op jit(solution)/shard_map/ppermute | solution.py:1369
  35.1 180.7 %collective-permute-start.4 = (bf16[1024,1408]{1,0:T(8,128)(2,1)}, bf16[1024,1408]{1,0:T(8,128)(2,1)}, u32[]{:S(2)}, u32[]{:S(2)}) collective-permute-start(bf16[1024,1408]{1,0:T(8,128)(2,1)} %get-tuple-element.76.refs_7_), channel_id=1, source_target_pairs={{0,16},{16,0},{1,17},{17,1},{2,18},{18,2},{3,19},{19,3},{4,20},{20... | collective-permute-start | bytes 8650760 | tf_op jit(solution)/shard_map/ppermute | solution.py:1369
  41.3 0.8 copy-start.11
  42.1 1.0 copy-start.9
  78.4 28.1 %copy-start.2 = (bf16[2048,512]{1,0:T(8,128)(2,1)S(1)}, bf16[2048,512]{1,0:T(8,128)(2,1)}, u32[]{:S(2)}) copy-start(bf16[2048,512]{1,0:T(8,128)(2,1)} %get-tuple-element.69.refs_1_) | copy-start | bytes 6291460
  84.6 24.6 %copy-start.10 = (bf16[256,2048]{1,0:T(8,128)(2,1)S(1)}, bf16[256,2048]{1,0:T(8,128)(2,1)}, u32[]{:S(2)}) copy-start(bf16[256,2048]{1,0:T(8,128)(2,1)} %get-tuple-element.70) | copy-start | bytes 3145732
  111.5 74.7 %copy-start.5 = (bf16[1024,1408]{1,0:T(8,128)(2,1)S(1)}, bf16[1024,1408]{1,0:T(8,128)(2,1)}, u32[]{:S(2)}) copy-start(bf16[1024,1408]{1,0:T(8,128)(2,1)} %get-tuple-element.74.refs_5_) | copy-start | bytes 8650756
  186.3 3.7 copy-start.8
  189.9 1.7 copy-start
  191.7 13.5 %copy-start.1 = (bf16[640,2048]{1,0:T(8,128)(2,1)}, bf16[640,2048]{1,0:T(8,128)(2,1)S(1)}, u32[]{:S(2)}) copy-start(bf16[640,2048]{1,0:T(8,128)(2,1)S(1)} %multiply_convert_fusion.refs_7_) | copy-start | bytes 7864324
  205.2 10.6 %copy-start.3 = (bf16[640,1408]{1,0:T(8,128)(2,1)}, bf16[640,1408]{1,0:T(8,128)(2,1)S(1)}, u32[]{:S(2)}) copy-start(bf16[640,1408]{1,0:T(8,128)(2,1)S(1)} %get-tuple-element.79.refs_2_.refs_8_) | copy-start | bytes 5406724
  205.2 4.7 copy-start.6
  209.4 83.0 %collective-permute-start.5 = (bf16[1024,1408]{1,0:T(8,128)(2,1)}, bf16[1024,1408]{1,0:T(8,128)(2,1)}, u32[]{:S(2)}, u32[]{:S(2)}) collective-permute-start(bf16[1024,1408]{1,0:T(8,128)(2,1)} %convolution_convert_fusion.1), channel_id=1, source_target_pairs={{0,16},{16,0},{1,17},{17,1},{2,18},{18,2},{3,19},{19,3},{4,20},{20... | collective-permute-start | bytes 8650760 | tf_op jit(solution)/shard_map/ppermute | solution.py:1369
  222.6 4.0 copy-start.4
  226.6 117.8 %collective-permute-start.6 = (bf16[1024,1408]{1,0:T(8,128)(2,1)}, bf16[1024,1408]{1,0:T(8,128)(2,1)S(1)}, u32[]{:S(2)}, u32[]{:S(2)}) collective-permute-start(bf16[1024,1408]{1,0:T(8,128)(2,1)} %convolution_convert_fusion), channel_id=1, source_target_pairs={{0,16},{16,0},{1,17},{17,1},{2,18},{18,2},{3,19},{19,3},{4,20},{20... | collective-permute-start | bytes 8650760 | tf_op jit(solution)/shard_map/ppermute | solution.py:1369
  290.4 109.9 %collective-permute-start.7 = (bf16[1024,1408]{1,0:T(8,128)(2,1)}, bf16[1024,1408]{1,0:T(8,128)(2,1)}, u32[]{:S(2)}, u32[]{:S(2)}) collective-permute-start(bf16[1024,1408]{1,0:T(8,128)(2,1)} %get-tuple-element.104), channel_id=1, source_target_pairs={{0,16},{16,0},{1,17},{17,1},{2,18},{18,2},{3,19},{19,3},{4,20},{20... | collective-permute-start | bytes 8650760 | tf_op jit(solution)/shard_map/ppermute | solution.py:1369
  344.4 1.6 copy-start.7

commit v8 on v7

--- a/solution.py
+++ b/solution.py
@@ -567,15 +567,17 @@
             for k in (2, 3, 1):
                 slab(k, step).start()
 
-        dispatch(0, low[...])
         route()
 
-        @pl.loop(1, n_tp)
+        @pl.loop(0, n_tp)
         def _(step):
-            place = out.at[:, columns(here, size)]
-            described(
-                low, place, sems[4:6], step - 1, {"tp": peer("tp", n_tp, step)}
-            ).wait()
+            @pl.when(step > 0)
+            def _():
+                described(
+                    low, out.at[:, columns(here, size)], sems[4:6], step - 1,
+                    {"tp": peer("tp", n_tp, step)},
+                ).wait()
+
             dispatch(step, out[:, columns(peer("tp", n_tp, n_tp - step), size)])
 
         for step in range(n_tp):
@@ -616,6 +618,81 @@
     )
 
 
+def expert_acts(tokens, gate_w, up_w, n_fsdp):
+    rows, width = tokens.shape
+    hidden = gate_w[0].shape[1]
+    count = len(gate_w)
+    part = gate_w[0].shape[0]
+    chunk = 256
+    per = part // chunk
+    steps = count * per
+    pair = count == 2
+
+    def kernel(tok, *refs):
+        wgt = [refs[:count], refs[count : 2 * count]]
+        to_gate, to_up, hid, buffer, loads = refs[2 * count :]
+        first = lax.axis_index("fsdp") if pair else 0
+
+        def load(step):
+            slot = lax.rem(step, 2)
+            at = stretch(lax.rem(step, per), chunk)
+            for lane in range(2):
+                for i in range(count):
+
+                    @pl.when(step // per == i)
+                    def _():
+                        pltpu.make_async_copy(
+                            wgt[lane][i].at[at], buffer.at[slot, lane], loads.at[slot, lane]
+                        ).start()
+
+        load(0)
+        to_gate[...] = jnp.zeros_like(to_gate)
+        to_up[...] = jnp.zeros_like(to_up)
+
+        @pl.loop(0, steps)
+        def _(step):
+            slot = lax.rem(step, 2)
+            for lane in range(2):
+                pltpu.make_async_copy(
+                    wgt[lane][0].at[pl.ds(0, chunk)], buffer.at[slot, lane], loads.at[slot, lane]
+                ).wait()
+
+            @pl.when(step + 1 < steps)
+            def _():
+                load(step + 1)
+
+            which = lax.rem(first + step // per, count)
+            column = which * part + lax.rem(step, per) * chunk
+            values = tok[:, pl.ds(pl.multiple_of(column, 128), chunk)]
+            to_gate[...] += mm(values, buffer[slot, 0])
+            to_up[...] += mm(values, buffer[slot, 1])
+
+        @pl.loop(0, rows // 32)
+        def _(i):
+            at = stretch(i, 32)
+            a, b = to_gate[at, :], to_up[at, :]
+            sigma = 1.0 / (1.0 + jnp.exp(-a))
+            silu = a * sigma
+            hid[at, :] = (silu * b).astype(BF)
+            to_up[at, :] = silu
+            to_gate[at, :] = b * sigma * (1.0 + a * (1.0 - sigma))
+
+    anywhere = pl.BlockSpec(memory_space=pl.ANY)
+    return pl.pallas_call(
+        kernel,
+        out_shape=(
+            shape((rows, hidden), F32),
+            shape((rows, hidden), F32),
+            shape((rows, hidden), BF),
+        ),
+        in_specs=[VM] + [anywhere] * (2 * count),
+        out_specs=(VM, VM, VM),
+        scratch_shapes=[pltpu.VMEM((2, 2, chunk, hidden), BF), DMA((2, 2))],
+        cost_estimate=pl.CostEstimate(flops=0, bytes_accessed=0, transcendentals=0),
+        name="expert_acts",
+    )(tokens, *gate_w, *up_w)
+
+
 def second_norm_back(
     acts, weights, tokens, dots, picks, gates, onehot, names, router, resid, scale, gain, grad,
     n_tp, n_ctx,
@@ -765,13 +842,17 @@
                 {"tp": peer("tp", n_tp, step)},
             )
 
-        @pl.loop(1, n_tp)
+        @pl.loop(1, n_tp + 1)
         def _(step):
-            parts[step - 1] = combined(step).astype(BF)
-            give(step).start()
+            d_resid[...] = combined(step)
+
+            @pl.when(step < n_tp)
+            def _():
+                parts[step - 1] = d_resid[...].astype(BF)
+                give(step).start()
 
         copies = [give(step) for step in range(1, n_tp)]
-        total = combined(n_tp)
+        total = d_resid[...]
         total = total + lax.dot_general(
             logits.astype(BF),
             rtr[...].astype(BF),
@@ -975,18 +1056,22 @@
     )
 
 
-def first_norm_back(d_qkv, weights, hidden, scale, gain, d_resid, payload, n_tp, n_ctx):
+def first_norm_back(d_qkv, weights, hidden, scale, gain, d_resid, sums, payload, n_tp, n_ctx):
+    more, more_input = sums
     rows, size = hidden.shape
     width = size * n_tp
 
     def kernel(*refs):
-        dpr, wgt, hid, scl, gn, dr = refs[:6]
-        n_in, n_out = 6 + len(payload.inputs), len(payload.outs)
-        out, d_gain = refs[n_in : n_in + 2]
-        scratch = refs[n_in + 2 + n_out :]
+        dpr, wgt, hid, scl, gn, dr, made = refs[:7]
+        n_in, n_out = 7 + len(payload.inputs), len(payload.outs)
+        out, d_gain, summed = refs[n_in : n_in + 3]
+        scratch = refs[n_in + 3 + n_out :]
         held, parts, slots, mine, sums, loads = scratch[:6]
         sems = scratch[6:10]
-        payload.take(refs[6:n_in], refs[n_in + 2 : n_in + 2 + n_out], scratch[10:])
+        more.take(made, scratch[10 : 10 + len(more.scratch)])
+        payload.take(
+            refs[7:n_in], refs[n_in + 3 : n_in + 3 + n_out], scratch[10 + len(more.scratch) :]
+        )
 
         def block(step):
             rank = peer("tp", n_tp, step)
@@ -1005,15 +1090,18 @@
                 {"tp": peer("tp", n_tp, step)},
             )
 
-        @pl.loop(1, n_tp)
+        @pl.loop(1, n_tp + 1)
         def _(step):
             block(step).wait()
-            parts[step - 1] = mm_t(dpr[...], held[step - 1]).astype(BF)
-            give(step).start()
+            out[...] = mm_t(dpr[...], held[step - 1])
+
+            @pl.when(step < n_tp)
+            def _():
+                parts[step - 1] = out[...].astype(BF)
+                give(step).start()
 
         copies = [give(step) for step in range(1, n_tp)]
-        block(n_tp).wait()
-        out[...] = mm_t(dpr[...], held[n_tp - 1])
+        more.start()
         payload.go()
         finish(copies)
         total = out[...]
@@ -1028,12 +1116,13 @@
         dot = as_column(dot, eighth())[:, 0:1] * (1.0 / width)
         unit = hid[...].astype(F32) * factor
         out[...] = dr[...] + factor * (out[...] - unit * dot)
+        summed[...] = more.total().astype(BF)
         payload.wait()
 
     return call(
         kernel,
-        (shape((rows, size), F32), shape((8, size), F32), *payload.outs),
-        (d_qkv, weights, hidden, scale, gain, d_resid, *payload.inputs),
+        (shape((rows, size), F32), shape((8, size), F32), shape(more.shape, BF), *payload.outs),
+        (d_qkv, weights, hidden, scale, gain, d_resid, more_input, *payload.inputs),
         [
             pltpu.VMEM((n_tp, size, d_qkv.shape[1]), BF),
             pltpu.VMEM((n_tp - 1, rows, size), BF),
@@ -1043,19 +1132,21 @@
             DMA((n_tp,)),
         ]
         + pair_of_sems(n_tp) * 2
+        + more.scratch
         + payload.scratch,
         6,
         "first_norm_back",
-        left=(1, 5 + len(payload.inputs), -len(payload.outs)),
+        left=(1, 6, 6 + len(payload.inputs), -len(payload.outs)),
     )
 
 
 class ExpertsOut:
 
     def __init__(self, made, done, picks, mix, resid, n_tp, n_ctx):
-        self.n_ctx = n_ctx
-        self.sums = RowSums(made, done.shape[0], made.shape[0] - done.shape[0], n_tp)
-        self.inputs = [made, done, picks, mix, resid]
+        self.n_ctx, self.n_done = n_ctx, len(done)
+        first = CAP * len(done)
+        self.sums = RowSums(made, first, made.shape[0] - first, n_tp)
+        self.inputs = [made, *done, picks, mix, resid]
         self.size = resid.shape[1]
         self.out = shape(resid.shape, BF)
         self.scratch = [
@@ -1069,11 +1160,9 @@
         self.sums.take(ins[0], scratch[4:])
 
     def block(self, k):
-        done, share = self.ins[1], self.held[0]
-        first = k * CAP
-        if first < done.shape[0]:
-            return done.at[pl.ds(first, CAP)]
-        return share.at[pl.ds(first - done.shape[0], CAP)]
+        if k < self.n_done:
+            return self.ins[1 + k]
+        return self.held[0].at[pl.ds((k - self.n_done) * CAP, CAP)]
 
     def give_back(self):
         share, back = self.held[:2]
@@ -1085,7 +1174,7 @@
         ]
 
     def mix(self):
-        made, done, picks, mix, resid = self.ins
+        picks, mix, resid = self.ins[-3:]
         back = self.held[1]
         finish(self.copies)
         order = lax.broadcasted_iota(jnp.int32, (8, 128), 0)
@@ -1177,7 +1266,7 @@
             hops.append(sent)
 
         near(0)
-        payload.go(0, 1)
+        payload.go()
         finish(gathers)
         totals = [
             remote(sml_full.at[:, columns(to, cut)], sml_slots.at[i], sems[2:4], i, device)
@@ -1187,8 +1276,6 @@
         for g in range(1, len(groups)):
             near(g)
             hop(g)
-            if g == 1:
-                payload.go(1, 4)
         lasts = []
         for g in range(len(groups)):
             far, one, last = scratch[6 * g + 3 : 6 * g + 6]
@@ -1198,12 +1285,13 @@
             lasts.append(
                 remote(one, last, sems[8 + 6 * g : 10 + 6 * g], 0, {"ctx": across})
             )
+            if g == 0:
+                experts_out.give_back()
         finish(totals)
         sums = sml_full[:, columns(place, cut)]
         for i in range(places - 1):
             sums = sums + sml_slots[i]
         small_out[...] = sums
-        experts_out.give_back()
         start = 0
         for g, (_, _, size) in enumerate(groups):
             far = scratch[6 * g + 3]
@@ -1464,10 +1552,7 @@
     )
     gate_rows = slot_gates[:, 0, :CAP].reshape(experts * CAP, 1)
 
-    gate_act = into(token_rows, gate_w)
-    up_act = into(token_rows, up_w)
-    sigma_act = jax.nn.sigmoid(gate_act)
-    hidden_act = (gate_act * sigma_act * up_act).astype(BF)
+    to_gate, to_up, hidden_act = expert_acts(token_rows, gate_w, up_w, n_fsdp)
     d_result = (gate_rows * grad_rows.astype(F32)).astype(BF)
 
     def away(left, right):
@@ -1500,8 +1585,8 @@
         jnp.pad(gate_dot, [(0, 0), (0, rows_here - CAP)])[:, None, :], (experts, 8, rows_here)
     )
     d_hidden = gate_rows * d_hidden
-    d_gate_act = (d_hidden * up_act * sigma_act * (1.0 + gate_act * (1.0 - sigma_act))).astype(BF)
-    d_up_act = (d_hidden * gate_act * sigma_act).astype(BF)
+    d_gate_act = (d_hidden * to_gate).astype(BF)
+    d_up_act = (d_hidden * to_up).astype(BF)
     if pair:
         gate_away, gate_come = away(token_rows, d_gate_act)
 
@@ -1535,8 +1620,9 @@
     )
     grad_down = came_and_own(outs, payload)
     payload = payload_of(token_rows, d_gate_act, gate_come)
-    in_grad, gain_one_part, *outs = first_norm_back(
-        d_qkv, qkv_w, hidden_in, scale_one, gain_one_here, d_resid, payload, n_tp, n_ctx
+    later = (RowSums(made, CAP, CAP, n_tp), made)
+    in_grad, gain_one_part, made_later, *outs = first_norm_back(
+        d_qkv, qkv_w, hidden_in, scale_one, gain_one_here, d_resid, later, payload, n_tp, n_ctx
     )
     grad_gate = came_and_own(outs, payload)
     payload = payload_of(token_rows, d_up_act, up_come)
@@ -1554,7 +1640,7 @@
     if pair:
         small_part = after(small_part, *written)
     grad_gate, grad_down = written
-    experts_out = ExpertsOut(made, made_early, picks, mix, resid, n_tp, n_ctx)
+    experts_out = ExpertsOut(made, (made_early, made_later), picks, mix, resid, n_tp, n_ctx)
     if pair:
         grad_attn, small_grad, block_out, *outs = weight_grads(
             [(d_attn, attended), (normed_one, d_qkv)],

time: 503 us -> 498 us (0.990); the launches traced: 497 us -> 497 us
  Pallas kernels: 411 us -> 431 us
  matrix products: 46.7 us -> 29.1 us
  other arithmetic: 5.26 us -> 11.6 us
    dot_general x10 -> x6, matrix products: 35.9 us -> 16.1 us  [mm(): return jnp.dot(left, right, preferred_element_type=F32)]
    pallas_call x0 -> x1, Pallas kernels: none -> 18.9 us  [expert_acts(): pl.pallas_call(kernel, out_shape=(shape((rows, hidden), F32), shape((rows...]
  transfers between devices with their start and end apart: 8 -> 8, of which waited for: 2 -> 0; matrix products, arithmetic and copies ran while one was open for 12% -> 10% of each run, Pallas kernels for 64% -> 70%
where the time goes in v8:
time: 498 us; the launch traced here: 497 us
  Pallas kernels  431 us (87%)
  matrix products  29.1 us (6%)
  local copies, waits for them, and re-layouts  13.9 us (3%)
  other arithmetic  11.6 us (2%)
  starting transfers between devices  9.88 us (2%)
    pallas_call x8, Pallas kernels, call(): pl.pallas_call(kernel, out_shape=out_shape, in_specs=[anywhere if i in le...  396 us
    pallas_call x1, Pallas kernels, expert_acts(): pl.pallas_call(kernel, out_shape=(shape((rows, hidden), F32), shape((rows...  18.9 us
    pallas_call x2, Pallas kernels, write_out(): pl.pallas_call(kernel, grid=(steps,), in_specs=in_specs, out_specs=out_sp...  16.4 us
    dot_general x6, matrix products, mm(): return jnp.dot(left, right, preferred_element_type=F32)  16.1 us
  transfers between devices with their start and end apart: 8, of which 0 were waited for; matrix products, arithmetic and copies ran while one was open for 10% of the time, Pallas kernels for 70%

profile of v8, /device:TPU:0, one launch (start us, length us, event | category | flops | bytes accessed | tf_op | source)
XLA Modules:
  0.0 496.7 jit_solution(15096674084846832171)
XLA Ops:
  0.7 1.1 constant_dynamic-slice_fusion.1
  1.8 1.1 constant_dynamic-slice_fusion.3
  2.8 1.1 pad_maximum_fusion
  3.9 2.9 collective-permute-start.1
  7.1 2.0 dynamic-slice_bitcast_fusion.refs_0_.refs_3_
  9.1 2.1 collective-permute-start.2
  11.2 22.6 %gather_tp.1 = (bf16[256,2048]{1,0:T(8,128)(2,1)}, bf16[1024,1408]{1,0:T(8,128)(2,1)}, bf16[1024,1408]{1,0:T(8,128)(2,1)}) custom-call(bf16[256,512]{1,0:T(8,128)(2,1)} %refs_2_.1, bf16[4,1024,1408]{2,1,0:T(8,128)(2,1)} %refs_0_.1, bf16[4,1024,1408]{2,1,0:T(8,128)(2,1)} %refs_1_.2), custom_call_target="tpu_custom_call" | custom-call | tf_op jit(solution)/shard_map/gather_tp/pallas_call | solution.py:285
  34.7 1.3 collective-permute-start.4
  39.7 0.9 fusion.24
  41.6 35.2 %first_norm.1 = (bf16[256,2048]{1,0:T(8,128)(2,1)}, f32[256,128]{1,0:T(8,128)}, bf16[256,2048]{1,0:T(8,128)(2,1)}, bf16[2048,1536]{1,0:T(8,128)(2,1)}, bf16[2048,512]{1,0:T(8,128)(2,1)}) custom-call(bf16[256,2048]{1,0:T(8,128)(2,1)} %get-tuple-element.69.refs_0_, bf16[256,512]{1,0:T(8,128)(2,1)} %refs_19_.1, f32[8,2048]{1,0:T(8,128)} %copy-done.11, ...), custom_call_target="tpu_custom_call" | custom-call | tf_op jit(solution)/shard_map/first_norm/pallas_call | solution.py:285
  76.8 6.1 %fusion.27.prj = f32[256,1536]{1,0:T(8,128)} fusion(bf16[256,2048]{1,0:T(8,128)(2,1)} %get-tuple-element.70.refs_2_, bf16[2048,1536]{1,0:T(8,128)(2,1)} %get-tuple-element.71.refs_1_), kind=kOutput, calls=%fused_computation.65 | convolution fusion | flops 1610612736 | bytes 8912896 | tf_op jit(solution)/shard_map/dot_general | solution.py:23
  82.8 21.7 %attention_forward.1 = (bf16[256,512]{1,0:T(8,128)(2,1)}, bf16[256,512]{1,0:T(8,128)(2,1)}, bf16[1024,1024]{1,0:T(8,128)(2,1)}) custom-call(f32[256,1536]{1,0:T(8,128)} %fusion.27.prj, f32[256,128]{1,0:T(8,128)} %pad_maximum_fusion.1.cs.refs_4_, f32[256,128]{1,0:T(8,128)} %get-tuple-element.127.sn), custom_call_target="tpu_custom_call" | custom-call | tf_op jit(solution)/shard_map/attention_forward/pallas_call | solution.py:285
  104.5 3.5 convolution_convert_fusion.3.prt
  108.0 2.3 convolution_convert_fusion.2.slb
  111.0 74.1 %second_norm.1 = (f32[256,512]{1,0:T(8,128)}, f32[256,128]{1,0:T(8,128)}, bf16[256,2048]{1,0:T(8,128)(2,1)}, bf16[640,2048]{1,0:T(8,128)(2,1)}, bf16[640,2048]{1...) custom-call(bf16[256,2048]{1,0:T(8,128)(2,1)} %convolution_convert_fusion.3.prt, ...), custom_call_target="tpu_custom_call" | custom-call | tf_op jit(solution)/shard_map/second_norm/pallas_call | solution.py:285
  185.9 3.8 multiply_convert_fusion.refs_7_
  189.7 18.9 %expert_acts.1 = (f32[640,1408]{1,0:T(8,128)}, f32[640,1408]{1,0:T(8,128)}, bf16[640,1408]{1,0:T(8,128)(2,1)}) custom-call(bf16[640,2048]{1,0:T(8,128)(2,1)} %get-tuple-element.77.tok.refs_9_.refs_7_.refs_11_, bf16[1024,1408]{1,0:T(8,128)(2,1)} %copy-done.1, bf16[1024,1408]{1,0:T(8,128)(2,1)} %collective-permute-done.2.refs_1_.refs_4_, ...), custom_call_target="tpu_custom_call" | custom-call | tf_op jit(solution)/shard_map/expert_acts/pallas_call | solution.py:681
  208.6 5.7 %convolution_convert_fusion.1 = bf16[1024,1408]{1,0:T(8,128)(2,1)} fusion(bf16[640,1408]{1,0:T(8,128)(2,1)} %get-tuple-element.86.refs_2_.refs_8_, bf16[640,2048]{1,0:T(8,128)(2,1)S(1)} %copy-done.4, s32[]{:T(128)S(6)} %select_n.56), kind=kOutput, calls=%fused_computation.2 | convolution fusion | flops 1846935552 | bytes 5996548 | tf_op jit(solution)/shard_map/dot_general | solution.py:31
  215.0 2.2 fusion.2
  217.2 4.2 convolution_add_fusion
  221.7 2.1 multiply_convert_fusion.1
  223.8 3.9 convolution_convert_fusion
  227.8 1.3 collective-permute-start.6
  229.8 65.9 %second_norm_back.1 = (f32[256,512]{1,0:T(8,128)}, bf16[256,512]{1,0:T(8,128)(2,1)}, f32[8,512]{1,0:T(8,128)}, f32[8,256]{1,0:T(8,128)}, bf16[640,2048]{1,0:T(8,128)(2,1)}, /*index=5*/bf16[1024,1408]{1,0:T(8,128)(2,1)}) custom-call(bf16[640,1408]{1,0:T(8,128)(2,1)} %copy-done.2, bf16[640,1408]{1,0:T(8,128)(2,1)} %get-tuple-element.85.refs_1_.refs_12_, ...), custom_call_target="tpu_custom_call" | custom-call | tf_op jit(solution)/shard_map/second_norm_back/pallas_call | solution.py:285
  297.2 1.1 fusion.6
  298.3 52.1 %attention_backward.1 = (bf16[256,2048]{1,0:T(8,128)(2,1)}, bf16[256,1536]{1,0:T(8,128)(2,1)}, bf16[160,512]{1,0:T(8,128)(2,1)}, bf16[3,256,1408]{2,1,0:T(8,128)(2,1)}, bf16[256,1408]{1,0:T(8,128)(2,1)}) custom-call(bf16[256,512]{1,0:T(8,128)(2,1)} %get-tuple-element.90.refs_0_, bf16[2048,512]{1,0:T(8,128)(2,1)} %get-tuple-element.73.refs_1_, ...), custom_call_target="tpu_custom_call" | custom-call | tf_op jit(solution)/shard_map/attention_backward/pallas_call | solution.py:285
  352.0 49.7 %first_norm_back.1 = (f32[256,512]{1,0:T(8,128)}, f32[8,512]{1,0:T(8,128)}, bf16[160,512]{1,0:T(8,128)(2,1)}, bf16[3,256,1408]{2,1,0:T(8,128)(2,1)}, bf16[256,1408]{1,0:T(8,128)(2,1)}) custom-call(bf16[256,1536]{1,0:T(8,128)(2,1)} %get-tuple-element.95.refs_0_.refs_3_, bf16[2048,1536]{1,0:T(8,128)(2,1)} %get-tuple-element.71.refs_1_, ...), custom_call_target="tpu_custom_call" | custom-call | tf_op jit(solution)/shard_map/first_norm_back/pallas_call | solution.py:285
  402.4 8.4 %write_out.2 = (f32[4,256,1408]{2,1,0:T(8,128)}, f32[4,256,1408]{2,1,0:T(8,128)}) custom-call(bf16[3,256,1408]{2,1,0:T(8,128)(2,1)} %get-tuple-element.102.refs_0_, bf16[256,1408]{1,0:T(8,128)(2,1)} %get-tuple-element.103.refs_1_, bf16[3,256,1408]{2,1,0:T(8,128)(2,1)} %get-tuple-element.104.refs_2_, bf16[256,1408]{1,0:T(8,128)(2,1)} %get-tuple-element.105.refs_3_), custom_call_target="tpu_custom_call" | custom-call | bytes 17301504 | tf_op jit(solution)/shard_map/write_out/pallas_call | solution.py:1410
  411.4 74.5 %weight_grads.1 = (f32[256,2048]{1,0:T(8,128)}, f32[8,256]{1,0:T(8,128)}, bf16[256,512]{1,0:T(8,128)(2,1)}, bf16[3,256,1408]{2,1,0:T(8,128)(2,1)}, bf16[256,1408]{1,0:T(8,128)(2,1)}) custom-call(bf16[256,2048]{1,0:T(8,128)(2,1)} %get-tuple-element.94.refs_0_, bf16[256,512]{1,0:T(8,128)(2,1)} %get-tuple-element.72.refs_1_, ...), custom_call_target="tpu_custom_call" | custom-call | tf_op jit(solution)/shard_map/weight_grads/pallas_call | solution.py:285
  485.9 1.3 slice_bitcast_fusion
  487.2 1.3 fusion.26
  488.5 8.0 %write_out.3 = (f32[4,256,1408]{2,1,0:T(8,128)}, bf16[256,512]{1,0:T(8,128)(2,1)}, f32[256,512]{1,0:T(8,128)}, f32[256,512]{1,0:T(8,128)}, f32[256,512]{1,0:T(8,...) custom-call(bf16[3,256,1408]{2,1,0:T(8,128)(2,1)} %get-tuple-element.113.refs_0_, ...), custom_call_target="tpu_custom_call" | custom-call | bytes 8650752 | tf_op jit(solution)/shard_map/write_out/pallas_call | solution.py:1410
  (80 shorter events, 13.3 us)
Async XLA Ops:
  0.6 6.2 %copy-start.14 = (bf16[1024]{0:T(1024)(128)(2,1)S(1)}, bf16[1024]{0:T(1024)(128)(2,1)}, u32[]{:S(2)}) copy-start(bf16[1024]{0:T(1024)(128)(2,1)} %param.15) | copy-start | bytes 6148
  0.7 6.2 %copy-start.15 = (bf16[1024]{0:T(1024)(128)(2,1)S(1)}, bf16[1024]{0:T(1024)(128)(2,1)}, u32[]{:S(2)}) copy-start(bf16[1024]{0:T(1024)(128)(2,1)} %param.20) | copy-start | bytes 6148
  0.7 6.3 %copy-start.12 = (bf16[1024,4]{0,1:T(4,128)(2,1)S(1)}, bf16[1024,4]{0,1:T(4,128)(2,1)}, u32[]{:S(2)}) copy-start(bf16[1024,4]{0,1:T(4,128)(2,1)} %param.21) | copy-start | bytes 24580
  3.9 37.6 %collective-permute-start.1 = (bf16[256,2048]{1,0:T(8,128)(2,1)}, bf16[256,2048]{1,0:T(8,128)(2,1)}, u32[]{:S(2)}, u32[]{:S(2)}) collective-permute-start(bf16[256,2048]{1,0:T(8,128)(2,1)} %pad_maximum_fusion), channel_id=1, source_target_pairs={{0,16},{16,0},{1,17},{17,1},{2,18},{18,2},{3,19},{19,3},{4,20},{20... | collective-permute-start | bytes 3145736 | tf_op jit(solution)/shard_map/ppermute | solution.py:1457
  7.1 33.6 %collective-permute-start = (bf16[8,1024]{1,0:T(8,128)(2,1)S(1)}, bf16[8,1024]{1,0:T(8,128)(2,1)S(1)}, u32[]{:S(2)}, u32[]{:S(2)}) collective-permute-start(bf16[8,1024]{1,0:T(8,128)(2,1)S(1)} %maximum_maximum_fusion), channel_id=1, source_target_pairs={{0,16},{16,0},{1,17},{17,1},{2,18},{18,2},{3,19},{19,3},{4,20},{20... | collective-permute-start | bytes 49160 | tf_op jit(solution)/shard_map/ppermute | solution.py:1457
  9.1 24.7 %copy-start.1 = (bf16[1024,1408]{1,0:T(8,128)(2,1)}, bf16[1024,1408]{1,0:T(8,128)(2,1)S(1)}, u32[]{:S(2)}) copy-start(bf16[1024,1408]{1,0:T(8,128)(2,1)S(1)} %dynamic-slice_bitcast_fusion.refs_0_.refs_3_) | copy-start | bytes 8650756
  9.1 26.9 %copy-start.13 = (s32[256,2]{0,1:T(2,128)S(1)}, s32[256,2]{0,1:T(2,128)}, u32[]{:S(2)}) copy-start(s32[256,2]{0,1:T(2,128)} %param.25) | copy-start | bytes 6148
  9.1 180.5 %collective-permute-start.2 = (bf16[1024,1408]{1,0:T(8,128)(2,1)S(1)}, bf16[1024,1408]{1,0:T(8,128)(2,1)}, u32[]{:S(2)}, u32[]{:S(2)}) collective-permute-start(bf16[1024,1408]{1,0:T(8,128)(2,1)S(1)} %dynamic-slice_bitcast_fusion.refs_0_.refs_3_), channel_id=1, source_target_pairs={{0,16},{16,0},{1,17},{17,1},{2,18},{18,2},{3,19},{19,3},{4,20},{20... | collective-permute-start | bytes 8650760 | tf_op jit(solution)/shard_map/ppermute | solution.py:1457
  33.9 155.8 %collective-permute-start.3 = (bf16[1024,1408]{1,0:T(8,128)(2,1)}, bf16[1024,1408]{1,0:T(8,128)(2,1)}, u32[]{:S(2)}, u32[]{:S(2)}) collective-permute-start(bf16[1024,1408]{1,0:T(8,128)(2,1)} %get-tuple-element.78.refs_2_.refs_5_), channel_id=1, source_target_pairs={{0,16},{16,0},{1,17},{17,1},{2,18},{18,2},{3,19},{19,3},{4,20},{20... | collective-permute-start | bytes 8650760 | tf_op jit(solution)/shard_map/ppermute | solution.py:1457
  34.7 182.6 %collective-permute-start.4 = (bf16[1024,1408]{1,0:T(8,128)(2,1)}, bf16[1024,1408]{1,0:T(8,128)(2,1)}, u32[]{:S(2)}, u32[]{:S(2)}) collective-permute-start(bf16[1024,1408]{1,0:T(8,128)(2,1)} %get-tuple-element.81.refs_7_), channel_id=1, source_target_pairs={{0,16},{16,0},{1,17},{17,1},{2,18},{18,2},{3,19},{19,3},{4,20},{20... | collective-permute-start | bytes 8650760 | tf_op jit(solution)/shard_map/ppermute | solution.py:1457
  40.8 0.8 copy-start.11
  104.5 3.5 copy-start.10
  189.6 18.9 %copy-start.4 = (bf16[640,2048]{1,0:T(8,128)(2,1)S(1)}, bf16[640,2048]{1,0:T(8,128)(2,1)}, u32[]{:S(2)}) copy-start(bf16[640,2048]{1,0:T(8,128)(2,1)} %multiply_convert_fusion.refs_7_) | copy-start | bytes 7864324
  208.6 6.4 %copy-start.7 = (bf16[1024,1408]{1,0:T(8,128)(2,1)S(1)}, bf16[1024,1408]{1,0:T(8,128)(2,1)}, u32[]{:S(2)}) copy-start(bf16[1024,1408]{1,0:T(8,128)(2,1)} %get-tuple-element.81.refs_7_) | copy-start | bytes 8650756
  208.6 6.4 %copy-start.9 = (bf16[640,2048]{1,0:T(8,128)(2,1)S(1)}, bf16[640,2048]{1,0:T(8,128)(2,1)}, u32[]{:S(2)}) copy-start(bf16[640,2048]{1,0:T(8,128)(2,1)} %get-tuple-element.80) | copy-start | bytes 7864324
  214.3 84.0 %collective-permute-start.5 = (bf16[1024,1408]{1,0:T(8,128)(2,1)}, bf16[1024,1408]{1,0:T(8,128)(2,1)}, u32[]{:S(2)}, u32[]{:S(2)}) collective-permute-start(bf16[1024,1408]{1,0:T(8,128)(2,1)} %convolution_convert_fusion.1), channel_id=1, source_target_pairs={{0,16},{16,0},{1,17},{17,1},{2,18},{18,2},{3,19},{19,3},{4,20},{20... | collective-permute-start | bytes 8650760 | tf_op jit(solution)/shard_map/ppermute | solution.py:1457
  217.2 4.3 copy-start.3
  217.2 4.3 copy-start.5
  217.2 4.5 copy-start.6
  221.7 2.1 copy-start
  223.8 4.0 copy-start.2
  227.8 122.6 %collective-permute-start.6 = (bf16[1024,1408]{1,0:T(8,128)(2,1)}, bf16[1024,1408]{1,0:T(8,128)(2,1)S(1)}, u32[]{:S(2)}, u32[]{:S(2)}) collective-permute-start(bf16[1024,1408]{1,0:T(8,128)(2,1)} %convolution_convert_fusion), channel_id=1, source_target_pairs={{0,16},{16,0},{1,17},{17,1},{2,18},{18,2},{3,19},{19,3},{4,20},{20... | collective-permute-start | bytes 8650760 | tf_op jit(solution)/shard_map/ppermute | solution.py:1457
  295.7 115.7 %collective-permute-start.7 = (bf16[1024,1408]{1,0:T(8,128)(2,1)}, bf16[1024,1408]{1,0:T(8,128)(2,1)}, u32[]{:S(2)}, u32[]{:S(2)}) collective-permute-start(bf16[1024,1408]{1,0:T(8,128)(2,1)} %get-tuple-element.112), channel_id=1, source_target_pairs={{0,16},{16,0},{1,17},{17,1},{2,18},{18,2},{3,19},{19,3},{4,20},{20... | collective-permute-start | bytes 8650760 | tf_op jit(solution)/shard_map/ppermute | solution.py:1457
  350.4 1.6 copy-start.8

commit v9 on v8

--- a/solution.py
+++ b/solution.py
@@ -784,28 +784,29 @@
             for k in (2, 3, 1):
                 slab(k, rank, step).start()
 
+        def combined(step):
+            rank = peer("tp", n_tp, step)
+            at = columns(rank, size)
+            for k in (2, 3, 1):
+                slab(k, rank, step - 1).wait()
+            block = t_mm(pck[0:CAP], drw[0:CAP, at])
+            for k in range(1, experts):
+                block = block + t_mm(pck[k * CAP : (k + 1) * CAP], back[k - 1, :, at])
+            return block
+
+        def give(step):
+            return described(
+                parts.at[step - 1], slots.at[step - 1], sems[6:8], step - 1,
+                {"tp": peer("tp", n_tp, step)},
+            )
+
+        def pass_on(begin, end):
+            @pl.loop(begin, end)
+            def _(step):
+                parts[step - 1] = combined(step).astype(BF)
+                give(step).start()
+
         load(2, 0, 0, 0)
-
-        @pl.loop(0, n_tp)
-        def _(rank):
-            slot = lax.rem(rank, 2)
-            loaded(2, slot, 0)
-
-            @pl.when(rank + 1 < n_tp)
-            def _():
-                load(2, rank + 1, 1 - slot, 0)
-
-            eo[:, columns(rank, size)] = mm_t(hid[...], buffer[slot, 0]).astype(BF)
-
-        pltpu.make_async_copy(eo, out_rows, out_sem).start()
-        if count == 2:
-
-            @pl.loop(0, part // 256)
-            def _(i):
-                at = pl.ds(pl.multiple_of((1 - first) * part + i * 256, 128), 256)
-                up_held[stretch(i, 256), :] = t_mm(tok[:, at], dup[...]).astype(BF)
-
-            pltpu.make_async_copy(up_held, up_away, up_sem).start()
         finish(small)
         order = lax.broadcasted_iota(jnp.int32, (8, rows), 0)
         own = jnp.zeros((8, rows), F32)
@@ -819,40 +820,46 @@
                 preferred_element_type=F32,
             )
             own = own + jnp.where(order == k, by_row, 0.0)
-        gate_grad = total_over(own, mine, sums, "tp", n_tp, sems[4:6])
+        mine[...] = own
+        shared = [
+            send(mine, sums.at[k - 1], "tp", n_tp, k, sems[4:6]) for k in range(1, n_tp)
+        ]
+        pass_on(1, n_tp - 1)
+
+
+        @pl.loop(0, n_tp)
+        def _(rank):
+            slot = lax.rem(rank, 2)
+            loaded(2, slot, 0)
+
+            @pl.when(rank + 1 < n_tp)
+            def _():
+                load(2, rank + 1, 1 - slot, 0)
+
+            eo[:, columns(rank, size)] = mm_t(hid[...], buffer[slot, 0]).astype(BF)
+
+        pltpu.make_async_copy(eo, out_rows, out_sem).start()
+        pass_on(n_tp - 1, n_tp)
+        if count == 2:
+
+            @pl.loop(0, part // 256)
+            def _(i):
+                at = pl.ds(pl.multiple_of((1 - first) * part + i * 256, 128), 256)
+                up_held[stretch(i, 256), :] = t_mm(tok[:, at], dup[...]).astype(BF)
+
+            pltpu.make_async_copy(up_held, up_away, up_sem).start()
+        finish(shared)
+        gate_grad = mine[...]
+        for k in range(1, n_tp):
+            gate_grad = gate_grad + sums[k - 1]
         both = [jnp.sum(nms[j] * gate_grad, axis=0, keepdims=True) for j in range(2)]
         gate = [gts[j : j + 1, :] for j in range(2)]
         mean = gate[0] * both[0] + gate[1] * both[1]
         logits = sum(gate[j] * (both[j] - mean) * one[j] for j in range(2))
         d_logits[...] = logits
 
-        def combined(step):
-            rank = peer("tp", n_tp, step)
-            at = columns(rank, size)
-            for k in (2, 3, 1):
-                slab(k, rank, step - 1).wait()
-            block = t_mm(pck[0:CAP], drw[0:CAP, at])
-            for k in range(1, experts):
-                block = block + t_mm(pck[k * CAP : (k + 1) * CAP], back[k - 1, :, at])
-            return block
-
-        def give(step):
-            return described(
-                parts.at[step - 1], slots.at[step - 1], sems[6:8], step - 1,
-                {"tp": peer("tp", n_tp, step)},
-            )
-
-        @pl.loop(1, n_tp + 1)
-        def _(step):
-            d_resid[...] = combined(step)
-
-            @pl.when(step < n_tp)
-            def _():
-                parts[step - 1] = d_resid[...].astype(BF)
-                give(step).start()
-
         copies = [give(step) for step in range(1, n_tp)]
-        total = d_resid[...]
+        total = combined(n_tp)
         total = total + lax.dot_general(
             logits.astype(BF),
             rtr[...].astype(BF),
@@ -1056,22 +1063,18 @@
     )
 
 
-def first_norm_back(d_qkv, weights, hidden, scale, gain, d_resid, sums, payload, n_tp, n_ctx):
-    more, more_input = sums
+def first_norm_back(d_qkv, weights, hidden, scale, gain, d_resid, payload, n_tp, n_ctx):
     rows, size = hidden.shape
     width = size * n_tp
 
     def kernel(*refs):
-        dpr, wgt, hid, scl, gn, dr, made = refs[:7]
-        n_in, n_out = 7 + len(payload.inputs), len(payload.outs)
-        out, d_gain, summed = refs[n_in : n_in + 3]
-        scratch = refs[n_in + 3 + n_out :]
+        dpr, wgt, hid, scl, gn, dr = refs[:6]
+        n_in, n_out = 6 + len(payload.inputs), len(payload.outs)
+        out, d_gain = refs[n_in : n_in + 2]
+        scratch = refs[n_in + 2 + n_out :]
         held, parts, slots, mine, sums, loads = scratch[:6]
         sems = scratch[6:10]
-        more.take(made, scratch[10 : 10 + len(more.scratch)])
-        payload.take(
-            refs[7:n_in], refs[n_in + 3 : n_in + 3 + n_out], scratch[10 + len(more.scratch) :]
-        )
+        payload.take(refs[6:n_in], refs[n_in + 2 : n_in + 2 + n_out], scratch[10:])
 
         def block(step):
             rank = peer("tp", n_tp, step)
@@ -1101,7 +1104,6 @@
                 give(step).start()
 
         copies = [give(step) for step in range(1, n_tp)]
-        more.start()
         payload.go()
         finish(copies)
         total = out[...]
@@ -1116,13 +1118,12 @@
         dot = as_column(dot, eighth())[:, 0:1] * (1.0 / width)
         unit = hid[...].astype(F32) * factor
         out[...] = dr[...] + factor * (out[...] - unit * dot)
-        summed[...] = more.total().astype(BF)
         payload.wait()
 
     return call(
         kernel,
-        (shape((rows, size), F32), shape((8, size), F32), shape(more.shape, BF), *payload.outs),
-        (d_qkv, weights, hidden, scale, gain, d_resid, more_input, *payload.inputs),
+        (shape((rows, size), F32), shape((8, size), F32), *payload.outs),
+        (d_qkv, weights, hidden, scale, gain, d_resid, *payload.inputs),
         [
             pltpu.VMEM((n_tp, size, d_qkv.shape[1]), BF),
             pltpu.VMEM((n_tp - 1, rows, size), BF),
@@ -1132,11 +1133,10 @@
             DMA((n_tp,)),
         ]
         + pair_of_sems(n_tp) * 2
-        + more.scratch
         + payload.scratch,
         6,
         "first_norm_back",
-        left=(1, 6, 6 + len(payload.inputs), -len(payload.outs)),
+        left=(1, 5 + len(payload.inputs), -len(payload.outs)),
     )
 
 
@@ -1265,8 +1265,8 @@
                 )
             hops.append(sent)
 
+        payload.go()
         near(0)
-        payload.go()
         finish(gathers)
         totals = [
             remote(sml_full.at[:, columns(to, cut)], sml_slots.at[i], sems[2:4], i, device)
@@ -1285,7 +1285,7 @@
             lasts.append(
                 remote(one, last, sems[8 + 6 * g : 10 + 6 * g], 0, {"ctx": across})
             )
-            if g == 0:
+            if g == 1:
                 experts_out.give_back()
         finish(totals)
         sums = sml_full[:, columns(place, cut)]
@@ -1620,9 +1620,8 @@
     )
     grad_down = came_and_own(outs, payload)
     payload = payload_of(token_rows, d_gate_act, gate_come)
-    later = (RowSums(made, CAP, CAP, n_tp), made)
-    in_grad, gain_one_part, made_later, *outs = first_norm_back(
-        d_qkv, qkv_w, hidden_in, scale_one, gain_one_here, d_resid, later, payload, n_tp, n_ctx
+    in_grad, gain_one_part, *outs = first_norm_back(
+        d_qkv, qkv_w, hidden_in, scale_one, gain_one_here, d_resid, payload, n_tp, n_ctx
     )
     grad_gate = came_and_own(outs, payload)
     payload = payload_of(token_rows, d_up_act, up_come)
@@ -1640,7 +1639,7 @@
     if pair:
         small_part = after(small_part, *written)
     grad_gate, grad_down = written
-    experts_out = ExpertsOut(made, (made_early, made_later), picks, mix, resid, n_tp, n_ctx)
+    experts_out = ExpertsOut(made, (made_early,), picks, mix, resid, n_tp, n_ctx)
     if pair:
         grad_attn, small_grad, block_out, *outs = weight_grads(
             [(d_attn, attended), (normed_one, d_qkv)],

time: 498 us -> 496 us (level)
  Pallas kernels: 431 us -> 426 us
    pallas_call x8, Pallas kernels: 396 us -> 390 us  [call(): pl.pallas_call(kernel, out_shape=out_shape, in_specs=[anywhere if i in le...]
  transfers between devices with their start and end apart: 8 -> 8, of which waited for: 0 -> 1; matrix products, arithmetic and copies ran while one was open for 10% -> 10% of each run, Pallas kernels for 70% -> 68%
where the time goes in v9:
time: 496 us; the launch traced here: 494 us
  Pallas kernels  426 us (86%)
  matrix products  29.1 us (6%)
  local copies, waits for them, and re-layouts  13.9 us (3%)
  other arithmetic  11.6 us (2%)
  starting transfers between devices  9.87 us (2%)
    pallas_call x8, Pallas kernels, call(): pl.pallas_call(kernel, out_shape=out_shape, in_specs=[anywhere if i in le...  390 us
    pallas_call x1, Pallas kernels, expert_acts(): pl.pallas_call(kernel, out_shape=(shape((rows, hidden), F32), shape((rows...  18.9 us
    pallas_call x2, Pallas kernels, write_out(): pl.pallas_call(kernel, grid=(steps,), in_specs=in_specs, out_specs=out_sp...  16.4 us
    dot_general x6, matrix products, mm(): return jnp.dot(left, right, preferred_element_type=F32)  16.1 us
  transfers between devices with their start and end apart: 8, of which 1 were waited for; matrix products, arithmetic and copies ran while one was open for 10% of the time, Pallas kernels for 68%

profile of v9, /device:TPU:0, one launch (start us, length us, event | category | flops | bytes accessed | tf_op | source)
XLA Modules:
  0.0 494.4 jit_solution(17105181124831217065)
XLA Ops:
  0.7 1.1 constant_dynamic-slice_fusion.1
  1.8 1.1 constant_dynamic-slice_fusion.3
  2.8 1.1 pad_maximum_fusion
  3.9 2.9 collective-permute-start.1
  7.1 2.0 dynamic-slice_bitcast_fusion.refs_0_.refs_3_
  9.1 2.1 collective-permute-start.2
  11.2 22.6 %gather_tp.1 = (bf16[256,2048]{1,0:T(8,128)(2,1)}, bf16[1024,1408]{1,0:T(8,128)(2,1)}, bf16[1024,1408]{1,0:T(8,128)(2,1)}) custom-call(bf16[256,512]{1,0:T(8,128)(2,1)} %refs_2_.1, bf16[4,1024,1408]{2,1,0:T(8,128)(2,1)} %refs_0_.1, bf16[4,1024,1408]{2,1,0:T(8,128)(2,1)} %refs_1_.2), custom_call_target="tpu_custom_call" | custom-call | tf_op jit(solution)/shard_map/gather_tp/pallas_call | solution.py:285
  34.7 1.3 collective-permute-start.4
  41.6 35.2 %first_norm.1 = (bf16[256,2048]{1,0:T(8,128)(2,1)}, f32[256,128]{1,0:T(8,128)}, bf16[256,2048]{1,0:T(8,128)(2,1)}, bf16[2048,1536]{1,0:T(8,128)(2,1)}, bf16[2048,512]{1,0:T(8,128)(2,1)}) custom-call(bf16[256,2048]{1,0:T(8,128)(2,1)} %get-tuple-element.68.refs_0_, bf16[256,512]{1,0:T(8,128)(2,1)} %refs_19_.1, f32[8,2048]{1,0:T(8,128)} %copy-done.11, ...), custom_call_target="tpu_custom_call" | custom-call | tf_op jit(solution)/shard_map/first_norm/pallas_call | solution.py:285
  76.8 6.1 %fusion.27.prj = f32[256,1536]{1,0:T(8,128)} fusion(bf16[256,2048]{1,0:T(8,128)(2,1)} %get-tuple-element.69.refs_2_, bf16[2048,1536]{1,0:T(8,128)(2,1)} %get-tuple-element.70.refs_1_), kind=kOutput, calls=%fused_computation.65 | convolution fusion | flops 1610612736 | bytes 8912896 | tf_op jit(solution)/shard_map/dot_general | solution.py:23
  82.8 21.7 %attention_forward.1 = (bf16[256,512]{1,0:T(8,128)(2,1)}, bf16[256,512]{1,0:T(8,128)(2,1)}, bf16[1024,1024]{1,0:T(8,128)(2,1)}) custom-call(f32[256,1536]{1,0:T(8,128)} %fusion.27.prj, f32[256,128]{1,0:T(8,128)} %pad_maximum_fusion.1.cs.refs_4_, f32[256,128]{1,0:T(8,128)} %get-tuple-element.125.sn), custom_call_target="tpu_custom_call" | custom-call | tf_op jit(solution)/shard_map/attention_forward/pallas_call | solution.py:285
  104.5 3.5 convolution_convert_fusion.3.prt
  108.0 2.3 convolution_convert_fusion.2.slb
  111.0 74.1 %second_norm.1 = (f32[256,512]{1,0:T(8,128)}, f32[256,128]{1,0:T(8,128)}, bf16[256,2048]{1,0:T(8,128)(2,1)}, bf16[640,2048]{1,0:T(8,128)(2,1)}, bf16[640,2048]{1...) custom-call(bf16[256,2048]{1,0:T(8,128)(2,1)} %convolution_convert_fusion.3.prt, ...), custom_call_target="tpu_custom_call" | custom-call | tf_op jit(solution)/shard_map/second_norm/pallas_call | solution.py:285
  185.9 3.8 multiply_convert_fusion.refs_7_
  189.7 18.9 %expert_acts.1 = (f32[640,1408]{1,0:T(8,128)}, f32[640,1408]{1,0:T(8,128)}, bf16[640,1408]{1,0:T(8,128)(2,1)}) custom-call(bf16[640,2048]{1,0:T(8,128)(2,1)} %get-tuple-element.76.tok.refs_9_.refs_6_.refs_10_, bf16[1024,1408]{1,0:T(8,128)(2,1)} %copy-done.1, bf16[1024,1408]{1,0:T(8,128)(2,1)} %collective-permute-done.2.refs_1_.refs_4_, ...), custom_call_target="tpu_custom_call" | custom-call | tf_op jit(solution)/shard_map/expert_acts/pallas_call | solution.py:681
  208.6 5.7 %convolution_convert_fusion.1 = bf16[1024,1408]{1,0:T(8,128)(2,1)} fusion(bf16[640,1408]{1,0:T(8,128)(2,1)} %get-tuple-element.85.refs_2_.refs_8_, bf16[640,2048]{1,0:T(8,128)(2,1)S(1)} %copy-done.4, s32[]{:T(128)S(6)} %select_n.56), kind=kOutput, calls=%fused_computation.2 | convolution fusion | flops 1846935552 | bytes 5996548 | tf_op jit(solution)/shard_map/dot_general | solution.py:31
  215.0 2.2 fusion.2
  217.2 4.2 convolution_add_fusion
  221.7 2.1 multiply_convert_fusion.1
  223.8 3.9 convolution_convert_fusion
  227.8 1.3 collective-permute-start.6
  229.8 56.5 %second_norm_back.1 = (f32[256,512]{1,0:T(8,128)}, bf16[256,512]{1,0:T(8,128)(2,1)}, f32[8,512]{1,0:T(8,128)}, f32[8,256]{1,0:T(8,128)}, bf16[640,2048]{1,0:T(8,128)(2,1)}, /*index=5*/bf16[1024,1408]{1,0:T(8,128)(2,1)}) custom-call(bf16[640,1408]{1,0:T(8,128)(2,1)} %copy-done.3, bf16[640,1408]{1,0:T(8,128)(2,1)} %get-tuple-element.84.refs_1_.refs_11_, ...), custom_call_target="tpu_custom_call" | custom-call | tf_op jit(solution)/shard_map/second_norm_back/pallas_call | solution.py:285
  287.8 1.1 fusion.6
  288.9 52.2 %attention_backward.1 = (bf16[256,2048]{1,0:T(8,128)(2,1)}, bf16[256,1536]{1,0:T(8,128)(2,1)}, bf16[160,512]{1,0:T(8,128)(2,1)}, bf16[3,256,1408]{2,1,0:T(8,128)(2,1)}, bf16[256,1408]{1,0:T(8,128)(2,1)}) custom-call(bf16[256,512]{1,0:T(8,128)(2,1)} %get-tuple-element.89.refs_0_, bf16[2048,512]{1,0:T(8,128)(2,1)} %get-tuple-element.72.refs_1_, ...), custom_call_target="tpu_custom_call" | custom-call | tf_op jit(solution)/shard_map/attention_backward/pallas_call | solution.py:285
  342.7 47.2 %first_norm_back.1 = (f32[256,512]{1,0:T(8,128)}, f32[8,512]{1,0:T(8,128)}, bf16[3,256,1408]{2,1,0:T(8,128)(2,1)}, bf16[256,1408]{1,0:T(8,128)(2,1)}) custom-call(bf16[256,1536]{1,0:T(8,128)(2,1)} %get-tuple-element.94.refs_0_.refs_3_, bf16[2048,1536]{1,0:T(8,128)(2,1)} %get-tuple-element.70.refs_1_, bf16[256,512]{1,0:T(8,128)(2,1)} %refs_2_.1, ...), custom_call_target="tpu_custom_call" | custom-call | tf_op jit(solution)/shard_map/first_norm_back/pallas_call | solution.py:285
  390.7 8.4 %write_out.2 = (f32[4,256,1408]{2,1,0:T(8,128)}, f32[4,256,1408]{2,1,0:T(8,128)}) custom-call(bf16[3,256,1408]{2,1,0:T(8,128)(2,1)} %get-tuple-element.101.refs_0_, bf16[256,1408]{1,0:T(8,128)(2,1)} %get-tuple-element.102.refs_1_, bf16[3,256,1408]{2,1,0:T(8,128)(2,1)} %get-tuple-element.103.refs_2_, bf16[256,1408]{1,0:T(8,128)(2,1)} %get-tuple-element.104.refs_3_), custom_call_target="tpu_custom_call" | custom-call | bytes 17301504 | tf_op jit(solution)/shard_map/write_out/pallas_call | solution.py:1410
  399.7 3.1 collective-permute-done.7.refs_12_
  402.8 80.7 %weight_grads.1 = (f32[256,2048]{1,0:T(8,128)}, f32[8,256]{1,0:T(8,128)}, bf16[256,512]{1,0:T(8,128)(2,1)}, bf16[3,256,1408]{2,1,0:T(8,128)(2,1)}, bf16[256,1408]{1,0:T(8,128)(2,1)}) custom-call(bf16[256,2048]{1,0:T(8,128)(2,1)} %get-tuple-element.93.refs_0_, bf16[256,512]{1,0:T(8,128)(2,1)} %get-tuple-element.71.refs_1_, ...), custom_call_target="tpu_custom_call" | custom-call | tf_op jit(solution)/shard_map/weight_grads/pallas_call | solution.py:285
  483.5 1.3 slice_bitcast_fusion
  484.8 1.3 fusion.26
  486.1 8.0 %write_out.3 = (f32[4,256,1408]{2,1,0:T(8,128)}, bf16[256,512]{1,0:T(8,128)(2,1)}, f32[256,512]{1,0:T(8,128)}, f32[256,512]{1,0:T(8,128)}, f32[256,512]{1,0:T(8,...) custom-call(bf16[3,256,1408]{2,1,0:T(8,128)(2,1)} %get-tuple-element.111.refs_0_, ...), custom_call_target="tpu_custom_call" | custom-call | bytes 8650752 | tf_op jit(solution)/shard_map/write_out/pallas_call | solution.py:1410
  (80 shorter events, 14.2 us)
Async XLA Ops:
  0.6 6.2 %copy-start.14 = (bf16[1024]{0:T(1024)(128)(2,1)S(1)}, bf16[1024]{0:T(1024)(128)(2,1)}, u32[]{:S(2)}) copy-start(bf16[1024]{0:T(1024)(128)(2,1)} %param.15) | copy-start | bytes 6148
  0.7 6.2 %copy-start.15 = (bf16[1024]{0:T(1024)(128)(2,1)S(1)}, bf16[1024]{0:T(1024)(128)(2,1)}, u32[]{:S(2)}) copy-start(bf16[1024]{0:T(1024)(128)(2,1)} %param.20) | copy-start | bytes 6148
  0.7 6.3 %copy-start.12 = (bf16[1024,4]{0,1:T(4,128)(2,1)S(1)}, bf16[1024,4]{0,1:T(4,128)(2,1)}, u32[]{:S(2)}) copy-start(bf16[1024,4]{0,1:T(4,128)(2,1)} %param.21) | copy-start | bytes 24580
  3.9 37.6 %collective-permute-start.1 = (bf16[256,2048]{1,0:T(8,128)(2,1)}, bf16[256,2048]{1,0:T(8,128)(2,1)}, u32[]{:S(2)}, u32[]{:S(2)}) collective-permute-start(bf16[256,2048]{1,0:T(8,128)(2,1)} %pad_maximum_fusion), channel_id=1, source_target_pairs={{0,16},{16,0},{1,17},{17,1},{2,18},{18,2},{3,19},{19,3},{4,20},{20... | collective-permute-start | bytes 3145736 | tf_op jit(solution)/shard_map/ppermute | solution.py:1457
  7.1 33.6 %collective-permute-start = (bf16[8,1024]{1,0:T(8,128)(2,1)S(1)}, bf16[8,1024]{1,0:T(8,128)(2,1)S(1)}, u32[]{:S(2)}, u32[]{:S(2)}) collective-permute-start(bf16[8,1024]{1,0:T(8,128)(2,1)S(1)} %maximum_maximum_fusion), channel_id=1, source_target_pairs={{0,16},{16,0},{1,17},{17,1},{2,18},{18,2},{3,19},{19,3},{4,20},{20... | collective-permute-start | bytes 49160 | tf_op jit(solution)/shard_map/ppermute | solution.py:1457
  9.1 24.7 %copy-start.1 = (bf16[1024,1408]{1,0:T(8,128)(2,1)}, bf16[1024,1408]{1,0:T(8,128)(2,1)S(1)}, u32[]{:S(2)}) copy-start(bf16[1024,1408]{1,0:T(8,128)(2,1)S(1)} %dynamic-slice_bitcast_fusion.refs_0_.refs_3_) | copy-start | bytes 8650756
  9.1 26.9 %copy-start.13 = (s32[256,2]{0,1:T(2,128)S(1)}, s32[256,2]{0,1:T(2,128)}, u32[]{:S(2)}) copy-start(s32[256,2]{0,1:T(2,128)} %param.25) | copy-start | bytes 6148
  9.1 180.5 %collective-permute-start.2 = (bf16[1024,1408]{1,0:T(8,128)(2,1)S(1)}, bf16[1024,1408]{1,0:T(8,128)(2,1)}, u32[]{:S(2)}, u32[]{:S(2)}) collective-permute-start(bf16[1024,1408]{1,0:T(8,128)(2,1)S(1)} %dynamic-slice_bitcast_fusion.refs_0_.refs_3_), channel_id=1, source_target_pairs={{0,16},{16,0},{1,17},{17,1},{2,18},{18,2},{3,19},{19,3},{4,20},{20... | collective-permute-start | bytes 8650760 | tf_op jit(solution)/shard_map/ppermute | solution.py:1457
  33.9 155.8 %collective-permute-start.3 = (bf16[1024,1408]{1,0:T(8,128)(2,1)}, bf16[1024,1408]{1,0:T(8,128)(2,1)}, u32[]{:S(2)}, u32[]{:S(2)}) collective-permute-start(bf16[1024,1408]{1,0:T(8,128)(2,1)} %get-tuple-element.77.refs_2_.refs_5_), channel_id=1, source_target_pairs={{0,16},{16,0},{1,17},{17,1},{2,18},{18,2},{3,19},{19,3},{4,20},{20... | collective-permute-start | bytes 8650760 | tf_op jit(solution)/shard_map/ppermute | solution.py:1457
  34.7 182.6 %collective-permute-start.4 = (bf16[1024,1408]{1,0:T(8,128)(2,1)}, bf16[1024,1408]{1,0:T(8,128)(2,1)}, u32[]{:S(2)}, u32[]{:S(2)}) collective-permute-start(bf16[1024,1408]{1,0:T(8,128)(2,1)} %get-tuple-element.80.refs_7_), channel_id=1, source_target_pairs={{0,16},{16,0},{1,17},{17,1},{2,18},{18,2},{3,19},{19,3},{4,20},{20... | collective-permute-start | bytes 8650760 | tf_op jit(solution)/shard_map/ppermute | solution.py:1457
  40.8 0.8 copy-start.11
  104.5 3.5 copy-start.10
  189.6 18.9 %copy-start.4 = (bf16[640,2048]{1,0:T(8,128)(2,1)S(1)}, bf16[640,2048]{1,0:T(8,128)(2,1)}, u32[]{:S(2)}) copy-start(bf16[640,2048]{1,0:T(8,128)(2,1)} %multiply_convert_fusion.refs_7_) | copy-start | bytes 7864324
  208.6 6.4 %copy-start.7 = (bf16[1024,1408]{1,0:T(8,128)(2,1)S(1)}, bf16[1024,1408]{1,0:T(8,128)(2,1)}, u32[]{:S(2)}) copy-start(bf16[1024,1408]{1,0:T(8,128)(2,1)} %get-tuple-element.80.refs_7_) | copy-start | bytes 8650756
  208.6 6.4 %copy-start.9 = (bf16[640,2048]{1,0:T(8,128)(2,1)S(1)}, bf16[640,2048]{1,0:T(8,128)(2,1)}, u32[]{:S(2)}) copy-start(bf16[640,2048]{1,0:T(8,128)(2,1)} %get-tuple-element.79) | copy-start | bytes 7864324
  214.3 74.6 %collective-permute-start.5 = (bf16[1024,1408]{1,0:T(8,128)(2,1)}, bf16[1024,1408]{1,0:T(8,128)(2,1)}, u32[]{:S(2)}, u32[]{:S(2)}) collective-permute-start(bf16[1024,1408]{1,0:T(8,128)(2,1)} %convolution_convert_fusion.1), channel_id=1, source_target_pairs={{0,16},{16,0},{1,17},{17,1},{2,18},{18,2},{3,19},{19,3},{4,20},{20... | collective-permute-start | bytes 8650760 | tf_op jit(solution)/shard_map/ppermute | solution.py:1457
  217.2 4.3 copy-start.2
  217.2 4.3 copy-start.5
  217.2 4.5 copy-start.6
  221.7 2.1 copy-start
  223.8 4.0 copy-start.3
  227.8 113.4 %collective-permute-start.6 = (bf16[1024,1408]{1,0:T(8,128)(2,1)}, bf16[1024,1408]{1,0:T(8,128)(2,1)S(1)}, u32[]{:S(2)}, u32[]{:S(2)}) collective-permute-start(bf16[1024,1408]{1,0:T(8,128)(2,1)} %convolution_convert_fusion), channel_id=1, source_target_pairs={{0,16},{16,0},{1,17},{17,1},{2,18},{18,2},{3,19},{19,3},{4,20},{20... | collective-permute-start | bytes 8650760 | tf_op jit(solution)/shard_map/ppermute | solution.py:1457
  286.3 116.5 %collective-permute-start.7 = (bf16[1024,1408]{1,0:T(8,128)(2,1)}, bf16[1024,1408]{1,0:T(8,128)(2,1)}, u32[]{:S(2)}, u32[]{:S(2)}) collective-permute-start(bf16[1024,1408]{1,0:T(8,128)(2,1)} %get-tuple-element.110), channel_id=1, source_target_pairs={{0,16},{16,0},{1,17},{17,1},{2,18},{18,2},{3,19},{19,3},{4,20},{20... | collective-permute-start | bytes 8650760 | tf_op jit(solution)/shard_map/ppermute | solution.py:1457
  341.1 1.6 copy-start.8

commit v10 on v9

--- a/solution.py
+++ b/solution.py
@@ -1063,18 +1063,18 @@
     )
 
 
-def first_norm_back(d_qkv, weights, hidden, scale, gain, d_resid, payload, n_tp, n_ctx):
+def first_norm_back(d_qkv, weights, hidden, scale, gain, d_resid, early, payload, n_tp, n_ctx):
     rows, size = hidden.shape
     width = size * n_tp
 
     def kernel(*refs):
-        dpr, wgt, hid, scl, gn, dr = refs[:6]
-        n_in, n_out = 6 + len(payload.inputs), len(payload.outs)
-        out, d_gain = refs[n_in : n_in + 2]
-        scratch = refs[n_in + 2 + n_out :]
+        dpr, wgt, hid, scl, gn, dr, erl = refs[:7]
+        n_in, n_out = 7 + len(payload.inputs), len(payload.outs)
+        out, d_gain, returned = refs[n_in : n_in + 3]
+        scratch = refs[n_in + 3 + n_out :]
         held, parts, slots, mine, sums, loads = scratch[:6]
         sems = scratch[6:10]
-        payload.take(refs[6:n_in], refs[n_in + 2 : n_in + 2 + n_out], scratch[10:])
+        payload.take(refs[7:n_in], refs[n_in + 3 : n_in + 3 + n_out], scratch[12:])
 
         def block(step):
             rank = peer("tp", n_tp, step)
@@ -1086,6 +1086,13 @@
             block(step).start()
         payload.load()
         greet([("tp", n_tp), ("ctx", n_ctx)])
+        given = [
+            send(
+                erl.at[pl.ds((k - 2) * CAP, CAP)], returned.at[k - 2],
+                "ctx", n_ctx, n_ctx - k, scratch[10:12],
+            )
+            for k in range(2, n_ctx)
+        ]
 
         def give(step):
             return described(
@@ -1118,12 +1125,18 @@
         dot = as_column(dot, eighth())[:, 0:1] * (1.0 / width)
         unit = hid[...].astype(F32) * factor
         out[...] = dr[...] + factor * (out[...] - unit * dot)
+        finish(given)
         payload.wait()
 
     return call(
         kernel,
-        (shape((rows, size), F32), shape((8, size), F32), *payload.outs),
-        (d_qkv, weights, hidden, scale, gain, d_resid, *payload.inputs),
+        (
+            shape((rows, size), F32),
+            shape((8, size), F32),
+            shape((n_ctx - 2, CAP, size), BF),
+            *payload.outs,
+        ),
+        (d_qkv, weights, hidden, scale, gain, d_resid, early, *payload.inputs),
         [
             pltpu.VMEM((n_tp, size, d_qkv.shape[1]), BF),
             pltpu.VMEM((n_tp - 1, rows, size), BF),
@@ -1133,55 +1146,66 @@
             DMA((n_tp,)),
         ]
         + pair_of_sems(n_tp) * 2
+        + pair_of_sems(n_ctx)
         + payload.scratch,
         6,
         "first_norm_back",
-        left=(1, 5 + len(payload.inputs), -len(payload.outs)),
+        left=(1, 6 + len(payload.inputs), -len(payload.outs)),
     )
 
 
 class ExpertsOut:
 
-    def __init__(self, made, done, picks, mix, resid, n_tp, n_ctx):
-        self.n_ctx, self.n_done = n_ctx, len(done)
-        first = CAP * len(done)
-        self.sums = RowSums(made, first, made.shape[0] - first, n_tp)
-        self.inputs = [made, *done, picks, mix, resid]
+    def __init__(self, made, returned, picks, mix, resid, n_tp, n_ctx):
+        self.n_ctx = n_ctx
+        self.left = n_ctx - returned.shape[0]
+        self.sums = RowSums(made, 0, self.left * CAP, n_tp)
+        self.inputs = [made, returned, picks, mix, resid]
         self.size = resid.shape[1]
         self.out = shape(resid.shape, BF)
         self.scratch = [
             pltpu.VMEM(self.sums.shape, BF),
-            pltpu.VMEM((n_ctx - 1, CAP, self.size), BF),
+            pltpu.VMEM((self.left - 1, CAP, self.size), BF),
         ]
-        self.scratch += pair_of_sems(n_ctx) + self.sums.scratch
+        self.scratch += pair_of_sems(n_ctx)
+        self.scratch += [pltpu.VMEM((n_ctx, resid.shape[0], 128), F32)] + self.sums.scratch
 
     def take(self, ins, out, scratch):
-        self.ins, self.out_ref, self.held = ins, out, scratch[:4]
-        self.sums.take(ins[0], scratch[4:])
-
-    def block(self, k):
-        if k < self.n_done:
-            return self.ins[1 + k]
-        return self.held[0].at[pl.ds((k - self.n_done) * CAP, CAP)]
+        self.ins, self.out_ref, self.held = ins, out, scratch[:5]
+        self.sums.take(ins[0], scratch[5:])
 
     def give_back(self):
         share, back = self.held[:2]
         share[...] = self.sums.total().astype(BF)
         n_ctx = self.n_ctx
         self.copies = [
-            send(self.block(k), back.at[k - 1], "ctx", n_ctx, n_ctx - k, self.held[2:4])
-            for k in range(1, n_ctx)
+            send(
+                share.at[pl.ds(k * CAP, CAP)], back.at[k - 1],
+                "ctx", n_ctx, n_ctx - k, self.held[2:4],
+            )
+            for k in range(1, self.left)
         ]
 
+    def prepare(self):
+        order = lax.broadcasted_iota(jnp.int32, (8, 128), 0)
+
+        @pl.loop(0, self.n_ctx)
+        def _(k):
+            self.held[4][k] = as_column(self.ins[-2][...], jnp.where(order == k, 1.0, 0.0))
+
     def mix(self):
-        picks, mix, resid = self.ins[-3:]
-        back = self.held[1]
+        returned, picks, mix, resid = self.ins[1:]
+        share, back = self.held[:2]
         finish(self.copies)
-        order = lax.broadcasted_iota(jnp.int32, (8, 128), 0)
         total = resid[...]
         for k in range(self.n_ctx):
-            gate = as_column(mix[...], jnp.where(order == k, 1.0, 0.0))[:, 0:1]
-            rows = self.block(0)[...] if k == 0 else back[k - 1]
+            gate = self.held[4][k, :, 0:1]
+            if k == 0:
+                rows = share[0:CAP]
+            elif k < self.left:
+                rows = back[k - 1]
+            else:
+                rows = returned[k - self.left]
             total = total + gate * t_mm(picks[k * CAP : (k + 1) * CAP], rows)
         self.out_ref[...] = total.astype(BF)
 
@@ -1276,6 +1300,7 @@
         for g in range(1, len(groups)):
             near(g)
             hop(g)
+        experts_out.prepare()
         lasts = []
         for g in range(len(groups)):
             far, one, last = scratch[6 * g + 3 : 6 * g + 6]
@@ -1285,7 +1310,7 @@
             lasts.append(
                 remote(one, last, sems[8 + 6 * g : 10 + 6 * g], 0, {"ctx": across})
             )
-            if g == 1:
+            if g == 0:
                 experts_out.give_back()
         finish(totals)
         sums = sml_full[:, columns(place, cut)]
@@ -1353,6 +1378,7 @@
         greet([("tp", n_tp), ("ctx", n_ctx)])
         experts_out.sums.start()
         payload.go()
+        experts_out.prepare()
         experts_out.give_back()
         experts_out.mix()
         payload.wait()
@@ -1614,14 +1640,23 @@
         up_come = swap_fsdp(up_away[0])
 
     payload = payload_of(d_result, hidden_act, down_come)
-    early = (RowSums(made, 0, CAP, n_tp), made)
+    early = (RowSums(made, 2 * CAP, 2 * CAP, n_tp), made)
     d_attn, d_qkv, made_early, *outs = attention_backward(
         d_attn_here, output_w, query, kv, cosine, -sine, early, payload, n_tp, n_ctx
     )
     grad_down = came_and_own(outs, payload)
     payload = payload_of(token_rows, d_gate_act, gate_come)
-    in_grad, gain_one_part, *outs = first_norm_back(
-        d_qkv, qkv_w, hidden_in, scale_one, gain_one_here, d_resid, payload, n_tp, n_ctx
+    in_grad, gain_one_part, returned, *outs = first_norm_back(
+        d_qkv,
+        qkv_w,
+        hidden_in,
+        scale_one,
+        gain_one_here,
+        d_resid,
+        made_early,
+        payload,
+        n_tp,
+        n_ctx,
     )
     grad_gate = came_and_own(outs, payload)
     payload = payload_of(token_rows, d_up_act, up_come)
@@ -1639,7 +1674,7 @@
     if pair:
         small_part = after(small_part, *written)
     grad_gate, grad_down = written
-    experts_out = ExpertsOut(made, (made_early,), picks, mix, resid, n_tp, n_ctx)
+    experts_out = ExpertsOut(made, returned, picks, mix, resid, n_tp, n_ctx)
     if pair:
         grad_attn, small_grad, block_out, *outs = weight_grads(
             [(d_attn, attended), (normed_one, d_qkv)],

time: 496 us -> 488 us (0.984)
  Pallas kernels: 426 us -> 421 us
  transfers between devices with their start and end apart: 8 -> 8, of which waited for: 1 -> 0; matrix products, arithmetic and copies ran while one was open for 10% -> 10% of each run, Pallas kernels for 68% -> 70%
where the time goes in v10:
time: 488 us; the launch traced here: 487 us
  Pallas kernels  421 us (86%)
  matrix products  29.1 us (6%)
  local copies, waits for them, and re-layouts  13.9 us (3%)
  other arithmetic  11.6 us (2%)
  starting transfers between devices  9.87 us (2%)
    pallas_call x8, Pallas kernels, call(): pl.pallas_call(kernel, out_shape=out_shape, in_specs=[anywhere if i in le...  386 us
    pallas_call x1, Pallas kernels, expert_acts(): pl.pallas_call(kernel, out_shape=(shape((rows, hidden), F32), shape((rows...  18.9 us
    pallas_call x2, Pallas kernels, write_out(): pl.pallas_call(kernel, grid=(steps,), in_specs=in_specs, out_specs=out_sp...  16.4 us
    dot_general x6, matrix products, mm(): return jnp.dot(left, right, preferred_element_type=F32)  16.1 us
    ppermute x8, starting transfers between devices, swap_fsdp(): return lax.ppermute(value, 'fsdp', [(0, 1), (1, 0)])  9.87 us
  transfers between devices with their start and end apart: 8, of which 0 were waited for; matrix products, arithmetic and copies ran while one was open for 10% of the time, Pallas kernels for 70%

profile of v10, /device:TPU:0, one launch (start us, length us, event | category | flops | bytes accessed | tf_op | source)
XLA Modules:
  0.0 487.0 jit_solution(8800455228209808320)
XLA Ops:
  0.7 1.1 constant_dynamic-slice_fusion.1
  1.8 1.1 constant_dynamic-slice_fusion.3
  2.8 1.1 pad_maximum_fusion
  3.9 2.9 collective-permute-start.1
  7.1 2.0 dynamic-slice_bitcast_fusion.refs_0_.refs_3_
  9.1 2.1 collective-permute-start.2
  11.2 22.6 %gather_tp.1 = (bf16[256,2048]{1,0:T(8,128)(2,1)}, bf16[1024,1408]{1,0:T(8,128)(2,1)}, bf16[1024,1408]{1,0:T(8,128)(2,1)}) custom-call(bf16[256,512]{1,0:T(8,128)(2,1)} %refs_2_.1, bf16[4,1024,1408]{2,1,0:T(8,128)(2,1)} %refs_0_.1, bf16[4,1024,1408]{2,1,0:T(8,128)(2,1)} %refs_1_.2), custom_call_target="tpu_custom_call" | custom-call | tf_op jit(solution)/shard_map/gather_tp/pallas_call | solution.py:285
  34.7 1.3 collective-permute-start.4
  39.7 0.9 fusion.24
  41.6 35.2 %first_norm.1 = (bf16[256,2048]{1,0:T(8,128)(2,1)}, f32[256,128]{1,0:T(8,128)}, bf16[256,2048]{1,0:T(8,128)(2,1)}, bf16[2048,1536]{1,0:T(8,128)(2,1)}, bf16[2048,512]{1,0:T(8,128)(2,1)}) custom-call(bf16[256,2048]{1,0:T(8,128)(2,1)} %get-tuple-element.69.refs_0_, bf16[256,512]{1,0:T(8,128)(2,1)} %refs_19_.1, f32[8,2048]{1,0:T(8,128)} %copy-done.11, ...), custom_call_target="tpu_custom_call" | custom-call | tf_op jit(solution)/shard_map/first_norm/pallas_call | solution.py:285
  76.8 6.1 %fusion.27.prj = f32[256,1536]{1,0:T(8,128)} fusion(bf16[256,2048]{1,0:T(8,128)(2,1)} %get-tuple-element.70.refs_2_, bf16[2048,1536]{1,0:T(8,128)(2,1)} %get-tuple-element.71.refs_1_), kind=kOutput, calls=%fused_computation.65 | convolution fusion | flops 1610612736 | bytes 8912896 | tf_op jit(solution)/shard_map/dot_general | solution.py:23
  82.8 21.7 %attention_forward.1 = (bf16[256,512]{1,0:T(8,128)(2,1)}, bf16[256,512]{1,0:T(8,128)(2,1)}, bf16[1024,1024]{1,0:T(8,128)(2,1)}) custom-call(f32[256,1536]{1,0:T(8,128)} %fusion.27.prj, f32[256,128]{1,0:T(8,128)} %pad_maximum_fusion.1.cs.refs_4_, f32[256,128]{1,0:T(8,128)} %get-tuple-element.127.sn), custom_call_target="tpu_custom_call" | custom-call | tf_op jit(solution)/shard_map/attention_forward/pallas_call | solution.py:285
  104.5 3.5 convolution_convert_fusion.3.prt
  108.0 2.3 convolution_convert_fusion.2.slb
  111.0 74.1 %second_norm.1 = (f32[256,512]{1,0:T(8,128)}, f32[256,128]{1,0:T(8,128)}, bf16[256,2048]{1,0:T(8,128)(2,1)}, bf16[640,2048]{1,0:T(8,128)(2,1)}, bf16[640,2048]{1...) custom-call(bf16[256,2048]{1,0:T(8,128)(2,1)} %convolution_convert_fusion.3.prt, ...), custom_call_target="tpu_custom_call" | custom-call | tf_op jit(solution)/shard_map/second_norm/pallas_call | solution.py:285
  185.9 3.8 multiply_convert_fusion.refs_7_
  189.7 18.9 %expert_acts.1 = (f32[640,1408]{1,0:T(8,128)}, f32[640,1408]{1,0:T(8,128)}, bf16[640,1408]{1,0:T(8,128)(2,1)}) custom-call(bf16[640,2048]{1,0:T(8,128)(2,1)} %get-tuple-element.77.tok.refs_9_.refs_7_.refs_10_, bf16[1024,1408]{1,0:T(8,128)(2,1)} %copy-done.1, bf16[1024,1408]{1,0:T(8,128)(2,1)} %collective-permute-done.2.refs_1_.refs_4_, ...), custom_call_target="tpu_custom_call" | custom-call | tf_op jit(solution)/shard_map/expert_acts/pallas_call | solution.py:681
  208.6 5.7 %convolution_convert_fusion.1 = bf16[1024,1408]{1,0:T(8,128)(2,1)} fusion(bf16[640,1408]{1,0:T(8,128)(2,1)} %get-tuple-element.86.refs_2_.refs_8_, bf16[640,2048]{1,0:T(8,128)(2,1)S(1)} %copy-done.4, s32[]{:T(128)S(6)} %select_n.56), kind=kOutput, calls=%fused_computation.2 | convolution fusion | flops 1846935552 | bytes 5996548 | tf_op jit(solution)/shard_map/dot_general | solution.py:31
  215.0 2.2 fusion.2
  217.2 4.2 convolution_add_fusion
  221.7 2.1 multiply_convert_fusion.1
  223.8 3.9 convolution_convert_fusion
  227.8 1.3 collective-permute-start.6
  229.8 56.5 %second_norm_back.1 = (f32[256,512]{1,0:T(8,128)}, bf16[256,512]{1,0:T(8,128)(2,1)}, f32[8,512]{1,0:T(8,128)}, f32[8,256]{1,0:T(8,128)}, bf16[640,2048]{1,0:T(8,128)(2,1)}, /*index=5*/bf16[1024,1408]{1,0:T(8,128)(2,1)}) custom-call(bf16[640,1408]{1,0:T(8,128)(2,1)} %copy-done.2, bf16[640,1408]{1,0:T(8,128)(2,1)} %get-tuple-element.85.refs_1_.refs_11_, ...), custom_call_target="tpu_custom_call" | custom-call | tf_op jit(solution)/shard_map/second_norm_back/pallas_call | solution.py:285
  287.8 1.1 fusion.6
  288.9 56.5 %attention_backward.1 = (bf16[256,2048]{1,0:T(8,128)(2,1)}, bf16[256,1536]{1,0:T(8,128)(2,1)}, bf16[320,512]{1,0:T(8,128)(2,1)}, bf16[3,256,1408]{2,1,0:T(8,128)(2,1)}, bf16[256,1408]{1,0:T(8,128)(2,1)}) custom-call(bf16[256,512]{1,0:T(8,128)(2,1)} %get-tuple-element.90.refs_0_, bf16[2048,512]{1,0:T(8,128)(2,1)} %get-tuple-element.73.refs_1_, ...), custom_call_target="tpu_custom_call" | custom-call | tf_op jit(solution)/shard_map/attention_backward/pallas_call | solution.py:285
  347.0 49.2 %first_norm_back.1 = (f32[256,512]{1,0:T(8,128)}, f32[8,512]{1,0:T(8,128)}, bf16[2,160,512]{2,1,0:T(8,128)(2,1)}, bf16[3,256,1408]{2,1,0:T(8,128)(2,1)}, bf16[256,1408]{1,0:T(8,128)(2,1)}) custom-call(bf16[256,1536]{1,0:T(8,128)(2,1)} %get-tuple-element.95.refs_0_.refs_3_, bf16[2048,1536]{1,0:T(8,128)(2,1)} %get-tuple-element.71.refs_1_, ...), custom_call_target="tpu_custom_call" | custom-call | tf_op jit(solution)/shard_map/first_norm_back/pallas_call | solution.py:285
  396.9 8.4 %write_out.2 = (f32[4,256,1408]{2,1,0:T(8,128)}, f32[4,256,1408]{2,1,0:T(8,128)}) custom-call(bf16[3,256,1408]{2,1,0:T(8,128)(2,1)} %get-tuple-element.103.refs_0_, bf16[256,1408]{1,0:T(8,128)(2,1)} %get-tuple-element.104.refs_1_, bf16[3,256,1408]{2,1,0:T(8,128)(2,1)} %get-tuple-element.105.refs_2_, bf16[256,1408]{1,0:T(8,128)(2,1)} %get-tuple-element.106.refs_3_), custom_call_target="tpu_custom_call" | custom-call | bytes 17301504 | tf_op jit(solution)/shard_map/write_out/pallas_call | solution.py:1436
  405.9 70.2 %weight_grads.1 = (f32[256,2048]{1,0:T(8,128)}, f32[8,256]{1,0:T(8,128)}, bf16[256,512]{1,0:T(8,128)(2,1)}, bf16[3,256,1408]{2,1,0:T(8,128)(2,1)}, bf16[256,1408]{1,0:T(8,128)(2,1)}) custom-call(bf16[256,2048]{1,0:T(8,128)(2,1)} %get-tuple-element.94.refs_0_, bf16[256,512]{1,0:T(8,128)(2,1)} %get-tuple-element.72.refs_1_, ...), custom_call_target="tpu_custom_call" | custom-call | tf_op jit(solution)/shard_map/weight_grads/pallas_call | solution.py:285
  476.2 1.3 slice_bitcast_fusion
  477.5 1.3 fusion.26
  478.8 8.0 %write_out.3 = (f32[4,256,1408]{2,1,0:T(8,128)}, bf16[256,512]{1,0:T(8,128)(2,1)}, f32[256,512]{1,0:T(8,128)}, f32[256,512]{1,0:T(8,128)}, f32[256,512]{1,0:T(8,...) custom-call(bf16[3,256,1408]{2,1,0:T(8,128)(2,1)} %get-tuple-element.113.refs_0_, ...), custom_call_target="tpu_custom_call" | custom-call | bytes 8650752 | tf_op jit(solution)/shard_map/write_out/pallas_call | solution.py:1436
  (80 shorter events, 13.2 us)
Async XLA Ops:
  0.6 6.2 %copy-start.14 = (bf16[1024]{0:T(1024)(128)(2,1)S(1)}, bf16[1024]{0:T(1024)(128)(2,1)}, u32[]{:S(2)}) copy-start(bf16[1024]{0:T(1024)(128)(2,1)} %param.15) | copy-start | bytes 6148
  0.7 6.2 %copy-start.15 = (bf16[1024]{0:T(1024)(128)(2,1)S(1)}, bf16[1024]{0:T(1024)(128)(2,1)}, u32[]{:S(2)}) copy-start(bf16[1024]{0:T(1024)(128)(2,1)} %param.20) | copy-start | bytes 6148
  0.7 6.3 %copy-start.12 = (bf16[1024,4]{0,1:T(4,128)(2,1)S(1)}, bf16[1024,4]{0,1:T(4,128)(2,1)}, u32[]{:S(2)}) copy-start(bf16[1024,4]{0,1:T(4,128)(2,1)} %param.21) | copy-start | bytes 24580
  3.9 37.6 %collective-permute-start.1 = (bf16[256,2048]{1,0:T(8,128)(2,1)}, bf16[256,2048]{1,0:T(8,128)(2,1)}, u32[]{:S(2)}, u32[]{:S(2)}) collective-permute-start(bf16[256,2048]{1,0:T(8,128)(2,1)} %pad_maximum_fusion), channel_id=1, source_target_pairs={{0,16},{16,0},{1,17},{17,1},{2,18},{18,2},{3,19},{19,3},{4,20},{20... | collective-permute-start | bytes 3145736 | tf_op jit(solution)/shard_map/ppermute | solution.py:1483
  7.1 33.6 %collective-permute-start = (bf16[8,1024]{1,0:T(8,128)(2,1)S(1)}, bf16[8,1024]{1,0:T(8,128)(2,1)S(1)}, u32[]{:S(2)}, u32[]{:S(2)}) collective-permute-start(bf16[8,1024]{1,0:T(8,128)(2,1)S(1)} %maximum_maximum_fusion), channel_id=1, source_target_pairs={{0,16},{16,0},{1,17},{17,1},{2,18},{18,2},{3,19},{19,3},{4,20},{20... | collective-permute-start | bytes 49160 | tf_op jit(solution)/shard_map/ppermute | solution.py:1483
  9.1 24.7 %copy-start.1 = (bf16[1024,1408]{1,0:T(8,128)(2,1)}, bf16[1024,1408]{1,0:T(8,128)(2,1)S(1)}, u32[]{:S(2)}) copy-start(bf16[1024,1408]{1,0:T(8,128)(2,1)S(1)} %dynamic-slice_bitcast_fusion.refs_0_.refs_3_) | copy-start | bytes 8650756
  9.1 26.9 %copy-start.13 = (s32[256,2]{0,1:T(2,128)S(1)}, s32[256,2]{0,1:T(2,128)}, u32[]{:S(2)}) copy-start(s32[256,2]{0,1:T(2,128)} %param.25) | copy-start | bytes 6148
  9.1 180.5 %collective-permute-start.2 = (bf16[1024,1408]{1,0:T(8,128)(2,1)S(1)}, bf16[1024,1408]{1,0:T(8,128)(2,1)}, u32[]{:S(2)}, u32[]{:S(2)}) collective-permute-start(bf16[1024,1408]{1,0:T(8,128)(2,1)S(1)} %dynamic-slice_bitcast_fusion.refs_0_.refs_3_), channel_id=1, source_target_pairs={{0,16},{16,0},{1,17},{17,1},{2,18},{18,2},{3,19},{19,3},{4,20},{20... | collective-permute-start | bytes 8650760 | tf_op jit(solution)/shard_map/ppermute | solution.py:1483
  33.9 155.8 %collective-permute-start.3 = (bf16[1024,1408]{1,0:T(8,128)(2,1)}, bf16[1024,1408]{1,0:T(8,128)(2,1)}, u32[]{:S(2)}, u32[]{:S(2)}) collective-permute-start(bf16[1024,1408]{1,0:T(8,128)(2,1)} %get-tuple-element.78.refs_2_.refs_5_), channel_id=1, source_target_pairs={{0,16},{16,0},{1,17},{17,1},{2,18},{18,2},{3,19},{19,3},{4,20},{20... | collective-permute-start | bytes 8650760 | tf_op jit(solution)/shard_map/ppermute | solution.py:1483
  34.7 182.6 %collective-permute-start.4 = (bf16[1024,1408]{1,0:T(8,128)(2,1)}, bf16[1024,1408]{1,0:T(8,128)(2,1)}, u32[]{:S(2)}, u32[]{:S(2)}) collective-permute-start(bf16[1024,1408]{1,0:T(8,128)(2,1)} %get-tuple-element.81.refs_7_), channel_id=1, source_target_pairs={{0,16},{16,0},{1,17},{17,1},{2,18},{18,2},{3,19},{19,3},{4,20},{20... | collective-permute-start | bytes 8650760 | tf_op jit(solution)/shard_map/ppermute | solution.py:1483
  40.8 0.8 copy-start.11
  104.5 3.5 copy-start.10
  189.6 18.9 %copy-start.4 = (bf16[640,2048]{1,0:T(8,128)(2,1)S(1)}, bf16[640,2048]{1,0:T(8,128)(2,1)}, u32[]{:S(2)}) copy-start(bf16[640,2048]{1,0:T(8,128)(2,1)} %multiply_convert_fusion.refs_7_) | copy-start | bytes 7864324
  208.6 6.4 %copy-start.7 = (bf16[1024,1408]{1,0:T(8,128)(2,1)S(1)}, bf16[1024,1408]{1,0:T(8,128)(2,1)}, u32[]{:S(2)}) copy-start(bf16[1024,1408]{1,0:T(8,128)(2,1)} %get-tuple-element.81.refs_7_) | copy-start | bytes 8650756
  208.6 6.4 %copy-start.9 = (bf16[640,2048]{1,0:T(8,128)(2,1)S(1)}, bf16[640,2048]{1,0:T(8,128)(2,1)}, u32[]{:S(2)}) copy-start(bf16[640,2048]{1,0:T(8,128)(2,1)} %get-tuple-element.80) | copy-start | bytes 7864324
  214.3 74.6 %collective-permute-start.5 = (bf16[1024,1408]{1,0:T(8,128)(2,1)}, bf16[1024,1408]{1,0:T(8,128)(2,1)}, u32[]{:S(2)}, u32[]{:S(2)}) collective-permute-start(bf16[1024,1408]{1,0:T(8,128)(2,1)} %convolution_convert_fusion.1), channel_id=1, source_target_pairs={{0,16},{16,0},{1,17},{17,1},{2,18},{18,2},{3,19},{19,3},{4,20},{20... | collective-permute-start | bytes 8650760 | tf_op jit(solution)/shard_map/ppermute | solution.py:1483
  217.2 4.3 copy-start.3
  217.2 4.3 copy-start.5
  217.2 4.5 copy-start.6
  221.7 2.1 copy-start
  223.8 4.0 copy-start.2
  227.8 117.6 %collective-permute-start.6 = (bf16[1024,1408]{1,0:T(8,128)(2,1)}, bf16[1024,1408]{1,0:T(8,128)(2,1)S(1)}, u32[]{:S(2)}, u32[]{:S(2)}) collective-permute-start(bf16[1024,1408]{1,0:T(8,128)(2,1)} %convolution_convert_fusion), channel_id=1, source_target_pairs={{0,16},{16,0},{1,17},{17,1},{2,18},{18,2},{3,19},{19,3},{4,20},{20... | collective-permute-start | bytes 8650760 | tf_op jit(solution)/shard_map/ppermute | solution.py:1483
  286.3 119.6 %collective-permute-start.7 = (bf16[1024,1408]{1,0:T(8,128)(2,1)}, bf16[1024,1408]{1,0:T(8,128)(2,1)}, u32[]{:S(2)}, u32[]{:S(2)}) collective-permute-start(bf16[1024,1408]{1,0:T(8,128)(2,1)} %get-tuple-element.112), channel_id=1, source_target_pairs={{0,16},{16,0},{1,17},{17,1},{2,18},{18,2},{3,19},{19,3},{4,20},{20... | collective-permute-start | bytes 8650760 | tf_op jit(solution)/shard_map/ppermute | solution.py:1483
  345.4 1.6 copy-start.8

commit v11 on v10

--- a/solution.py
+++ b/solution.py
@@ -124,15 +124,26 @@
             self.scratch += [
                 pltpu.VMEM((self.rows, self.hidden), BF),
                 pltpu.VMEM((self.rows, self.hidden), BF),
-                DMA,
+                pltpu.VMEM((self.inputs[0].shape[0], self.rows), BF),
+                pltpu.VMEM(self.inputs[1].shape, BF),
+                DMA((3,)),
             ]
 
     def take(self, ins, outs, scratch):
         self.ins, self.out_refs, self.held = ins, outs, scratch
 
+    def fetches(self):
+        left, right, other = self.ins
+        mine = left.at[:, columns(lax.axis_index("fsdp"), self.rows)]
+        return [
+            pltpu.make_async_copy(source, self.held[i], self.held[6].at[j])
+            for j, (source, i) in enumerate([(mine, 4), (right, 5), (other, 2)])
+        ]
+
     def load(self):
         if self.product:
-            pltpu.make_async_copy(self.ins[2], self.held[2], self.held[4]).start()
+            for copy in self.fetches():
+                copy.start()
 
     def copy(self, k):
         to = peer("ctx", self.n_ctx, k)
@@ -142,29 +153,27 @@
             self.held[0:2], k - 1, {"ctx": to},
         )
 
-    def go(self, first=0, last=4):
+    def go(self, between=lambda j: None):
         n_ctx, cut = self.n_ctx, self.cut
         if not self.product:
-            for j in range(first, last):
-                if (j + 2) % n_ctx:
-                    self.copy((j + 2) % n_ctx).start()
+            for k in (2, 3, 1):
+                self.copy(k).start()
             return
-        left, right, other = self.ins
-        if first == 0:
-            pltpu.make_async_copy(other, self.held[2], self.held[4]).wait()
-        base = lax.axis_index("fsdp") * self.rows
-
-        @pl.loop(first, last)
+        finish(self.fetches())
+
+        @pl.loop(0, n_ctx)
         def _(j):
             k = lax.rem(j + 2, n_ctx)
             to = peer("ctx", n_ctx, k)
-            value = t_mm(left[:, pl.ds(pl.multiple_of(base + to * cut, 128), cut)], right[...])
+            value = t_mm(self.held[4][:, columns(to, cut)], self.held[5][...])
             value = value + self.held[2][stretch(to, cut), :].astype(F32)
             self.held[3][stretch(to, cut), :] = value.astype(BF)
 
             @pl.when(j != n_ctx - 2)
             def _():
                 self.copy(k).start()
+
+            between(j)
 
     def wait(self):
         if self.product:
@@ -705,10 +714,10 @@
     part = weights[0][0].shape[0]
 
     def kernel(*refs):
-        dga, dup, hid = refs[:3]
+        dga, dup, hid_far = refs[:3]
         wgt = [refs[3 + i * count : 3 + (i + 1) * count] for i in range(3)]
         refs = refs[3 + 3 * count :]
-        tok, dts, pck, gts, one, nms, rtr, rsd, scl, gn, grd = refs[:11]
+        tok_far, dts, pck, gts, one, nms, rtr, rsd, scl, gn, grd = refs[:11]
         d_resid, low, d_gain, d_logits, out_rows = refs[11:16]
         refs = refs[16:]
         if count == 2:
@@ -716,9 +725,13 @@
             refs = refs[3:]
         (
             drw, eo, buffer, back, back_dots, parts, slots, mine, sums, mine_two, sums_two, loads,
-            out_sem,
-        ) = refs[:13]
-        sems = refs[13:]
+            out_sem, hid, tok, late,
+        ) = refs[:16]
+        sems = refs[16:]
+        fetches = [
+            pltpu.make_async_copy(hid_far, hid, late.at[0]),
+            pltpu.make_async_copy(tok_far, tok, late.at[1]),
+        ]
         here = lax.axis_index("tp")
         first = lax.axis_index("fsdp")
 
@@ -752,6 +765,8 @@
 
         load(0, peer("tp", n_tp, 1), 0, 0)
         load(1, peer("tp", n_tp, 1), 0, 1)
+        for copy in fetches:
+            copy.start()
         greet([("tp", n_tp), ("ctx", n_ctx)])
         small = []
         for k in range(1, n_ctx):
@@ -826,6 +841,7 @@
         ]
         pass_on(1, n_tp - 1)
 
+        finish(fetches)
 
         @pl.loop(0, n_tp)
         def _(rank):
@@ -914,13 +930,16 @@
             pltpu.VMEM((n_tp - 1, 8, rows), F32),
             DMA((2, 2)),
             DMA,
+            pltpu.VMEM((experts * CAP, hidden), BF),
+            pltpu.VMEM((experts * CAP, width), BF),
+            DMA((2,)),
         ]
         + pair_of_sems(n_ctx)
         + pair_of_sems(n_tp * n_ctx)
         + pair_of_sems(n_tp) * 3,
         4,
         "second_norm_back",
-        left=tuple(range(3, 3 + 3 * count)) + ((-2, -1) if count == 2 else (-1,)),
+        left=tuple(range(2, 4 + 3 * count)) + ((-2, -1) if count == 2 else (-1,)),
     )
 
 
@@ -938,23 +957,31 @@
     lane = 2 * half * HD
 
     def kernel(*refs):
-        lw, wgt, qry, full, cs, sn, made = refs[:7]
+        lw, wgt_far, qry_far, full_far, cs, sn, made = refs[:7]
         n_in, n_out = 7 + len(payload.inputs), len(payload.outs)
         d_attn, d_qkv, summed = refs[n_in : n_in + 3]
         scratch = refs[n_in + 3 + n_out :]
         dot, dqs, dkv, slots, last, both, total, kept = scratch[:8]
         sems = scratch[8:12]
-        sums.take(made, scratch[12 : 12 + len(sums.scratch)])
+        wgt, qry, full, late = scratch[12:16]
+        sums.take(made, scratch[16 : 16 + len(sums.scratch)])
         payload.take(
-            refs[7:n_in], refs[n_in + 3 : n_in + 3 + n_out], scratch[12 + len(sums.scratch) :]
+            refs[7:n_in], refs[n_in + 3 : n_in + 3 + n_out], scratch[16 + len(sums.scratch) :]
         )
         payload.load()
+        fetches = [
+            pltpu.make_async_copy(far, near, late.at[i])
+            for i, (far, near) in enumerate([(qry_far, qry), (full_far, full), (wgt_far, wgt)])
+        ]
+        for copy in fetches:
+            copy.start()
         greet([("tp", n_tp), ("ctx", n_ctx)])
         here, beside, across = quad()
         beyond = lax.rem(beside + 2, 4)
         copies = gather_columns(lw, d_attn, "tp", n_tp, sems[2:4])
         sums.start()
         payload.go()
+        finish(fetches)
 
         @pl.loop(0, heads)
         def _(h):
@@ -1055,11 +1082,15 @@
         ]
         + pair_of_sems(6)
         + pair_of_sems(n_tp)
+        + [
+            pltpu.VMEM(array.shape, BF) for array in (output_w, query, kv)
+        ]
+        + [DMA((3,))]
         + sums.scratch
         + payload.scratch,
         5,
         "attention_backward",
-        left=(6, 6 + len(payload.inputs), -len(payload.outs)),
+        left=(1, 2, 3, *range(6, 7 + len(payload.inputs)), -len(payload.outs)),
     )
 
 
@@ -1150,7 +1181,7 @@
         + payload.scratch,
         6,
         "first_norm_back",
-        left=(1, 6 + len(payload.inputs), -len(payload.outs)),
+        left=(1, *range(7, 7 + len(payload.inputs)), -len(payload.outs)),
     )
 
 
@@ -1210,16 +1241,17 @@
         self.out_ref[...] = total.astype(BF)
 
 
-def weight_grads(products, groups, small, payload, experts_out, n_tp, n_ctx):
+def weight_grads(ready, products, groups, small, payload, experts_out, n_tp, n_ctx):
     width = products[0][0].shape[1]
     places = 2 * n_ctx
     cut = width // places
     total_columns = sum(size for _, _, size in groups)
     flat = [array for pair in products for array in pair]
-    inputs = [*flat, small, *experts_out.inputs, *payload.inputs]
+    ready = ready.reshape(places, cut, -1)
+    inputs = [ready, *flat, small, *experts_out.inputs, *payload.inputs]
 
     def kernel(*refs):
-        factors, refs = refs[: len(flat)], refs[len(flat) :]
+        made_ready, factors, refs = refs[0], refs[1 : 1 + len(flat)], refs[1 + len(flat) :]
         sml, refs = refs[0], refs[1:]
         given, refs = refs[: len(experts_out.inputs)], refs[len(experts_out.inputs) :]
         paid, refs = refs[: len(payload.inputs)], refs[len(payload.inputs) :]
@@ -1230,7 +1262,9 @@
         experts_out.take(given, block_out, refs[: len(experts_out.scratch)])
         refs = refs[len(experts_out.scratch) :]
         payload.take(paid, paid_out, refs[: len(payload.scratch)])
-        sems = refs[len(payload.scratch) :]
+        sems = refs[len(payload.scratch) : -1]
+        fetch = pltpu.make_async_copy(made_ready, scratch[0], refs[-1])
+        fetch.start()
         payload.load()
         barrier = pltpu.get_barrier_semaphore()
         here, beside, across = quad()
@@ -1248,69 +1282,74 @@
         pl.semaphore_wait(barrier, n_tp - 1 + places - 1)
         gathers = gather_columns(sml, sml_full, "tp", n_tp, sems[0:2])
         experts_out.sums.start()
-        moves = []
+        blocks = [(other, beyond), (other, beside), (mine, beyond), (mine, beside)]
+
+        def near_copy(g, i):
+            prt, come = scratch[6 * g : 6 * g + 2]
+            rank, column = blocks[i]
+            return described(
+                prt.at[rank * n_ctx + column], come.at[i],
+                sems[4 + 6 * g : 6 + 6 * g], i, {"ctx": beside},
+            )
 
         def near(g):
             which, start, size = groups[g]
-            prt, come = scratch[6 * g : 6 * g + 2]
-            left, right = factors[2 * which : 2 * which + 2]
-
-            @pl.loop(0, places)
-            def _(i):
-                prt[i] = t_mm(left[:, columns(i, cut)], right[:, start : start + size]).astype(BF)
-
-            blocks = [(other, beyond), (other, beside), (mine, beyond), (mine, beside)]
-            moves.append(
-                [
-                    remote(
-                        prt.at[rank * n_ctx + column], come.at[i],
-                        sems[4 + 6 * g : 6 + 6 * g], i, {"ctx": beside},
-                    )
-                    for i, (rank, column) in enumerate(blocks)
-                ]
-            )
+            prt = scratch[6 * g]
+            if which is None:
+                fetch.wait()
+            else:
+                left, right = factors[2 * which : 2 * which + 2]
+
+                @pl.loop(0, places)
+                def _(i):
+                    prt[i] = t_mm(
+                        left[:, columns(i, cut)], right[:, start : start + size]
+                    ).astype(BF)
+
+            for i in range(4):
+                near_copy(g, i).start()
 
         def chip(g, i, rank, column):
             prt, come = scratch[6 * g : 6 * g + 2]
-            moves[g][i].wait()
+            near_copy(g, i).wait()
             return prt[rank * n_ctx + column].astype(F32) + come[i].astype(F32)
 
-        hops = []
+        def hop_copy(g, i):
+            two, far = scratch[6 * g + 2 : 6 * g + 4]
+            return described(
+                two.at[i], far.at[i], sems[6 + 6 * g : 8 + 6 * g], i, {"fsdp": other}
+            )
 
         def hop(g):
-            two, far = scratch[6 * g + 2 : 6 * g + 4]
-            sent = []
             for i, column in enumerate((across, here)):
-                two[i] = chip(g, i, other, column).astype(BF)
-                sent.append(
-                    remote(
-                        two.at[i], far.at[i], sems[6 + 6 * g : 8 + 6 * g], i, {"fsdp": other}
-                    )
-                )
-            hops.append(sent)
-
-        payload.go()
+                scratch[6 * g + 2][i] = chip(g, i, other, column).astype(BF)
+                hop_copy(g, i).start()
+
+        def between(j):
+            for turn_of, act in enumerate(
+                (lambda: hop(0), lambda: near(1), lambda: hop(1), lambda: near(2))
+            ):
+                pl.when(j == turn_of)(act)
+
         near(0)
+        payload.go(between)
+        hop(2)
         finish(gathers)
         totals = [
             remote(sml_full.at[:, columns(to, cut)], sml_slots.at[i], sems[2:4], i, device)
             for i, (to, device) in enumerate(others)
         ]
-        hop(0)
-        for g in range(1, len(groups)):
-            near(g)
-            hop(g)
         experts_out.prepare()
         lasts = []
         for g in range(len(groups)):
             far, one, last = scratch[6 * g + 3 : 6 * g + 6]
             value = chip(g, 2, mine, across)
-            hops[g][0].wait()
+            hop_copy(g, 0).wait()
             one[...] = (value + far[0].astype(F32)).astype(BF)
             lasts.append(
                 remote(one, last, sems[8 + 6 * g : 10 + 6 * g], 0, {"ctx": across})
             )
-            if g == 0:
+            if g == 1:
                 experts_out.give_back()
         finish(totals)
         sums = sml_full[:, columns(place, cut)]
@@ -1321,7 +1360,7 @@
         for g, (_, _, size) in enumerate(groups):
             far = scratch[6 * g + 3]
             value = chip(g, 3, mine, here)
-            hops[g][1].wait()
+            hop_copy(g, 1).wait()
             value = value + far[1].astype(F32)
             out[:, start : start + size] = value
             start += size
@@ -1355,12 +1394,13 @@
             *payload.outs,
         ),
         inputs,
-        buffers + experts_out.scratch + payload.scratch + sems,
+        buffers + experts_out.scratch + payload.scratch + sems + [DMA],
         10,
         "weight_grads",
         left=(
-            len(flat) + 1,
-            len(inputs) - 1,
+            0,
+            len(flat) + 2,
+            *range(len(inputs) - len(payload.inputs), len(inputs)),
             -len(payload.outs),
         ),
     )
@@ -1390,13 +1430,13 @@
         experts_out.scratch + payload.scratch,
         9,
         "experts_back",
-        left=(0, len(inputs) - 1, -len(payload.outs)),
+        left=(0, *range(given, len(inputs)), -len(payload.outs)),
     )
 
 
 def write_out(experts_grads, attn_grad, plain, n_ctx):
     _, rows, size = experts_grads[0][0].shape
-    steps = max(1, rows // 32)
+    steps = max(1, rows // 128)
     tile = rows // steps
     many = len(experts_grads)
     plain = list(plain)
@@ -1677,8 +1717,9 @@
     experts_out = ExpertsOut(made, returned, picks, mix, resid, n_tp, n_ctx)
     if pair:
         grad_attn, small_grad, block_out, *outs = weight_grads(
-            [(d_attn, attended), (normed_one, d_qkv)],
-            [(0, 0, heads_width), (1, 0, 2 * heads_width), (1, 2 * heads_width, heads_width)],
+            t_mm(d_attn, attended).astype(BF),
+            [(normed_one, d_qkv)],
+            [(None, 0, heads_width), (0, 0, 2 * heads_width), (0, 2 * heads_width, heads_width)],
             small_part,
             payload,
             experts_out,

time: 488 us -> 483 us (0.990)
  Pallas kernels: 421 us -> 411 us
    pallas_call x8, Pallas kernels: 386 us -> 380 us  [call(): pl.pallas_call(kernel, out_shape=out_shape, in_specs=[anywhere if i in le...]
    dot_general x2 -> x3, matrix products: 9.61 us -> 11.7 us  [t_mm(): lax.dot_general(left, right, (((0,), (0,)), ((), ())), preferred_element_...]
  transfers between devices with their start and end apart: 8 -> 8, of which waited for: 0 -> 1; matrix products, arithmetic and copies ran while one was open for 10% -> 10% of each run, Pallas kernels for 70% -> 70%
where the time goes in v11:
time: 483 us; the launch traced here: 481 us
  Pallas kernels  411 us (85%)
  matrix products  31.2 us (6%)
  local copies, waits for them, and re-layouts  13.9 us (3%)
  other arithmetic  11.6 us (2%)
  starting transfers between devices  10 us (2%)
    pallas_call x8, Pallas kernels, call(): pl.pallas_call(kernel, out_shape=out_shape, in_specs=[anywhere if i in le...  380 us
    pallas_call x1, Pallas kernels, expert_acts(): pl.pallas_call(kernel, out_shape=(shape((rows, hidden), F32), shape((rows...  18.9 us
    dot_general x6, matrix products, mm(): return jnp.dot(left, right, preferred_element_type=F32)  16.1 us
    pallas_call x2, Pallas kernels, write_out(): pl.pallas_call(kernel, grid=(steps,), in_specs=in_specs, out_specs=out_sp...  12 us
    dot_general x3, matrix products, t_mm(): lax.dot_general(left, right, (((0,), (0,)), ((), ())), preferred_element_...  11.7 us
    ppermute x8, starting transfers between devices, swap_fsdp(): return lax.ppermute(value, 'fsdp', [(0, 1), (1, 0)])  10 us
  transfers between devices with their start and end apart: 8, of which 1 were waited for; matrix products, arithmetic and copies ran while one was open for 10% of the time, Pallas kernels for 70%

profile of v11, /device:TPU:0, one launch (start us, length us, event | category | flops | bytes accessed | tf_op | source)
XLA Modules:
  0.0 480.8 jit_solution(14904392997286277882)
XLA Ops:
  0.7 1.1 constant_dynamic-slice_fusion.1
  2.8 1.1 pad_maximum_fusion
  3.9 2.9 collective-permute-start.1
  7.1 2.0 dynamic-slice_bitcast_fusion.refs_0_.refs_3_
  9.1 2.1 collective-permute-start.2
  11.2 22.6 %gather_tp.1 = (bf16[256,2048]{1,0:T(8,128)(2,1)}, bf16[1024,1408]{1,0:T(8,128)(2,1)}, bf16[1024,1408]{1,0:T(8,128)(2,1)}) custom-call(bf16[256,512]{1,0:T(8,128)(2,1)} %refs_2_.1, bf16[4,1024,1408]{2,1,0:T(8,128)(2,1)} %refs_0_.1, bf16[4,1024,1408]{2,1,0:T(8,128)(2,1)} %refs_1_.2), custom_call_target="tpu_custom_call" | custom-call | tf_op jit(solution)/shard_map/gather_tp/pallas_call | solution.py:294
  34.7 1.3 collective-permute-start.4
  41.6 35.2 %first_norm.1 = (bf16[256,2048]{1,0:T(8,128)(2,1)}, f32[256,128]{1,0:T(8,128)}, bf16[256,2048]{1,0:T(8,128)(2,1)}, bf16[2048,1536]{1,0:T(8,128)(2,1)}, bf16[2048,512]{1,0:T(8,128)(2,1)}) custom-call(bf16[256,2048]{1,0:T(8,128)(2,1)} %get-tuple-element.69.refs_0_, bf16[256,512]{1,0:T(8,128)(2,1)} %refs_19_.1, f32[8,2048]{1,0:T(8,128)} %copy-done.13, ...), custom_call_target="tpu_custom_call" | custom-call | tf_op jit(solution)/shard_map/first_norm/pallas_call | solution.py:294
  76.8 6.1 %fusion.27.prj = f32[256,1536]{1,0:T(8,128)} fusion(bf16[256,2048]{1,0:T(8,128)(2,1)} %get-tuple-element.70.refs_1_, bf16[2048,1536]{1,0:T(8,128)(2,1)} %get-tuple-element.71.refs_1_), kind=kOutput, calls=%fused_computation.66 | convolution fusion | flops 1610612736 | bytes 8912896 | tf_op jit(solution)/shard_map/dot_general | solution.py:23
  82.8 21.7 %attention_forward.1 = (bf16[256,512]{1,0:T(8,128)(2,1)}, bf16[256,512]{1,0:T(8,128)(2,1)}, bf16[1024,1024]{1,0:T(8,128)(2,1)}) custom-call(f32[256,1536]{1,0:T(8,128)} %fusion.27.prj, f32[256,128]{1,0:T(8,128)} %pad_maximum_fusion.1.cs.refs_4_, f32[256,128]{1,0:T(8,128)} %get-tuple-element.127.sn), custom_call_target="tpu_custom_call" | custom-call | tf_op jit(solution)/shard_map/attention_forward/pallas_call | solution.py:294
  104.5 3.5 convolution_convert_fusion.4.prt
  108.0 2.3 convolution_convert_fusion.2.slb
  111.0 74.0 %second_norm.1 = (f32[256,512]{1,0:T(8,128)}, f32[256,128]{1,0:T(8,128)}, bf16[256,2048]{1,0:T(8,128)(2,1)}, bf16[640,2048]{1,0:T(8,128)(2,1)}, bf16[640,2048]{1...) custom-call(bf16[256,2048]{1,0:T(8,128)(2,1)} %convolution_convert_fusion.4.prt, ...), custom_call_target="tpu_custom_call" | custom-call | tf_op jit(solution)/shard_map/second_norm/pallas_call | solution.py:294
  185.8 3.8 multiply_convert_fusion.refs_7_
  189.6 18.9 %expert_acts.1 = (f32[640,1408]{1,0:T(8,128)}, f32[640,1408]{1,0:T(8,128)}, bf16[640,1408]{1,0:T(8,128)(2,1)}) custom-call(bf16[640,2048]{1,0:T(8,128)(2,1)} %get-tuple-element.77.tok.refs_9_.refs_7_, bf16[1024,1408]{1,0:T(8,128)(2,1)} %copy-done.1, bf16[1024,1408]{1,0:T(8,128)(2,1)} %collective-permute-done.2.refs_1_.refs_4_, ...), custom_call_target="tpu_custom_call" | custom-call | tf_op jit(solution)/shard_map/expert_acts/pallas_call | solution.py:690
  208.6 5.7 %convolution_convert_fusion.1 = bf16[1024,1408]{1,0:T(8,128)(2,1)} fusion(bf16[640,1408]{1,0:T(8,128)(2,1)} %get-tuple-element.86.refs_2_.refs_8_, bf16[640,2048]{1,0:T(8,128)(2,1)S(1)} %copy-done.4, s32[]{:T(128)S(6)} %select_n.56), kind=kOutput, calls=%fused_computation.2 | convolution fusion | flops 1846935552 | bytes 5996548 | tf_op jit(solution)/shard_map/dot_general | solution.py:31
  215.0 2.2 fusion.2
  217.2 4.2 convolution_add_fusion
  221.7 2.1 multiply_convert_fusion.1
  223.8 3.9 convolution_convert_fusion
  227.8 1.3 collective-permute-start.6
  229.8 55.1 %second_norm_back.1 = (f32[256,512]{1,0:T(8,128)}, bf16[256,512]{1,0:T(8,128)(2,1)}, f32[8,512]{1,0:T(8,128)}, f32[8,256]{1,0:T(8,128)}, bf16[640,2048]{1,0:T(8,128)(2,1)}, /*index=5*/bf16[1024,1408]{1,0:T(8,128)(2,1)}) custom-call(bf16[640,1408]{1,0:T(8,128)(2,1)} %copy-done.2, bf16[640,1408]{1,0:T(8,128)(2,1)} %get-tuple-element.85.refs_1_.refs_10_, ...), custom_call_target="tpu_custom_call" | custom-call | tf_op jit(solution)/shard_map/second_norm_back/pallas_call | solution.py:294
  286.5 1.1 fusion.6
  287.6 53.8 %attention_backward.1 = (bf16[256,2048]{1,0:T(8,128)(2,1)}, bf16[256,1536]{1,0:T(8,128)(2,1)}, bf16[320,512]{1,0:T(8,128)(2,1)}, bf16[3,256,1408]{2,1,0:T(8,128)(2,1)}, bf16[256,1408]{1,0:T(8,128)(2,1)}) custom-call(bf16[256,512]{1,0:T(8,128)(2,1)} %get-tuple-element.90.refs_0_, bf16[2048,512]{1,0:T(8,128)(2,1)} %get-tuple-element.73.refs_1_, ...), custom_call_target="tpu_custom_call" | custom-call | tf_op jit(solution)/shard_map/attention_backward/pallas_call | solution.py:294
  343.1 47.6 %first_norm_back.1 = (f32[256,512]{1,0:T(8,128)}, f32[8,512]{1,0:T(8,128)}, bf16[2,160,512]{2,1,0:T(8,128)(2,1)}, bf16[3,256,1408]{2,1,0:T(8,128)(2,1)}, bf16[256,1408]{1,0:T(8,128)(2,1)}) custom-call(bf16[256,1536]{1,0:T(8,128)(2,1)} %get-tuple-element.95.refs_0_.refs_2_, bf16[2048,1536]{1,0:T(8,128)(2,1)} %get-tuple-element.71.refs_1_, ...), custom_call_target="tpu_custom_call" | custom-call | tf_op jit(solution)/shard_map/first_norm_back/pallas_call | solution.py:294
  391.4 6.6 %write_out.2 = (f32[4,256,1408]{2,1,0:T(8,128)}, f32[4,256,1408]{2,1,0:T(8,128)}) custom-call(bf16[3,256,1408]{2,1,0:T(8,128)(2,1)} %get-tuple-element.103.refs_0_, bf16[256,1408]{1,0:T(8,128)(2,1)} %get-tuple-element.104.refs_1_, bf16[3,256,1408]{2,1,0:T(8,128)(2,1)} %get-tuple-element.105.refs_2_, bf16[256,1408]{1,0:T(8,128)(2,1)} %get-tuple-element.106.refs_3_), custom_call_target="tpu_custom_call" | custom-call | bytes 17301504 | tf_op jit(solution)/shard_map/write_out/pallas_call | solution.py:1476
  398.6 2.1 convolution_convert_fusion.3
  400.7 2.1 collective-permute-done.7.refs_11_
  402.7 69.8 %weight_grads.1 = (f32[256,2048]{1,0:T(8,128)}, f32[8,256]{1,0:T(8,128)}, bf16[256,512]{1,0:T(8,128)(2,1)}, bf16[3,256,1408]{2,1,0:T(8,128)(2,1)}, bf16[256,1408]{1,0:T(8,128)(2,1)}) custom-call(bf16[8,256,512]{2,1,0:T(8,128)(2,1)} %bitcast.33, bf16[256,2048]{1,0:T(8,128)(2,1)} %get-tuple-element.70.refs_1_, ...), custom_call_target="tpu_custom_call" | custom-call | tf_op jit(solution)/shard_map/weight_grads/pallas_call | solution.py:294
  472.6 1.3 slice_bitcast_fusion
  473.9 1.3 fusion.26
  475.2 5.4 %write_out.3 = (f32[4,256,1408]{2,1,0:T(8,128)}, bf16[256,512]{1,0:T(8,128)(2,1)}, f32[256,512]{1,0:T(8,128)}, f32[256,512]{1,0:T(8,128)}, f32[256,512]{1,0:T(8,...) custom-call(bf16[3,256,1408]{2,1,0:T(8,128)(2,1)} %get-tuple-element.113.refs_0_, ...), custom_call_target="tpu_custom_call" | custom-call | bytes 8650752 | tf_op jit(solution)/shard_map/write_out/pallas_call | solution.py:1476
  (85 shorter events, 15.4 us)
Async XLA Ops:
  0.6 6.2 %copy-start.16 = (bf16[1024]{0:T(1024)(128)(2,1)S(1)}, bf16[1024]{0:T(1024)(128)(2,1)}, u32[]{:S(2)}) copy-start(bf16[1024]{0:T(1024)(128)(2,1)} %param.15) | copy-start | bytes 6148
  0.7 6.2 %copy-start.17 = (bf16[1024]{0:T(1024)(128)(2,1)S(1)}, bf16[1024]{0:T(1024)(128)(2,1)}, u32[]{:S(2)}) copy-start(bf16[1024]{0:T(1024)(128)(2,1)} %param.20) | copy-start | bytes 6148
  0.7 6.3 %copy-start.14 = (bf16[1024,4]{0,1:T(4,128)(2,1)S(1)}, bf16[1024,4]{0,1:T(4,128)(2,1)}, u32[]{:S(2)}) copy-start(bf16[1024,4]{0,1:T(4,128)(2,1)} %param.21) | copy-start | bytes 24580
  3.9 37.6 %collective-permute-start.1 = (bf16[256,2048]{1,0:T(8,128)(2,1)}, bf16[256,2048]{1,0:T(8,128)(2,1)}, u32[]{:S(2)}, u32[]{:S(2)}) collective-permute-start(bf16[256,2048]{1,0:T(8,128)(2,1)} %pad_maximum_fusion), channel_id=1, source_target_pairs={{0,16},{16,0},{1,17},{17,1},{2,18},{18,2},{3,19},{19,3},{4,20},{20... | collective-permute-start | bytes 3145736 | tf_op jit(solution)/shard_map/ppermute | solution.py:1523
  7.1 33.6 %collective-permute-start = (bf16[8,1024]{1,0:T(8,128)(2,1)S(1)}, bf16[8,1024]{1,0:T(8,128)(2,1)S(1)}, u32[]{:S(2)}, u32[]{:S(2)}) collective-permute-start(bf16[8,1024]{1,0:T(8,128)(2,1)S(1)} %maximum_maximum_fusion), channel_id=1, source_target_pairs={{0,16},{16,0},{1,17},{17,1},{2,18},{18,2},{3,19},{19,3},{4,20},{20... | collective-permute-start | bytes 49160 | tf_op jit(solution)/shard_map/ppermute | solution.py:1523
  9.1 24.7 %copy-start.1 = (bf16[1024,1408]{1,0:T(8,128)(2,1)}, bf16[1024,1408]{1,0:T(8,128)(2,1)S(1)}, u32[]{:S(2)}) copy-start(bf16[1024,1408]{1,0:T(8,128)(2,1)S(1)} %dynamic-slice_bitcast_fusion.refs_0_.refs_3_) | copy-start | bytes 8650756
  9.1 26.9 %copy-start.15 = (s32[256,2]{0,1:T(2,128)S(1)}, s32[256,2]{0,1:T(2,128)}, u32[]{:S(2)}) copy-start(s32[256,2]{0,1:T(2,128)} %param.25) | copy-start | bytes 6148
  9.1 180.5 %collective-permute-start.2 = (bf16[1024,1408]{1,0:T(8,128)(2,1)S(1)}, bf16[1024,1408]{1,0:T(8,128)(2,1)}, u32[]{:S(2)}, u32[]{:S(2)}) collective-permute-start(bf16[1024,1408]{1,0:T(8,128)(2,1)S(1)} %dynamic-slice_bitcast_fusion.refs_0_.refs_3_), channel_id=1, source_target_pairs={{0,16},{16,0},{1,17},{17,1},{2,18},{18,2},{3,19},{19,3},{4,20},{20... | collective-permute-start | bytes 8650760 | tf_op jit(solution)/shard_map/ppermute | solution.py:1523
  33.9 155.7 %collective-permute-start.3 = (bf16[1024,1408]{1,0:T(8,128)(2,1)}, bf16[1024,1408]{1,0:T(8,128)(2,1)}, u32[]{:S(2)}, u32[]{:S(2)}) collective-permute-start(bf16[1024,1408]{1,0:T(8,128)(2,1)} %get-tuple-element.78.refs_2_.refs_5_), channel_id=1, source_target_pairs={{0,16},{16,0},{1,17},{17,1},{2,18},{18,2},{3,19},{19,3},{4,20},{20... | collective-permute-start | bytes 8650760 | tf_op jit(solution)/shard_map/ppermute | solution.py:1523
  34.7 182.6 %collective-permute-start.4 = (bf16[1024,1408]{1,0:T(8,128)(2,1)}, bf16[1024,1408]{1,0:T(8,128)(2,1)}, u32[]{:S(2)}, u32[]{:S(2)}) collective-permute-start(bf16[1024,1408]{1,0:T(8,128)(2,1)} %get-tuple-element.81.refs_7_), channel_id=1, source_target_pairs={{0,16},{16,0},{1,17},{17,1},{2,18},{18,2},{3,19},{19,3},{4,20},{20... | collective-permute-start | bytes 8650760 | tf_op jit(solution)/shard_map/ppermute | solution.py:1523
  40.8 0.8 copy-start.13
  104.5 3.5 copy-start.11
  189.6 18.9 %copy-start.4 = (bf16[640,2048]{1,0:T(8,128)(2,1)S(1)}, bf16[640,2048]{1,0:T(8,128)(2,1)}, u32[]{:S(2)}) copy-start(bf16[640,2048]{1,0:T(8,128)(2,1)} %multiply_convert_fusion.refs_7_) | copy-start | bytes 7864324
  208.6 6.4 %copy-start.8 = (bf16[1024,1408]{1,0:T(8,128)(2,1)S(1)}, bf16[1024,1408]{1,0:T(8,128)(2,1)}, u32[]{:S(2)}) copy-start(bf16[1024,1408]{1,0:T(8,128)(2,1)} %get-tuple-element.81.refs_7_) | copy-start | bytes 8650756
  208.6 6.4 %copy-start.10 = (bf16[640,2048]{1,0:T(8,128)(2,1)S(1)}, bf16[640,2048]{1,0:T(8,128)(2,1)}, u32[]{:S(2)}) copy-start(bf16[640,2048]{1,0:T(8,128)(2,1)} %get-tuple-element.80) | copy-start | bytes 7864324
  214.2 73.4 %collective-permute-start.5 = (bf16[1024,1408]{1,0:T(8,128)(2,1)}, bf16[1024,1408]{1,0:T(8,128)(2,1)}, u32[]{:S(2)}, u32[]{:S(2)}) collective-permute-start(bf16[1024,1408]{1,0:T(8,128)(2,1)} %convolution_convert_fusion.1), channel_id=1, source_target_pairs={{0,16},{16,0},{1,17},{17,1},{2,18},{18,2},{3,19},{19,3},{4,20},{20... | collective-permute-start | bytes 8650760 | tf_op jit(solution)/shard_map/ppermute | solution.py:1523
  217.2 4.3 copy-start.3
  217.2 4.3 copy-start.6
  217.2 4.5 copy-start.7
  221.7 2.1 copy-start
  223.8 4.0 copy-start.2
  227.8 113.7 %collective-permute-start.6 = (bf16[1024,1408]{1,0:T(8,128)(2,1)}, bf16[1024,1408]{1,0:T(8,128)(2,1)S(1)}, u32[]{:S(2)}, u32[]{:S(2)}) collective-permute-start(bf16[1024,1408]{1,0:T(8,128)(2,1)} %convolution_convert_fusion), channel_id=1, source_target_pairs={{0,16},{16,0},{1,17},{17,1},{2,18},{18,2},{3,19},{19,3},{4,20},{20... | collective-permute-start | bytes 8650760 | tf_op jit(solution)/shard_map/ppermute | solution.py:1523
  284.9 117.8 %collective-permute-start.7 = (bf16[1024,1408]{1,0:T(8,128)(2,1)}, bf16[1024,1408]{1,0:T(8,128)(2,1)}, u32[]{:S(2)}, u32[]{:S(2)}) collective-permute-start(bf16[1024,1408]{1,0:T(8,128)(2,1)} %get-tuple-element.112), channel_id=1, source_target_pairs={{0,16},{16,0},{1,17},{17,1},{2,18},{18,2},{3,19},{19,3},{4,20},{20... | collective-permute-start | bytes 8650760 | tf_op jit(solution)/shard_map/ppermute | solution.py:1523
  341.5 1.6 copy-start.9
  391.4 7.3 %copy-start.5 = (bf16[256,2048]{1,0:T(8,128)(2,1)S(1)}, bf16[256,2048]{1,0:T(8,128)(2,1)}, u32[]{:S(2)}) copy-start(bf16[256,2048]{1,0:T(8,128)(2,1)} %get-tuple-element.94) | copy-start | bytes 3145732
  391.4 7.3 %copy-start.12 = (bf16[256,512]{1,0:T(8,128)(2,1)S(1)}, bf16[256,512]{1,0:T(8,128)(2,1)}, u32[]{:S(2)}) copy-start(bf16[256,512]{1,0:T(8,128)(2,1)} %get-tuple-element.72) | copy-start | bytes 786436

commit v12 on v11

--- a/solution.py
+++ b/solution.py
@@ -1094,18 +1094,30 @@
     )
 
 
-def first_norm_back(d_qkv, weights, hidden, scale, gain, d_resid, early, payload, n_tp, n_ctx):
+def first_norm_back(d_qkv, weights, hidden, scale, gain, d_resid, early, later, square, payload, n_tp, n_ctx):
+    n_square = len(square.inputs) if square else 0
+    more, more_input = later
     rows, size = hidden.shape
     width = size * n_tp
 
     def kernel(*refs):
-        dpr, wgt, hid, scl, gn, dr, erl = refs[:7]
+        dpr, wgt, hid, scl, gn, dr, erl, made = refs[:8]
+        refs = refs[:7] + refs[8:]
+        squared, refs = refs[7 : 7 + n_square], refs[:7] + refs[7 + n_square :]
         n_in, n_out = 7 + len(payload.inputs), len(payload.outs)
-        out, d_gain, returned = refs[n_in : n_in + 3]
+        out, d_gain, returned, summed = refs[n_in : n_in + 4]
+        refs = refs[: n_in + 3] + refs[n_in + 4 :]
+        squared_out = refs[n_in + 3 : n_in + 3 + 2 * n_square]
+        refs = refs[: n_in + 3] + refs[n_in + 3 + 2 * n_square :]
         scratch = refs[n_in + 3 + n_out :]
         held, parts, slots, mine, sums, loads = scratch[:6]
         sems = scratch[6:10]
-        payload.take(refs[7:n_in], refs[n_in + 3 : n_in + 3 + n_out], scratch[12:])
+        begin = 12 + len(more.scratch)
+        more.take(made, scratch[12:begin])
+        first = begin + (len(square.scratch) if square else 0)
+        payload.take(refs[7:n_in], refs[n_in + 3 : n_in + 3 + n_out], scratch[first:])
+        if square:
+            square.take(squared, squared_out, scratch[begin:first])
 
         def block(step):
             rank = peer("tp", n_tp, step)
@@ -1118,12 +1130,10 @@
         payload.load()
         greet([("tp", n_tp), ("ctx", n_ctx)])
         given = [
-            send(
-                erl.at[pl.ds((k - 2) * CAP, CAP)], returned.at[k - 2],
-                "ctx", n_ctx, n_ctx - k, scratch[10:12],
-            )
-            for k in range(2, n_ctx)
+            send(erl, returned, "ctx", n_ctx, n_ctx - 2, scratch[10:12])
         ]
+        if square:
+            square.start()
 
         def give(step):
             return described(
@@ -1143,6 +1153,8 @@
 
         copies = [give(step) for step in range(1, n_tp)]
         payload.go()
+        if square:
+            square.cross()
         finish(copies)
         total = out[...]
         for k in range(1, n_tp):
@@ -1154,9 +1166,13 @@
         out[...] = gained
         dot = total_over(row_sums(unit * gained), mine, sums, "tp", n_tp, sems[2:4])
         dot = as_column(dot, eighth())[:, 0:1] * (1.0 / width)
+        more.start()
         unit = hid[...].astype(F32) * factor
         out[...] = dr[...] + factor * (out[...] - unit * dot)
         finish(given)
+        summed[...] = more.total().astype(BF)
+        if square:
+            square.end()
         payload.wait()
 
     return call(
@@ -1164,10 +1180,16 @@
         (
             shape((rows, size), F32),
             shape((8, size), F32),
-            shape((n_ctx - 2, CAP, size), BF),
+            shape((CAP, size), BF),
+            shape(more.shape, BF),
+            *(square.outs if square else []),
             *payload.outs,
         ),
-        (d_qkv, weights, hidden, scale, gain, d_resid, early, *payload.inputs),
+        (
+            *(d_qkv, weights, hidden, scale, gain, d_resid, early, more_input),
+            *(square.inputs if square else []),
+            *payload.inputs,
+        ),
         [
             pltpu.VMEM((n_tp, size, d_qkv.shape[1]), BF),
             pltpu.VMEM((n_tp - 1, rows, size), BF),
@@ -1178,25 +1200,93 @@
         ]
         + pair_of_sems(n_tp) * 2
         + pair_of_sems(n_ctx)
+        + more.scratch
+        + (square.scratch if square else [])
         + payload.scratch,
         6,
         "first_norm_back",
-        left=(1, *range(7, 7 + len(payload.inputs)), -len(payload.outs)),
-    )
+        left=(1, *range(7, 8 + n_square + len(payload.inputs)), -len(payload.outs)),
+    )
+
+
+class SquareSum:
+
+    def __init__(self, ready, n_ctx):
+        self.n_ctx = n_ctx
+        _, rows, size = ready.shape
+        self.inputs = [ready]
+        self.outs = [shape((rows, size), BF), shape((rows, size), F32)]
+        self.scratch = [
+            pltpu.VMEM((4, rows, size), BF),
+            pltpu.VMEM((4, rows, size), BF),
+            pltpu.VMEM((2, rows, size), BF),
+            pltpu.VMEM((2, rows, size), BF),
+            DMA((4,)),
+        ]
+        self.scratch += pair_of_sems(4) + pair_of_sems(2)
+
+    def take(self, ins, outs, scratch):
+        self.ready, self.out_refs, self.held = ins[0], outs, scratch
+
+    def start(self):
+        here, beside, across = quad()
+        beyond = lax.rem(beside + 2, 4)
+        mine = lax.axis_index("fsdp")
+        other = 1 - mine
+
+        def block(rank, column):
+            return self.ready.at[rank * self.n_ctx + column]
+
+        self.fetches, self.near = [], []
+        for i, (rank, theirs, ours) in enumerate(
+            [(other, beyond, across), (mine, beyond, across),
+             (other, beside, here), (mine, beside, here)]
+        ):
+            self.near.append(
+                remote(
+                    block(rank, theirs), self.held[1].at[i], self.held[5:7], i, {"ctx": beside}
+                )
+            )
+            copy = pltpu.make_async_copy(
+                block(rank, ours), self.held[0].at[i], self.held[4].at[i]
+            )
+            copy.start()
+            self.fetches.append(copy)
+
+    def chip(self, i):
+        self.fetches[i].wait()
+        self.near[i].wait()
+        return self.held[0][i].astype(F32) + self.held[1][i].astype(F32)
+
+    def cross(self):
+        across = quad()[2]
+        two, far = self.held[2:4]
+        self.far = []
+        for i in range(2):
+            two[i] = self.chip(i).astype(BF)
+            self.far.append(
+                remote(two.at[i], far.at[i], self.held[7:9], i, {"ctx": across})
+            )
+
+    def end(self):
+        for i in range(2):
+            value = self.chip(2 + i)
+            self.far[i].wait()
+            value = value + self.held[3][i].astype(F32)
+            self.out_refs[i][...] = value.astype(BF) if i == 0 else value
 
 
 class ExpertsOut:
 
-    def __init__(self, made, returned, picks, mix, resid, n_tp, n_ctx):
+    def __init__(self, made, returned, last, picks, mix, resid, n_tp, n_ctx):
         self.n_ctx = n_ctx
-        self.left = n_ctx - returned.shape[0]
-        self.sums = RowSums(made, 0, self.left * CAP, n_tp)
-        self.inputs = [made, returned, picks, mix, resid]
+        self.sums = RowSums(made, 0, 2 * CAP, n_tp)
+        self.inputs = [made, returned, last, picks, mix, resid]
         self.size = resid.shape[1]
         self.out = shape(resid.shape, BF)
         self.scratch = [
             pltpu.VMEM(self.sums.shape, BF),
-            pltpu.VMEM((self.left - 1, CAP, self.size), BF),
+            pltpu.VMEM((2, CAP, self.size), BF),
         ]
         self.scratch += pair_of_sems(n_ctx)
         self.scratch += [pltpu.VMEM((n_ctx, resid.shape[0], 128), F32)] + self.sums.scratch
@@ -1210,11 +1300,8 @@
         share[...] = self.sums.total().astype(BF)
         n_ctx = self.n_ctx
         self.copies = [
-            send(
-                share.at[pl.ds(k * CAP, CAP)], back.at[k - 1],
-                "ctx", n_ctx, n_ctx - k, self.held[2:4],
-            )
-            for k in range(1, self.left)
+            send(share.at[pl.ds(CAP, CAP)], back.at[0], "ctx", n_ctx, n_ctx - 1, self.held[2:4]),
+            send(self.ins[2], back.at[1], "ctx", n_ctx, 1, self.held[2:4]),
         ]
 
     def prepare(self):
@@ -1225,33 +1312,29 @@
             self.held[4][k] = as_column(self.ins[-2][...], jnp.where(order == k, 1.0, 0.0))
 
     def mix(self):
-        returned, picks, mix, resid = self.ins[1:]
+        returned, _, picks, mix, resid = self.ins[1:]
         share, back = self.held[:2]
         finish(self.copies)
         total = resid[...]
         for k in range(self.n_ctx):
             gate = self.held[4][k, :, 0:1]
-            if k == 0:
-                rows = share[0:CAP]
-            elif k < self.left:
-                rows = back[k - 1]
-            else:
-                rows = returned[k - self.left]
+            rows = (share[0:CAP], back[0], returned[...], back[1])[k]
             total = total + gate * t_mm(picks[k * CAP : (k + 1) * CAP], rows)
         self.out_ref[...] = total.astype(BF)
 
 
-def weight_grads(ready, products, groups, small, payload, experts_out, n_tp, n_ctx):
+def weight_grads(squared, products, groups, small, payload, experts_out, n_tp, n_ctx):
     width = products[0][0].shape[1]
     places = 2 * n_ctx
     cut = width // places
-    total_columns = sum(size for _, _, size in groups)
+    total_columns = squared[0].shape[1] + sum(size for _, _, size in groups)
     flat = [array for pair in products for array in pair]
-    ready = ready.reshape(places, cut, -1)
-    inputs = [ready, *flat, small, *experts_out.inputs, *payload.inputs]
+    done = squared[0].shape[1]
+    inputs = [*squared, *flat, small, *experts_out.inputs, *payload.inputs]
 
     def kernel(*refs):
-        made_ready, factors, refs = refs[0], refs[1 : 1 + len(flat)], refs[1 + len(flat) :]
+        theirs, ours, refs = refs[0], refs[1], refs[2:]
+        factors, refs = refs[: len(flat)], refs[len(flat) :]
         sml, refs = refs[0], refs[1:]
         given, refs = refs[: len(experts_out.inputs)], refs[len(experts_out.inputs) :]
         paid, refs = refs[: len(payload.inputs)], refs[len(payload.inputs) :]
@@ -1262,9 +1345,8 @@
         experts_out.take(given, block_out, refs[: len(experts_out.scratch)])
         refs = refs[len(experts_out.scratch) :]
         payload.take(paid, paid_out, refs[: len(payload.scratch)])
-        sems = refs[len(payload.scratch) : -1]
-        fetch = pltpu.make_async_copy(made_ready, scratch[0], refs[-1])
-        fetch.start()
+        refs = refs[len(payload.scratch) :]
+        come, come_sems, sems = refs[0], refs[1:3], refs[3:]
         payload.load()
         barrier = pltpu.get_barrier_semaphore()
         here, beside, across = quad()
@@ -1281,6 +1363,7 @@
             pl.semaphore_signal(barrier, inc=1, device_id=device, device_id_type=MESH)
         pl.semaphore_wait(barrier, n_tp - 1 + places - 1)
         gathers = gather_columns(sml, sml_full, "tp", n_tp, sems[0:2])
+        early = remote(theirs, come, come_sems, 0, {"fsdp": other})
         experts_out.sums.start()
         blocks = [(other, beyond), (other, beside), (mine, beyond), (mine, beside)]
 
@@ -1295,16 +1378,11 @@
         def near(g):
             which, start, size = groups[g]
             prt = scratch[6 * g]
-            if which is None:
-                fetch.wait()
-            else:
-                left, right = factors[2 * which : 2 * which + 2]
-
-                @pl.loop(0, places)
-                def _(i):
-                    prt[i] = t_mm(
-                        left[:, columns(i, cut)], right[:, start : start + size]
-                    ).astype(BF)
+            left, right = factors[2 * which : 2 * which + 2]
+
+            @pl.loop(0, places)
+            def _(i):
+                prt[i] = t_mm(left[:, columns(i, cut)], right[:, start : start + size]).astype(BF)
 
             for i in range(4):
                 near_copy(g, i).start()
@@ -1327,13 +1405,11 @@
 
         def between(j):
             for turn_of, act in enumerate(
-                (lambda: hop(0), lambda: near(1), lambda: hop(1), lambda: near(2))
+                (lambda: near(0), lambda: hop(0), lambda: near(1), lambda: hop(1))
             ):
                 pl.when(j == turn_of)(act)
 
-        near(0)
         payload.go(between)
-        hop(2)
         finish(gathers)
         totals = [
             remote(sml_full.at[:, columns(to, cut)], sml_slots.at[i], sems[2:4], i, device)
@@ -1349,14 +1425,14 @@
             lasts.append(
                 remote(one, last, sems[8 + 6 * g : 10 + 6 * g], 0, {"ctx": across})
             )
-            if g == 1:
+            if g == 0:
                 experts_out.give_back()
         finish(totals)
         sums = sml_full[:, columns(place, cut)]
         for i in range(places - 1):
             sums = sums + sml_slots[i]
         small_out[...] = sums
-        start = 0
+        start = done
         for g, (_, _, size) in enumerate(groups):
             far = scratch[6 * g + 3]
             value = chip(g, 3, mine, here)
@@ -1364,9 +1440,11 @@
             value = value + far[1].astype(F32)
             out[:, start : start + size] = value
             start += size
+        early.wait()
+        out[:, 0:done] = ours[...] + come[...].astype(F32)
         experts_out.mix()
         payload.wait()
-        start = 0
+        start = done
         for g, (_, _, size) in enumerate(groups):
             lasts[g].wait()
             at = pl.ds(start, size)
@@ -1394,12 +1472,16 @@
             *payload.outs,
         ),
         inputs,
-        buffers + experts_out.scratch + payload.scratch + sems + [DMA],
+        buffers
+        + experts_out.scratch
+        + payload.scratch
+        + [pltpu.VMEM(squared[0].shape, BF)]
+        + pair_of_sems(1)
+        + sems,
         10,
         "weight_grads",
         left=(
-            0,
-            len(flat) + 2,
+            len(flat) + 3,
             *range(len(inputs) - len(payload.inputs), len(inputs)),
             -len(payload.outs),
         ),
@@ -1680,13 +1762,18 @@
         up_come = swap_fsdp(up_away[0])
 
     payload = payload_of(d_result, hidden_act, down_come)
-    early = (RowSums(made, 2 * CAP, 2 * CAP, n_tp), made)
+    early = (RowSums(made, 2 * CAP, CAP, n_tp), made)
     d_attn, d_qkv, made_early, *outs = attention_backward(
         d_attn_here, output_w, query, kv, cosine, -sine, early, payload, n_tp, n_ctx
     )
     grad_down = came_and_own(outs, payload)
     payload = payload_of(token_rows, d_gate_act, gate_come)
-    in_grad, gain_one_part, returned, *outs = first_norm_back(
+    square = None
+    if pair:
+        share = t_mm(d_attn, attended).astype(BF)
+        square = SquareSum(share.reshape(n_fsdp * n_ctx, quarter, heads_width), n_ctx)
+    later = (RowSums(made, 3 * CAP, CAP, n_tp), made)
+    in_grad, gain_one_part, returned, made_later, *outs = first_norm_back(
         d_qkv,
         qkv_w,
         hidden_in,
@@ -1694,10 +1781,14 @@
         gain_one_here,
         d_resid,
         made_early,
+        later,
+        square,
         payload,
         n_tp,
         n_ctx,
     )
+    if pair:
+        squared, outs = outs[:2], outs[2:]
     grad_gate = came_and_own(outs, payload)
     payload = payload_of(token_rows, d_up_act, up_come)
 
@@ -1714,12 +1805,12 @@
     if pair:
         small_part = after(small_part, *written)
     grad_gate, grad_down = written
-    experts_out = ExpertsOut(made, returned, picks, mix, resid, n_tp, n_ctx)
+    experts_out = ExpertsOut(made, returned, made_later, picks, mix, resid, n_tp, n_ctx)
     if pair:
         grad_attn, small_grad, block_out, *outs = weight_grads(
-            t_mm(d_attn, attended).astype(BF),
+            squared,
             [(normed_one, d_qkv)],
-            [(None, 0, heads_width), (0, 0, 2 * heads_width), (0, 2 * heads_width, heads_width)],
+            [(0, 0, 2 * heads_width), (0, 2 * heads_width, heads_width)],
             small_part,
             payload,
             experts_out,

time: 483 us -> 481 us (level)
  transfers between devices with their start and end apart: 8 -> 8, of which waited for: 1 -> 0; matrix products, arithmetic and copies ran while one was open for 10% -> 11% of each run, Pallas kernels for 70% -> 71%
where the time goes in v12:
time: 481 us; the launch traced here: 480 us
  Pallas kernels  411 us (85%)
  matrix products  32.4 us (7%)
  local copies, waits for them, and re-layouts  14.5 us (3%)
  other arithmetic  11.6 us (2%)
  starting transfers between devices  10 us (2%)
    pallas_call x8, Pallas kernels, call(): pl.pallas_call(kernel, out_shape=out_shape, in_specs=[anywhere if i in le...  380 us
    pallas_call x1, Pallas kernels, expert_acts(): pl.pallas_call(kernel, out_shape=(shape((rows, hidden), F32), shape((rows...  19 us
    dot_general x6, matrix products, mm(): return jnp.dot(left, right, preferred_element_type=F32)  16.1 us
    dot_general x3, matrix products, t_mm(): lax.dot_general(left, right, (((0,), (0,)), ((), ())), preferred_element_...  12.9 us
    pallas_call x2, Pallas kernels, write_out(): pl.pallas_call(kernel, grid=(steps,), in_specs=in_specs, out_specs=out_sp...  11.9 us
    ppermute x8, starting transfers between devices, swap_fsdp(): return lax.ppermute(value, 'fsdp', [(0, 1), (1, 0)])  10 us
  transfers between devices with their start and end apart: 8, of which 0 were waited for; matrix products, arithmetic and copies ran while one was open for 11% of the time, Pallas kernels for 71%

profile of v12, /device:TPU:0, one launch (start us, length us, event | category | flops | bytes accessed | tf_op | source)
XLA Modules:
  0.0 480.2 jit_solution(14394307996830815948)
XLA Ops:
  0.7 1.1 constant_dynamic-slice_fusion.1
  2.8 1.1 pad_maximum_fusion
  3.9 2.9 collective-permute-start.1
  7.1 2.0 dynamic-slice_bitcast_fusion.refs_0_.refs_3_
  9.1 2.1 collective-permute-start.2
  11.2 22.8 %gather_tp.1 = (bf16[256,2048]{1,0:T(8,128)(2,1)}, bf16[1024,1408]{1,0:T(8,128)(2,1)}, bf16[1024,1408]{1,0:T(8,128)(2,1)}) custom-call(bf16[256,512]{1,0:T(8,128)(2,1)} %refs_2_.1, bf16[4,1024,1408]{2,1,0:T(8,128)(2,1)} %refs_0_.1, bf16[4,1024,1408]{2,1,0:T(8,128)(2,1)} %refs_1_.2), custom_call_target="tpu_custom_call" | custom-call | tf_op jit(solution)/shard_map/gather_tp/pallas_call | solution.py:294
  34.8 1.3 collective-permute-start.4
  41.7 35.3 %first_norm.1 = (bf16[256,2048]{1,0:T(8,128)(2,1)}, f32[256,128]{1,0:T(8,128)}, bf16[256,2048]{1,0:T(8,128)(2,1)}, bf16[2048,1536]{1,0:T(8,128)(2,1)}, bf16[2048,512]{1,0:T(8,128)(2,1)}) custom-call(bf16[256,2048]{1,0:T(8,128)(2,1)} %get-tuple-element.72.refs_0_, bf16[256,512]{1,0:T(8,128)(2,1)} %refs_19_.1, f32[8,2048]{1,0:T(8,128)} %copy-done.12, ...), custom_call_target="tpu_custom_call" | custom-call | tf_op jit(solution)/shard_map/first_norm/pallas_call | solution.py:294
  77.0 6.1 %fusion.27.prj = f32[256,1536]{1,0:T(8,128)} fusion(bf16[256,2048]{1,0:T(8,128)(2,1)} %get-tuple-element.73.refs_2_, bf16[2048,1536]{1,0:T(8,128)(2,1)} %get-tuple-element.74.refs_1_), kind=kOutput, calls=%fused_computation.66 | convolution fusion | flops 1610612736 | bytes 8912896 | tf_op jit(solution)/shard_map/dot_general | solution.py:23
  83.0 21.7 %attention_forward.1 = (bf16[256,512]{1,0:T(8,128)(2,1)}, bf16[256,512]{1,0:T(8,128)(2,1)}, bf16[1024,1024]{1,0:T(8,128)(2,1)}) custom-call(f32[256,1536]{1,0:T(8,128)} %fusion.27.prj, f32[256,128]{1,0:T(8,128)} %pad_maximum_fusion.1.cs.refs_4_, f32[256,128]{1,0:T(8,128)} %get-tuple-element.133.sn), custom_call_target="tpu_custom_call" | custom-call | tf_op jit(solution)/shard_map/attention_forward/pallas_call | solution.py:294
  104.8 3.5 convolution_convert_fusion.4.prt
  108.2 2.3 convolution_convert_fusion.2.slb
  111.2 74.0 %second_norm.1 = (f32[256,512]{1,0:T(8,128)}, f32[256,128]{1,0:T(8,128)}, bf16[256,2048]{1,0:T(8,128)(2,1)}, bf16[640,2048]{1,0:T(8,128)(2,1)}, bf16[640,2048]{1...) custom-call(bf16[256,2048]{1,0:T(8,128)(2,1)} %convolution_convert_fusion.4.prt, ...), custom_call_target="tpu_custom_call" | custom-call | tf_op jit(solution)/shard_map/second_norm/pallas_call | solution.py:294
  186.0 3.7 multiply_convert_fusion.refs_7_
  189.8 19.0 %expert_acts.1 = (f32[640,1408]{1,0:T(8,128)}, f32[640,1408]{1,0:T(8,128)}, bf16[640,1408]{1,0:T(8,128)(2,1)}) custom-call(bf16[640,2048]{1,0:T(8,128)(2,1)} %get-tuple-element.80.tok.refs_9_.refs_11_, bf16[1024,1408]{1,0:T(8,128)(2,1)} %copy-done.1, bf16[1024,1408]{1,0:T(8,128)(2,1)} %collective-permute-done.2.refs_1_.refs_4_, ...), custom_call_target="tpu_custom_call" | custom-call | tf_op jit(solution)/shard_map/expert_acts/pallas_call | solution.py:690
  208.8 5.6 %convolution_convert_fusion.1 = bf16[1024,1408]{1,0:T(8,128)(2,1)} fusion(bf16[640,1408]{1,0:T(8,128)(2,1)} %get-tuple-element.89.refs_2_.refs_8_, bf16[640,2048]{1,0:T(8,128)(2,1)S(1)} %copy-done.4, s32[]{:T(128)S(6)} %select_n.56), kind=kOutput, calls=%fused_computation.2 | convolution fusion | flops 1846935552 | bytes 5996548 | tf_op jit(solution)/shard_map/dot_general | solution.py:31
  215.2 2.2 fusion.2
  217.4 4.2 convolution_add_fusion
  221.9 2.1 multiply_convert_fusion.1
  224.0 3.9 convolution_convert_fusion
  227.9 1.3 collective-permute-start.6
  229.9 55.2 %second_norm_back.1 = (f32[256,512]{1,0:T(8,128)}, bf16[256,512]{1,0:T(8,128)(2,1)}, f32[8,512]{1,0:T(8,128)}, f32[8,256]{1,0:T(8,128)}, bf16[640,2048]{1,0:T(8,128)(2,1)}, /*index=5*/bf16[1024,1408]{1,0:T(8,128)(2,1)}) custom-call(bf16[640,1408]{1,0:T(8,128)(2,1)} %copy-done.2, bf16[640,1408]{1,0:T(8,128)(2,1)} %get-tuple-element.88.refs_1_.refs_12_, ...), custom_call_target="tpu_custom_call" | custom-call | tf_op jit(solution)/shard_map/second_norm_back/pallas_call | solution.py:294
  286.7 1.1 fusion.6
  287.8 51.3 %attention_backward.1 = (bf16[256,2048]{1,0:T(8,128)(2,1)}, bf16[256,1536]{1,0:T(8,128)(2,1)}, bf16[160,512]{1,0:T(8,128)(2,1)}, bf16[3,256,1408]{2,1,0:T(8,128)(2,1)}, bf16[256,1408]{1,0:T(8,128)(2,1)}) custom-call(bf16[256,512]{1,0:T(8,128)(2,1)} %get-tuple-element.93.refs_0_, bf16[2048,512]{1,0:T(8,128)(2,1)} %get-tuple-element.76.refs_1_, ...), custom_call_target="tpu_custom_call" | custom-call | tf_op jit(solution)/shard_map/attention_backward/pallas_call | solution.py:294
  339.1 3.3 convolution_convert_fusion.3
  343.0 56.7 %first_norm_back.1 = (f32[256,512]{1,0:T(8,128)}, f32[8,512]{1,0:T(8,128)}, bf16[160,512]{1,0:T(8,128)(2,1)}, bf16[160,512]{1,0:T(8,128)(2,1)}, bf16[256,512]{1,...) custom-call(bf16[256,1536]{1,0:T(8,128)(2,1)} %get-tuple-element.97.refs_0_.refs_3_, ...), custom_call_target="tpu_custom_call" | custom-call | tf_op jit(solution)/shard_map/first_norm_back/pallas_call | solution.py:294
  400.5 6.5 %write_out.2 = (f32[4,256,1408]{2,1,0:T(8,128)}, f32[4,256,1408]{2,1,0:T(8,128)}) custom-call(bf16[3,256,1408]{2,1,0:T(8,128)(2,1)} %get-tuple-element.108.refs_0_, bf16[256,1408]{1,0:T(8,128)(2,1)} %get-tuple-element.109.refs_1_, bf16[3,256,1408]{2,1,0:T(8,128)(2,1)} %get-tuple-element.110.refs_2_, bf16[256,1408]{1,0:T(8,128)(2,1)} %get-tuple-element.111.refs_3_), custom_call_target="tpu_custom_call" | custom-call | bytes 17301504 | tf_op jit(solution)/shard_map/write_out/pallas_call | solution.py:1558
  407.6 1.6 copy-done.8
  409.2 62.8 %weight_grads.1 = (f32[256,2048]{1,0:T(8,128)}, f32[8,256]{1,0:T(8,128)}, bf16[256,512]{1,0:T(8,128)(2,1)}, bf16[3,256,1408]{2,1,0:T(8,128)(2,1)}, bf16[256,1408]{1,0:T(8,128)(2,1)}) custom-call(bf16[256,512]{1,0:T(8,128)(2,1)} %get-tuple-element.102.refs_0_, f32[256,512]{1,0:T(8,128)} %get-tuple-element.103.refs_1_, ...), custom_call_target="tpu_custom_call" | custom-call | tf_op jit(solution)/shard_map/weight_grads/pallas_call | solution.py:294
  472.0 1.3 slice_bitcast_fusion
  473.3 1.3 fusion.26
  474.6 5.4 %write_out.3 = (f32[4,256,1408]{2,1,0:T(8,128)}, bf16[256,512]{1,0:T(8,128)(2,1)}, f32[256,512]{1,0:T(8,128)}, f32[256,512]{1,0:T(8,128)}, f32[256,512]{1,0:T(8,...) custom-call(bf16[3,256,1408]{2,1,0:T(8,128)(2,1)} %get-tuple-element.119.refs_0_, ...), custom_call_target="tpu_custom_call" | custom-call | bytes 8650752 | tf_op jit(solution)/shard_map/write_out/pallas_call | solution.py:1558
  (83 shorter events, 14.5 us)
Async XLA Ops:
  0.6 6.2 %copy-start.15 = (bf16[1024]{0:T(1024)(128)(2,1)S(1)}, bf16[1024]{0:T(1024)(128)(2,1)}, u32[]{:S(2)}) copy-start(bf16[1024]{0:T(1024)(128)(2,1)} %param.15) | copy-start | bytes 6148
  0.7 6.2 %copy-start.16 = (bf16[1024]{0:T(1024)(128)(2,1)S(1)}, bf16[1024]{0:T(1024)(128)(2,1)}, u32[]{:S(2)}) copy-start(bf16[1024]{0:T(1024)(128)(2,1)} %param.20) | copy-start | bytes 6148
  0.7 6.3 %copy-start.13 = (bf16[1024,4]{0,1:T(4,128)(2,1)S(1)}, bf16[1024,4]{0,1:T(4,128)(2,1)}, u32[]{:S(2)}) copy-start(bf16[1024,4]{0,1:T(4,128)(2,1)} %param.21) | copy-start | bytes 24580
  3.9 37.7 %collective-permute-start.1 = (bf16[256,2048]{1,0:T(8,128)(2,1)}, bf16[256,2048]{1,0:T(8,128)(2,1)}, u32[]{:S(2)}, u32[]{:S(2)}) collective-permute-start(bf16[256,2048]{1,0:T(8,128)(2,1)} %pad_maximum_fusion), channel_id=1, source_target_pairs={{0,16},{16,0},{1,17},{17,1},{2,18},{18,2},{3,19},{19,3},{4,20},{20... | collective-permute-start | bytes 3145736 | tf_op jit(solution)/shard_map/ppermute | solution.py:1605
  7.1 33.7 %collective-permute-start = (bf16[8,1024]{1,0:T(8,128)(2,1)S(1)}, bf16[8,1024]{1,0:T(8,128)(2,1)S(1)}, u32[]{:S(2)}, u32[]{:S(2)}) collective-permute-start(bf16[8,1024]{1,0:T(8,128)(2,1)S(1)} %maximum_maximum_fusion), channel_id=1, source_target_pairs={{0,16},{16,0},{1,17},{17,1},{2,18},{18,2},{3,19},{19,3},{4,20},{20... | collective-permute-start | bytes 49160 | tf_op jit(solution)/shard_map/ppermute | solution.py:1605
  9.1 24.9 %copy-start.1 = (bf16[1024,1408]{1,0:T(8,128)(2,1)}, bf16[1024,1408]{1,0:T(8,128)(2,1)S(1)}, u32[]{:S(2)}) copy-start(bf16[1024,1408]{1,0:T(8,128)(2,1)S(1)} %dynamic-slice_bitcast_fusion.refs_0_.refs_3_) | copy-start | bytes 8650756
  9.1 27.0 %copy-start.14 = (s32[256,2]{0,1:T(2,128)S(1)}, s32[256,2]{0,1:T(2,128)}, u32[]{:S(2)}) copy-start(s32[256,2]{0,1:T(2,128)} %param.25) | copy-start | bytes 6148
  9.1 180.6 %collective-permute-start.2 = (bf16[1024,1408]{1,0:T(8,128)(2,1)S(1)}, bf16[1024,1408]{1,0:T(8,128)(2,1)}, u32[]{:S(2)}, u32[]{:S(2)}) collective-permute-start(bf16[1024,1408]{1,0:T(8,128)(2,1)S(1)} %dynamic-slice_bitcast_fusion.refs_0_.refs_3_), channel_id=1, source_target_pairs={{0,16},{16,0},{1,17},{17,1},{2,18},{18,2},{3,19},{19,3},{4,20},{20... | collective-permute-start | bytes 8650760 | tf_op jit(solution)/shard_map/ppermute | solution.py:1605
  34.0 155.8 %collective-permute-start.3 = (bf16[1024,1408]{1,0:T(8,128)(2,1)}, bf16[1024,1408]{1,0:T(8,128)(2,1)}, u32[]{:S(2)}, u32[]{:S(2)}) collective-permute-start(bf16[1024,1408]{1,0:T(8,128)(2,1)} %get-tuple-element.81.refs_2_.refs_5_), channel_id=1, source_target_pairs={{0,16},{16,0},{1,17},{17,1},{2,18},{18,2},{3,19},{19,3},{4,20},{20... | collective-permute-start | bytes 8650760 | tf_op jit(solution)/shard_map/ppermute | solution.py:1605
  34.8 182.6 %collective-permute-start.4 = (bf16[1024,1408]{1,0:T(8,128)(2,1)}, bf16[1024,1408]{1,0:T(8,128)(2,1)}, u32[]{:S(2)}, u32[]{:S(2)}) collective-permute-start(bf16[1024,1408]{1,0:T(8,128)(2,1)} %get-tuple-element.84.refs_7_), channel_id=1, source_target_pairs={{0,16},{16,0},{1,17},{17,1},{2,18},{18,2},{3,19},{19,3},{4,20},{20... | collective-permute-start | bytes 8650760 | tf_op jit(solution)/shard_map/ppermute | solution.py:1605
  40.9 0.8 copy-start.12
  104.7 3.5 copy-start.10
  189.8 19.0 %copy-start.4 = (bf16[640,2048]{1,0:T(8,128)(2,1)S(1)}, bf16[640,2048]{1,0:T(8,128)(2,1)}, u32[]{:S(2)}) copy-start(bf16[640,2048]{1,0:T(8,128)(2,1)} %multiply_convert_fusion.refs_7_) | copy-start | bytes 7864324
  208.8 6.4 %copy-start.7 = (bf16[1024,1408]{1,0:T(8,128)(2,1)S(1)}, bf16[1024,1408]{1,0:T(8,128)(2,1)}, u32[]{:S(2)}) copy-start(bf16[1024,1408]{1,0:T(8,128)(2,1)} %get-tuple-element.84.refs_7_) | copy-start | bytes 8650756
  208.8 6.4 %copy-start.9 = (bf16[640,2048]{1,0:T(8,128)(2,1)S(1)}, bf16[640,2048]{1,0:T(8,128)(2,1)}, u32[]{:S(2)}) copy-start(bf16[640,2048]{1,0:T(8,128)(2,1)} %get-tuple-element.83) | copy-start | bytes 7864324
  214.4 73.4 %collective-permute-start.5 = (bf16[1024,1408]{1,0:T(8,128)(2,1)}, bf16[1024,1408]{1,0:T(8,128)(2,1)}, u32[]{:S(2)}, u32[]{:S(2)}) collective-permute-start(bf16[1024,1408]{1,0:T(8,128)(2,1)} %convolution_convert_fusion.1), channel_id=1, source_target_pairs={{0,16},{16,0},{1,17},{17,1},{2,18},{18,2},{3,19},{19,3},{4,20},{20... | collective-permute-start | bytes 8650760 | tf_op jit(solution)/shard_map/ppermute | solution.py:1605
  217.4 4.3 copy-start.3
  217.4 4.3 copy-start.5
  217.4 4.5 copy-start.6
  221.9 2.1 copy-start
  224.0 4.0 copy-start.2
  227.9 114.5 %collective-permute-start.6 = (bf16[1024,1408]{1,0:T(8,128)(2,1)}, bf16[1024,1408]{1,0:T(8,128)(2,1)}, u32[]{:S(2)}, u32[]{:S(2)}) collective-permute-start(bf16[1024,1408]{1,0:T(8,128)(2,1)} %convolution_convert_fusion), channel_id=1, source_target_pairs={{0,16},{16,0},{1,17},{17,1},{2,18},{18,2},{3,19},{19,3},{4,20},{20... | collective-permute-start | bytes 8650760 | tf_op jit(solution)/shard_map/ppermute | solution.py:1605
  285.1 122.6 %collective-permute-start.7 = (bf16[1024,1408]{1,0:T(8,128)(2,1)}, bf16[1024,1408]{1,0:T(8,128)(2,1)S(1)}, u32[]{:S(2)}, u32[]{:S(2)}) collective-permute-start(bf16[1024,1408]{1,0:T(8,128)(2,1)} %get-tuple-element.118), channel_id=1, source_target_pairs={{0,16},{16,0},{1,17},{17,1},{2,18},{18,2},{3,19},{19,3},{4,20},{20... | collective-permute-start | bytes 8650760 | tf_op jit(solution)/shard_map/ppermute | solution.py:1605
  287.8 51.3 %copy-start.11 = (bf16[256,512]{1,0:T(8,128)(2,1)S(1)}, bf16[256,512]{1,0:T(8,128)(2,1)}, u32[]{:S(2)}) copy-start(bf16[256,512]{1,0:T(8,128)(2,1)} %get-tuple-element.75) | copy-start | bytes 786436
  407.6 1.6 copy-start.8

commit v13 on v12

--- a/solution.py
+++ b/solution.py
@@ -1516,7 +1516,7 @@
     )
 
 
-def write_out(experts_grads, attn_grad, plain, n_ctx):
+def write_out(experts_grads, attn_grad, plain, n_ctx, gains=None):
     _, rows, size = experts_grads[0][0].shape
     steps = max(1, rows // 128)
     tile = rows // steps
@@ -1530,6 +1530,10 @@
 
     def kernel(*refs):
         here = lax.axis_index("ctx")
+        if gains is not None:
+            rows_in, refs, rows_out = refs[0], refs[1:-2], refs[-2:]
+            for i in range(2):
+                rows_out[i][...] = rows_in[i : i + 1, :]
         ins, outs = refs[: 2 * many + len(plain)], refs[2 * many + len(plain) :]
         for i in range(many):
             came, mine = ins[2 * i : 2 * i + 2]
@@ -1555,6 +1559,12 @@
         out_shape.append(shape(array.shape, array.dtype))
     in_specs += [flat(array) for array in plain]
     inputs = [array for pair in experts_grads for array in pair] + plain
+    if gains is not None:
+        inputs = [gains] + inputs
+        in_specs = [pl.BlockSpec(gains.shape, lambda i: (0, 0))] + in_specs
+        for _ in range(2):
+            out_specs.append(pl.BlockSpec((1, gains.shape[1]), lambda i: (0, 0)))
+            out_shape.append(shape((1, gains.shape[1]), F32))
     return pl.pallas_call(
         kernel,
         grid=(steps,),
@@ -1827,18 +1837,21 @@
         small_grad = scatter(small_grad.T).T
         block_out, *outs = experts_back(experts_out, payload, n_tp, n_ctx)
     grad_up = came_and_own(outs, payload)
-    grad_up, block_out, in_grad, grad_output, grad_query, grad_key, grad_value = write_out(
-        [grad_up], grad_attn, (block_out, in_grad), n_ctx
+    (
+        grad_up, block_out, in_grad, grad_output, grad_query, grad_key, grad_value,
+        gain_one_grad, gain_two_grad,
+    ) = write_out(
+        [grad_up], grad_attn, (block_out, in_grad), n_ctx, small_grad
     )
     return (
         block_out,
         in_grad,
-        small_grad[0],
+        gain_one_grad.reshape(-1),
         grad_query,
         grad_key,
         grad_value,
         grad_output,
-        small_grad[1],
+        gain_two_grad.reshape(-1),
         small_grad[2 : 2 + experts].T,
         grad_gate,
         grad_up,

time: 481 us -> 480 us (level)
  transfers between devices with their start and end apart: 8 -> 8, of which waited for: 0 -> 0; matrix products, arithmetic and copies ran while one was open for 11% -> 11% of each run, Pallas kernels for 71% -> 72%
where the time goes in v13:
time: 480 us; the launch traced here: 479 us
  Pallas kernels  411 us (86%)
  matrix products  32.4 us (7%)
  local copies, waits for them, and re-layouts  13.2 us (3%)
  other arithmetic  11.6 us (2%)
  starting transfers between devices  9.94 us (2%)
    pallas_call x8, Pallas kernels, call(): pl.pallas_call(kernel, out_shape=out_shape, in_specs=[anywhere if i in le...  380 us
    pallas_call x1, Pallas kernels, expert_acts(): pl.pallas_call(kernel, out_shape=(shape((rows, hidden), F32), shape((rows...  19 us
    dot_general x6, matrix products, mm(): return jnp.dot(left, right, preferred_element_type=F32)  16.1 us
    dot_general x3, matrix products, t_mm(): lax.dot_general(left, right, (((0,), (0,)), ((), ())), preferred_element_...  12.8 us
    pallas_call x2, Pallas kernels, write_out(): pl.pallas_call(kernel, grid=(steps,), in_specs=in_specs, out_specs=out_sp...  11.9 us
    ppermute x8, starting transfers between devices, swap_fsdp(): return lax.ppermute(value, 'fsdp', [(0, 1), (1, 0)])  9.94 us
  transfers between devices with their start and end apart: 8, of which 0 were waited for; matrix products, arithmetic and copies ran while one was open for 11% of the time, Pallas kernels for 72%

profile of v13, /device:TPU:0, one launch (start us, length us, event | category | flops | bytes accessed | tf_op | source)
XLA Modules:
  0.0 479.0 jit_solution(2579528531342782913)
XLA Ops:
  0.7 1.1 constant_dynamic-slice_fusion.1
  1.8 1.1 constant_dynamic-slice_fusion.3
  2.8 1.1 pad_maximum_fusion
  3.9 2.9 collective-permute-start.1
  7.1 2.0 dynamic-slice_bitcast_fusion.refs_0_.refs_3_
  9.1 2.1 collective-permute-start.2
  11.2 22.7 %gather_tp.1 = (bf16[256,2048]{1,0:T(8,128)(2,1)}, bf16[1024,1408]{1,0:T(8,128)(2,1)}, bf16[1024,1408]{1,0:T(8,128)(2,1)}) custom-call(bf16[256,512]{1,0:T(8,128)(2,1)} %refs_2_.1, bf16[4,1024,1408]{2,1,0:T(8,128)(2,1)} %refs_0_.1, bf16[4,1024,1408]{2,1,0:T(8,128)(2,1)} %refs_1_.2), custom_call_target="tpu_custom_call" | custom-call | tf_op jit(solution)/shard_map/gather_tp/pallas_call | solution.py:294
  34.8 1.3 collective-permute-start.4
  41.7 35.3 %first_norm.1 = (bf16[256,2048]{1,0:T(8,128)(2,1)}, f32[256,128]{1,0:T(8,128)}, bf16[256,2048]{1,0:T(8,128)(2,1)}, bf16[2048,1536]{1,0:T(8,128)(2,1)}, bf16[2048,512]{1,0:T(8,128)(2,1)}) custom-call(bf16[256,2048]{1,0:T(8,128)(2,1)} %get-tuple-element.74.refs_0_, bf16[256,512]{1,0:T(8,128)(2,1)} %refs_19_.1, f32[8,2048]{1,0:T(8,128)} %copy-done.12, ...), custom_call_target="tpu_custom_call" | custom-call | tf_op jit(solution)/shard_map/first_norm/pallas_call | solution.py:294
  77.0 6.1 %fusion.26.prj = f32[256,1536]{1,0:T(8,128)} fusion(bf16[256,2048]{1,0:T(8,128)(2,1)} %get-tuple-element.75.refs_2_, bf16[2048,1536]{1,0:T(8,128)(2,1)} %get-tuple-element.76.refs_1_), kind=kOutput, calls=%fused_computation.65 | convolution fusion | flops 1610612736 | bytes 8912896 | tf_op jit(solution)/shard_map/dot_general | solution.py:23
  83.0 21.7 %attention_forward.1 = (bf16[256,512]{1,0:T(8,128)(2,1)}, bf16[256,512]{1,0:T(8,128)(2,1)}, bf16[1024,1024]{1,0:T(8,128)(2,1)}) custom-call(f32[256,1536]{1,0:T(8,128)} %fusion.26.prj, f32[256,128]{1,0:T(8,128)} %pad_maximum_fusion.1.cs.refs_4_, f32[256,128]{1,0:T(8,128)} %get-tuple-element.137.sn), custom_call_target="tpu_custom_call" | custom-call | tf_op jit(solution)/shard_map/attention_forward/pallas_call | solution.py:294
  104.7 3.5 convolution_convert_fusion.4.prt
  108.2 2.3 convolution_convert_fusion.2.slb
  111.2 74.1 %second_norm.1 = (f32[256,512]{1,0:T(8,128)}, f32[256,128]{1,0:T(8,128)}, bf16[256,2048]{1,0:T(8,128)(2,1)}, bf16[640,2048]{1,0:T(8,128)(2,1)}, bf16[640,2048]{1...) custom-call(bf16[256,2048]{1,0:T(8,128)(2,1)} %convolution_convert_fusion.4.prt, ...), custom_call_target="tpu_custom_call" | custom-call | tf_op jit(solution)/shard_map/second_norm/pallas_call | solution.py:294
  186.1 3.7 multiply_convert_fusion.refs_7_
  189.8 19.0 %expert_acts.1 = (f32[640,1408]{1,0:T(8,128)}, f32[640,1408]{1,0:T(8,128)}, bf16[640,1408]{1,0:T(8,128)(2,1)}) custom-call(bf16[640,2048]{1,0:T(8,128)(2,1)} %get-tuple-element.82.tok.refs_9_.refs_11_, bf16[1024,1408]{1,0:T(8,128)(2,1)} %copy-done.1, bf16[1024,1408]{1,0:T(8,128)(2,1)} %collective-permute-done.2.refs_1_.refs_4_, ...), custom_call_target="tpu_custom_call" | custom-call | tf_op jit(solution)/shard_map/expert_acts/pallas_call | solution.py:690
  208.8 5.6 %convolution_convert_fusion.1 = bf16[1024,1408]{1,0:T(8,128)(2,1)} fusion(bf16[640,1408]{1,0:T(8,128)(2,1)} %get-tuple-element.91.refs_2_.refs_8_, bf16[640,2048]{1,0:T(8,128)(2,1)S(1)} %copy-done.4, s32[]{:T(128)S(6)} %select_n.56), kind=kOutput, calls=%fused_computation.2 | convolution fusion | flops 1846935552 | bytes 5996548 | tf_op jit(solution)/shard_map/dot_general | solution.py:31
  215.2 2.2 fusion.2
  217.4 4.2 convolution_add_fusion
  221.9 2.1 multiply_convert_fusion.1
  224.0 3.9 convolution_convert_fusion
  227.9 1.3 collective-permute-start.6
  229.9 55.2 %second_norm_back.1 = (f32[256,512]{1,0:T(8,128)}, bf16[256,512]{1,0:T(8,128)(2,1)}, f32[8,512]{1,0:T(8,128)}, f32[8,256]{1,0:T(8,128)}, bf16[640,2048]{1,0:T(8,128)(2,1)}, /*index=5*/bf16[1024,1408]{1,0:T(8,128)(2,1)}) custom-call(bf16[640,1408]{1,0:T(8,128)(2,1)} %copy-done.2, bf16[640,1408]{1,0:T(8,128)(2,1)} %get-tuple-element.90.refs_1_.refs_12_, ...), custom_call_target="tpu_custom_call" | custom-call | tf_op jit(solution)/shard_map/second_norm_back/pallas_call | solution.py:294
  286.7 1.1 fusion.6
  287.8 51.3 %attention_backward.1 = (bf16[256,2048]{1,0:T(8,128)(2,1)}, bf16[256,1536]{1,0:T(8,128)(2,1)}, bf16[160,512]{1,0:T(8,128)(2,1)}, bf16[3,256,1408]{2,1,0:T(8,128)(2,1)}, bf16[256,1408]{1,0:T(8,128)(2,1)}) custom-call(bf16[256,512]{1,0:T(8,128)(2,1)} %get-tuple-element.95.refs_0_, bf16[2048,512]{1,0:T(8,128)(2,1)} %get-tuple-element.78.refs_1_, ...), custom_call_target="tpu_custom_call" | custom-call | tf_op jit(solution)/shard_map/attention_backward/pallas_call | solution.py:294
  339.1 3.3 convolution_convert_fusion.3
  343.0 56.8 %first_norm_back.1 = (f32[256,512]{1,0:T(8,128)}, f32[8,512]{1,0:T(8,128)}, bf16[160,512]{1,0:T(8,128)(2,1)}, bf16[160,512]{1,0:T(8,128)(2,1)}, bf16[256,512]{1,...) custom-call(bf16[256,1536]{1,0:T(8,128)(2,1)} %get-tuple-element.99.refs_0_.refs_3_, ...), custom_call_target="tpu_custom_call" | custom-call | tf_op jit(solution)/shard_map/first_norm_back/pallas_call | solution.py:294
  400.6 6.5 %write_out.2 = (f32[4,256,1408]{2,1,0:T(8,128)}, f32[4,256,1408]{2,1,0:T(8,128)}) custom-call(bf16[3,256,1408]{2,1,0:T(8,128)(2,1)} %get-tuple-element.110.refs_0_, bf16[256,1408]{1,0:T(8,128)(2,1)} %get-tuple-element.111.refs_1_, bf16[3,256,1408]{2,1,0:T(8,128)(2,1)} %get-tuple-element.112.refs_2_, bf16[256,1408]{1,0:T(8,128)(2,1)} %get-tuple-element.113.refs_3_), custom_call_target="tpu_custom_call" | custom-call | bytes 17301504 | tf_op jit(solution)/shard_map/write_out/pallas_call | solution.py:1568
  407.7 1.6 copy-done.8
  409.3 62.8 %weight_grads.1 = (f32[256,2048]{1,0:T(8,128)}, f32[8,256]{1,0:T(8,128)}, bf16[256,512]{1,0:T(8,128)(2,1)}, bf16[3,256,1408]{2,1,0:T(8,128)(2,1)}, bf16[256,1408]{1,0:T(8,128)(2,1)}) custom-call(bf16[256,512]{1,0:T(8,128)(2,1)} %get-tuple-element.104.refs_0_, f32[256,512]{1,0:T(8,128)} %get-tuple-element.105.refs_1_, ...), custom_call_target="tpu_custom_call" | custom-call | tf_op jit(solution)/shard_map/weight_grads/pallas_call | solution.py:294
  472.1 1.3 slice_bitcast_fusion
  473.4 5.4 %write_out.3 = (f32[4,256,1408]{2,1,0:T(8,128)}, bf16[256,512]{1,0:T(8,128)(2,1)}, f32[256,512]{1,0:T(8,128)}, f32[256,512]{1,0:T(8,128)}, f32[256,512]{1,0:T(8,...) custom-call(f32[8,256]{1,0:T(8,128)} %get-tuple-element.121.refs_0_, ...), custom_call_target="tpu_custom_call" | custom-call | bytes 8650752 | tf_op jit(solution)/shard_map/write_out/pallas_call | solution.py:1568
  (82 shorter events, 13.3 us)
Async XLA Ops:
  0.6 6.2 %copy-start.15 = (bf16[1024]{0:T(1024)(128)(2,1)S(1)}, bf16[1024]{0:T(1024)(128)(2,1)}, u32[]{:S(2)}) copy-start(bf16[1024]{0:T(1024)(128)(2,1)} %param.15) | copy-start | bytes 6148
  0.7 6.2 %copy-start.16 = (bf16[1024]{0:T(1024)(128)(2,1)S(1)}, bf16[1024]{0:T(1024)(128)(2,1)}, u32[]{:S(2)}) copy-start(bf16[1024]{0:T(1024)(128)(2,1)} %param.20) | copy-start | bytes 6148
  0.7 6.3 %copy-start.13 = (bf16[1024,4]{0,1:T(4,128)(2,1)S(1)}, bf16[1024,4]{0,1:T(4,128)(2,1)}, u32[]{:S(2)}) copy-start(bf16[1024,4]{0,1:T(4,128)(2,1)} %param.21) | copy-start | bytes 24580
  3.9 37.7 %collective-permute-start.1 = (bf16[256,2048]{1,0:T(8,128)(2,1)}, bf16[256,2048]{1,0:T(8,128)(2,1)}, u32[]{:S(2)}, u32[]{:S(2)}) collective-permute-start(bf16[256,2048]{1,0:T(8,128)(2,1)} %pad_maximum_fusion), channel_id=1, source_target_pairs={{0,16},{16,0},{1,17},{17,1},{2,18},{18,2},{3,19},{19,3},{4,20},{20... | collective-permute-start | bytes 3145736 | tf_op jit(solution)/shard_map/ppermute | solution.py:1615
  7.1 33.7 %collective-permute-start = (bf16[8,1024]{1,0:T(8,128)(2,1)S(1)}, bf16[8,1024]{1,0:T(8,128)(2,1)S(1)}, u32[]{:S(2)}, u32[]{:S(2)}) collective-permute-start(bf16[8,1024]{1,0:T(8,128)(2,1)S(1)} %maximum_maximum_fusion), channel_id=1, source_target_pairs={{0,16},{16,0},{1,17},{17,1},{2,18},{18,2},{3,19},{19,3},{4,20},{20... | collective-permute-start | bytes 49160 | tf_op jit(solution)/shard_map/ppermute | solution.py:1615
  9.1 24.8 %copy-start.1 = (bf16[1024,1408]{1,0:T(8,128)(2,1)}, bf16[1024,1408]{1,0:T(8,128)(2,1)S(1)}, u32[]{:S(2)}) copy-start(bf16[1024,1408]{1,0:T(8,128)(2,1)S(1)} %dynamic-slice_bitcast_fusion.refs_0_.refs_3_) | copy-start | bytes 8650756
  9.1 27.0 %copy-start.14 = (s32[256,2]{0,1:T(2,128)S(1)}, s32[256,2]{0,1:T(2,128)}, u32[]{:S(2)}) copy-start(s32[256,2]{0,1:T(2,128)} %param.25) | copy-start | bytes 6148
  9.1 180.7 %collective-permute-start.2 = (bf16[1024,1408]{1,0:T(8,128)(2,1)S(1)}, bf16[1024,1408]{1,0:T(8,128)(2,1)}, u32[]{:S(2)}, u32[]{:S(2)}) collective-permute-start(bf16[1024,1408]{1,0:T(8,128)(2,1)S(1)} %dynamic-slice_bitcast_fusion.refs_0_.refs_3_), channel_id=1, source_target_pairs={{0,16},{16,0},{1,17},{17,1},{2,18},{18,2},{3,19},{19,3},{4,20},{20... | collective-permute-start | bytes 8650760 | tf_op jit(solution)/shard_map/ppermute | solution.py:1615
  34.0 155.8 %collective-permute-start.3 = (bf16[1024,1408]{1,0:T(8,128)(2,1)}, bf16[1024,1408]{1,0:T(8,128)(2,1)}, u32[]{:S(2)}, u32[]{:S(2)}) collective-permute-start(bf16[1024,1408]{1,0:T(8,128)(2,1)} %get-tuple-element.83.refs_2_.refs_5_), channel_id=1, source_target_pairs={{0,16},{16,0},{1,17},{17,1},{2,18},{18,2},{3,19},{19,3},{4,20},{20... | collective-permute-start | bytes 8650760 | tf_op jit(solution)/shard_map/ppermute | solution.py:1615
  34.8 182.6 %collective-permute-start.4 = (bf16[1024,1408]{1,0:T(8,128)(2,1)}, bf16[1024,1408]{1,0:T(8,128)(2,1)}, u32[]{:S(2)}, u32[]{:S(2)}) collective-permute-start(bf16[1024,1408]{1,0:T(8,128)(2,1)} %get-tuple-element.86.refs_7_), channel_id=1, source_target_pairs={{0,16},{16,0},{1,17},{17,1},{2,18},{18,2},{3,19},{19,3},{4,20},{20... | collective-permute-start | bytes 8650760 | tf_op jit(solution)/shard_map/ppermute | solution.py:1615
  40.9 0.8 copy-start.12
  104.7 3.5 copy-start.10
  189.8 19.0 %copy-start.4 = (bf16[640,2048]{1,0:T(8,128)(2,1)S(1)}, bf16[640,2048]{1,0:T(8,128)(2,1)}, u32[]{:S(2)}) copy-start(bf16[640,2048]{1,0:T(8,128)(2,1)} %multiply_convert_fusion.refs_7_) | copy-start | bytes 7864324
  208.8 6.4 %copy-start.7 = (bf16[1024,1408]{1,0:T(8,128)(2,1)S(1)}, bf16[1024,1408]{1,0:T(8,128)(2,1)}, u32[]{:S(2)}) copy-start(bf16[1024,1408]{1,0:T(8,128)(2,1)} %get-tuple-element.86.refs_7_) | copy-start | bytes 8650756
  208.8 6.3 %copy-start.9 = (bf16[640,2048]{1,0:T(8,128)(2,1)S(1)}, bf16[640,2048]{1,0:T(8,128)(2,1)}, u32[]{:S(2)}) copy-start(bf16[640,2048]{1,0:T(8,128)(2,1)} %get-tuple-element.85) | copy-start | bytes 7864324
  214.4 73.4 %collective-permute-start.5 = (bf16[1024,1408]{1,0:T(8,128)(2,1)}, bf16[1024,1408]{1,0:T(8,128)(2,1)}, u32[]{:S(2)}, u32[]{:S(2)}) collective-permute-start(bf16[1024,1408]{1,0:T(8,128)(2,1)} %convolution_convert_fusion.1), channel_id=1, source_target_pairs={{0,16},{16,0},{1,17},{17,1},{2,18},{18,2},{3,19},{19,3},{4,20},{20... | collective-permute-start | bytes 8650760 | tf_op jit(solution)/shard_map/ppermute | solution.py:1615
  217.4 4.3 copy-start.3
  217.4 4.3 copy-start.5
  217.4 4.5 copy-start.6
  221.9 2.1 copy-start
  224.0 4.0 copy-start.2
  227.9 114.5 %collective-permute-start.6 = (bf16[1024,1408]{1,0:T(8,128)(2,1)}, bf16[1024,1408]{1,0:T(8,128)(2,1)}, u32[]{:S(2)}, u32[]{:S(2)}) collective-permute-start(bf16[1024,1408]{1,0:T(8,128)(2,1)} %convolution_convert_fusion), channel_id=1, source_target_pairs={{0,16},{16,0},{1,17},{17,1},{2,18},{18,2},{3,19},{19,3},{4,20},{20... | collective-permute-start | bytes 8650760 | tf_op jit(solution)/shard_map/ppermute | solution.py:1615
  285.2 122.5 %collective-permute-start.7 = (bf16[1024,1408]{1,0:T(8,128)(2,1)}, bf16[1024,1408]{1,0:T(8,128)(2,1)S(1)}, u32[]{:S(2)}, u32[]{:S(2)}) collective-permute-start(bf16[1024,1408]{1,0:T(8,128)(2,1)} %get-tuple-element.120), channel_id=1, source_target_pairs={{0,16},{16,0},{1,17},{17,1},{2,18},{18,2},{3,19},{19,3},{4,20},{20... | collective-permute-start | bytes 8650760 | tf_op jit(solution)/shard_map/ppermute | solution.py:1615
  287.8 51.3 %copy-start.11 = (bf16[256,512]{1,0:T(8,128)(2,1)S(1)}, bf16[256,512]{1,0:T(8,128)(2,1)}, u32[]{:S(2)}) copy-start(bf16[256,512]{1,0:T(8,128)(2,1)} %get-tuple-element.77) | copy-start | bytes 786436
  407.7 1.6 copy-start.8

commit v14 on v13

--- a/solution.py
+++ b/solution.py
@@ -1425,7 +1425,7 @@
             lasts.append(
                 remote(one, last, sems[8 + 6 * g : 10 + 6 * g], 0, {"ctx": across})
             )
-            if g == 0:
+            if g == 1:
                 experts_out.give_back()
         finish(totals)
         sums = sml_full[:, columns(place, cut)]

time: 480 us -> 480 us (level)
  no operation moved by 1% of the time
where the time goes in v14:
time: 480 us; the launch traced here: 478 us
  Pallas kernels  410 us (85%)
  matrix products  32.4 us (7%)
  local copies, waits for them, and re-layouts  13.2 us (3%)
  other arithmetic  11.6 us (2%)
  starting transfers between devices  9.94 us (2%)
    pallas_call x8, Pallas kernels, call(): pl.pallas_call(kernel, out_shape=out_shape, in_specs=[anywhere if i in le...  379 us
    pallas_call x1, Pallas kernels, expert_acts(): pl.pallas_call(kernel, out_shape=(shape((rows, hidden), F32), shape((rows...  19 us
    dot_general x6, matrix products, mm(): return jnp.dot(left, right, preferred_element_type=F32)  16.1 us
    dot_general x3, matrix products, t_mm(): lax.dot_general(left, right, (((0,), (0,)), ((), ())), preferred_element_...  12.8 us
    pallas_call x2, Pallas kernels, write_out(): pl.pallas_call(kernel, grid=(steps,), in_specs=in_specs, out_specs=out_sp...  11.9 us
    ppermute x8, starting transfers between devices, swap_fsdp(): return lax.ppermute(value, 'fsdp', [(0, 1), (1, 0)])  9.94 us
  transfers between devices with their start and end apart: 8, of which 0 were waited for; matrix products, arithmetic and copies ran while one was open for 11% of the time, Pallas kernels for 72%

profile of v14, /device:TPU:0, one launch (start us, length us, event | category | flops | bytes accessed | tf_op | source)
XLA Modules:
  0.0 478.5 jit_solution(17740094852367952792)
XLA Ops:
  0.7 1.1 constant_dynamic-slice_fusion.1
  1.8 1.1 constant_dynamic-slice_fusion.3
  2.8 1.1 pad_maximum_fusion
  3.9 2.9 collective-permute-start.1
  7.1 2.0 dynamic-slice_bitcast_fusion.refs_0_.refs_3_
  9.1 2.1 collective-permute-start.2
  11.2 22.7 %gather_tp.1 = (bf16[256,2048]{1,0:T(8,128)(2,1)}, bf16[1024,1408]{1,0:T(8,128)(2,1)}, bf16[1024,1408]{1,0:T(8,128)(2,1)}) custom-call(bf16[256,512]{1,0:T(8,128)(2,1)} %refs_2_.1, bf16[4,1024,1408]{2,1,0:T(8,128)(2,1)} %refs_0_.1, bf16[4,1024,1408]{2,1,0:T(8,128)(2,1)} %refs_1_.2), custom_call_target="tpu_custom_call" | custom-call | tf_op jit(solution)/shard_map/gather_tp/pallas_call | solution.py:294
  34.8 1.3 collective-permute-start.4
  41.7 35.3 %first_norm.1 = (bf16[256,2048]{1,0:T(8,128)(2,1)}, f32[256,128]{1,0:T(8,128)}, bf16[256,2048]{1,0:T(8,128)(2,1)}, bf16[2048,1536]{1,0:T(8,128)(2,1)}, bf16[2048,512]{1,0:T(8,128)(2,1)}) custom-call(bf16[256,2048]{1,0:T(8,128)(2,1)} %get-tuple-element.74.refs_0_, bf16[256,512]{1,0:T(8,128)(2,1)} %refs_19_.1, f32[8,2048]{1,0:T(8,128)} %copy-done.12, ...), custom_call_target="tpu_custom_call" | custom-call | tf_op jit(solution)/shard_map/first_norm/pallas_call | solution.py:294
  77.0 6.1 %fusion.26.prj = f32[256,1536]{1,0:T(8,128)} fusion(bf16[256,2048]{1,0:T(8,128)(2,1)} %get-tuple-element.75.refs_2_, bf16[2048,1536]{1,0:T(8,128)(2,1)} %get-tuple-element.76.refs_1_), kind=kOutput, calls=%fused_computation.65 | convolution fusion | flops 1610612736 | bytes 8912896 | tf_op jit(solution)/shard_map/dot_general | solution.py:23
  83.0 21.7 %attention_forward.1 = (bf16[256,512]{1,0:T(8,128)(2,1)}, bf16[256,512]{1,0:T(8,128)(2,1)}, bf16[1024,1024]{1,0:T(8,128)(2,1)}) custom-call(f32[256,1536]{1,0:T(8,128)} %fusion.26.prj, f32[256,128]{1,0:T(8,128)} %pad_maximum_fusion.1.cs.refs_4_, f32[256,128]{1,0:T(8,128)} %get-tuple-element.137.sn), custom_call_target="tpu_custom_call" | custom-call | tf_op jit(solution)/shard_map/attention_forward/pallas_call | solution.py:294
  104.7 3.5 convolution_convert_fusion.4.prt
  108.2 2.3 convolution_convert_fusion.2.slb
  111.2 74.1 %second_norm.1 = (f32[256,512]{1,0:T(8,128)}, f32[256,128]{1,0:T(8,128)}, bf16[256,2048]{1,0:T(8,128)(2,1)}, bf16[640,2048]{1,0:T(8,128)(2,1)}, bf16[640,2048]{1...) custom-call(bf16[256,2048]{1,0:T(8,128)(2,1)} %convolution_convert_fusion.4.prt, ...), custom_call_target="tpu_custom_call" | custom-call | tf_op jit(solution)/shard_map/second_norm/pallas_call | solution.py:294
  186.1 3.7 multiply_convert_fusion.refs_7_
  189.8 19.0 %expert_acts.1 = (f32[640,1408]{1,0:T(8,128)}, f32[640,1408]{1,0:T(8,128)}, bf16[640,1408]{1,0:T(8,128)(2,1)}) custom-call(bf16[640,2048]{1,0:T(8,128)(2,1)} %get-tuple-element.82.tok.refs_9_.refs_11_, bf16[1024,1408]{1,0:T(8,128)(2,1)} %copy-done.1, bf16[1024,1408]{1,0:T(8,128)(2,1)} %collective-permute-done.2.refs_1_.refs_4_, ...), custom_call_target="tpu_custom_call" | custom-call | tf_op jit(solution)/shard_map/expert_acts/pallas_call | solution.py:690
  208.8 5.6 %convolution_convert_fusion.1 = bf16[1024,1408]{1,0:T(8,128)(2,1)} fusion(bf16[640,1408]{1,0:T(8,128)(2,1)} %get-tuple-element.91.refs_2_.refs_8_, bf16[640,2048]{1,0:T(8,128)(2,1)S(1)} %copy-done.4, s32[]{:T(128)S(6)} %select_n.56), kind=kOutput, calls=%fused_computation.2 | convolution fusion | flops 1846935552 | bytes 5996548 | tf_op jit(solution)/shard_map/dot_general | solution.py:31
  215.2 2.2 fusion.2
  217.4 4.2 convolution_add_fusion
  221.9 2.1 multiply_convert_fusion.1
  224.0 3.9 convolution_convert_fusion
  227.9 1.3 collective-permute-start.6
  229.9 55.2 %second_norm_back.1 = (f32[256,512]{1,0:T(8,128)}, bf16[256,512]{1,0:T(8,128)(2,1)}, f32[8,512]{1,0:T(8,128)}, f32[8,256]{1,0:T(8,128)}, bf16[640,2048]{1,0:T(8,128)(2,1)}, /*index=5*/bf16[1024,1408]{1,0:T(8,128)(2,1)}) custom-call(bf16[640,1408]{1,0:T(8,128)(2,1)} %copy-done.2, bf16[640,1408]{1,0:T(8,128)(2,1)} %get-tuple-element.90.refs_1_.refs_12_, ...), custom_call_target="tpu_custom_call" | custom-call | tf_op jit(solution)/shard_map/second_norm_back/pallas_call | solution.py:294
  286.7 1.1 fusion.6
  287.8 51.3 %attention_backward.1 = (bf16[256,2048]{1,0:T(8,128)(2,1)}, bf16[256,1536]{1,0:T(8,128)(2,1)}, bf16[160,512]{1,0:T(8,128)(2,1)}, bf16[3,256,1408]{2,1,0:T(8,128)(2,1)}, bf16[256,1408]{1,0:T(8,128)(2,1)}) custom-call(bf16[256,512]{1,0:T(8,128)(2,1)} %get-tuple-element.95.refs_0_, bf16[2048,512]{1,0:T(8,128)(2,1)} %get-tuple-element.78.refs_1_, ...), custom_call_target="tpu_custom_call" | custom-call | tf_op jit(solution)/shard_map/attention_backward/pallas_call | solution.py:294
  339.1 3.3 convolution_convert_fusion.3
  343.0 56.8 %first_norm_back.1 = (f32[256,512]{1,0:T(8,128)}, f32[8,512]{1,0:T(8,128)}, bf16[160,512]{1,0:T(8,128)(2,1)}, bf16[160,512]{1,0:T(8,128)(2,1)}, bf16[256,512]{1,...) custom-call(bf16[256,1536]{1,0:T(8,128)(2,1)} %get-tuple-element.99.refs_0_.refs_3_, ...), custom_call_target="tpu_custom_call" | custom-call | tf_op jit(solution)/shard_map/first_norm_back/pallas_call | solution.py:294
  400.6 6.5 %write_out.2 = (f32[4,256,1408]{2,1,0:T(8,128)}, f32[4,256,1408]{2,1,0:T(8,128)}) custom-call(bf16[3,256,1408]{2,1,0:T(8,128)(2,1)} %get-tuple-element.110.refs_0_, bf16[256,1408]{1,0:T(8,128)(2,1)} %get-tuple-element.111.refs_1_, bf16[3,256,1408]{2,1,0:T(8,128)(2,1)} %get-tuple-element.112.refs_2_, bf16[256,1408]{1,0:T(8,128)(2,1)} %get-tuple-element.113.refs_3_), custom_call_target="tpu_custom_call" | custom-call | bytes 17301504 | tf_op jit(solution)/shard_map/write_out/pallas_call | solution.py:1568
  407.7 1.6 copy-done.8
  409.3 62.3 %weight_grads.1 = (f32[256,2048]{1,0:T(8,128)}, f32[8,256]{1,0:T(8,128)}, bf16[256,512]{1,0:T(8,128)(2,1)}, bf16[3,256,1408]{2,1,0:T(8,128)(2,1)}, bf16[256,1408]{1,0:T(8,128)(2,1)}) custom-call(bf16[256,512]{1,0:T(8,128)(2,1)} %get-tuple-element.104.refs_0_, f32[256,512]{1,0:T(8,128)} %get-tuple-element.105.refs_1_, ...), custom_call_target="tpu_custom_call" | custom-call | tf_op jit(solution)/shard_map/weight_grads/pallas_call | solution.py:294
  471.6 1.3 slice_bitcast_fusion
  472.8 5.4 %write_out.3 = (f32[4,256,1408]{2,1,0:T(8,128)}, bf16[256,512]{1,0:T(8,128)(2,1)}, f32[256,512]{1,0:T(8,128)}, f32[256,512]{1,0:T(8,128)}, f32[256,512]{1,0:T(8,...) custom-call(f32[8,256]{1,0:T(8,128)} %get-tuple-element.121.refs_0_, ...), custom_call_target="tpu_custom_call" | custom-call | bytes 8650752 | tf_op jit(solution)/shard_map/write_out/pallas_call | solution.py:1568
  (82 shorter events, 13.3 us)
Async XLA Ops:
  0.6 6.2 %copy-start.15 = (bf16[1024]{0:T(1024)(128)(2,1)S(1)}, bf16[1024]{0:T(1024)(128)(2,1)}, u32[]{:S(2)}) copy-start(bf16[1024]{0:T(1024)(128)(2,1)} %param.15) | copy-start | bytes 6148
  0.7 6.2 %copy-start.16 = (bf16[1024]{0:T(1024)(128)(2,1)S(1)}, bf16[1024]{0:T(1024)(128)(2,1)}, u32[]{:S(2)}) copy-start(bf16[1024]{0:T(1024)(128)(2,1)} %param.20) | copy-start | bytes 6148
  0.7 6.3 %copy-start.13 = (bf16[1024,4]{0,1:T(4,128)(2,1)S(1)}, bf16[1024,4]{0,1:T(4,128)(2,1)}, u32[]{:S(2)}) copy-start(bf16[1024,4]{0,1:T(4,128)(2,1)} %param.21) | copy-start | bytes 24580
  3.9 37.7 %collective-permute-start.1 = (bf16[256,2048]{1,0:T(8,128)(2,1)}, bf16[256,2048]{1,0:T(8,128)(2,1)}, u32[]{:S(2)}, u32[]{:S(2)}) collective-permute-start(bf16[256,2048]{1,0:T(8,128)(2,1)} %pad_maximum_fusion), channel_id=1, source_target_pairs={{0,16},{16,0},{1,17},{17,1},{2,18},{18,2},{3,19},{19,3},{4,20},{20... | collective-permute-start | bytes 3145736 | tf_op jit(solution)/shard_map/ppermute | solution.py:1615
  7.1 33.7 %collective-permute-start = (bf16[8,1024]{1,0:T(8,128)(2,1)S(1)}, bf16[8,1024]{1,0:T(8,128)(2,1)S(1)}, u32[]{:S(2)}, u32[]{:S(2)}) collective-permute-start(bf16[8,1024]{1,0:T(8,128)(2,1)S(1)} %maximum_maximum_fusion), channel_id=1, source_target_pairs={{0,16},{16,0},{1,17},{17,1},{2,18},{18,2},{3,19},{19,3},{4,20},{20... | collective-permute-start | bytes 49160 | tf_op jit(solution)/shard_map/ppermute | solution.py:1615
  9.1 24.8 %copy-start.1 = (bf16[1024,1408]{1,0:T(8,128)(2,1)}, bf16[1024,1408]{1,0:T(8,128)(2,1)S(1)}, u32[]{:S(2)}) copy-start(bf16[1024,1408]{1,0:T(8,128)(2,1)S(1)} %dynamic-slice_bitcast_fusion.refs_0_.refs_3_) | copy-start | bytes 8650756
  9.1 27.0 %copy-start.14 = (s32[256,2]{0,1:T(2,128)S(1)}, s32[256,2]{0,1:T(2,128)}, u32[]{:S(2)}) copy-start(s32[256,2]{0,1:T(2,128)} %param.25) | copy-start | bytes 6148
  9.1 180.7 %collective-permute-start.2 = (bf16[1024,1408]{1,0:T(8,128)(2,1)S(1)}, bf16[1024,1408]{1,0:T(8,128)(2,1)}, u32[]{:S(2)}, u32[]{:S(2)}) collective-permute-start(bf16[1024,1408]{1,0:T(8,128)(2,1)S(1)} %dynamic-slice_bitcast_fusion.refs_0_.refs_3_), channel_id=1, source_target_pairs={{0,16},{16,0},{1,17},{17,1},{2,18},{18,2},{3,19},{19,3},{4,20},{20... | collective-permute-start | bytes 8650760 | tf_op jit(solution)/shard_map/ppermute | solution.py:1615
  34.0 155.8 %collective-permute-start.3 = (bf16[1024,1408]{1,0:T(8,128)(2,1)}, bf16[1024,1408]{1,0:T(8,128)(2,1)}, u32[]{:S(2)}, u32[]{:S(2)}) collective-permute-start(bf16[1024,1408]{1,0:T(8,128)(2,1)} %get-tuple-element.83.refs_2_.refs_5_), channel_id=1, source_target_pairs={{0,16},{16,0},{1,17},{17,1},{2,18},{18,2},{3,19},{19,3},{4,20},{20... | collective-permute-start | bytes 8650760 | tf_op jit(solution)/shard_map/ppermute | solution.py:1615
  34.8 182.6 %collective-permute-start.4 = (bf16[1024,1408]{1,0:T(8,128)(2,1)}, bf16[1024,1408]{1,0:T(8,128)(2,1)}, u32[]{:S(2)}, u32[]{:S(2)}) collective-permute-start(bf16[1024,1408]{1,0:T(8,128)(2,1)} %get-tuple-element.86.refs_7_), channel_id=1, source_target_pairs={{0,16},{16,0},{1,17},{17,1},{2,18},{18,2},{3,19},{19,3},{4,20},{20... | collective-permute-start | bytes 8650760 | tf_op jit(solution)/shard_map/ppermute | solution.py:1615
  40.9 0.8 copy-start.12
  104.7 3.5 copy-start.10
  189.8 19.0 %copy-start.4 = (bf16[640,2048]{1,0:T(8,128)(2,1)S(1)}, bf16[640,2048]{1,0:T(8,128)(2,1)}, u32[]{:S(2)}) copy-start(bf16[640,2048]{1,0:T(8,128)(2,1)} %multiply_convert_fusion.refs_7_) | copy-start | bytes 7864324
  208.8 6.4 %copy-start.7 = (bf16[1024,1408]{1,0:T(8,128)(2,1)S(1)}, bf16[1024,1408]{1,0:T(8,128)(2,1)}, u32[]{:S(2)}) copy-start(bf16[1024,1408]{1,0:T(8,128)(2,1)} %get-tuple-element.86.refs_7_) | copy-start | bytes 8650756
  208.8 6.3 %copy-start.9 = (bf16[640,2048]{1,0:T(8,128)(2,1)S(1)}, bf16[640,2048]{1,0:T(8,128)(2,1)}, u32[]{:S(2)}) copy-start(bf16[640,2048]{1,0:T(8,128)(2,1)} %get-tuple-element.85) | copy-start | bytes 7864324
  214.4 73.4 %collective-permute-start.5 = (bf16[1024,1408]{1,0:T(8,128)(2,1)}, bf16[1024,1408]{1,0:T(8,128)(2,1)}, u32[]{:S(2)}, u32[]{:S(2)}) collective-permute-start(bf16[1024,1408]{1,0:T(8,128)(2,1)} %convolution_convert_fusion.1), channel_id=1, source_target_pairs={{0,16},{16,0},{1,17},{17,1},{2,18},{18,2},{3,19},{19,3},{4,20},{20... | collective-permute-start | bytes 8650760 | tf_op jit(solution)/shard_map/ppermute | solution.py:1615
  217.4 4.3 copy-start.3
  217.4 4.3 copy-start.5
  217.4 4.5 copy-start.6
  221.9 2.1 copy-start
  224.0 4.0 copy-start.2
  227.9 114.5 %collective-permute-start.6 = (bf16[1024,1408]{1,0:T(8,128)(2,1)}, bf16[1024,1408]{1,0:T(8,128)(2,1)}, u32[]{:S(2)}, u32[]{:S(2)}) collective-permute-start(bf16[1024,1408]{1,0:T(8,128)(2,1)} %convolution_convert_fusion), channel_id=1, source_target_pairs={{0,16},{16,0},{1,17},{17,1},{2,18},{18,2},{3,19},{19,3},{4,20},{20... | collective-permute-start | bytes 8650760 | tf_op jit(solution)/shard_map/ppermute | solution.py:1615
  285.2 122.5 %collective-permute-start.7 = (bf16[1024,1408]{1,0:T(8,128)(2,1)}, bf16[1024,1408]{1,0:T(8,128)(2,1)S(1)}, u32[]{:S(2)}, u32[]{:S(2)}) collective-permute-start(bf16[1024,1408]{1,0:T(8,128)(2,1)} %get-tuple-element.120), channel_id=1, source_target_pairs={{0,16},{16,0},{1,17},{17,1},{2,18},{18,2},{3,19},{19,3},{4,20},{20... | collective-permute-start | bytes 8650760 | tf_op jit(solution)/shard_map/ppermute | solution.py:1615
  287.8 51.3 %copy-start.11 = (bf16[256,512]{1,0:T(8,128)(2,1)S(1)}, bf16[256,512]{1,0:T(8,128)(2,1)}, u32[]{:S(2)}) copy-start(bf16[256,512]{1,0:T(8,128)(2,1)} %get-tuple-element.77) | copy-start | bytes 786436
  407.7 1.6 copy-start.8
